TPU v7x, 32 devices: a whole 2x2x4 slice. The times are simulated.
32 devices in a mesh: grp: 2 (over x), seq: 16 (over z, y, core).
Axes of the slice: x: 2, y: 2, z: 4, core: 2. Of those that a mesh axis runs over, the one named last changes fastest.
Arguments:
- queries: bfloat16 [6144, 4096], P(('grp', 'seq')), parts along dimension 0, may hold values from -6 to 6
- keys: bfloat16 [6144, 4096], P(('grp', 'seq')), parts along dimension 0, may hold values from -6 to 6
- values: bfloat16 [6144, 4096], P(('grp', 'seq')), parts along dimension 0, may hold values from -6 to 6
- latent_in: float32 [6144, 64], P(('grp', 'seq')), parts along dimension 0, may hold values from -6 to 6
- mod_table: float32 [16, 2, 4096], replicated, may hold values from -3 to 3
- step_size: float32 [16], replicated, may hold values from 0.25 to 1
- timestep: int32 [64], P('grp'), parts along dimension 0, may hold values from 0 to 15
- head_weight: float32 [4096, 64], replicated, may hold values from -0.09375 to 0.09375
- conv_in_weight: bfloat16 [27, 16, 384], replicated, may hold values from -0.3125 to 0.3125
- conv_in_bias: float32 [384], replicated, may hold values from -3 to 3
- norm_gain: float32 [384], replicated, may hold values from 0.1 to 1.9
- conv_weight: bfloat16 [27, 384, 384], replicated, may hold values from -0.0625 to 0.0625
- conv_bias: float32 [384], replicated, may hold values from -3 to 3
- patch_weight: bfloat16 [1536, 1024], replicated, may hold values from -0.15625 to 0.15625
- patch_gain: float32 [1024], replicated, may hold values from 0.1 to 1.9
- post_gain: float32 [1024], replicated, may hold values from 0.1 to 1.9
- proj_weight: float32 [1024, 768], replicated, may hold values from -0.1875 to 0.1875
- text_table: bfloat16 [24704, 768], P(None, 'seq'), may hold values from -6 to 6
- prompt_ids: int32 [154], P('grp'), parts along dimension 0, may hold values from 0 to 24703
- frame_order: int32 [64], P('grp'), parts along dimension 0, may hold values from 0 to 31, each once
Outputs:
- latent_next: float32 [6144, 64], P(('grp', 'seq')), parts along dimension 0
- decoded: bfloat16 [64, 16, 24, 384], P(('grp', 'seq')), parts along dimension 0
- image_embed: float32 [64, 768], P(('grp', 'seq')), parts along dimension 0
- scores: float32 [64], P(('grp', 'seq')), parts along dimension 0
There are 2 independent parts, one for each index of `grp`. A program takes and returns all parts, laid end to end along the dimension named above; an argument that names none is the same for every part. Nothing has to cross between parts.
All inputs are finite; a program needn't handle non-finite values.
Results may differ from a plain program's by a relative error of at most 0.009.
Values may be sent and summed in bfloat16 or wider, within the bound.
No kernel may reach another device: no remote copies, remote signals or barrier semaphores. Data moves between devices by JAX's collectives and lax.ppermute only.
A program may use at most 128 MiB of HBM per device.

v0:
```python
import functools

import jax
import jax.numpy as jnp
import numpy as np
from jax import lax
from jax.experimental import pallas as pl
from jax.experimental.pallas import tpu as pltpu
from jax.sharding import PartitionSpec as P

GRID_H = 8
GRID_W = 12
PATCH = GRID_H * GRID_W
HD = 128
LAT = 64
LAT_C = 16
CH = 384
TEXT_W = 768
KEY_CHUNK = 512


highest = lax.Precision.HIGHEST
VM = pl.BlockSpec(memory_space=pltpu.VMEM)
SM = pl.BlockSpec(memory_space=pltpu.SMEM)
ANY = pl.BlockSpec(memory_space=pl.ANY)


def shifted(value, axis, steps):
    count = lax.axis_size(axis)
    initial, last = (max(0, -steps), min(count, count - steps))
    return lax.ppermute(value, axis, [(source, source + steps) for source in range(initial, last)])


def rotate(value, axis, steps):
    count = lax.axis_size(axis)
    return lax.ppermute(value, axis, [(i, (i + 2 * steps) % count) for i in range(count)])


def swap_core(value, axis):
    count = lax.axis_size(axis)
    return lax.ppermute(value, axis, [(i, i ^ 1) for i in range(count)])


def pack_kernel(blocks, at_ref, k_hbm, v_hbm, q_hbm, *refs):
    out_refs, (buf, in_sem, out_sem) = refs[:blocks], refs[blocks:]
    width = buf.shape[3]
    gets = []
    for n in range(blocks):
        at = pl.multiple_of(at_ref[n], HD)
        gets.append(
            [
                pltpu.make_async_copy(src.at[:, pl.ds(at, width)], buf.at[n, i], in_sem.at[n, i])
                for i, src in enumerate((k_hbm, v_hbm, q_hbm))
            ]
        )
        for get in gets[-1]:
            get.start()
    puts = [
        pltpu.make_async_copy(buf.at[n], out_refs[n], out_sem.at[n]) for n in range(blocks)
    ]
    for n in range(blocks):
        for get in gets[n]:
            get.wait()
        puts[n].start()
    for put in puts:
        put.wait()


def pack(keys, values, queries, starts, width):
    rows, blocks = keys.shape[0], starts.shape[0]
    return pl.pallas_call(
        functools.partial(pack_kernel, blocks),
        out_shape=[jax.ShapeDtypeStruct((3, rows, width), jnp.bfloat16)] * blocks,
        in_specs=[SM, ANY, ANY, ANY],
        out_specs=[ANY] * blocks,
        scratch_shapes=[
            pltpu.VMEM((blocks, 3, rows, width), jnp.bfloat16),
            pltpu.SemaphoreType.DMA((blocks, 3)),
            pltpu.SemaphoreType.DMA((blocks,)),
        ],
        name="pack",
    )(starts, keys, values, queries)


def attend_kernel(blocks, heads, frames, resumed, last, t_ref, sc_ref, w_ref, *refs):
    if resumed:
        prev_ref, refs = refs[0], refs[1:]
    near_refs, far_refs, refs = refs[:blocks], refs[blocks : 2 * blocks], refs[2 * blocks :]
    if last:
        out_refs, refs = refs[:blocks], refs[blocks:]
    else:
        sum_ref, refs = refs[0], refs[1:]
    q_s, k_s, v_s, s_a, s_b, m_a, m_b, acc_s, tot_s, sem, q_sem = refs[:11]
    if last:
        sum_ref = refs[11]
    sources = near_refs + far_refs
    rows = near_refs[0].shape[1]
    keys = len(sources) * rows
    scale = np.float32(HD**-0.5 * np.log2(np.e))

    def fetch(h, which):
        dst = (k_s, v_s)[which]
        for j, src in enumerate(sources):
            pltpu.make_async_copy(
                src.at[which, :, pl.ds(h * HD, HD)],
                dst.at[h, pl.ds(j * rows, rows), :],
                sem.at[h, which],
            ).start()

    fetch(0, 0)
    for b in range(blocks):
        pltpu.make_async_copy(near_refs[b].at[2], q_s.at[b], q_sem).start()
    fetch(0, 1)
    for h in range(1, heads):
        fetch(h, 0)
        fetch(h, 1)
    if resumed:
        sum_ref[...] = prev_ref[...]
    else:
        sum_ref[...] = jnp.zeros(sum_ref.shape, jnp.float32)

    def arrived(h, which):
        whole = (k_s, v_s)[which].at[h]
        pltpu.make_async_copy(whole, whole, sem.at[h, which]).wait()

    def logits(h, b, at, s_ref, peak):
        q = q_s[b, :, pl.ds(pl.multiple_of(h * HD, HD), HD)]
        s = lax.dot_general(
            q,
            k_s[h, at : at + KEY_CHUNK, :],
            (((1,), (1,)), ((), ())),
            preferred_element_type=jnp.float32,
        )
        s_ref[:, at : at + KEY_CHUNK] = s
        folded = functools.reduce(
            jnp.maximum, [s[:, i : i + 128] for i in range(0, KEY_CHUNK, 128)]
        )
        return folded if peak is None else jnp.maximum(peak, folded)

    def keep_peak(peak, m_ref):
        m_ref[...] = jnp.broadcast_to(jnp.max(peak, axis=-1, keepdims=True) * scale, m_ref.shape)

    def finish(h, b, acc, total):
        o = acc / jnp.sum(total, axis=-1, keepdims=True)
        o = o.astype(jnp.bfloat16).astype(jnp.float32)
        square = jnp.sum(o * o, axis=-1, keepdims=True)
        per = rows // frames
        scaled = jnp.concatenate(
            [
                o[f * per : (f + 1) * per] * (1.0 + sc_ref[t_ref[b * frames + f], h])
                for f in range(frames)
            ],
            axis=0,
        )
        part = jnp.dot(scaled, w_ref[h], precision=highest, preferred_element_type=jnp.float32)
        lane = lax.broadcasted_iota(jnp.int32, part.shape, 1)
        return part + jnp.where(lane >= LAT, square, 0.0)

    def one_unit(h, now, top_ref, next_h, next_b, later, later_top_ref):
        top = top_ref[:, :1]
        peak, total = None, None
        acc = jnp.zeros((rows, HD), jnp.float32)
        for at in chunks:
            peak = logits(next_h, next_b, at, later, peak)
            e = jnp.exp2(now[:, at : at + KEY_CHUNK] * scale - top)
            folded = functools.reduce(jnp.add, [e[:, i : i + 128] for i in range(0, KEY_CHUNK, 128)])
            total = folded if total is None else total + folded
            acc = acc + jnp.dot(
                e.astype(jnp.bfloat16),
                v_s[h, at : at + KEY_CHUNK, :],
                preferred_element_type=jnp.float32,
            )
        keep_peak(peak, later_top_ref)
        return acc, total

    chunks = range(0, keys, KEY_CHUNK)
    pltpu.make_async_copy(q_s, q_s, q_sem).wait()
    arrived(0, 0)
    peak = None
    for at in chunks:
        peak = logits(0, 0, at, s_a, peak)
    keep_peak(peak, m_a)
    pairs = blocks // 2
    acc_s[...] = jnp.zeros(acc_s.shape, jnp.float32)
    tot_s[...] = jnp.ones(tot_s.shape, jnp.float32)

    def one_pair(n, carry):
        h, p = n // pairs, n % pairs
        after = jnp.minimum(n + 1, heads * pairs - 1)
        after_h, after_p = after // pairs, after % pairs
        before = jnp.maximum(n - 1, 0)
        before_h, before_p = before // pairs, before % pairs

        @pl.when(p == 0)
        def _():
            arrived(h, 1)

        @pl.when(after_h > h)
        def _():
            arrived(after_h, 0)

        late = finish(before_h, 2 * before_p + 1, acc_s[...], tot_s[...])
        sum_ref[2 * before_p + 1] = sum_ref[2 * before_p + 1] + late
        even = one_unit(h, s_a, m_a, h, 2 * p + 1, s_b, m_b)
        sum_ref[2 * p] = sum_ref[2 * p] + finish(h, 2 * p, *even)
        acc, total = one_unit(h, s_b, m_b, after_h, 2 * after_p, s_a, m_a)
        acc_s[...] = acc
        tot_s[...] = total
        return carry

    lax.fori_loop(0, heads * pairs, one_pair, 0)
    sum_ref[blocks - 1] = sum_ref[blocks - 1] + finish(
        heads - 1, blocks - 1, acc_s[...], tot_s[...]
    )
    if last:
        for b in range(blocks):
            share = sum_ref[b]
            high = share.astype(jnp.bfloat16)
            rest = (share - high.astype(jnp.float32)).astype(jnp.bfloat16)
            lane = lax.broadcasted_iota(jnp.int32, share.shape, 1)
            out_refs[b][...] = jnp.where(lane < 3 * LAT // 2, high, rest)


def attend(near, far, steps, scale, weight, previous, last):
    blocks = len(near)
    _, rows, cols = near[0].shape
    heads, keys = cols // HD, 2 * blocks * rows
    frames = rows // PATCH
    resumed = previous is not None
    sums = (blocks, rows, 128)
    if last:
        out_shape = [jax.ShapeDtypeStruct(sums[1:], jnp.bfloat16)] * blocks
        out_specs = [VM] * blocks
    else:
        out_shape, out_specs = jax.ShapeDtypeStruct(sums, jnp.float32), VM
    return pl.pallas_call(
        functools.partial(attend_kernel, blocks, heads, frames, resumed, last),
        out_shape=out_shape,
        in_specs=[SM, VM, VM] + [VM] * resumed + [ANY] * (2 * blocks),
        out_specs=out_specs,
        scratch_shapes=[
            pltpu.VMEM((blocks, rows, cols), jnp.bfloat16),
            pltpu.VMEM((heads, keys, HD), jnp.bfloat16),
            pltpu.VMEM((heads, keys, HD), jnp.bfloat16),
            pltpu.VMEM((rows, keys), jnp.float32),
            pltpu.VMEM((rows, keys), jnp.float32),
            pltpu.VMEM((rows, 128), jnp.float32),
            pltpu.VMEM((rows, 128), jnp.float32),
            pltpu.VMEM((rows, HD), jnp.float32),
            pltpu.VMEM((rows, 128), jnp.float32),
            pltpu.SemaphoreType.DMA((heads, 2)),
            pltpu.SemaphoreType.DMA,
        ]
        + [pltpu.VMEM(sums, jnp.float32)] * last,
        cost_estimate=pl.CostEstimate(
            flops=4 * blocks * rows * keys * cols,
            bytes_accessed=4 * keys * cols,
            transcendentals=blocks * rows * keys * heads,
        ),
        name="attend",
    )(steps, scale, weight, *([previous] if resumed else []), *near, *far)


WINDOW = ((-1, 1), (0, 0), (0, 1), (1, 0))


OFFSETS = [(di, dj) for di in (-1, 0, 1) for dj in (-1, 0, 1)]


def one_hot(index, count):
    hit = jnp.asarray(index, jnp.int32)[..., None] == jnp.arange(count, dtype=jnp.int32)
    return hit.astype(jnp.bfloat16)


def moved(di, dj):
    seen = np.full((GRID_H, GRID_W), -1)
    for i in range(GRID_H):
        for j in range(GRID_W):
            if 0 <= i + di < GRID_H and 0 <= j + dj < GRID_W:
                seen[i, j] = (i + di) * GRID_W + j + dj
    return seen.reshape(-1)


def gather_matrices():
    move = one_hot(np.stack([moved(di, dj) for di, dj in OFFSETS], axis=1), PATCH)
    place = np.full((len(OFFSETS), 4, 4, LAT_C), -1)
    for u, (di, a) in enumerate(WINDOW):
        for w, (dj, b) in enumerate(WINDOW):
            place[OFFSETS.index((di, dj)), u, w] = (2 * a + b) * LAT_C + np.arange(LAT_C)
    source = jnp.asarray(place.reshape(1, -1), jnp.int32)
    placed = (jnp.arange(LAT, dtype=jnp.int32)[:, None] == source).astype(jnp.bfloat16)
    return move.reshape(PATCH, -1), placed


def plane_moves():
    planes = []
    for a in (0, 1):
        for b in (0, 1):
            da, db = (1, -1)[a], (1, -1)[b]
            planes.append(np.concatenate([moved(da, 0), moved(0, db), moved(da, db)]))
    return one_hot(np.stack(planes), PATCH)


def pixel_order():
    index = np.zeros((GRID_H, 2, GRID_W, 2), np.int64)
    for a in (0, 1):
        for b in (0, 1):
            index[:, a, :, b] = (2 * a + b) * PATCH + np.arange(PATCH).reshape(GRID_H, GRID_W)
    return one_hot(index.reshape(-1), 4 * PATCH)


def latent_kernel(parts, width, frames, dt_ref, *refs):
    part_refs, refs = refs[:parts], refs[parts:]
    lat_ref, base_ref, move_ref, place_ref, next_ref, win_ref = refs
    total = part_refs[0][...].astype(jnp.float32)
    for r in part_refs[1:]:
        total = total + r[...].astype(jnp.float32)
    half = LAT // 2
    square = total[:, LAT : LAT + half] + total[:, LAT + half :]
    inverse = lax.rsqrt(square * np.float32(1.0 / width) + 1e-06)
    scaled = total[:, :LAT] * jnp.concatenate([inverse, inverse], axis=1)
    for f in range(frames):
        at = slice(f * PATCH, (f + 1) * PATCH)
        value = lat_ref[at] + dt_ref[f] * (scaled[at] + base_ref[f : f + 1])
        next_ref[at] = value
        spread = jnp.dot(
            value.astype(jnp.bfloat16), place_ref[...], preferred_element_type=jnp.float32
        ).astype(jnp.bfloat16)
        cols = 16 * LAT_C
        stacked = jnp.concatenate(
            [spread[:, o * cols : (o + 1) * cols] for o in range(len(OFFSETS))], axis=0
        )
        win_ref[at] = jnp.dot(
            move_ref[...], stacked, preferred_element_type=jnp.float32
        ).astype(jnp.bfloat16)


def step_latent(parts, latent_in, base, step_dt, width, move, place):
    rows = latent_in.shape[0]
    return pl.pallas_call(
        functools.partial(latent_kernel, len(parts), width, rows // PATCH),
        out_shape=[
            jax.ShapeDtypeStruct((rows, LAT), jnp.float32),
            jax.ShapeDtypeStruct((rows, 16 * LAT_C), jnp.bfloat16),
        ],
        in_specs=[SM] + [VM] * (len(parts) + 4),
        out_specs=[VM, VM],
        name="latent",
    )(step_dt, *parts, latent_in, base, move, place)


def decode_kernel(
    frames,
    lead_ref,
    far_ref,
    near_ref,
    own_ref,
    w1_ref,
    b1_ref,
    gain_ref,
    b2_ref,
    pg_ref,
    post_ref,
    text_ref,
    moves_ref,
    order_ref,
    w2_hbm,
    pw_hbm,
    proj_hbm,
    out_ref,
    sent_ref,
    w2_s,
    pw_s,
    proj_s,
    win_s,
    x_s,
    sem,
):
    taps = 9 * CH
    w2_copy = pltpu.make_async_copy(w2_hbm, w2_s, sem.at[0])
    pw_copy = pltpu.make_async_copy(pw_hbm, pw_s, sem.at[1])
    w2_copy.start()
    pw_copy.start()
    proj_copy = pltpu.make_async_copy(proj_hbm, proj_s, sem.at[2])
    proj_copy.start()
    rows = frames * PATCH
    for n, r in enumerate((far_ref, near_ref, own_ref)):
        win_s[n * rows : (n + 1) * rows] = r[...]
    wide = frames + 2
    skip = 3 * frames - wide - 2
    cols = 16 * LAT_C
    firsts = []
    for q in range(4):
        acc = jnp.zeros((wide * PATCH, CH), jnp.float32)
        for t in range(3):
            acc = acc + jnp.dot(
                win_s[(skip + t) * PATCH : (skip + t + wide) * PATCH],
                w1_ref[t * cols : (t + 1) * cols, q * CH : (q + 1) * CH],
                preferred_element_type=jnp.float32,
            )
        first = (acc + b1_ref[...]).astype(jnp.bfloat16).astype(jnp.float32)
        firsts.append(first[2 * PATCH :])
        mean = jnp.mean(first * first, axis=-1, keepdims=True)
        v = first * lax.rsqrt(mean + 1e-06) * gain_ref[...]
        act = v / (1.0 + jnp.exp(-v))
        row = lax.broadcasted_iota(jnp.int32, (wide * PATCH, 1), 0)
        act = jnp.where((row >= 2 * PATCH) | (lead_ref[0] == 0), act, 0.0).astype(jnp.bfloat16)
        a, b = q // 2, q % 2
        for f in range(wide):
            plane = act[f * PATCH : (f + 1) * PATCH]
            moved = jnp.dot(
                moves_ref[q], plane, preferred_element_type=jnp.float32
            ).astype(jnp.bfloat16)
            pieces = {
                (0, 0): plane,
                (1, 0): moved[:PATCH],
                (0, 1): moved[PATCH : 2 * PATCH],
                (1, 1): moved[2 * PATCH :],
            }
            for (ma, mb), piece in pieces.items():
                u = WINDOW.index(((1, -1)[a] if ma else 0, a))
                w = WINDOW.index(((1, -1)[b] if mb else 0, b))
                for oa in (0, 1):
                    for ob in (0, 1):
                        dy, dz = u - oa, w - ob
                        if 0 <= dy < 3 and 0 <= dz < 3:
                            at = (f * 4 + 2 * oa + ob) * PATCH
                            tap = (3 * dy + dz) * CH
                            x_s[at : at + PATCH, tap : tap + CH] = piece
    w2_copy.wait()
    block = 4 * PATCH
    out = jnp.zeros((frames * block, CH), jnp.float32)
    for t in range(3):
        out = out + jnp.dot(
            x_s[t * block : (t + frames) * block],
            w2_s[t * taps : (t + 1) * taps],
            preferred_element_type=jnp.float32,
        )
    first = jnp.concatenate(
        [firsts[q][f * PATCH : (f + 1) * PATCH] for f in range(frames) for q in range(4)], axis=0
    )
    dec = (out + b2_ref[...] + first).astype(jnp.bfloat16)
    for f in range(frames):
        out_ref[f * block : (f + 1) * block] = jnp.dot(
            order_ref[...], dec[f * block : (f + 1) * block], preferred_element_type=jnp.float32
        ).astype(jnp.bfloat16)
    pw_copy.wait()
    emb = jnp.zeros((rows, pw_s.shape[1]), jnp.float32)
    for q in range(4):
        lhs = jnp.concatenate(
            [dec[(f * 4 + q) * PATCH : (f * 4 + q + 1) * PATCH] for f in range(frames)], axis=0
        )
        emb = emb + jnp.dot(
            lhs, pw_s[q * CH : (q + 1) * CH], preferred_element_type=jnp.float32
        )
    emb = emb.astype(jnp.bfloat16).astype(jnp.float32)
    centered = emb - jnp.mean(emb, axis=-1, keepdims=True)
    variance = jnp.mean(centered * centered, axis=-1, keepdims=True)
    normed = centered * lax.rsqrt(variance + 1e-05) * pg_ref[...]
    pooled = jnp.concatenate(
        [
            jnp.mean(normed[f * PATCH : (f + 1) * PATCH], axis=0, keepdims=True)
            for f in range(frames)
        ],
        axis=0,
    )
    centered = pooled - jnp.mean(pooled, axis=-1, keepdims=True)
    variance = jnp.mean(centered * centered, axis=-1, keepdims=True)
    vec = centered * lax.rsqrt(variance + 1e-05) * post_ref[...]
    columns = jnp.transpose(
        jnp.concatenate([vec, jnp.zeros((8 - frames, vec.shape[1]), jnp.float32)], axis=0)
    )
    proj_copy.wait()
    for f in range(frames):
        row = jnp.sum(columns[:, f : f + 1] * proj_s[...], axis=0, keepdims=True)
        for n in range(sent_ref.shape[0]):
            sent_ref[n, f : f + 1, :] = row
    for n in range(sent_ref.shape[0]):
        sent_ref[n, frames : frames + 1, :] = text_ref[...]


def window_weight(weight):
    taps = weight.reshape(3, 3, 3, LAT_C, CH)
    grown = [
        jnp.pad(taps, ((0, 0), (a, 1 - a), (b, 1 - b), (0, 0), (0, 0))).reshape(-1, CH)
        for a in (0, 1)
        for b in (0, 1)
    ]
    return jnp.concatenate(grown, axis=1)


def decode(
    lead, far, near, own, w1, b1, gain, w2, b2, pw, patch_gain, post_gain, proj, text, moves, order, devices
):
    rows = own.shape[0]
    frames = rows // PATCH
    wide = frames + 2
    return pl.pallas_call(
        functools.partial(decode_kernel, frames),
        out_shape=[
            jax.ShapeDtypeStruct((frames * 4 * PATCH, CH), jnp.bfloat16),
            jax.ShapeDtypeStruct((devices, frames + 1, proj.shape[1]), jnp.float32),
        ],
        in_specs=[SM] + [VM] * 12 + [ANY, ANY, ANY],
        out_specs=[VM, VM],
        scratch_shapes=[
            pltpu.VMEM(w2.shape, jnp.bfloat16),
            pltpu.VMEM(pw.shape, jnp.bfloat16),
            pltpu.VMEM(proj.shape, jnp.float32),
            pltpu.VMEM((3 * rows, 16 * LAT_C), jnp.bfloat16),
            pltpu.VMEM((wide * 4 * PATCH, 9 * CH), jnp.bfloat16),
            pltpu.SemaphoreType.DMA((3,)),
        ],
        name="decode",
    )(
        lead,
        far,
        near,
        own,
        w1,
        b1,
        gain,
        b2,
        patch_gain,
        post_gain,
        text,
        moves,
        order,
        w2,
        pw,
        proj,
    )


def rate_kernel(frames, slot_ref, got_ref, vec_ref, score_ref):
    text = jnp.sum(got_ref[:, frames, :], axis=0, keepdims=True)
    text_rms = jnp.sqrt(jnp.mean(text * text) + 1e-06)
    for f in range(frames):
        slot = slot_ref[f]
        block = got_ref[slot // frames]
        row = block[:1]
        for n in range(1, frames):
            row = jnp.where(slot % frames == n, block[n : n + 1], row)
        vec_ref[f : f + 1] = row
        inner = jnp.sum(row * text)
        image_rms = jnp.sqrt(jnp.mean(row * row) + 1e-06)
        score_ref[f] = 100.0 * inner / (TEXT_W * image_rms * text_rms)


def rate(slots, got):
    frames = slots.shape[0]
    return pl.pallas_call(
        functools.partial(rate_kernel, frames),
        out_shape=[
            jax.ShapeDtypeStruct((frames, got.shape[2]), jnp.float32),
            jax.ShapeDtypeStruct((frames,), jnp.float32),
        ],
        in_specs=[SM, VM],
        out_specs=[VM, SM],
        name="rate",
    )(slots, got)


def local(
    queries,
    keys,
    values,
    latent_in,
    mod_table,
    step_size,
    timestep,
    head_weight,
    conv_in_weight,
    conv_in_bias,
    norm_gain,
    conv_weight,
    conv_bias,
    patch_weight,
    patch_gain,
    post_gain,
    proj_weight,
    text_table,
    prompt_ids,
    frame_order,
):
    rows, width = queries.shape
    devices = lax.axis_size("seq")
    chips = devices // 2
    cols = width // chips
    heads = cols // HD
    frames = rows // PATCH
    me = lax.axis_index("seq")
    chip, core = me // 2, me % 2

    tail = max(1, heads // 4)
    phases = tuple(n for n in (heads - 2 * tail, tail, tail) if n > 0) if heads > tail else (tail,)
    firsts = [sum(phases[:n]) for n in range(len(phases))]

    order = sorted(range(1, chips), key=lambda t: abs(2 * t - chips))

    def packed(first, count):
        at = ((chip + jnp.arange(chips)) % chips) * cols + first * HD
        return pack(keys, values, queries, at.astype(jnp.int32), count * HD)

    blocks = packed(firsts[0], phases[0])
    got = [blocks[0]] * chips
    got[order[0]] = rotate(blocks[order[0]], "seq", order[0])
    for turn in order[1:]:
        got[turn] = rotate(blocks[turn], "seq", turn)
    move, place = gather_matrices()
    scale = lax.dynamic_slice_in_dim(mod_table[:, 1, :], chip * cols, cols, 1)
    scale = scale.reshape(-1, heads, 1, HD)
    weight = lax.dynamic_slice_in_dim(head_weight, chip * cols, cols, 0).reshape(heads, HD, LAT)
    weight = jnp.pad(weight, ((0, 0), (0, 0), (0, 128 - LAT)))
    origin = 2 * ((chip - jnp.arange(chips)) % chips) + core
    steps = jnp.take(timestep.reshape(devices, frames), origin, axis=0).reshape(-1)
    own_steps = lax.dynamic_slice_in_dim(timestep, me * frames, frames, 0)
    base = jnp.dot(jnp.take(mod_table[:, 0, :], own_steps, axis=0), head_weight, precision=highest)
    step_dt = jnp.take(step_size, own_steps)
    own_text = jnp.mean(jnp.take(text_table, prompt_ids, axis=0).astype(jnp.float32), axis=0)
    text_row = lax.dynamic_update_slice_in_dim(
        jnp.zeros((TEXT_W,), jnp.float32), own_text, me * own_text.shape[0], 0
    )
    slots = lax.dynamic_slice_in_dim(frame_order, me * frames, frames, 0)
    prepared = dict(
        scales=[scale[:, f : f + n] for f, n in zip(firsts, phases)],
        weights=[weight[f : f + n] for f, n in zip(firsts, phases)],
        steps=steps,
        base=base,
        step_dt=step_dt,
        text=text_row.reshape(1, -1),
        slots=slots,
        w1=window_weight(conv_in_weight),
        b1=conv_in_bias.reshape(1, -1),
        gain=norm_gain.reshape(1, -1),
        b2=conv_bias.reshape(1, -1),
        patch_gain=patch_gain.reshape(1, -1),
        post_gain=post_gain.reshape(1, -1),
        lead=(me == 0).astype(jnp.int32).reshape(1),
        latent_in=latent_in,
        move=move,
        place=place,
        moves=plane_moves(),
        order=pixel_order(),
        later=[packed(f, n) for f, n in zip(firsts[1:], phases[1:])],
    )
    phase_blocks = [got]
    for blocks in prepared["later"]:
        got = [blocks[0]] * chips
        for turn in order:
            got[turn] = rotate(blocks[turn], "seq", turn)
        phase_blocks.append(got)
    sums = None
    for n, got in enumerate(phase_blocks):
        if sums is not None:
            sums, *got = lax.optimization_barrier((sums, *got))
        other = [swap_core(block, "seq") for block in got]
        sums = attend(
            got,
            other,
            prepared["steps"],
            prepared["scales"][n],
            prepared["weights"][n],
            sums,
            n + 1 == len(phase_blocks),
        )
    parts = [sums[0]] + [rotate(sums[t], "seq", chips - t) for t in order]

    latent_next, window = step_latent(
        parts,
        prepared["latent_in"],
        prepared["base"],
        prepared["step_dt"],
        width,
        prepared["move"],
        prepared["place"],
    )
    near = shifted(window, "seq", 1)
    far = shifted(window, "seq", 2)
    decoded, sent = decode(
        prepared["lead"],
        far,
        near,
        window,
        prepared["w1"],
        prepared["b1"],
        prepared["gain"],
        conv_weight.reshape(-1, CH),
        prepared["b2"],
        patch_weight,
        prepared["patch_gain"],
        prepared["post_gain"],
        proj_weight,
        prepared["text"],
        prepared["moves"],
        prepared["order"],
        devices,
    )
    decoded = decoded.reshape(frames, 2 * GRID_H, 2 * GRID_W, CH)
    spread = lax.all_to_all(sent, "seq", split_axis=0, concat_axis=0, tiled=True)
    image_vec, scores = rate(prepared["slots"], spread)
    return (latent_next, decoded, image_vec, scores)


def solution(mesh):
    in_specs = (
        P(("grp", "seq"), None),
        P(("grp", "seq"), None),
        P(("grp", "seq"), None),
        P(("grp", "seq"), None),
        P(),
        P(),
        P("grp"),
        P(),
        P(),
        P(),
        P(),
        P(),
        P(),
        P(),
        P(),
        P(),
        P(),
        P(None, "seq"),
        P("grp"),
        P("grp"),
    )
    out_specs = (
        P(("grp", "seq"), None),
        P(("grp", "seq"), None, None, None),
        P(("grp", "seq"), None),
        P(("grp", "seq")),
    )

    return jax.shard_map(local, mesh=mesh, in_specs=in_specs, out_specs=out_specs, check_vma=False)
```

profile of v0, /device:TPU:0, one launch (start us, length us, event | category | flops | bytes accessed | tf_op | source)
XLA Modules:
  0.0 244.4 jit_solution(1348750313132374509)
XLA Ops:
  1.2 3.5 %pack.3 = (bf16[3,192,256]{2,1,0:T(8,128)(2,1)}, bf16[3,192,256]{2,1,0:T(8,128)(2,1)}, bf16[3,192,256]{2,1,0:T(8,128)(2,1)}, bf16[3,192,256]{2,1,0:T(8,128)(2,1)...) custom-call(s32[8]{0:T(128)} %get-tuple-element.136.at_ref, ...), custom_call_target="tpu_custom_call" | custom-call | tf_op jit(solution)/shard_map/pack/pallas_call | solution.py:71
  4.7 4.1 %collective-permute-start.2 = (bf16[3,192,256]{2,1,0:T(8,128)(2,1)}, bf16[3,192,256]{2,1,0:T(8,128)(2,1)}, u32[]{:S(2)}, u32[]{:S(2)}) collective-permute-start(bf16[3,192,256]{2,1,0:T(8,128)(2,1)} %get-tuple-element.63), channel_id=1, source_target_pairs={{0,6},{1,7},{2,8},{3,9},{4,10},{5,11},{6,12},{7,13},{8,14},{9,15},... | collective-permute-start | bytes 884744 | tf_op jit(solution)/shard_map/ppermute | solution.py:36
  8.8 2.6 %collective-permute-start.3 = (bf16[3,192,256]{2,1,0:T(8,128)(2,1)}, bf16[3,192,256]{2,1,0:T(8,128)(2,1)}, u32[]{:S(2)}, u32[]{:S(2)}) collective-permute-start(bf16[3,192,256]{2,1,0:T(8,128)(2,1)} %get-tuple-element.64), channel_id=1, source_target_pairs={{0,8},{1,9},{2,10},{3,11},{4,12},{5,13},{6,14},{7,15},{8,0},{9,1},... | collective-permute-start | bytes 884744 | tf_op jit(solution)/shard_map/ppermute | solution.py:36
  13.2 3.1 %pack.4 = (bf16[3,192,128]{2,1,0:T(8,128)(2,1)}, bf16[3,192,128]{2,1,0:T(8,128)(2,1)}, bf16[3,192,128]{2,1,0:T(8,128)(2,1)}, bf16[3,192,128]{2,1,0:T(8,128)(2,1)...) custom-call(s32[8]{0:T(128)} %broadcast_add_fusion.1.at_ref, ...), custom_call_target="tpu_custom_call" | custom-call | tf_op jit(solution)/shard_map/pack/pallas_call | solution.py:71
  25.0 1.8 fusion.18
  26.9 8.2 %collective-permute-done.15.refs_2_ = bf16[3,192,128]{2,1,0:T(8,128)(2,1)} collective-permute-done((bf16[3,192,128]{2,1,0:T(8,128)(2,1)}, bf16[3,192,128]{2,1,0:T(8,128)(2,1)}, u32[]{:S(2)}, u32[]{:S(2)}) %collective-permute-start.15) | collective-permute-done | bytes 147488 | tf_op jit(solution)/shard_map/ppermute | solution.py:36
  35.2 17.2 %collective-permute-start.6 = (bf16[3,192,256]{2,1,0:T(8,128)(2,1)}, bf16[3,192,256]{2,1,0:T(8,128)(2,1)S(1)}, u32[]{:S(2)}, u32[]{:S(2)}) collective-permute-start(bf16[3,192,256]{2,1,0:T(8,128)(2,1)} %get-tuple-element.67), channel_id=1, source_target_pairs={{0,14},{1,15},{2,0},{3,1},{4,2},{5,3},{6,4},{7,5},{8,6},{9,7},{10,... | collective-permute-start | bytes 884744 | tf_op jit(solution)/shard_map/ppermute | solution.py:36
  52.4 1.7 compare_convert_fusion.refs_10_
  54.1 4.5 %collective-permute-start.1 = (bf16[3,192,256]{2,1,0:T(8,128)(2,1)}, bf16[3,192,256]{2,1,0:T(8,128)(2,1)}, u32[]{:S(2)}, u32[]{:S(2)}) collective-permute-start(bf16[3,192,256]{2,1,0:T(8,128)(2,1)} %get-tuple-element.62), channel_id=1, source_target_pairs={{0,4},{1,5},{2,6},{3,7},{4,8},{5,9},{6,10},{7,11},{8,12},{9,13},{1... | collective-permute-start | bytes 884744 | tf_op jit(solution)/shard_map/ppermute | solution.py:36
  61.2 2.9 %pack.5 = (bf16[3,192,128]{2,1,0:T(8,128)(2,1)}, bf16[3,192,128]{2,1,0:T(8,128)(2,1)}, bf16[3,192,128]{2,1,0:T(8,128)(2,1)}, bf16[3,192,128]{2,1,0:T(8,128)(2,1)...) custom-call(s32[8]{0:T(128)} %get-tuple-element.137.at_ref, ...), custom_call_target="tpu_custom_call" | custom-call | tf_op jit(solution)/shard_map/pack/pallas_call | solution.py:71
  64.1 1.8 copy.41
  69.7 6.1 %collective-permute-done.1.refs_2_ = bf16[3,192,256]{2,1,0:T(8,128)(2,1)} collective-permute-done((bf16[3,192,256]{2,1,0:T(8,128)(2,1)}, bf16[3,192,256]{2,1,0:T(8,128)(2,1)}, u32[]{:S(2)}, u32[]{:S(2)}) %collective-permute-start.1) | collective-permute-done | bytes 294944 | tf_op jit(solution)/shard_map/ppermute | solution.py:36
  78.6 9.5 %collective-permute-start.17 = (bf16[3,192,128]{2,1,0:T(8,128)(2,1)}, bf16[3,192,128]{2,1,0:T(8,128)(2,1)S(1)}, u32[]{:S(2)}, u32[]{:S(2)}) collective-permute-start(bf16[3,192,128]{2,1,0:T(8,128)(2,1)} %get-tuple-element.71), channel_id=1, source_target_pairs={{0,6},{1,7},{2,8},{3,9},{4,10},{5,11},{6,12},{7,13},{8,14},{9,15},... | collective-permute-start | bytes 442376 | tf_op jit(solution)/shard_map/ppermute | solution.py:36
  91.4 4.0 %collective-permute-start.21 = (bf16[3,192,128]{2,1,0:T(8,128)(2,1)}, bf16[3,192,128]{2,1,0:T(8,128)(2,1)}, u32[]{:S(2)}, u32[]{:S(2)}) collective-permute-start(bf16[3,192,128]{2,1,0:T(8,128)(2,1)} %get-tuple-element.75), channel_id=1, source_target_pairs={{0,14},{1,15},{2,0},{3,1},{4,2},{5,3},{6,4},{7,5},{8,6},{9,7},{10,... | collective-permute-start | bytes 442376 | tf_op jit(solution)/shard_map/ppermute | solution.py:36
  95.4 22.3 %attend.3.refs_0_ = f32[8,192,128]{2,1,0:T(8,128)} custom-call(s32[16]{0:T(128)} %select_n.105.t_ref, f32[16,2,1,128]{3,2,1,0:T(1,128)} %slice.42.sc_ref, f32[2,128,128]{2,1,0:T(8,128)} %pad_slice_fusion.w_ref, bf16[3,192,256]{2,1,0:T(8,128)(2,1)} %get-tuple-element.60.refs_0_, bf16[3,192,256]{2,1,0:T(8,128)(2,1)} %collective-permute-done.refs_1_, ...), custom_call_target="tpu_custom_call" | custom-call | flops 4831838208 | bytes 3145728 | tf_op jit(solution)/shard_map/attend/pallas_call | solution.py:236
  120.1 6.5 %collective-permute-done.30.refs_2_ = bf16[3,192,128]{2,1,0:T(8,128)(2,1)S(1)} collective-permute-done((bf16[3,192,128]{2,1,0:T(8,128)(2,1)S(1)}, bf16[3,192,128]{2,1,0:T(8,128)(2,1)S(1)}, u32[]{:S(2)}, u32[]{:S(2)}) %collective-permute-start.30) | collective-permute-done | bytes 147488 | tf_op jit(solution)/shard_map/ppermute | solution.py:36
  130.6 3.3 %collective-permute-start.34 = (bf16[3,192,128]{2,1,0:T(8,128)(2,1)S(1)}, bf16[3,192,128]{2,1,0:T(8,128)(2,1)S(1)}, u32[]{:S(2)}, u32[]{:S(2)}) collective-permute-start(bf16[3,192,128]{2,1,0:T(8,128)(2,1)S(1)} %copy-done.37), channel_id=1, source_target_pairs={{0,10},{1,11},{2,12},{3,13},{4,14},{5,15},{6,0},{7,1},{8,2},{9,3},... | collective-permute-start | bytes 442376 | tf_op jit(solution)/shard_map/ppermute | solution.py:36
  135.0 4.1 %collective-permute-start.36 = (bf16[3,192,128]{2,1,0:T(8,128)(2,1)S(1)}, bf16[3,192,128]{2,1,0:T(8,128)(2,1)}, u32[]{:S(2)}, u32[]{:S(2)}) collective-permute-start(bf16[3,192,128]{2,1,0:T(8,128)(2,1)S(1)} %copy-done.35), channel_id=1, source_target_pairs={{0,14},{1,15},{2,0},{3,1},{4,2},{5,3},{6,4},{7,5},{8,6},{9,7},{10,... | collective-permute-start | bytes 442376 | tf_op jit(solution)/shard_map/ppermute | solution.py:36
  139.1 13.2 %attend.4.refs_0_ = f32[8,192,128]{2,1,0:T(8,128)} custom-call(s32[16]{0:T(128)} %select_n.105.t_ref, f32[16,1,1,128]{3,2,1,0:T(1,128)} %get-tuple-element.134.sc_ref, f32[1,128,128]{2,1,0:T(8,128)} %get-tuple-element.132.w_ref, f32[8,192,128]{2,1,0:T(8,128)} %attend.3.refs_0_, bf16[3,192,128]{2,1,0:T(8,128)(2,1)} %get-tuple-element.77.refs_1_, ...), custom_call_target="tpu_custom_call" | custom-call | flops 2415919104 | bytes 1572864 | tf_op jit(solution)/shard_map/attend/pallas_call | solution.py:236
  156.6 13.1 %attend.5 = (bf16[192,128]{1,0:T(8,128)(2,1)}, bf16[192,128]{1,0:T(8,128)(2,1)}, bf16[192,128]{1,0:T(8,128)(2,1)}, bf16[192,128]{1,0:T(8,128)(2,1)}, bf16[192,12...) custom-call(s32[16]{0:T(128)} %select_n.105.t_ref, ...), custom_call_target="tpu_custom_call" | custom-call | flops 2415919104 | bytes 1572864 | tf_op jit(solution)/shard_map/attend/pallas_call | solution.py:236
  169.7 2.7 %collective-permute-start.45 = (bf16[192,128]{1,0:T(8,128)(2,1)}, bf16[192,128]{1,0:T(8,128)(2,1)S(1)}, u32[]{:S(2)}, u32[]{:S(2)}) collective-permute-start(bf16[192,128]{1,0:T(8,128)(2,1)} %get-tuple-element.103), channel_id=1, source_target_pairs={{0,8},{1,9},{2,10},{3,11},{4,12},{5,13},{6,14},{7,15},{8,0},{9,1},... | collective-permute-start | bytes 147464 | tf_op jit(solution)/shard_map/ppermute | solution.py:36
  172.4 4.8 %copy.37 = bf16[24704,48]{1,0:T(8,128)(2,1)} copy(bf16[24704,48]{0,1:T(8,128)(2,1)S(1)} %copy-done.2) | data formatting | bytes 4743168 | tf_op args[17]
  177.2 4.2 %gather_fusion.3 = bf16[77,48]{1,0:T(8,128)(2,1)S(1)} fusion(bf16[24704,48]{1,0:T(8,128)(2,1)} %copy.37, s32[1024]{0:T(1024)S(1)} %pad_clamp_fusion), kind=kCustom, calls=%fused_computation.3 | custom fusion | bytes 15092 | tf_op jit(solution)/shard_map/jit(_take)/gather | solution.py:620
  181.4 3.0 %collective-permute-start.47 = (bf16[192,128]{1,0:T(8,128)(2,1)}, bf16[192,128]{1,0:T(8,128)(2,1)S(1)}, u32[]{:S(2)}, u32[]{:S(2)}) collective-permute-start(bf16[192,128]{1,0:T(8,128)(2,1)} %get-tuple-element.105), channel_id=1, source_target_pairs={{0,6},{1,7},{2,8},{3,9},{4,10},{5,11},{6,12},{7,13},{8,14},{9,15},... | collective-permute-start | bytes 147464 | tf_op jit(solution)/shard_map/ppermute | solution.py:36
  184.4 2.7 %collective-permute-start.48 = (bf16[192,128]{1,0:T(8,128)(2,1)}, bf16[192,128]{1,0:T(8,128)(2,1)S(1)}, u32[]{:S(2)}, u32[]{:S(2)}) collective-permute-start(bf16[192,128]{1,0:T(8,128)(2,1)} %get-tuple-element.106), channel_id=1, source_target_pairs={{0,12},{1,13},{2,14},{3,15},{4,0},{5,1},{6,2},{7,3},{8,4},{9,5},{1... | collective-permute-start | bytes 147464 | tf_op jit(solution)/shard_map/ppermute | solution.py:36
  187.1 6.5 %collective-permute-start.50 = (bf16[192,128]{1,0:T(8,128)(2,1)}, bf16[192,128]{1,0:T(8,128)(2,1)S(1)}, u32[]{:S(2)}, u32[]{:S(2)}) collective-permute-start(bf16[192,128]{1,0:T(8,128)(2,1)} %get-tuple-element.108), channel_id=1, source_target_pairs={{0,14},{1,15},{2,0},{3,1},{4,2},{5,3},{6,4},{7,5},{8,6},{9,7},{10,... | collective-permute-start | bytes 147464 | tf_op jit(solution)/shard_map/ppermute | solution.py:36
  195.6 4.9 %collective-permute-done.51.refs_7_ = bf16[192,128]{1,0:T(8,128)(2,1)S(1)} collective-permute-done((bf16[192,128]{1,0:T(8,128)(2,1)}, bf16[192,128]{1,0:T(8,128)(2,1)S(1)}, u32[]{:S(2)}, u32[]{:S(2)}) %collective-permute-start.51) | collective-permute-done | bytes 49184 | tf_op jit(solution)/shard_map/ppermute | solution.py:36
  201.1 2.8 %latent.1 = (f32[192,64]{1,0:T(8,128)}, bf16[192,256]{1,0:T(8,128)(2,1)}) custom-call(f32[2]{0:T(128)} %broadcast_select_fusion.1.dt_ref, bf16[192,128]{1,0:T(8,128)(2,1)} %get-tuple-element.102.refs_0_, bf16[192,128]{1,0:T(8,128)(2,1)} %copy-done.11, bf16[192,128]{1,0:T(8,128)(2,1)} %collective-permute-done.46.refs_2_, bf16[192,128]{1,0:T(8,128)(2,1)} %copy-done.12, ...), custom_call_target="tpu_custom_call" | custom-call | tf_op jit(solution)/shard_map/latent/pallas_call | solution.py:340
  209.4 17.3 %decode.1 = (bf16[768,384]{1,0:T(8,128)(2,1)}, f32[16,3,768]{2,1,0:T(4,128)}) custom-call(s32[1]{0:T(128)} %bitcast.5.lead_ref, bf16[192,256]{1,0:T(8,128)(2,1)} %copy-done.7, bf16[192,256]{1,0:T(8,128)(2,1)} %copy-done.8, bf16[192,256]{1,0:T(8,128)(2,1)} %get-tuple-element.111.own_ref, bf16[768,1536]{1,0:T(8,128)(2,1)} %pad_maximum_fusion.w1_ref, ...), custom_call_target="tpu_custom_call" | custom-call | tf_op jit(solution)/shard_map/decode/pallas_call | solution.py:498
  226.6 6.2 %all-to-all-start = ((f32[16,3,768]{2,1,0:T(4,128)}), f32[16,3,768]{2,1,0:T(4,128)S(1)}, u32[]{:S(2)}, u32[]{:S(2)}) async-start(f32[16,3,768]{2,1,0:T(4,128)} %get-tuple-element.113), calls=%async_computation | async-start | bytes 393216 | tf_op jit(solution)/shard_map/all_to_all | solution.py:700
  234.2 7.6 %all-to-all-done.got_ref = f32[16,3,768]{2,1,0:T(4,128)S(1)} async-done(((f32[16,3,768]{2,1,0:T(4,128)}), f32[16,3,768]{2,1,0:T(4,128)S(1)}, u32[]{:S(2)}, u32[]{:S(2)}) %all-to-all-start) | async-done | bytes 147488 | tf_op jit(solution)/shard_map/all_to_all | solution.py:700
  242.4 1.8 rate.1
  (276 shorter events, 44.9 us)
Async XLA Ops:
  4.7 49.4 %collective-permute-start.2 = (bf16[3,192,256]{2,1,0:T(8,128)(2,1)}, bf16[3,192,256]{2,1,0:T(8,128)(2,1)}, u32[]{:S(2)}, u32[]{:S(2)}) collective-permute-start(bf16[3,192,256]{2,1,0:T(8,128)(2,1)} %get-tuple-element.63), channel_id=1, source_target_pairs={{0,6},{1,7},{2,8},{3,9},{4,10},{5,11},{6,12},{7,13},{8,14},{9,15},... | collective-permute-start | bytes 884744 | tf_op jit(solution)/shard_map/ppermute | solution.py:36
  8.8 45.4 %collective-permute-start.3 = (bf16[3,192,256]{2,1,0:T(8,128)(2,1)}, bf16[3,192,256]{2,1,0:T(8,128)(2,1)}, u32[]{:S(2)}, u32[]{:S(2)}) collective-permute-start(bf16[3,192,256]{2,1,0:T(8,128)(2,1)} %get-tuple-element.64), channel_id=1, source_target_pairs={{0,8},{1,9},{2,10},{3,11},{4,12},{5,13},{6,14},{7,15},{8,0},{9,1},... | collective-permute-start | bytes 884744 | tf_op jit(solution)/shard_map/ppermute | solution.py:36
  11.4 47.3 %collective-permute-start.4 = (bf16[3,192,256]{2,1,0:T(8,128)(2,1)}, bf16[3,192,256]{2,1,0:T(8,128)(2,1)}, u32[]{:S(2)}, u32[]{:S(2)}) collective-permute-start(bf16[3,192,256]{2,1,0:T(8,128)(2,1)} %get-tuple-element.65), channel_id=1, source_target_pairs={{0,10},{1,11},{2,12},{3,13},{4,14},{5,15},{6,0},{7,1},{8,2},{9,3},... | collective-permute-start | bytes 884744 | tf_op jit(solution)/shard_map/ppermute | solution.py:36
  16.3 18.9 %collective-permute-start.15 = (bf16[3,192,128]{2,1,0:T(8,128)(2,1)}, bf16[3,192,128]{2,1,0:T(8,128)(2,1)}, u32[]{:S(2)}, u32[]{:S(2)}) collective-permute-start(bf16[3,192,128]{2,1,0:T(8,128)(2,1)} %get-tuple-element.69), channel_id=1, source_target_pairs={{0,2},{1,3},{2,4},{3,5},{4,6},{5,7},{6,8},{7,9},{8,10},{9,11},{10,... | collective-permute-start | bytes 442376 | tf_op jit(solution)/shard_map/ppermute | solution.py:36
  17.8 17.3 %collective-permute-start.16 = (bf16[3,192,128]{2,1,0:T(8,128)(2,1)}, bf16[3,192,128]{2,1,0:T(8,128)(2,1)}, u32[]{:S(2)}, u32[]{:S(2)}) collective-permute-start(bf16[3,192,128]{2,1,0:T(8,128)(2,1)} %get-tuple-element.70), channel_id=1, source_target_pairs={{0,4},{1,5},{2,6},{3,7},{4,8},{5,9},{6,10},{7,11},{8,12},{9,13},{1... | collective-permute-start | bytes 442376 | tf_op jit(solution)/shard_map/ppermute | solution.py:36
  35.1 23.5 %collective-permute-start.5 = (bf16[3,192,256]{2,1,0:T(8,128)(2,1)}, bf16[3,192,256]{2,1,0:T(8,128)(2,1)S(1)}, u32[]{:S(2)}, u32[]{:S(2)}) collective-permute-start(bf16[3,192,256]{2,1,0:T(8,128)(2,1)} %get-tuple-element.66), channel_id=1, source_target_pairs={{0,12},{1,13},{2,14},{3,15},{4,0},{5,1},{6,2},{7,3},{8,4},{9,5},{1... | collective-permute-start | bytes 884744 | tf_op jit(solution)/shard_map/ppermute | solution.py:36
  35.2 24.0 %collective-permute-start.6 = (bf16[3,192,256]{2,1,0:T(8,128)(2,1)}, bf16[3,192,256]{2,1,0:T(8,128)(2,1)S(1)}, u32[]{:S(2)}, u32[]{:S(2)}) collective-permute-start(bf16[3,192,256]{2,1,0:T(8,128)(2,1)} %get-tuple-element.67), channel_id=1, source_target_pairs={{0,14},{1,15},{2,0},{3,1},{4,2},{5,3},{6,4},{7,5},{8,6},{9,7},{10,... | collective-permute-start | bytes 884744 | tf_op jit(solution)/shard_map/ppermute | solution.py:36
  54.1 15.5 %collective-permute-start = (bf16[3,192,256]{2,1,0:T(8,128)(2,1)}, bf16[3,192,256]{2,1,0:T(8,128)(2,1)}, u32[]{:S(2)}, u32[]{:S(2)}) collective-permute-start(bf16[3,192,256]{2,1,0:T(8,128)(2,1)} %get-tuple-element.61), channel_id=1, source_target_pairs={{0,2},{1,3},{2,4},{3,5},{4,6},{5,7},{6,8},{7,9},{8,10},{9,11},{10,... | collective-permute-start | bytes 884744 | tf_op jit(solution)/shard_map/ppermute | solution.py:36
  54.1 21.7 %collective-permute-start.1 = (bf16[3,192,256]{2,1,0:T(8,128)(2,1)}, bf16[3,192,256]{2,1,0:T(8,128)(2,1)}, u32[]{:S(2)}, u32[]{:S(2)}) collective-permute-start(bf16[3,192,256]{2,1,0:T(8,128)(2,1)} %get-tuple-element.62), channel_id=1, source_target_pairs={{0,4},{1,5},{2,6},{3,7},{4,8},{5,9},{6,10},{7,11},{8,12},{9,13},{1... | collective-permute-start | bytes 884744 | tf_op jit(solution)/shard_map/ppermute | solution.py:36
  58.7 17.2 %collective-permute-start.7 = (bf16[3,192,256]{2,1,0:T(8,128)(2,1)}, bf16[3,192,256]{2,1,0:T(8,128)(2,1)}, u32[]{:S(2)}, u32[]{:S(2)}) collective-permute-start(bf16[3,192,256]{2,1,0:T(8,128)(2,1)} %get-tuple-element.60.refs_0_), channel_id=1, source_target_pairs={{0,1},{1,0},{2,3},{3,2},{4,5},{5,4},{6,7},{7,6},{8,9},{9,8},{10,11... | collective-permute-start | bytes 884744 | tf_op jit(solution)/shard_map/ppermute | solution.py:41
  58.7 17.7 %collective-permute-start.10 = (bf16[3,192,256]{2,1,0:T(8,128)(2,1)}, bf16[3,192,256]{2,1,0:T(8,128)(2,1)}, u32[]{:S(2)}, u32[]{:S(2)}) collective-permute-start(bf16[3,192,256]{2,1,0:T(8,128)(2,1)} %collective-permute-done.2.refs_3_), channel_id=1, source_target_pairs={{0,1},{1,0},{2,3},{3,2},{4,5},{5,4},{6,7},{7,6},{8,9},{9,8},{10,11... | collective-permute-start | bytes 884744 | tf_op jit(solution)/shard_map/ppermute | solution.py:41
  59.2 17.3 %collective-permute-start.11 = (bf16[3,192,256]{2,1,0:T(8,128)(2,1)}, bf16[3,192,256]{2,1,0:T(8,128)(2,1)}, u32[]{:S(2)}, u32[]{:S(2)}) collective-permute-start(bf16[3,192,256]{2,1,0:T(8,128)(2,1)} %collective-permute-done.3.refs_4_), channel_id=1, source_target_pairs={{0,1},{1,0},{2,3},{3,2},{4,5},{5,4},{6,7},{7,6},{8,9},{9,8},{10,11... | collective-permute-start | bytes 884744 | tf_op jit(solution)/shard_map/ppermute | solution.py:41
  69.7 8.9 %collective-permute-start.12 = (bf16[3,192,256]{2,1,0:T(8,128)(2,1)}, bf16[3,192,256]{2,1,0:T(8,128)(2,1)S(1)}, u32[]{:S(2)}, u32[]{:S(2)}) collective-permute-start(bf16[3,192,256]{2,1,0:T(8,128)(2,1)} %collective-permute-done.4.refs_5_), channel_id=1, source_target_pairs={{0,1},{1,0},{2,3},{3,2},{4,5},{5,4},{6,7},{7,6},{8,9},{9,8},{10,11... | collective-permute-start | bytes 884744 | tf_op jit(solution)/shard_map/ppermute | solution.py:41
  75.9 12.2 %collective-permute-start.13 = (bf16[3,192,256]{2,1,0:T(8,128)(2,1)}, bf16[3,192,256]{2,1,0:T(8,128)(2,1)S(1)}, u32[]{:S(2)}, u32[]{:S(2)}) collective-permute-start(bf16[3,192,256]{2,1,0:T(8,128)(2,1)} %copy-done.26), channel_id=1, source_target_pairs={{0,1},{1,0},{2,3},{3,2},{4,5},{5,4},{6,7},{7,6},{8,9},{9,8},{10,11... | collective-permute-start | bytes 884744 | tf_op jit(solution)/shard_map/ppermute | solution.py:41
  75.9 12.2 %collective-permute-start.14 = (bf16[3,192,256]{2,1,0:T(8,128)(2,1)}, bf16[3,192,256]{2,1,0:T(8,128)(2,1)S(1)}, u32[]{:S(2)}, u32[]{:S(2)}) collective-permute-start(bf16[3,192,256]{2,1,0:T(8,128)(2,1)} %copy-done.27), channel_id=1, source_target_pairs={{0,1},{1,0},{2,3},{3,2},{4,5},{5,4},{6,7},{7,6},{8,9},{9,8},{10,11... | collective-permute-start | bytes 884744 | tf_op jit(solution)/shard_map/ppermute | solution.py:41
  76.4 13.0 %collective-permute-start.8 = (bf16[3,192,256]{2,1,0:T(8,128)(2,1)}, bf16[3,192,256]{2,1,0:T(8,128)(2,1)S(1)}, u32[]{:S(2)}, u32[]{:S(2)}) collective-permute-start(bf16[3,192,256]{2,1,0:T(8,128)(2,1)} %collective-permute-done.refs_1_), channel_id=1, source_target_pairs={{0,1},{1,0},{2,3},{3,2},{4,5},{5,4},{6,7},{7,6},{8,9},{9,8},{10,11... | collective-permute-start | bytes 884744 | tf_op jit(solution)/shard_map/ppermute | solution.py:41
  76.5 14.2 %collective-permute-start.9 = (bf16[3,192,256]{2,1,0:T(8,128)(2,1)}, bf16[3,192,256]{2,1,0:T(8,128)(2,1)S(1)}, u32[]{:S(2)}, u32[]{:S(2)}) collective-permute-start(bf16[3,192,256]{2,1,0:T(8,128)(2,1)} %collective-permute-done.1.refs_2_), channel_id=1, source_target_pairs={{0,1},{1,0},{2,3},{3,2},{4,5},{5,4},{6,7},{7,6},{8,9},{9,8},{10,11... | collective-permute-start | bytes 884744 | tf_op jit(solution)/shard_map/ppermute | solution.py:41
  78.6 39.1 %collective-permute-start.17 = (bf16[3,192,128]{2,1,0:T(8,128)(2,1)}, bf16[3,192,128]{2,1,0:T(8,128)(2,1)S(1)}, u32[]{:S(2)}, u32[]{:S(2)}) collective-permute-start(bf16[3,192,128]{2,1,0:T(8,128)(2,1)} %get-tuple-element.71), channel_id=1, source_target_pairs={{0,6},{1,7},{2,8},{3,9},{4,10},{5,11},{6,12},{7,13},{8,14},{9,15},... | collective-permute-start | bytes 442376 | tf_op jit(solution)/shard_map/ppermute | solution.py:36
  88.1 29.7 %collective-permute-start.18 = (bf16[3,192,128]{2,1,0:T(8,128)(2,1)}, bf16[3,192,128]{2,1,0:T(8,128)(2,1)S(1)}, u32[]{:S(2)}, u32[]{:S(2)}) collective-permute-start(bf16[3,192,128]{2,1,0:T(8,128)(2,1)} %get-tuple-element.72), channel_id=1, source_target_pairs={{0,8},{1,9},{2,10},{3,11},{4,12},{5,13},{6,14},{7,15},{8,0},{9,1},... | collective-permute-start | bytes 442376 | tf_op jit(solution)/shard_map/ppermute | solution.py:36
  88.1 30.6 %collective-permute-start.19 = (bf16[3,192,128]{2,1,0:T(8,128)(2,1)}, bf16[3,192,128]{2,1,0:T(8,128)(2,1)S(1)}, u32[]{:S(2)}, u32[]{:S(2)}) collective-permute-start(bf16[3,192,128]{2,1,0:T(8,128)(2,1)} %get-tuple-element.73), channel_id=1, source_target_pairs={{0,10},{1,11},{2,12},{3,13},{4,14},{5,15},{6,0},{7,1},{8,2},{9,3},... | collective-permute-start | bytes 442376 | tf_op jit(solution)/shard_map/ppermute | solution.py:36
  89.4 29.4 %collective-permute-start.20 = (bf16[3,192,128]{2,1,0:T(8,128)(2,1)}, bf16[3,192,128]{2,1,0:T(8,128)(2,1)S(1)}, u32[]{:S(2)}, u32[]{:S(2)}) collective-permute-start(bf16[3,192,128]{2,1,0:T(8,128)(2,1)} %get-tuple-element.74), channel_id=1, source_target_pairs={{0,12},{1,13},{2,14},{3,15},{4,0},{5,1},{6,2},{7,3},{8,4},{9,5},{1... | collective-permute-start | bytes 442376 | tf_op jit(solution)/shard_map/ppermute | solution.py:36
  91.4 27.3 %collective-permute-start.21 = (bf16[3,192,128]{2,1,0:T(8,128)(2,1)}, bf16[3,192,128]{2,1,0:T(8,128)(2,1)}, u32[]{:S(2)}, u32[]{:S(2)}) collective-permute-start(bf16[3,192,128]{2,1,0:T(8,128)(2,1)} %get-tuple-element.75), channel_id=1, source_target_pairs={{0,14},{1,15},{2,0},{3,1},{4,2},{5,3},{6,4},{7,5},{8,6},{9,7},{10,... | collective-permute-start | bytes 442376 | tf_op jit(solution)/shard_map/ppermute | solution.py:36
  128.8 23.5 %collective-permute-start.32 = (bf16[3,192,128]{2,1,0:T(8,128)(2,1)S(1)}, bf16[3,192,128]{2,1,0:T(8,128)(2,1)S(1)}, u32[]{:S(2)}, u32[]{:S(2)}) collective-permute-start(bf16[3,192,128]{2,1,0:T(8,128)(2,1)S(1)} %copy-done.39), channel_id=1, source_target_pairs={{0,6},{1,7},{2,8},{3,9},{4,10},{5,11},{6,12},{7,13},{8,14},{9,15},... | collective-permute-start | bytes 442376 | tf_op jit(solution)/shard_map/ppermute | solution.py:36
  129.5 22.8 %collective-permute-start.33 = (bf16[3,192,128]{2,1,0:T(8,128)(2,1)S(1)}, bf16[3,192,128]{2,1,0:T(8,128)(2,1)S(1)}, u32[]{:S(2)}, u32[]{:S(2)}) collective-permute-start(bf16[3,192,128]{2,1,0:T(8,128)(2,1)S(1)} %copy-done.38), channel_id=1, source_target_pairs={{0,8},{1,9},{2,10},{3,11},{4,12},{5,13},{6,14},{7,15},{8,0},{9,1},... | collective-permute-start | bytes 442376 | tf_op jit(solution)/shard_map/ppermute | solution.py:36
  130.6 21.7 %collective-permute-start.34 = (bf16[3,192,128]{2,1,0:T(8,128)(2,1)S(1)}, bf16[3,192,128]{2,1,0:T(8,128)(2,1)S(1)}, u32[]{:S(2)}, u32[]{:S(2)}) collective-permute-start(bf16[3,192,128]{2,1,0:T(8,128)(2,1)S(1)} %copy-done.37), channel_id=1, source_target_pairs={{0,10},{1,11},{2,12},{3,13},{4,14},{5,15},{6,0},{7,1},{8,2},{9,3},... | collective-permute-start | bytes 442376 | tf_op jit(solution)/shard_map/ppermute | solution.py:36
  134.0 18.4 %collective-permute-start.35 = (bf16[3,192,128]{2,1,0:T(8,128)(2,1)S(1)}, bf16[3,192,128]{2,1,0:T(8,128)(2,1)S(1)}, u32[]{:S(2)}, u32[]{:S(2)}) collective-permute-start(bf16[3,192,128]{2,1,0:T(8,128)(2,1)S(1)} %copy-done.36), channel_id=1, source_target_pairs={{0,12},{1,13},{2,14},{3,15},{4,0},{5,1},{6,2},{7,3},{8,4},{9,5},{1... | collective-permute-start | bytes 442376 | tf_op jit(solution)/shard_map/ppermute | solution.py:36
  135.0 17.4 %collective-permute-start.36 = (bf16[3,192,128]{2,1,0:T(8,128)(2,1)S(1)}, bf16[3,192,128]{2,1,0:T(8,128)(2,1)}, u32[]{:S(2)}, u32[]{:S(2)}) collective-permute-start(bf16[3,192,128]{2,1,0:T(8,128)(2,1)S(1)} %copy-done.35), channel_id=1, source_target_pairs={{0,14},{1,15},{2,0},{3,1},{4,2},{5,3},{6,4},{7,5},{8,6},{9,7},{10,... | collective-permute-start | bytes 442376 | tf_op jit(solution)/shard_map/ppermute | solution.py:36
  169.7 17.4 %collective-permute-start.45 = (bf16[192,128]{1,0:T(8,128)(2,1)}, bf16[192,128]{1,0:T(8,128)(2,1)S(1)}, u32[]{:S(2)}, u32[]{:S(2)}) collective-permute-start(bf16[192,128]{1,0:T(8,128)(2,1)} %get-tuple-element.103), channel_id=1, source_target_pairs={{0,8},{1,9},{2,10},{3,11},{4,12},{5,13},{6,14},{7,15},{8,0},{9,1},... | collective-permute-start | bytes 147464 | tf_op jit(solution)/shard_map/ppermute | solution.py:36
  172.3 21.2 %collective-permute-start.46 = (bf16[192,128]{1,0:T(8,128)(2,1)}, bf16[192,128]{1,0:T(8,128)(2,1)}, u32[]{:S(2)}, u32[]{:S(2)}) collective-permute-start(bf16[192,128]{1,0:T(8,128)(2,1)} %get-tuple-element.104), channel_id=1, source_target_pairs={{0,10},{1,11},{2,12},{3,13},{4,14},{5,15},{6,0},{7,1},{8,2},{9,3},... | collective-permute-start | bytes 147464 | tf_op jit(solution)/shard_map/ppermute | solution.py:36
  181.4 12.9 %collective-permute-start.47 = (bf16[192,128]{1,0:T(8,128)(2,1)}, bf16[192,128]{1,0:T(8,128)(2,1)S(1)}, u32[]{:S(2)}, u32[]{:S(2)}) collective-permute-start(bf16[192,128]{1,0:T(8,128)(2,1)} %get-tuple-element.105), channel_id=1, source_target_pairs={{0,6},{1,7},{2,8},{3,9},{4,10},{5,11},{6,12},{7,13},{8,14},{9,15},... | collective-permute-start | bytes 147464 | tf_op jit(solution)/shard_map/ppermute | solution.py:36
  184.4 10.0 %collective-permute-start.48 = (bf16[192,128]{1,0:T(8,128)(2,1)}, bf16[192,128]{1,0:T(8,128)(2,1)S(1)}, u32[]{:S(2)}, u32[]{:S(2)}) collective-permute-start(bf16[192,128]{1,0:T(8,128)(2,1)} %get-tuple-element.106), channel_id=1, source_target_pairs={{0,12},{1,13},{2,14},{3,15},{4,0},{5,1},{6,2},{7,3},{8,4},{9,5},{1... | collective-permute-start | bytes 147464 | tf_op jit(solution)/shard_map/ppermute | solution.py:36
  226.6 15.2 %all-to-all-start = ((f32[16,3,768]{2,1,0:T(4,128)}), f32[16,3,768]{2,1,0:T(4,128)S(1)}, u32[]{:S(2)}, u32[]{:S(2)}) async-start(f32[16,3,768]{2,1,0:T(4,128)} %get-tuple-element.113), calls=%async_computation | async-start | bytes 393216 | tf_op jit(solution)/shard_map/all_to_all | solution.py:700
  (93 other events, 1041.1 us)
where the time goes:
time: 245 us; the launch traced here: 244 us
  starting transfers between devices  87.9 us (36%)
  Pallas kernels  79.9 us (33%)
  waiting for transfers between devices  36.2 us (15%)
  local copies, waits for them, and re-layouts  29.3 us (12%)
  other arithmetic  7.78 us (3%)
    ppermute x28, starting transfers between devices, rotate(): lax.ppermute(value, axis, [(i, (i + 2 * steps) % count) for i in range(co...  73.7 us
    pallas_call x3, Pallas kernels, attend(): pl.pallas_call(functools.partial(attend_kernel, blocks, heads, frames, re...  48.5 us
    ppermute x28, waiting for transfers between devices, rotate(): lax.ppermute(value, axis, [(i, (i + 2 * steps) % count) for i in range(co...  27 us
    pallas_call x1, Pallas kernels, decode(): pl.pallas_call(functools.partial(decode_kernel, frames), out_shape=[jax.S...  17.3 us
    unnamed x144, local copies, waits for them, and re-layouts  12.2 us
    pallas_call x3, Pallas kernels, pack(): pl.pallas_call(functools.partial(pack_kernel, blocks), out_shape=[jax.Sha...  9.47 us
    all_to_all x1, waiting for transfers between devices, local(): lax.all_to_all(sent, 'seq', split_axis=0, concat_axis=0, tiled=True)  7.58 us
    all_to_all x1, starting transfers between devices, local(): lax.all_to_all(sent, 'seq', split_axis=0, concat_axis=0, tiled=True)  6.18 us
  transfers between devices with their start and end apart: 55, of which 11 were waited for; matrix products, arithmetic and copies ran while one was open for 14% of the time, Pallas kernels for 17%

commit v1 on v0

--- a/solution.py
+++ b/solution.py
@@ -82,9 +82,8 @@
     )(starts, keys, values, queries)
 
 
-def attend_kernel(blocks, heads, frames, resumed, last, t_ref, sc_ref, w_ref, *refs):
-    if resumed:
-        prev_ref, refs = refs[0], refs[1:]
+def attend_kernel(blocks, heads, frames, earlier, last, t_ref, sc_ref, w_ref, *refs):
+    prev_refs, refs = refs[:earlier], refs[earlier:]
     near_refs, far_refs, refs = refs[:blocks], refs[blocks : 2 * blocks], refs[2 * blocks :]
     if last:
         out_refs, refs = refs[:blocks], refs[blocks:]
@@ -92,7 +91,7 @@
         sum_ref, refs = refs[0], refs[1:]
     q_s, k_s, v_s, s_a, s_b, m_a, m_b, acc_s, tot_s, sem, q_sem = refs[:11]
     if last:
-        sum_ref = refs[11]
+        sum_ref, prev_s, prev_sem = refs[11:]
     sources = near_refs + far_refs
     rows = near_refs[0].shape[1]
     keys = len(sources) * rows
@@ -114,10 +113,11 @@
     for h in range(1, heads):
         fetch(h, 0)
         fetch(h, 1)
-    if resumed:
-        sum_ref[...] = prev_ref[...]
-    else:
-        sum_ref[...] = jnp.zeros(sum_ref.shape, jnp.float32)
+    gets = []
+    for n, prev in enumerate(prev_refs):
+        gets.append(pltpu.make_async_copy(prev, prev_s.at[n], prev_sem.at[n]))
+        gets[-1].start()
+    sum_ref[...] = jnp.zeros(sum_ref.shape, jnp.float32)
 
     def arrived(h, which):
         whole = (k_s, v_s)[which].at[h]
@@ -213,30 +213,49 @@
         heads - 1, blocks - 1, acc_s[...], tot_s[...]
     )
     if last:
+        for get in gets:
+            get.wait()
+        row, lane = grid_iota(8, 128)
+        pick = jnp.where(lane == LAT, 1.0, 0.0)
         for b in range(blocks):
             share = sum_ref[b]
-            high = share.astype(jnp.bfloat16)
-            rest = (share - high.astype(jnp.float32)).astype(jnp.bfloat16)
-            lane = lax.broadcasted_iota(jnp.int32, share.shape, 1)
-            out_refs[b][...] = jnp.where(lane < 3 * LAT // 2, high, rest)
-
-
-def attend(near, far, steps, scale, weight, previous, last):
+            for n in range(earlier):
+                share = share + prev_s[n, b]
+            out_refs[b][:PATCH] = jnp.concatenate(
+                [share[f * PATCH : (f + 1) * PATCH, :LAT] for f in range(frames)], axis=1
+            ).astype(jnp.bfloat16)
+            for f in range(frames):
+                square = lax.dot_general(
+                    pick,
+                    share[f * PATCH : (f + 1) * PATCH],
+                    (((1,), (1,)), ((), ())),
+                    precision=highest,
+                    preferred_element_type=jnp.float32,
+                )
+                square = jnp.concatenate(
+                    [square, jnp.zeros((8, 128 - PATCH), jnp.float32)], axis=1
+                )
+                high = square.astype(jnp.bfloat16).astype(jnp.float32)
+                both = jnp.where(row == 0, high, jnp.where(row == 1, square - high, 0.0))
+                out_refs[b][PATCH + 8 * f : PATCH + 8 * (f + 1)] = both.astype(jnp.bfloat16)
+
+
+def attend(near, far, steps, scale, weight, earlier, last):
     blocks = len(near)
     _, rows, cols = near[0].shape
     heads, keys = cols // HD, 2 * blocks * rows
     frames = rows // PATCH
-    resumed = previous is not None
     sums = (blocks, rows, 128)
     if last:
-        out_shape = [jax.ShapeDtypeStruct(sums[1:], jnp.bfloat16)] * blocks
+        share = (PATCH + 8 * frames, frames * LAT)
+        out_shape = [jax.ShapeDtypeStruct(share, jnp.bfloat16)] * blocks
         out_specs = [VM] * blocks
     else:
         out_shape, out_specs = jax.ShapeDtypeStruct(sums, jnp.float32), VM
     return pl.pallas_call(
-        functools.partial(attend_kernel, blocks, heads, frames, resumed, last),
+        functools.partial(attend_kernel, blocks, heads, frames, len(earlier), last),
         out_shape=out_shape,
-        in_specs=[SM, VM, VM] + [VM] * resumed + [ANY] * (2 * blocks),
+        in_specs=[SM, VM, VM] + [ANY] * (len(earlier) + 2 * blocks),
         out_specs=out_specs,
         scratch_shapes=[
             pltpu.VMEM((blocks, rows, cols), jnp.bfloat16),
@@ -251,14 +270,19 @@
             pltpu.SemaphoreType.DMA((heads, 2)),
             pltpu.SemaphoreType.DMA,
         ]
-        + [pltpu.VMEM(sums, jnp.float32)] * last,
+        + [
+            pltpu.VMEM(sums, jnp.float32),
+            pltpu.VMEM((max(1, len(earlier)),) + sums, jnp.float32),
+            pltpu.SemaphoreType.DMA((max(1, len(earlier)),)),
+        ]
+        * last,
         cost_estimate=pl.CostEstimate(
             flops=4 * blocks * rows * keys * cols,
             bytes_accessed=4 * keys * cols,
             transcendentals=blocks * rows * keys * heads,
         ),
         name="attend",
-    )(steps, scale, weight, *([previous] if resumed else []), *near, *far)
+    )(steps, scale, weight, *earlier, *near, *far)
 
 
 WINDOW = ((-1, 1), (0, 0), (0, 1), (1, 0))
@@ -267,75 +291,84 @@
 OFFSETS = [(di, dj) for di in (-1, 0, 1) for dj in (-1, 0, 1)]
 
 
-def one_hot(index, count):
-    hit = jnp.asarray(index, jnp.int32)[..., None] == jnp.arange(count, dtype=jnp.int32)
-    return hit.astype(jnp.bfloat16)
-
-
-def moved(di, dj):
-    seen = np.full((GRID_H, GRID_W), -1)
-    for i in range(GRID_H):
-        for j in range(GRID_W):
-            if 0 <= i + di < GRID_H and 0 <= j + dj < GRID_W:
-                seen[i, j] = (i + di) * GRID_W + j + dj
-    return seen.reshape(-1)
-
-
-def gather_matrices():
-    move = one_hot(np.stack([moved(di, dj) for di, dj in OFFSETS], axis=1), PATCH)
-    place = np.full((len(OFFSETS), 4, 4, LAT_C), -1)
-    for u, (di, a) in enumerate(WINDOW):
-        for w, (dj, b) in enumerate(WINDOW):
-            place[OFFSETS.index((di, dj)), u, w] = (2 * a + b) * LAT_C + np.arange(LAT_C)
-    source = jnp.asarray(place.reshape(1, -1), jnp.int32)
-    placed = (jnp.arange(LAT, dtype=jnp.int32)[:, None] == source).astype(jnp.bfloat16)
-    return move.reshape(PATCH, -1), placed
-
-
-def plane_moves():
-    planes = []
-    for a in (0, 1):
-        for b in (0, 1):
-            da, db = (1, -1)[a], (1, -1)[b]
-            planes.append(np.concatenate([moved(da, 0), moved(0, db), moved(da, db)]))
-    return one_hot(np.stack(planes), PATCH)
-
-
-def pixel_order():
-    index = np.zeros((GRID_H, 2, GRID_W, 2), np.int64)
-    for a in (0, 1):
-        for b in (0, 1):
-            index[:, a, :, b] = (2 * a + b) * PATCH + np.arange(PATCH).reshape(GRID_H, GRID_W)
-    return one_hot(index.reshape(-1), 4 * PATCH)
+def grid_iota(rows, cols):
+    shape = (rows, cols)
+    return lax.broadcasted_iota(jnp.int32, shape, 0), lax.broadcasted_iota(jnp.int32, shape, 1)
+
+
+def over(value, count):
+    return jnp.floor((value.astype(jnp.float32) + 0.5) * np.float32(1.0 / count)).astype(jnp.int32)
+
+
+def as_matrix(hit):
+    return jnp.where(hit, 1.0, 0.0).astype(jnp.bfloat16)
+
+
+def move_matrix(di, dj, cols=PATCH):
+    row, col = grid_iota(PATCH, cols)
+    j = row - GRID_W * over(row, GRID_W)
+    inside = (j + dj >= 0) & (j + dj < GRID_W) & (col < PATCH)
+    return as_matrix((col - row == GRID_W * di + dj) & inside)
+
+
+def place_matrix(di, dj):
+    row, col = grid_iota(LAT, 16 * LAT_C)
+    u, w, c = col >> 6, (col >> 4) & 3, col & 15
+    source = 2 * LAT_C * (1 - (u & 1)) + LAT_C * (1 - (w & 1)) + c
+
+    def seen(at, step):
+        return {-1: at == 0, 0: (at == 1) | (at == 2), 1: at == 3}[step]
+
+    return as_matrix((row == source) & seen(u, di) & seen(w, dj))
+
+
+def order_matrix():
+    row, col = grid_iota(4 * PATCH, 4 * PATCH)
+    y = over(row, 2 * GRID_W)
+    z = row - 2 * GRID_W * y
+    source = (2 * (y & 1) + (z & 1)) * PATCH + (y >> 1) * GRID_W + (z >> 1)
+    return as_matrix(col == source)
 
 
 def latent_kernel(parts, width, frames, dt_ref, *refs):
     part_refs, refs = refs[:parts], refs[parts:]
-    lat_ref, base_ref, move_ref, place_ref, next_ref, win_ref = refs
+    lat_ref, base_ref, next_ref, win_ref = refs
     total = part_refs[0][...].astype(jnp.float32)
     for r in part_refs[1:]:
         total = total + r[...].astype(jnp.float32)
-    half = LAT // 2
-    square = total[:, LAT : LAT + half] + total[:, LAT + half :]
-    inverse = lax.rsqrt(square * np.float32(1.0 / width) + 1e-06)
-    scaled = total[:, :LAT] * jnp.concatenate([inverse, inverse], axis=1)
+    row, _ = grid_iota(8, 128)
+    pick = jnp.where(row < 2, 1.0, 0.0)
+    cols = 16 * LAT_C
+    moves = jnp.concatenate([move_matrix(di, dj, 128) for di, dj in OFFSETS], axis=1)
+    places = jnp.concatenate([place_matrix(di, dj) for di, dj in OFFSETS], axis=1)
+    none = jnp.zeros((128 - PATCH, cols), jnp.bfloat16)
     for f in range(frames):
         at = slice(f * PATCH, (f + 1) * PATCH)
-        value = lat_ref[at] + dt_ref[f] * (scaled[at] + base_ref[f : f + 1])
+        squares = total[PATCH + 8 * f : PATCH + 8 * (f + 1)]
+        square = lax.dot_general(
+            squares,
+            pick,
+            (((0,), (0,)), ((), ())),
+            precision=highest,
+            preferred_element_type=jnp.float32,
+        )[:PATCH, :LAT]
+        inverse = lax.rsqrt(square * np.float32(1.0 / width) + 1e-06)
+        scaled = total[:PATCH, f * LAT : (f + 1) * LAT] * inverse
+        value = lat_ref[at] + dt_ref[f] * (scaled + base_ref[f : f + 1])
         next_ref[at] = value
         spread = jnp.dot(
-            value.astype(jnp.bfloat16), place_ref[...], preferred_element_type=jnp.float32
+            value.astype(jnp.bfloat16), places, preferred_element_type=jnp.float32
         ).astype(jnp.bfloat16)
-        cols = 16 * LAT_C
         stacked = jnp.concatenate(
-            [spread[:, o * cols : (o + 1) * cols] for o in range(len(OFFSETS))], axis=0
-        )
-        win_ref[at] = jnp.dot(
-            move_ref[...], stacked, preferred_element_type=jnp.float32
-        ).astype(jnp.bfloat16)
-
-
-def step_latent(parts, latent_in, base, step_dt, width, move, place):
+            [x for o in range(len(OFFSETS)) for x in (spread[:, o * cols : (o + 1) * cols], none)],
+            axis=0,
+        )
+        win_ref[at] = jnp.dot(moves, stacked, preferred_element_type=jnp.float32).astype(
+            jnp.bfloat16
+        )
+
+
+def step_latent(parts, latent_in, base, step_dt, width):
     rows = latent_in.shape[0]
     return pl.pallas_call(
         functools.partial(latent_kernel, len(parts), width, rows // PATCH),
@@ -343,10 +376,58 @@
             jax.ShapeDtypeStruct((rows, LAT), jnp.float32),
             jax.ShapeDtypeStruct((rows, 16 * LAT_C), jnp.bfloat16),
         ],
-        in_specs=[SM] + [VM] * (len(parts) + 4),
+        in_specs=[SM] + [VM] * (len(parts) + 2),
         out_specs=[VM, VM],
         name="latent",
-    )(step_dt, *parts, latent_in, base, move, place)
+    )(step_dt, *parts, latent_in, base)
+
+
+def text_kernel(at_ref, id_ref, table_hbm, out_ref, buf, sem):
+    count = id_ref.shape[0]
+
+    def block(n):
+        start = pl.multiple_of((id_ref[n] // 128) * 128, 128)
+        return pltpu.make_async_copy(table_hbm.at[:, pl.ds(start, 128)], buf.at[n], sem)
+
+    def fetch(n, carry):
+        block(n).start()
+        return carry
+
+    lax.fori_loop(0, count, fetch, 0)
+    pltpu.make_async_copy(buf, buf, sem).wait()
+    width = buf.shape[1]
+    _, lane = grid_iota(width, 128)
+
+    def add(n, acc):
+        return acc + jnp.where(lane == id_ref[n] % 128, buf[n].astype(jnp.float32), 0.0)
+
+    acc = lax.fori_loop(0, count, add, jnp.zeros((width, 128), jnp.float32))
+    own = lax.dot_general(
+        jnp.ones((8, 128), jnp.float32),
+        acc,
+        (((1,), (1,)), ((), ())),
+        precision=highest,
+        preferred_element_type=jnp.float32,
+    )
+    row, col = grid_iota(width, out_ref.shape[1])
+    spot = jnp.where(col == row + at_ref[0], 1.0, 0.0)
+    placed = jnp.dot(own, spot, precision=highest, preferred_element_type=jnp.float32)
+    out_ref[...] = placed[:1] * np.float32(1.0 / count)
+
+
+def text_mean(at, ids, table):
+    width = table.shape[0]
+    return pl.pallas_call(
+        text_kernel,
+        out_shape=jax.ShapeDtypeStruct((1, TEXT_W), jnp.float32),
+        in_specs=[SM, SM, ANY],
+        out_specs=VM,
+        scratch_shapes=[
+            pltpu.VMEM((ids.shape[0], width, 128), jnp.bfloat16),
+            pltpu.SemaphoreType.DMA,
+        ],
+        name="text",
+    )(at, ids, table)
 
 
 def decode_kernel(
@@ -362,8 +443,6 @@
     pg_ref,
     post_ref,
     text_ref,
-    moves_ref,
-    order_ref,
     w2_hbm,
     pw_hbm,
     proj_hbm,
@@ -406,10 +485,14 @@
         row = lax.broadcasted_iota(jnp.int32, (wide * PATCH, 1), 0)
         act = jnp.where((row >= 2 * PATCH) | (lead_ref[0] == 0), act, 0.0).astype(jnp.bfloat16)
         a, b = q // 2, q % 2
+        da, db = (1, -1)[a], (1, -1)[b]
+        moves = jnp.concatenate(
+            [move_matrix(da, 0), move_matrix(0, db), move_matrix(da, db)], axis=0
+        )
         for f in range(wide):
             plane = act[f * PATCH : (f + 1) * PATCH]
             moved = jnp.dot(
-                moves_ref[q], plane, preferred_element_type=jnp.float32
+                moves, plane, preferred_element_type=jnp.float32
             ).astype(jnp.bfloat16)
             pieces = {
                 (0, 0): plane,
@@ -440,9 +523,10 @@
         [firsts[q][f * PATCH : (f + 1) * PATCH] for f in range(frames) for q in range(4)], axis=0
     )
     dec = (out + b2_ref[...] + first).astype(jnp.bfloat16)
+    order = order_matrix()
     for f in range(frames):
         out_ref[f * block : (f + 1) * block] = jnp.dot(
-            order_ref[...], dec[f * block : (f + 1) * block], preferred_element_type=jnp.float32
+            order, dec[f * block : (f + 1) * block], preferred_element_type=jnp.float32
         ).astype(jnp.bfloat16)
     pw_copy.wait()
     emb = jnp.zeros((rows, pw_s.shape[1]), jnp.float32)
@@ -490,7 +574,7 @@
 
 
 def decode(
-    lead, far, near, own, w1, b1, gain, w2, b2, pw, patch_gain, post_gain, proj, text, moves, order, devices
+    lead, far, near, own, w1, b1, gain, w2, b2, pw, patch_gain, post_gain, proj, text, devices
 ):
     rows = own.shape[0]
     frames = rows // PATCH
@@ -501,7 +585,7 @@
             jax.ShapeDtypeStruct((frames * 4 * PATCH, CH), jnp.bfloat16),
             jax.ShapeDtypeStruct((devices, frames + 1, proj.shape[1]), jnp.float32),
         ],
-        in_specs=[SM] + [VM] * 12 + [ANY, ANY, ANY],
+        in_specs=[SM] + [VM] * 10 + [ANY, ANY, ANY],
         out_specs=[VM, VM],
         scratch_shapes=[
             pltpu.VMEM(w2.shape, jnp.bfloat16),
@@ -524,8 +608,6 @@
         patch_gain,
         post_gain,
         text,
-        moves,
-        order,
         w2,
         pw,
         proj,
@@ -607,7 +689,6 @@
     got[order[0]] = rotate(blocks[order[0]], "seq", order[0])
     for turn in order[1:]:
         got[turn] = rotate(blocks[turn], "seq", turn)
-    move, place = gather_matrices()
     scale = lax.dynamic_slice_in_dim(mod_table[:, 1, :], chip * cols, cols, 1)
     scale = scale.reshape(-1, heads, 1, HD)
     weight = lax.dynamic_slice_in_dim(head_weight, chip * cols, cols, 0).reshape(heads, HD, LAT)
@@ -617,9 +698,8 @@
     own_steps = lax.dynamic_slice_in_dim(timestep, me * frames, frames, 0)
     base = jnp.dot(jnp.take(mod_table[:, 0, :], own_steps, axis=0), head_weight, precision=highest)
     step_dt = jnp.take(step_size, own_steps)
-    own_text = jnp.mean(jnp.take(text_table, prompt_ids, axis=0).astype(jnp.float32), axis=0)
-    text_row = lax.dynamic_update_slice_in_dim(
-        jnp.zeros((TEXT_W,), jnp.float32), own_text, me * own_text.shape[0], 0
+    text_row = text_mean(
+        (me * text_table.shape[1]).astype(jnp.int32).reshape(1), prompt_ids, text_table.T
     )
     slots = lax.dynamic_slice_in_dim(frame_order, me * frames, frames, 0)
     prepared = dict(
@@ -628,7 +708,7 @@
         steps=steps,
         base=base,
         step_dt=step_dt,
-        text=text_row.reshape(1, -1),
+        text=text_row,
         slots=slots,
         w1=window_weight(conv_in_weight),
         b1=conv_in_bias.reshape(1, -1),
@@ -638,10 +718,6 @@
         post_gain=post_gain.reshape(1, -1),
         lead=(me == 0).astype(jnp.int32).reshape(1),
         latent_in=latent_in,
-        move=move,
-        place=place,
-        moves=plane_moves(),
-        order=pixel_order(),
         later=[packed(f, n) for f, n in zip(firsts[1:], phases[1:])],
     )
     phase_blocks = [got]
@@ -650,21 +726,24 @@
         for turn in order:
             got[turn] = rotate(blocks[turn], "seq", turn)
         phase_blocks.append(got)
-    sums = None
+    sums = []
     for n, got in enumerate(phase_blocks):
-        if sums is not None:
-            sums, *got = lax.optimization_barrier((sums, *got))
+        if n:
+            sums[-1], *got = lax.optimization_barrier((sums[-1], *got))
         other = [swap_core(block, "seq") for block in got]
-        sums = attend(
+        last = n + 1 == len(phase_blocks)
+        shares = attend(
             got,
             other,
             prepared["steps"],
             prepared["scales"][n],
             prepared["weights"][n],
-            sums,
-            n + 1 == len(phase_blocks),
-        )
-    parts = [sums[0]] + [rotate(sums[t], "seq", chips - t) for t in order]
+            sums if last else [],
+            last,
+        )
+        if not last:
+            sums.append(shares)
+    parts = [shares[0]] + [rotate(shares[t], "seq", chips - t) for t in order]
 
     latent_next, window = step_latent(
         parts,
@@ -672,8 +751,6 @@
         prepared["base"],
         prepared["step_dt"],
         width,
-        prepared["move"],
-        prepared["place"],
     )
     near = shifted(window, "seq", 1)
     far = shifted(window, "seq", 2)
@@ -692,8 +769,6 @@
         prepared["post_gain"],
         proj_weight,
         prepared["text"],
-        prepared["moves"],
-        prepared["order"],
         devices,
     )
     decoded = decoded.reshape(frames, 2 * GRID_H, 2 * GRID_W, CH)

time: 245 us -> 230 us (0.939)
  local copies, waits for them, and re-layouts: 29.3 us -> 16.2 us
  starting transfers between devices: 87.9 us -> 81 us
  waiting for transfers between devices: 36.2 us -> 41 us
  Pallas kernels: 79.9 us -> 84.5 us
  other arithmetic: 7.78 us -> 3.35 us
    ppermute x28, waiting for transfers between devices: 27 us -> 33.3 us  [rotate(): lax.ppermute(value, axis, [(i, (i + 2 * steps) % count) for i in range(co...]
    ppermute x28, starting transfers between devices: 73.7 us -> 67.7 us  [rotate(): lax.ppermute(value, axis, [(i, (i + 2 * steps) % count) for i in range(co...]
    unnamed x144 -> x95, local copies, waits for them, and re-layouts: 12.2 us -> 6.44 us
    pallas_call x3 -> x4, Pallas kernels: 48.5 us -> 53.2 us  [the longest x3 49 us: attend(): pl.pallas_call(functools.partial(attend_kernel, blocks, heads, frames, le...]
    convert_element_type x4 -> x0, other arithmetic: 4.23 us -> none  [the longest x3 3.45 us: one_hot(): return hit.astype(jnp.bfloat16)]
    gather x1 -> x0, local copies, waits for them, and re-layouts: 4.22 us -> none  [local(): jnp.take(text_table, prompt_ids, axis=0).astype(jnp.float32)]
  transfers between devices with their start and end apart: 55 -> 55, of which waited for: 11 -> 7; matrix products, arithmetic and copies ran while one was open for 14% -> 7% of each run, Pallas kernels for 17% -> 20%
where the time goes in v1:
time: 230 us; the launch traced here: 229 us
  Pallas kernels  84.5 us (37%)
  starting transfers between devices  81 us (35%)
  waiting for transfers between devices  41 us (18%)
  local copies, waits for them, and re-layouts  16.2 us (7%)
  other arithmetic  3.35 us (1%)
    ppermute x28, starting transfers between devices, rotate(): lax.ppermute(value, axis, [(i, (i + 2 * steps) % count) for i in range(co...  67.7 us
    pallas_call x3, Pallas kernels, attend(): pl.pallas_call(functools.partial(attend_kernel, blocks, heads, frames, le...  49 us
    ppermute x28, waiting for transfers between devices, rotate(): lax.ppermute(value, axis, [(i, (i + 2 * steps) % count) for i in range(co...  33.3 us
    pallas_call x1, Pallas kernels, decode(): pl.pallas_call(functools.partial(decode_kernel, frames), out_shape=[jax.S...  17.1 us
    pallas_call x3, Pallas kernels, pack(): pl.pallas_call(functools.partial(pack_kernel, blocks), out_shape=[jax.Sha...  9.27 us
    all_to_all x1, waiting for transfers between devices, local(): lax.all_to_all(sent, 'seq', split_axis=0, concat_axis=0, tiled=True)  7.65 us
    unnamed x95, local copies, waits for them, and re-layouts  6.44 us
    ppermute x24, starting transfers between devices, swap_core(): return lax.ppermute(value, axis, [(i, i ^ 1) for i in range(count)])  5.61 us
  transfers between devices with their start and end apart: 55, of which 7 were waited for; matrix products, arithmetic and copies ran while one was open for 7% of the time, Pallas kernels for 20%

profile of v1, /device:TPU:0, one launch (start us, length us, event | category | flops | bytes accessed | tf_op | source)
XLA Modules:
  0.0 229.1 jit_solution(12894093087170319196)
XLA Ops:
  1.2 2.9 %pack.4 = (bf16[3,192,128]{2,1,0:T(8,128)(2,1)}, bf16[3,192,128]{2,1,0:T(8,128)(2,1)}, bf16[3,192,128]{2,1,0:T(8,128)(2,1)}, bf16[3,192,128]{2,1,0:T(8,128)(2,1)...) custom-call(s32[8]{0:T(128)} %broadcast_add_fusion.1.at_ref, ...), custom_call_target="tpu_custom_call" | custom-call | tf_op jit(solution)/shard_map/pack/pallas_call | solution.py:71
  4.1 3.0 %collective-permute-start.15 = (bf16[3,192,128]{2,1,0:T(8,128)(2,1)}, bf16[3,192,128]{2,1,0:T(8,128)(2,1)S(1)}, u32[]{:S(2)}, u32[]{:S(2)}) collective-permute-start(bf16[3,192,128]{2,1,0:T(8,128)(2,1)} %get-tuple-element.69), channel_id=1, source_target_pairs={{0,2},{1,3},{2,4},{3,5},{4,6},{5,7},{6,8},{7,9},{8,10},{9,11},{10,... | collective-permute-start | bytes 442376 | tf_op jit(solution)/shard_map/ppermute | solution.py:36
  9.3 3.4 %pack.3 = (bf16[3,192,256]{2,1,0:T(8,128)(2,1)}, bf16[3,192,256]{2,1,0:T(8,128)(2,1)}, bf16[3,192,256]{2,1,0:T(8,128)(2,1)}, bf16[3,192,256]{2,1,0:T(8,128)(2,1)...) custom-call(s32[8]{0:T(128)} %get-tuple-element.136.at_ref, ...), custom_call_target="tpu_custom_call" | custom-call | tf_op jit(solution)/shard_map/pack/pallas_call | solution.py:71
  17.0 2.6 %collective-permute-start.3 = (bf16[3,192,256]{2,1,0:T(8,128)(2,1)}, bf16[3,192,256]{2,1,0:T(8,128)(2,1)S(1)}, u32[]{:S(2)}, u32[]{:S(2)}) collective-permute-start(bf16[3,192,256]{2,1,0:T(8,128)(2,1)} %get-tuple-element.64), channel_id=1, source_target_pairs={{0,8},{1,9},{2,10},{3,11},{4,12},{5,13},{6,14},{7,15},{8,0},{9,1},... | collective-permute-start | bytes 884744 | tf_op jit(solution)/shard_map/ppermute | solution.py:36
  22.8 2.9 %collective-permute-done.refs_1_ = bf16[3,192,256]{2,1,0:T(8,128)(2,1)S(1)} collective-permute-done((bf16[3,192,256]{2,1,0:T(8,128)(2,1)}, bf16[3,192,256]{2,1,0:T(8,128)(2,1)S(1)}, u32[]{:S(2)}, u32[]{:S(2)}) %collective-permute-start) | collective-permute-done | bytes 294944 | tf_op jit(solution)/shard_map/ppermute | solution.py:36
  26.5 5.7 %collective-permute-start.6 = (bf16[3,192,256]{2,1,0:T(8,128)(2,1)}, bf16[3,192,256]{2,1,0:T(8,128)(2,1)}, u32[]{:S(2)}, u32[]{:S(2)}) collective-permute-start(bf16[3,192,256]{2,1,0:T(8,128)(2,1)} %get-tuple-element.67), channel_id=1, source_target_pairs={{0,14},{1,15},{2,0},{3,1},{4,2},{5,3},{6,4},{7,5},{8,6},{9,7},{10,... | collective-permute-start | bytes 884744 | tf_op jit(solution)/shard_map/ppermute | solution.py:36
  32.3 17.0 %collective-permute-done.2.refs_3_ = bf16[3,192,256]{2,1,0:T(8,128)(2,1)S(1)} collective-permute-done((bf16[3,192,256]{2,1,0:T(8,128)(2,1)}, bf16[3,192,256]{2,1,0:T(8,128)(2,1)S(1)}, u32[]{:S(2)}, u32[]{:S(2)}) %collective-permute-start.2) | collective-permute-done | bytes 294944 | tf_op jit(solution)/shard_map/ppermute | solution.py:36
  51.0 2.2 collective-permute-done.6.refs_7_
  55.0 3.0 %pack.5 = (bf16[3,192,128]{2,1,0:T(8,128)(2,1)}, bf16[3,192,128]{2,1,0:T(8,128)(2,1)}, bf16[3,192,128]{2,1,0:T(8,128)(2,1)}, bf16[3,192,128]{2,1,0:T(8,128)(2,1)...) custom-call(s32[8]{0:T(128)} %get-tuple-element.137.at_ref, ...), custom_call_target="tpu_custom_call" | custom-call | tf_op jit(solution)/shard_map/pack/pallas_call | solution.py:71
  58.7 16.8 %collective-permute-start.17 = (bf16[3,192,128]{2,1,0:T(8,128)(2,1)}, bf16[3,192,128]{2,1,0:T(8,128)(2,1)}, u32[]{:S(2)}, u32[]{:S(2)}) collective-permute-start(bf16[3,192,128]{2,1,0:T(8,128)(2,1)} %get-tuple-element.71), channel_id=1, source_target_pairs={{0,6},{1,7},{2,8},{3,9},{4,10},{5,11},{6,12},{7,13},{8,14},{9,15},... | collective-permute-start | bytes 442376 | tf_op jit(solution)/shard_map/ppermute | solution.py:36
  75.5 1.7 collective-permute-start.18
  77.4 2.2 collective-permute-start.20
  80.9 22.3 %attend.3.refs_0_ = f32[8,192,128]{2,1,0:T(8,128)} custom-call(s32[16]{0:T(128)} %select_n.93.t_ref, f32[16,2,1,128]{3,2,1,0:T(1,128)} %slice.39.sc_ref, f32[2,128,128]{2,1,0:T(8,128)} %pad_slice_fusion.1.w_ref, bf16[3,192,256]{2,1,0:T(8,128)(2,1)} %get-tuple-element.60.refs_0_, bf16[3,192,256]{2,1,0:T(8,128)(2,1)} %copy-done.13, ...), custom_call_target="tpu_custom_call" | custom-call | flops 4831838208 | bytes 3145728 | tf_op jit(solution)/shard_map/attend/pallas_call | solution.py:255
  106.0 6.5 %collective-permute-done.30.refs_3_ = bf16[3,192,128]{2,1,0:T(8,128)(2,1)S(1)} collective-permute-done((bf16[3,192,128]{2,1,0:T(8,128)(2,1)}, bf16[3,192,128]{2,1,0:T(8,128)(2,1)S(1)}, u32[]{:S(2)}, u32[]{:S(2)}) %collective-permute-start.30) | collective-permute-done | bytes 147488 | tf_op jit(solution)/shard_map/ppermute | solution.py:36
  117.9 2.0 collective-permute-start.34
  120.6 1.6 collective-permute-start.35
  122.9 3.6 %collective-permute-start.36 = (bf16[3,192,128]{2,1,0:T(8,128)(2,1)}, bf16[3,192,128]{2,1,0:T(8,128)(2,1)S(1)}, u32[]{:S(2)}, u32[]{:S(2)}) collective-permute-start(bf16[3,192,128]{2,1,0:T(8,128)(2,1)} %get-tuple-element.92), channel_id=1, source_target_pairs={{0,14},{1,15},{2,0},{3,1},{4,2},{5,3},{6,4},{7,5},{8,6},{9,7},{10,... | collective-permute-start | bytes 442376 | tf_op jit(solution)/shard_map/ppermute | solution.py:36
  126.6 12.8 %attend.4.refs_1_ = f32[8,192,128]{2,1,0:T(8,128)} custom-call(s32[16]{0:T(128)} %select_n.93.t_ref, f32[16,1,1,128]{3,2,1,0:T(1,128)} %get-tuple-element.134.sc_ref, f32[1,128,128]{2,1,0:T(8,128)} %get-tuple-element.132.w_ref, bf16[3,192,128]{2,1,0:T(8,128)(2,1)} %get-tuple-element.77.refs_0_, bf16[3,192,128]{2,1,0:T(8,128)(2,1)} %copy-done.19, ...), custom_call_target="tpu_custom_call" | custom-call | flops 2415919104 | bytes 1572864 | tf_op jit(solution)/shard_map/attend/pallas_call | solution.py:255
  145.6 13.9 %attend.5 = (bf16[112,128]{1,0:T(8,128)(2,1)}, bf16[112,128]{1,0:T(8,128)(2,1)}, bf16[112,128]{1,0:T(8,128)(2,1)}, bf16[112,128]{1,0:T(8,128)(2,1)}, bf16[112,12...) custom-call(s32[16]{0:T(128)} %select_n.93.t_ref, ...), custom_call_target="tpu_custom_call" | custom-call | flops 2415919104 | bytes 1572864 | tf_op jit(solution)/shard_map/attend/pallas_call | solution.py:255
  159.5 2.6 %collective-permute-start.45 = (bf16[112,128]{1,0:T(8,128)(2,1)}, bf16[112,128]{1,0:T(8,128)(2,1)S(1)}, u32[]{:S(2)}, u32[]{:S(2)}) collective-permute-start(bf16[112,128]{1,0:T(8,128)(2,1)} %get-tuple-element.103), channel_id=1, source_target_pairs={{0,8},{1,9},{2,10},{3,11},{4,12},{5,13},{6,14},{7,15},{8,0},{9,1},... | collective-permute-start | bytes 86024 | tf_op jit(solution)/shard_map/ppermute | solution.py:36
  162.7 2.9 %collective-permute-start.47 = (bf16[112,128]{1,0:T(8,128)(2,1)}, bf16[112,128]{1,0:T(8,128)(2,1)}, u32[]{:S(2)}, u32[]{:S(2)}) collective-permute-start(bf16[112,128]{1,0:T(8,128)(2,1)} %get-tuple-element.105), channel_id=1, source_target_pairs={{0,6},{1,7},{2,8},{3,9},{4,10},{5,11},{6,12},{7,13},{8,14},{9,15},... | collective-permute-start | bytes 86024 | tf_op jit(solution)/shard_map/ppermute | solution.py:36
  165.6 2.7 %collective-permute-start.48 = (bf16[112,128]{1,0:T(8,128)(2,1)}, bf16[112,128]{1,0:T(8,128)(2,1)}, u32[]{:S(2)}, u32[]{:S(2)}) collective-permute-start(bf16[112,128]{1,0:T(8,128)(2,1)} %get-tuple-element.106), channel_id=1, source_target_pairs={{0,12},{1,13},{2,14},{3,15},{4,0},{5,1},{6,2},{7,3},{8,4},{9,5},{1... | collective-permute-start | bytes 86024 | tf_op jit(solution)/shard_map/ppermute | solution.py:36
  168.3 6.2 %collective-permute-start.50 = (bf16[112,128]{1,0:T(8,128)(2,1)}, bf16[112,128]{1,0:T(8,128)(2,1)}, u32[]{:S(2)}, u32[]{:S(2)}) collective-permute-start(bf16[112,128]{1,0:T(8,128)(2,1)} %get-tuple-element.108), channel_id=1, source_target_pairs={{0,14},{1,15},{2,0},{3,1},{4,2},{5,3},{6,4},{7,5},{8,6},{9,7},{10,... | collective-permute-start | bytes 86024 | tf_op jit(solution)/shard_map/ppermute | solution.py:36
  174.5 1.8 fusion.15
  177.1 4.3 %collective-permute-done.51.refs_7_ = bf16[112,128]{1,0:T(8,128)(2,1)} collective-permute-done((bf16[112,128]{1,0:T(8,128)(2,1)}, bf16[112,128]{1,0:T(8,128)(2,1)}, u32[]{:S(2)}, u32[]{:S(2)}) %collective-permute-start.51) | collective-permute-done | bytes 28704 | tf_op jit(solution)/shard_map/ppermute | solution.py:36
  181.4 3.1 %latent.1 = (f32[192,64]{1,0:T(8,128)}, bf16[192,256]{1,0:T(8,128)(2,1)}) custom-call(f32[2]{0:T(128)} %broadcast_select_fusion.1.dt_ref, bf16[112,128]{1,0:T(8,128)(2,1)} %get-tuple-element.102.refs_0_, bf16[112,128]{1,0:T(8,128)(2,1)} %copy-done.7, bf16[112,128]{1,0:T(8,128)(2,1)} %copy-done.8, bf16[112,128]{1,0:T(8,128)(2,1)} %collective-permute-done.47.refs_3_, ...), custom_call_target="tpu_custom_call" | custom-call | tf_op jit(solution)/shard_map/latent/pallas_call | solution.py:373
  185.7 1.9 collective-permute-start.53
  191.0 4.2 %text.1.text_ref = f32[1,768]{1,0:T(1,128)} custom-call(s32[1]{0:T(128)} %bitcast.12.at_ref, s32[77]{0:T(128)} %id_ref.1, bf16[48,24704]{1,0:T(8,128)(2,1)} %bitcast.22), custom_call_target="tpu_custom_call" | custom-call | tf_op jit(solution)/shard_map/text/pallas_call | solution.py:420
  195.9 17.1 %decode.1 = (bf16[768,384]{1,0:T(8,128)(2,1)}, f32[16,3,768]{2,1,0:T(4,128)}) custom-call(s32[1]{0:T(128)} %bitcast.4.lead_ref, bf16[192,256]{1,0:T(8,128)(2,1)} %copy-done.4, bf16[192,256]{1,0:T(8,128)(2,1)} %collective-permute-done.53.near_ref, bf16[192,256]{1,0:T(8,128)(2,1)} %get-tuple-element.111.own_ref, bf16[768,1536]{1,0:T(8,128)(2,1)} %pad_maximum_fusion.w1_ref, ...), custom_call_target="tpu_custom_call" | custom-call | tf_op jit(solution)/shard_map/decode/pallas_call | solution.py:582
  213.0 4.4 %all-to-all-start = ((f32[16,3,768]{2,1,0:T(4,128)}), f32[16,3,768]{2,1,0:T(4,128)S(1)}, u32[]{:S(2)}, u32[]{:S(2)}) async-start(f32[16,3,768]{2,1,0:T(4,128)} %get-tuple-element.113), calls=%async_computation | async-start | bytes 393216 | tf_op jit(solution)/shard_map/all_to_all | solution.py:775
  218.7 7.6 %all-to-all-done.got_ref = f32[16,3,768]{2,1,0:T(4,128)S(1)} async-done(((f32[16,3,768]{2,1,0:T(4,128)}), f32[16,3,768]{2,1,0:T(4,128)S(1)}, u32[]{:S(2)}, u32[]{:S(2)}) %all-to-all-start) | async-done | bytes 147488 | tf_op jit(solution)/shard_map/all_to_all | solution.py:775
  227.1 1.8 rate.1
  (212 shorter events, 40.6 us)
Async XLA Ops:
  4.1 12.9 %collective-permute-start.15 = (bf16[3,192,128]{2,1,0:T(8,128)(2,1)}, bf16[3,192,128]{2,1,0:T(8,128)(2,1)S(1)}, u32[]{:S(2)}, u32[]{:S(2)}) collective-permute-start(bf16[3,192,128]{2,1,0:T(8,128)(2,1)} %get-tuple-element.69), channel_id=1, source_target_pairs={{0,2},{1,3},{2,4},{3,5},{4,6},{5,7},{6,8},{7,9},{8,10},{9,11},{10,... | collective-permute-start | bytes 442376 | tf_op jit(solution)/shard_map/ppermute | solution.py:36
  7.2 12.4 %collective-permute-start.16 = (bf16[3,192,128]{2,1,0:T(8,128)(2,1)}, bf16[3,192,128]{2,1,0:T(8,128)(2,1)S(1)}, u32[]{:S(2)}, u32[]{:S(2)}) collective-permute-start(bf16[3,192,128]{2,1,0:T(8,128)(2,1)} %get-tuple-element.70), channel_id=1, source_target_pairs={{0,4},{1,5},{2,6},{3,7},{4,8},{5,9},{6,10},{7,11},{8,12},{9,13},{1... | collective-permute-start | bytes 442376 | tf_op jit(solution)/shard_map/ppermute | solution.py:36
  12.7 13.0 %collective-permute-start = (bf16[3,192,256]{2,1,0:T(8,128)(2,1)}, bf16[3,192,256]{2,1,0:T(8,128)(2,1)S(1)}, u32[]{:S(2)}, u32[]{:S(2)}) collective-permute-start(bf16[3,192,256]{2,1,0:T(8,128)(2,1)} %get-tuple-element.61), channel_id=1, source_target_pairs={{0,2},{1,3},{2,4},{3,5},{4,6},{5,7},{6,8},{7,9},{8,10},{9,11},{10,... | collective-permute-start | bytes 884744 | tf_op jit(solution)/shard_map/ppermute | solution.py:36
  14.3 12.3 %collective-permute-start.1 = (bf16[3,192,256]{2,1,0:T(8,128)(2,1)}, bf16[3,192,256]{2,1,0:T(8,128)(2,1)S(1)}, u32[]{:S(2)}, u32[]{:S(2)}) collective-permute-start(bf16[3,192,256]{2,1,0:T(8,128)(2,1)} %get-tuple-element.62), channel_id=1, source_target_pairs={{0,4},{1,5},{2,6},{3,7},{4,8},{5,9},{6,10},{7,11},{8,12},{9,13},{1... | collective-permute-start | bytes 884744 | tf_op jit(solution)/shard_map/ppermute | solution.py:36
  15.8 33.4 %collective-permute-start.2 = (bf16[3,192,256]{2,1,0:T(8,128)(2,1)}, bf16[3,192,256]{2,1,0:T(8,128)(2,1)S(1)}, u32[]{:S(2)}, u32[]{:S(2)}) collective-permute-start(bf16[3,192,256]{2,1,0:T(8,128)(2,1)} %get-tuple-element.63), channel_id=1, source_target_pairs={{0,6},{1,7},{2,8},{3,9},{4,10},{5,11},{6,12},{7,13},{8,14},{9,15},... | collective-permute-start | bytes 884744 | tf_op jit(solution)/shard_map/ppermute | solution.py:36
  17.0 32.6 %collective-permute-start.3 = (bf16[3,192,256]{2,1,0:T(8,128)(2,1)}, bf16[3,192,256]{2,1,0:T(8,128)(2,1)S(1)}, u32[]{:S(2)}, u32[]{:S(2)}) collective-permute-start(bf16[3,192,256]{2,1,0:T(8,128)(2,1)} %get-tuple-element.64), channel_id=1, source_target_pairs={{0,8},{1,9},{2,10},{3,11},{4,12},{5,13},{6,14},{7,15},{8,0},{9,1},... | collective-permute-start | bytes 884744 | tf_op jit(solution)/shard_map/ppermute | solution.py:36
  20.3 29.5 %collective-permute-start.4 = (bf16[3,192,256]{2,1,0:T(8,128)(2,1)}, bf16[3,192,256]{2,1,0:T(8,128)(2,1)}, u32[]{:S(2)}, u32[]{:S(2)}) collective-permute-start(bf16[3,192,256]{2,1,0:T(8,128)(2,1)} %get-tuple-element.65), channel_id=1, source_target_pairs={{0,10},{1,11},{2,12},{3,13},{4,14},{5,15},{6,0},{7,1},{8,2},{9,3},... | collective-permute-start | bytes 884744 | tf_op jit(solution)/shard_map/ppermute | solution.py:36
  25.7 25.1 %collective-permute-start.5 = (bf16[3,192,256]{2,1,0:T(8,128)(2,1)}, bf16[3,192,256]{2,1,0:T(8,128)(2,1)S(1)}, u32[]{:S(2)}, u32[]{:S(2)}) collective-permute-start(bf16[3,192,256]{2,1,0:T(8,128)(2,1)} %get-tuple-element.66), channel_id=1, source_target_pairs={{0,12},{1,13},{2,14},{3,15},{4,0},{5,1},{6,2},{7,3},{8,4},{9,5},{1... | collective-permute-start | bytes 884744 | tf_op jit(solution)/shard_map/ppermute | solution.py:36
  26.5 26.7 %collective-permute-start.6 = (bf16[3,192,256]{2,1,0:T(8,128)(2,1)}, bf16[3,192,256]{2,1,0:T(8,128)(2,1)}, u32[]{:S(2)}, u32[]{:S(2)}) collective-permute-start(bf16[3,192,256]{2,1,0:T(8,128)(2,1)} %get-tuple-element.67), channel_id=1, source_target_pairs={{0,14},{1,15},{2,0},{3,1},{4,2},{5,3},{6,4},{7,5},{8,6},{9,7},{10,... | collective-permute-start | bytes 884744 | tf_op jit(solution)/shard_map/ppermute | solution.py:36
  53.2 22.3 %collective-permute-start.11 = (bf16[3,192,256]{2,1,0:T(8,128)(2,1)S(1)}, bf16[3,192,256]{2,1,0:T(8,128)(2,1)}, u32[]{:S(2)}, u32[]{:S(2)}) collective-permute-start(bf16[3,192,256]{2,1,0:T(8,128)(2,1)S(1)} %collective-permute-done.3.refs_4_), channel_id=1, source_target_pairs={{0,1},{1,0},{2,3},{3,2},{4,5},{5,4},{6,7},{7,6},{8,9},{9,8},{10,11... | collective-permute-start | bytes 884744 | tf_op jit(solution)/shard_map/ppermute | solution.py:41
  53.2 23.9 %collective-permute-start.12 = (bf16[3,192,256]{2,1,0:T(8,128)(2,1)}, bf16[3,192,256]{2,1,0:T(8,128)(2,1)}, u32[]{:S(2)}, u32[]{:S(2)}) collective-permute-start(bf16[3,192,256]{2,1,0:T(8,128)(2,1)} %collective-permute-done.4.refs_5_), channel_id=1, source_target_pairs={{0,1},{1,0},{2,3},{3,2},{4,5},{5,4},{6,7},{7,6},{8,9},{9,8},{10,11... | collective-permute-start | bytes 884744 | tf_op jit(solution)/shard_map/ppermute | solution.py:41
  53.7 23.6 %collective-permute-start.13 = (bf16[3,192,256]{2,1,0:T(8,128)(2,1)S(1)}, bf16[3,192,256]{2,1,0:T(8,128)(2,1)}, u32[]{:S(2)}, u32[]{:S(2)}) collective-permute-start(bf16[3,192,256]{2,1,0:T(8,128)(2,1)S(1)} %collective-permute-done.5.refs_6_), channel_id=1, source_target_pairs={{0,1},{1,0},{2,3},{3,2},{4,5},{5,4},{6,7},{7,6},{8,9},{9,8},{10,11... | collective-permute-start | bytes 884744 | tf_op jit(solution)/shard_map/ppermute | solution.py:41
  53.8 25.8 %collective-permute-start.14 = (bf16[3,192,256]{2,1,0:T(8,128)(2,1)}, bf16[3,192,256]{2,1,0:T(8,128)(2,1)}, u32[]{:S(2)}, u32[]{:S(2)}) collective-permute-start(bf16[3,192,256]{2,1,0:T(8,128)(2,1)} %collective-permute-done.6.refs_7_), channel_id=1, source_target_pairs={{0,1},{1,0},{2,3},{3,2},{4,5},{5,4},{6,7},{7,6},{8,9},{9,8},{10,11... | collective-permute-start | bytes 884744 | tf_op jit(solution)/shard_map/ppermute | solution.py:41
  58.7 44.5 %collective-permute-start.17 = (bf16[3,192,128]{2,1,0:T(8,128)(2,1)}, bf16[3,192,128]{2,1,0:T(8,128)(2,1)}, u32[]{:S(2)}, u32[]{:S(2)}) collective-permute-start(bf16[3,192,128]{2,1,0:T(8,128)(2,1)} %get-tuple-element.71), channel_id=1, source_target_pairs={{0,6},{1,7},{2,8},{3,9},{4,10},{5,11},{6,12},{7,13},{8,14},{9,15},... | collective-permute-start | bytes 442376 | tf_op jit(solution)/shard_map/ppermute | solution.py:36
  75.5 28.5 %collective-permute-start.18 = (bf16[3,192,128]{2,1,0:T(8,128)(2,1)}, bf16[3,192,128]{2,1,0:T(8,128)(2,1)}, u32[]{:S(2)}, u32[]{:S(2)}) collective-permute-start(bf16[3,192,128]{2,1,0:T(8,128)(2,1)} %get-tuple-element.72), channel_id=1, source_target_pairs={{0,8},{1,9},{2,10},{3,11},{4,12},{5,13},{6,14},{7,15},{8,0},{9,1},... | collective-permute-start | bytes 442376 | tf_op jit(solution)/shard_map/ppermute | solution.py:36
  77.2 28.1 %collective-permute-start.19 = (bf16[3,192,128]{2,1,0:T(8,128)(2,1)}, bf16[3,192,128]{2,1,0:T(8,128)(2,1)}, u32[]{:S(2)}, u32[]{:S(2)}) collective-permute-start(bf16[3,192,128]{2,1,0:T(8,128)(2,1)} %get-tuple-element.73), channel_id=1, source_target_pairs={{0,10},{1,11},{2,12},{3,13},{4,14},{5,15},{6,0},{7,1},{8,2},{9,3},... | collective-permute-start | bytes 442376 | tf_op jit(solution)/shard_map/ppermute | solution.py:36
  77.4 27.9 %collective-permute-start.20 = (bf16[3,192,128]{2,1,0:T(8,128)(2,1)}, bf16[3,192,128]{2,1,0:T(8,128)(2,1)}, u32[]{:S(2)}, u32[]{:S(2)}) collective-permute-start(bf16[3,192,128]{2,1,0:T(8,128)(2,1)} %get-tuple-element.74), channel_id=1, source_target_pairs={{0,12},{1,13},{2,14},{3,15},{4,0},{5,1},{6,2},{7,3},{8,4},{9,5},{1... | collective-permute-start | bytes 442376 | tf_op jit(solution)/shard_map/ppermute | solution.py:36
  79.6 25.7 %collective-permute-start.21 = (bf16[3,192,128]{2,1,0:T(8,128)(2,1)}, bf16[3,192,128]{2,1,0:T(8,128)(2,1)}, u32[]{:S(2)}, u32[]{:S(2)}) collective-permute-start(bf16[3,192,128]{2,1,0:T(8,128)(2,1)} %get-tuple-element.75), channel_id=1, source_target_pairs={{0,14},{1,15},{2,0},{3,1},{4,2},{5,3},{6,4},{7,5},{8,6},{9,7},{10,... | collective-permute-start | bytes 442376 | tf_op jit(solution)/shard_map/ppermute | solution.py:36
  103.2 9.2 %collective-permute-start.30 = (bf16[3,192,128]{2,1,0:T(8,128)(2,1)}, bf16[3,192,128]{2,1,0:T(8,128)(2,1)S(1)}, u32[]{:S(2)}, u32[]{:S(2)}) collective-permute-start(bf16[3,192,128]{2,1,0:T(8,128)(2,1)} %get-tuple-element.86), channel_id=1, source_target_pairs={{0,2},{1,3},{2,4},{3,5},{4,6},{5,7},{6,8},{7,9},{8,10},{9,11},{10,... | collective-permute-start | bytes 442376 | tf_op jit(solution)/shard_map/ppermute | solution.py:36
  114.8 24.6 %collective-permute-start.32 = (bf16[3,192,128]{2,1,0:T(8,128)(2,1)}, bf16[3,192,128]{2,1,0:T(8,128)(2,1)S(1)}, u32[]{:S(2)}, u32[]{:S(2)}) collective-permute-start(bf16[3,192,128]{2,1,0:T(8,128)(2,1)} %get-tuple-element.88), channel_id=1, source_target_pairs={{0,6},{1,7},{2,8},{3,9},{4,10},{5,11},{6,12},{7,13},{8,14},{9,15},... | collective-permute-start | bytes 442376 | tf_op jit(solution)/shard_map/ppermute | solution.py:36
  116.9 22.6 %collective-permute-start.33 = (bf16[3,192,128]{2,1,0:T(8,128)(2,1)}, bf16[3,192,128]{2,1,0:T(8,128)(2,1)S(1)}, u32[]{:S(2)}, u32[]{:S(2)}) collective-permute-start(bf16[3,192,128]{2,1,0:T(8,128)(2,1)} %get-tuple-element.89), channel_id=1, source_target_pairs={{0,8},{1,9},{2,10},{3,11},{4,12},{5,13},{6,14},{7,15},{8,0},{9,1},... | collective-permute-start | bytes 442376 | tf_op jit(solution)/shard_map/ppermute | solution.py:36
  117.9 21.5 %collective-permute-start.34 = (bf16[3,192,128]{2,1,0:T(8,128)(2,1)}, bf16[3,192,128]{2,1,0:T(8,128)(2,1)S(1)}, u32[]{:S(2)}, u32[]{:S(2)}) collective-permute-start(bf16[3,192,128]{2,1,0:T(8,128)(2,1)} %get-tuple-element.90), channel_id=1, source_target_pairs={{0,10},{1,11},{2,12},{3,13},{4,14},{5,15},{6,0},{7,1},{8,2},{9,3},... | collective-permute-start | bytes 442376 | tf_op jit(solution)/shard_map/ppermute | solution.py:36
  120.6 18.9 %collective-permute-start.35 = (bf16[3,192,128]{2,1,0:T(8,128)(2,1)}, bf16[3,192,128]{2,1,0:T(8,128)(2,1)S(1)}, u32[]{:S(2)}, u32[]{:S(2)}) collective-permute-start(bf16[3,192,128]{2,1,0:T(8,128)(2,1)} %get-tuple-element.91), channel_id=1, source_target_pairs={{0,12},{1,13},{2,14},{3,15},{4,0},{5,1},{6,2},{7,3},{8,4},{9,5},{1... | collective-permute-start | bytes 442376 | tf_op jit(solution)/shard_map/ppermute | solution.py:36
  122.9 16.6 %collective-permute-start.36 = (bf16[3,192,128]{2,1,0:T(8,128)(2,1)}, bf16[3,192,128]{2,1,0:T(8,128)(2,1)S(1)}, u32[]{:S(2)}, u32[]{:S(2)}) collective-permute-start(bf16[3,192,128]{2,1,0:T(8,128)(2,1)} %get-tuple-element.92), channel_id=1, source_target_pairs={{0,14},{1,15},{2,0},{3,1},{4,2},{5,3},{6,4},{7,5},{8,6},{9,7},{10,... | collective-permute-start | bytes 442376 | tf_op jit(solution)/shard_map/ppermute | solution.py:36
  162.1 12.3 %collective-permute-start.46 = (bf16[112,128]{1,0:T(8,128)(2,1)}, bf16[112,128]{1,0:T(8,128)(2,1)S(1)}, u32[]{:S(2)}, u32[]{:S(2)}) collective-permute-start(bf16[112,128]{1,0:T(8,128)(2,1)} %get-tuple-element.104), channel_id=1, source_target_pairs={{0,10},{1,11},{2,12},{3,13},{4,14},{5,15},{6,0},{7,1},{8,2},{9,3},... | collective-permute-start | bytes 86024 | tf_op jit(solution)/shard_map/ppermute | solution.py:36
  162.7 14.4 %collective-permute-start.47 = (bf16[112,128]{1,0:T(8,128)(2,1)}, bf16[112,128]{1,0:T(8,128)(2,1)}, u32[]{:S(2)}, u32[]{:S(2)}) collective-permute-start(bf16[112,128]{1,0:T(8,128)(2,1)} %get-tuple-element.105), channel_id=1, source_target_pairs={{0,6},{1,7},{2,8},{3,9},{4,10},{5,11},{6,12},{7,13},{8,14},{9,15},... | collective-permute-start | bytes 86024 | tf_op jit(solution)/shard_map/ppermute | solution.py:36
  165.6 11.5 %collective-permute-start.48 = (bf16[112,128]{1,0:T(8,128)(2,1)}, bf16[112,128]{1,0:T(8,128)(2,1)}, u32[]{:S(2)}, u32[]{:S(2)}) collective-permute-start(bf16[112,128]{1,0:T(8,128)(2,1)} %get-tuple-element.106), channel_id=1, source_target_pairs={{0,12},{1,13},{2,14},{3,15},{4,0},{5,1},{6,2},{7,3},{8,4},{9,5},{1... | collective-permute-start | bytes 86024 | tf_op jit(solution)/shard_map/ppermute | solution.py:36
  168.3 8.8 %collective-permute-start.49 = (bf16[112,128]{1,0:T(8,128)(2,1)}, bf16[112,128]{1,0:T(8,128)(2,1)}, u32[]{:S(2)}, u32[]{:S(2)}) collective-permute-start(bf16[112,128]{1,0:T(8,128)(2,1)} %get-tuple-element.107), channel_id=1, source_target_pairs={{0,4},{1,5},{2,6},{3,7},{4,8},{5,9},{6,10},{7,11},{8,12},{9,13},{1... | collective-permute-start | bytes 86024 | tf_op jit(solution)/shard_map/ppermute | solution.py:36
  168.3 8.8 %collective-permute-start.50 = (bf16[112,128]{1,0:T(8,128)(2,1)}, bf16[112,128]{1,0:T(8,128)(2,1)}, u32[]{:S(2)}, u32[]{:S(2)}) collective-permute-start(bf16[112,128]{1,0:T(8,128)(2,1)} %get-tuple-element.108), channel_id=1, source_target_pairs={{0,14},{1,15},{2,0},{3,1},{4,2},{5,3},{6,4},{7,5},{8,6},{9,7},{10,... | collective-permute-start | bytes 86024 | tf_op jit(solution)/shard_map/ppermute | solution.py:36
  184.5 10.8 %collective-permute-start.52 = (bf16[192,256]{1,0:T(8,128)(2,1)}, bf16[192,256]{1,0:T(8,128)(2,1)S(1)}, u32[]{:S(2)}, u32[]{:S(2)}) collective-permute-start(bf16[192,256]{1,0:T(8,128)(2,1)} %get-tuple-element.111.own_ref), channel_id=1, source_target_pairs={{0,2},{1,3},{2,4},{3,5},{4,6},{5,7},{6,8},{7,9},{8,10},{9,11},{10,... | collective-permute-start | bytes 294920 | tf_op jit(solution)/shard_map/ppermute | solution.py:31
  185.7 9.5 %collective-permute-start.53 = (bf16[192,256]{1,0:T(8,128)(2,1)}, bf16[192,256]{1,0:T(8,128)(2,1)}, u32[]{:S(2)}, u32[]{:S(2)}) collective-permute-start(bf16[192,256]{1,0:T(8,128)(2,1)} %get-tuple-element.111.own_ref), channel_id=1, source_target_pairs={{0,1},{1,2},{2,3},{3,4},{4,5},{5,6},{6,7},{7,8},{8,9},{9,10},{10,1... | collective-permute-start | bytes 294920 | tf_op jit(solution)/shard_map/ppermute | solution.py:31
  213.0 13.3 %all-to-all-start = ((f32[16,3,768]{2,1,0:T(4,128)}), f32[16,3,768]{2,1,0:T(4,128)S(1)}, u32[]{:S(2)}, u32[]{:S(2)}) async-start(f32[16,3,768]{2,1,0:T(4,128)} %get-tuple-element.113), calls=%async_computation | async-start | bytes 393216 | tf_op jit(solution)/shard_map/all_to_all | solution.py:775
  (69 other events, 753.1 us)

commit v2 on v1

--- a/solution.py
+++ b/solution.py
@@ -17,18 +17,13 @@
 CH = 384
 TEXT_W = 768
 KEY_CHUNK = 512
+GATES = (2, 4)
 
 
 highest = lax.Precision.HIGHEST
 VM = pl.BlockSpec(memory_space=pltpu.VMEM)
 SM = pl.BlockSpec(memory_space=pltpu.SMEM)
 ANY = pl.BlockSpec(memory_space=pl.ANY)
-
-
-def shifted(value, axis, steps):
-    count = lax.axis_size(axis)
-    initial, last = (max(0, -steps), min(count, count - steps))
-    return lax.ppermute(value, axis, [(source, source + steps) for source in range(initial, last)])
 
 
 def rotate(value, axis, steps):
@@ -221,9 +216,13 @@
             share = sum_ref[b]
             for n in range(earlier):
                 share = share + prev_s[n, b]
-            out_refs[b][:PATCH] = jnp.concatenate(
+            half = PATCH + 8 * frames
+            spots = ((out_refs[b], 0), (out_refs[(b - 1) % blocks], half))
+            beside = jnp.concatenate(
                 [share[f * PATCH : (f + 1) * PATCH, :LAT] for f in range(frames)], axis=1
             ).astype(jnp.bfloat16)
+            for ref, at in spots:
+                ref[at : at + PATCH] = beside
             for f in range(frames):
                 square = lax.dot_general(
                     pick,
@@ -237,7 +236,9 @@
                 )
                 high = square.astype(jnp.bfloat16).astype(jnp.float32)
                 both = jnp.where(row == 0, high, jnp.where(row == 1, square - high, 0.0))
-                out_refs[b][PATCH + 8 * f : PATCH + 8 * (f + 1)] = both.astype(jnp.bfloat16)
+                for ref, at in spots:
+                    at = at + PATCH + 8 * f
+                    ref[at : at + 8] = both.astype(jnp.bfloat16)
 
 
 def attend(near, far, steps, scale, weight, earlier, last):
@@ -247,7 +248,7 @@
     frames = rows // PATCH
     sums = (blocks, rows, 128)
     if last:
-        share = (PATCH + 8 * frames, frames * LAT)
+        share = (2 * (PATCH + 8 * frames), frames * LAT)
         out_shape = [jax.ShapeDtypeStruct(share, jnp.bfloat16)] * blocks
         out_specs = [VM] * blocks
     else:
@@ -330,9 +331,9 @@
     return as_matrix(col == source)
 
 
-def latent_kernel(parts, width, frames, dt_ref, *refs):
+def latent_kernel(parts, width, frames, flag_ref, dt_ref, *refs):
     part_refs, refs = refs[:parts], refs[parts:]
-    lat_ref, base_ref, next_ref, win_ref = refs
+    own_ref, far_ref, base_ref, next_ref, win_ref, before_ref, pass_ref = refs
     total = part_refs[0][...].astype(jnp.float32)
     for r in part_refs[1:]:
         total = total + r[...].astype(jnp.float32)
@@ -342,44 +343,50 @@
     moves = jnp.concatenate([move_matrix(di, dj, 128) for di, dj in OFFSETS], axis=1)
     places = jnp.concatenate([place_matrix(di, dj) for di, dj in OFFSETS], axis=1)
     none = jnp.zeros((128 - PATCH, cols), jnp.bfloat16)
-    for f in range(frames):
-        at = slice(f * PATCH, (f + 1) * PATCH)
-        squares = total[PATCH + 8 * f : PATCH + 8 * (f + 1)]
-        square = lax.dot_general(
-            squares,
-            pick,
-            (((0,), (0,)), ((), ())),
-            precision=highest,
-            preferred_element_type=jnp.float32,
-        )[:PATCH, :LAT]
-        inverse = lax.rsqrt(square * np.float32(1.0 / width) + 1e-06)
-        scaled = total[:PATCH, f * LAT : (f + 1) * LAT] * inverse
-        value = lat_ref[at] + dt_ref[f] * (scaled + base_ref[f : f + 1])
-        next_ref[at] = value
-        spread = jnp.dot(
-            value.astype(jnp.bfloat16), places, preferred_element_type=jnp.float32
-        ).astype(jnp.bfloat16)
-        stacked = jnp.concatenate(
-            [x for o in range(len(OFFSETS)) for x in (spread[:, o * cols : (o + 1) * cols], none)],
-            axis=0,
-        )
-        win_ref[at] = jnp.dot(moves, stacked, preferred_element_type=jnp.float32).astype(
-            jnp.bfloat16
-        )
-
-
-def step_latent(parts, latent_in, base, step_dt, width):
-    rows = latent_in.shape[0]
+    first_chip, core = flag_ref[0], flag_ref[1]
+    for side, latent in enumerate((jnp.transpose(own_ref[...]), jnp.transpose(far_ref[...]))):
+        skip = side * (PATCH + 8 * frames)
+        for f in range(frames):
+            at = slice(f * PATCH, (f + 1) * PATCH)
+            squares = total[skip + PATCH + 8 * f : skip + PATCH + 8 * (f + 1)]
+            square = lax.dot_general(
+                squares,
+                pick,
+                (((0,), (0,)), ((), ())),
+                precision=highest,
+                preferred_element_type=jnp.float32,
+            )[:PATCH, :LAT]
+            inverse = lax.rsqrt(square * np.float32(1.0 / width) + 1e-06)
+            scaled = total[skip : skip + PATCH, f * LAT : (f + 1) * LAT] * inverse
+            g = side * frames + f
+            value = latent[at] + dt_ref[g] * (scaled + base_ref[g : g + 1])
+            spread = jnp.dot(
+                value.astype(jnp.bfloat16), places, preferred_element_type=jnp.float32
+            ).astype(jnp.bfloat16)
+            stacked = jnp.concatenate(
+                [x for o in range(len(OFFSETS)) for x in (spread[:, o * cols : (o + 1) * cols], none)],
+                axis=0,
+            )
+            window = jnp.dot(moves, stacked, preferred_element_type=jnp.float32)
+            if side:
+                window = jnp.where(first_chip == 1, 0.0, window)
+                before_ref[at] = window.astype(jnp.bfloat16)
+                pass_ref[at] = jnp.where(core == 0, win_ref[at], before_ref[at])
+            else:
+                next_ref[at] = value
+                win_ref[at] = window.astype(jnp.bfloat16)
+
+
+def step_latent(flags, parts, own, far, base, step_dt, width):
+    rows = own.shape[1]
+    window = jax.ShapeDtypeStruct((rows, 16 * LAT_C), jnp.bfloat16)
     return pl.pallas_call(
         functools.partial(latent_kernel, len(parts), width, rows // PATCH),
-        out_shape=[
-            jax.ShapeDtypeStruct((rows, LAT), jnp.float32),
-            jax.ShapeDtypeStruct((rows, 16 * LAT_C), jnp.bfloat16),
-        ],
-        in_specs=[SM] + [VM] * (len(parts) + 2),
-        out_specs=[VM, VM],
+        out_shape=[jax.ShapeDtypeStruct((rows, LAT), jnp.float32), window, window, window],
+        in_specs=[SM, SM] + [VM] * (len(parts) + 3),
+        out_specs=[VM] * 4,
         name="latent",
-    )(step_dt, *parts, latent_in, base)
+    )(flags, step_dt, *parts, own, far, base)
 
 
 def text_kernel(at_ref, id_ref, table_hbm, out_ref, buf, sem):
@@ -442,7 +449,6 @@
     b2_ref,
     pg_ref,
     post_ref,
-    text_ref,
     w2_hbm,
     pw_hbm,
     proj_hbm,
@@ -559,8 +565,6 @@
         row = jnp.sum(columns[:, f : f + 1] * proj_s[...], axis=0, keepdims=True)
         for n in range(sent_ref.shape[0]):
             sent_ref[n, f : f + 1, :] = row
-    for n in range(sent_ref.shape[0]):
-        sent_ref[n, frames : frames + 1, :] = text_ref[...]
 
 
 def window_weight(weight):
@@ -574,7 +578,7 @@
 
 
 def decode(
-    lead, far, near, own, w1, b1, gain, w2, b2, pw, patch_gain, post_gain, proj, text, devices
+    lead, far, near, own, w1, b1, gain, w2, b2, pw, patch_gain, post_gain, proj, devices
 ):
     rows = own.shape[0]
     frames = rows // PATCH
@@ -583,9 +587,9 @@
         functools.partial(decode_kernel, frames),
         out_shape=[
             jax.ShapeDtypeStruct((frames * 4 * PATCH, CH), jnp.bfloat16),
-            jax.ShapeDtypeStruct((devices, frames + 1, proj.shape[1]), jnp.float32),
+            jax.ShapeDtypeStruct((devices, frames, proj.shape[1]), jnp.float32),
         ],
-        in_specs=[SM] + [VM] * 10 + [ANY, ANY, ANY],
+        in_specs=[SM] + [VM] * 9 + [ANY, ANY, ANY],
         out_specs=[VM, VM],
         scratch_shapes=[
             pltpu.VMEM(w2.shape, jnp.bfloat16),
@@ -607,15 +611,14 @@
         b2,
         patch_gain,
         post_gain,
-        text,
         w2,
         pw,
         proj,
     )
 
 
-def rate_kernel(frames, slot_ref, got_ref, vec_ref, score_ref):
-    text = jnp.sum(got_ref[:, frames, :], axis=0, keepdims=True)
+def rate_kernel(frames, slot_ref, text_ref, got_ref, vec_ref, score_ref):
+    text = text_ref[...]
     text_rms = jnp.sqrt(jnp.mean(text * text) + 1e-06)
     for f in range(frames):
         slot = slot_ref[f]
@@ -629,7 +632,7 @@
         score_ref[f] = 100.0 * inner / (TEXT_W * image_rms * text_rms)
 
 
-def rate(slots, got):
+def rate(slots, text, got):
     frames = slots.shape[0]
     return pl.pallas_call(
         functools.partial(rate_kernel, frames),
@@ -637,10 +640,10 @@
             jax.ShapeDtypeStruct((frames, got.shape[2]), jnp.float32),
             jax.ShapeDtypeStruct((frames,), jnp.float32),
         ],
-        in_specs=[SM, VM],
+        in_specs=[SM, VM, VM],
         out_specs=[VM, SM],
         name="rate",
-    )(slots, got)
+    )(slots, text, got)
 
 
 def local(
@@ -686,8 +689,7 @@
 
     blocks = packed(firsts[0], phases[0])
     got = [blocks[0]] * chips
-    got[order[0]] = rotate(blocks[order[0]], "seq", order[0])
-    for turn in order[1:]:
+    for turn in order:
         got[turn] = rotate(blocks[turn], "seq", turn)
     scale = lax.dynamic_slice_in_dim(mod_table[:, 1, :], chip * cols, cols, 1)
     scale = scale.reshape(-1, heads, 1, HD)
@@ -695,9 +697,14 @@
     weight = jnp.pad(weight, ((0, 0), (0, 0), (0, 128 - LAT)))
     origin = 2 * ((chip - jnp.arange(chips)) % chips) + core
     steps = jnp.take(timestep.reshape(devices, frames), origin, axis=0).reshape(-1)
-    own_steps = lax.dynamic_slice_in_dim(timestep, me * frames, frames, 0)
-    base = jnp.dot(jnp.take(mod_table[:, 0, :], own_steps, axis=0), head_weight, precision=highest)
-    step_dt = jnp.take(step_size, own_steps)
+    near_steps = jnp.stack(
+        [
+            lax.dynamic_slice_in_dim(timestep, at * frames, frames, 0)
+            for at in (me, jnp.maximum(me - 2, 0))
+        ]
+    ).reshape(-1)
+    base = jnp.dot(jnp.take(mod_table[:, 0, :], near_steps, axis=0), head_weight, precision=highest)
+    step_dt = jnp.take(step_size, near_steps)
     text_row = text_mean(
         (me * text_table.shape[1]).astype(jnp.int32).reshape(1), prompt_ids, text_table.T
     )
@@ -717,11 +724,18 @@
         patch_gain=patch_gain.reshape(1, -1),
         post_gain=post_gain.reshape(1, -1),
         lead=(me == 0).astype(jnp.int32).reshape(1),
-        latent_in=latent_in,
+        flags=jnp.stack([chip == 0, core]).astype(jnp.int32),
         later=[packed(f, n) for f, n in zip(firsts[1:], phases[1:])],
     )
+    words = jnp.broadcast_to(prepared["text"][None], (devices, 1, TEXT_W))
+    words = lax.all_to_all(words, "seq", split_axis=0, concat_axis=0, tiled=True)
+    words = jnp.sum(words, axis=0)
+    far_latent = rotate(latent_in.T, "seq", 1)
+    steps, words, far_latent = lax.optimization_barrier((prepared["steps"], words, far_latent))
     phase_blocks = [got]
-    for blocks in prepared["later"]:
+    for gate, blocks in zip(GATES, prepared["later"]):
+        before = phase_blocks[0][order[min(gate, len(order) - 1)]]
+        blocks, _ = lax.optimization_barrier((blocks, before))
         got = [blocks[0]] * chips
         for turn in order:
             got[turn] = rotate(blocks[turn], "seq", turn)
@@ -735,7 +749,7 @@
         shares = attend(
             got,
             other,
-            prepared["steps"],
+            steps,
             prepared["scales"][n],
             prepared["weights"][n],
             sums if last else [],
@@ -745,15 +759,16 @@
             sums.append(shares)
     parts = [shares[0]] + [rotate(shares[t], "seq", chips - t) for t in order]
 
-    latent_next, window = step_latent(
+    latent_next, window, far, passed = step_latent(
+        prepared["flags"],
         parts,
-        prepared["latent_in"],
+        latent_in.T,
+        far_latent,
         prepared["base"],
         prepared["step_dt"],
         width,
     )
-    near = shifted(window, "seq", 1)
-    far = shifted(window, "seq", 2)
+    near = swap_core(passed, "seq")
     decoded, sent = decode(
         prepared["lead"],
         far,
@@ -768,12 +783,11 @@
         prepared["patch_gain"],
         prepared["post_gain"],
         proj_weight,
-        prepared["text"],
         devices,
     )
     decoded = decoded.reshape(frames, 2 * GRID_H, 2 * GRID_W, CH)
     spread = lax.all_to_all(sent, "seq", split_axis=0, concat_axis=0, tiled=True)
-    image_vec, scores = rate(prepared["slots"], spread)
+    image_vec, scores = rate(prepared["slots"], words, spread)
     return (latent_next, decoded, image_vec, scores)
 
 

time: 230 us -> 238 us (1.035)
  starting transfers between devices: 81 us -> 87.9 us
    all_to_all x0 -> x1, starting transfers between devices: none -> 7.41 us  [local(): lax.all_to_all(words, 'seq', split_axis=0, concat_axis=0, tiled=True)]
    ppermute x28 -> x29, starting transfers between devices: 67.7 us -> 71.6 us  [rotate(): lax.ppermute(value, axis, [(i, (i + 2 * steps) % count) for i in range(co...]
    unnamed x95 -> x94, local copies, waits for them, and re-layouts: 6.44 us -> 3.1 us
    ppermute x2 -> x0, starting transfers between devices: 3.23 us -> none  [shifted(): lax.ppermute(value, axis, [(source, source + steps) for source in range(i...]
    ppermute x28 -> x29, waiting for transfers between devices: 33.3 us -> 35.2 us  [rotate(): lax.ppermute(value, axis, [(i, (i + 2 * steps) % count) for i in range(co...]
    ppermute x24 -> x25, starting transfers between devices: 5.61 us -> 5.35 us  [swap_core(): return lax.ppermute(value, axis, [(i, i ^ 1) for i in range(count)])]
  transfers between devices with their start and end apart: 55 -> 56, of which waited for: 7 -> 9; matrix products, arithmetic and copies ran while one was open for 7% -> 7% of each run, Pallas kernels for 20% -> 19%
where the time goes in v2:
time: 238 us; the launch traced here: 237 us
  starting transfers between devices  87.9 us (37%)
  Pallas kernels  85.7 us (36%)
  waiting for transfers between devices  41.2 us (17%)
  local copies, waits for them, and re-layouts  14.2 us (6%)
  other arithmetic  4.57 us (2%)
    ppermute x29, starting transfers between devices, rotate(): lax.ppermute(value, axis, [(i, (i + 2 * steps) % count) for i in range(co...  71.6 us
    pallas_call x3, Pallas kernels, attend(): pl.pallas_call(functools.partial(attend_kernel, blocks, heads, frames, le...  49 us
    ppermute x29, waiting for transfers between devices, rotate(): lax.ppermute(value, axis, [(i, (i + 2 * steps) % count) for i in range(co...  35.2 us
    pallas_call x1, Pallas kernels, decode(): pl.pallas_call(functools.partial(decode_kernel, frames), out_shape=[jax.S...  17.1 us
    pallas_call x3, Pallas kernels, pack(): pl.pallas_call(functools.partial(pack_kernel, blocks), out_shape=[jax.Sha...  9.3 us
    all_to_all x1, starting transfers between devices, local(): lax.all_to_all(words, 'seq', split_axis=0, concat_axis=0, tiled=True)  7.41 us
    all_to_all x1, waiting for transfers between devices, local(): lax.all_to_all(sent, 'seq', split_axis=0, concat_axis=0, tiled=True)  6.02 us
    ppermute x25, starting transfers between devices, swap_core(): return lax.ppermute(value, axis, [(i, i ^ 1) for i in range(count)])  5.35 us
  transfers between devices with their start and end apart: 56, of which 9 were waited for; matrix products, arithmetic and copies ran while one was open for 7% of the time, Pallas kernels for 19%

profile of v2, /device:TPU:0, one launch (start us, length us, event | category | flops | bytes accessed | tf_op | source)
XLA Modules:
  0.0 236.8 jit_solution(163014004398778776)
XLA Ops:
  0.7 4.3 %text.1 = f32[1,768]{1,0:T(1,128)} custom-call(s32[1]{0:T(128)} %bitcast.6.at_ref, s32[77]{0:T(128)} %id_ref.1, bf16[48,24704]{1,0:T(8,128)(2,1)} %bitcast.31), custom_call_target="tpu_custom_call" | custom-call | tf_op jit(solution)/shard_map/text/pallas_call | solution.py:427
  6.4 7.4 %all-to-all-start = ((f32[16,1,768]{2,1,0:T(1,128)}), f32[16,1,768]{2,1,0:T(1,128)S(1)}, u32[]{:S(2)}, u32[]{:S(2)}) async-start(f32[16,1,768]{2,1,0:T(1,128)} %broadcast_in_dim.28), calls=%async_computation | async-start | bytes 98304 | tf_op jit(solution)/shard_map/all_to_all | solution.py:731
  13.8 1.9 collective-permute-start
  16.3 3.4 %pack.3 = (bf16[3,192,256]{2,1,0:T(8,128)(2,1)}, bf16[3,192,256]{2,1,0:T(8,128)(2,1)}, bf16[3,192,256]{2,1,0:T(8,128)(2,1)}, bf16[3,192,256]{2,1,0:T(8,128)(2,1)...) custom-call(s32[8]{0:T(128)} %get-tuple-element.188.at_ref, ...), custom_call_target="tpu_custom_call" | custom-call | tf_op jit(solution)/shard_map/pack/pallas_call | solution.py:66
  22.6 2.4 collective-permute-start.3
  27.6 3.0 %pack.4 = (bf16[3,192,128]{2,1,0:T(8,128)(2,1)}, bf16[3,192,128]{2,1,0:T(8,128)(2,1)}, bf16[3,192,128]{2,1,0:T(8,128)(2,1)}, bf16[3,192,128]{2,1,0:T(8,128)(2,1)...) custom-call(s32[8]{0:T(128)} %broadcast_add_fusion.1.at_ref, ...), custom_call_target="tpu_custom_call" | custom-call | tf_op jit(solution)/shard_map/pack/pallas_call | solution.py:66
  32.6 2.5 %collective-permute-start.6 = (bf16[3,192,256]{2,1,0:T(8,128)(2,1)}, bf16[3,192,256]{2,1,0:T(8,128)(2,1)S(1)}, u32[]{:S(2)}, u32[]{:S(2)}) collective-permute-start(bf16[3,192,256]{2,1,0:T(8,128)(2,1)} %get-tuple-element.88), channel_id=1, source_target_pairs={{0,12},{1,13},{2,14},{3,15},{4,0},{5,1},{6,2},{7,3},{8,4},{9,5},{1... | collective-permute-start | bytes 884744 | tf_op jit(solution)/shard_map/ppermute | solution.py:31
  35.1 4.4 %collective-permute-start.7 = (bf16[3,192,256]{2,1,0:T(8,128)(2,1)}, bf16[3,192,256]{2,1,0:T(8,128)(2,1)S(1)}, u32[]{:S(2)}, u32[]{:S(2)}) collective-permute-start(bf16[3,192,256]{2,1,0:T(8,128)(2,1)} %get-tuple-element.89), channel_id=1, source_target_pairs={{0,14},{1,15},{2,0},{3,1},{4,2},{5,3},{6,4},{7,5},{8,6},{9,7},{10,... | collective-permute-start | bytes 884744 | tf_op jit(solution)/shard_map/ppermute | solution.py:31
  39.6 17.3 %collective-permute-done.3.refs_3_ = bf16[3,192,256]{2,1,0:T(8,128)(2,1)} collective-permute-done((bf16[3,192,256]{2,1,0:T(8,128)(2,1)}, bf16[3,192,256]{2,1,0:T(8,128)(2,1)}, u32[]{:S(2)}, u32[]{:S(2)}) %collective-permute-start.3) | collective-permute-done | bytes 294944 | tf_op jit(solution)/shard_map/ppermute | solution.py:31
  57.8 7.2 %collective-permute-start.16 = (bf16[3,192,128]{2,1,0:T(8,128)(2,1)}, bf16[3,192,128]{2,1,0:T(8,128)(2,1)}, u32[]{:S(2)}, u32[]{:S(2)}) collective-permute-start(bf16[3,192,128]{2,1,0:T(8,128)(2,1)} %get-tuple-element.99), channel_id=1, source_target_pairs={{0,2},{1,3},{2,4},{3,5},{4,6},{5,7},{6,8},{7,9},{8,10},{9,11},{10,... | collective-permute-start | bytes 442376 | tf_op jit(solution)/shard_map/ppermute | solution.py:31
  65.0 11.9 %collective-permute-start.17 = (bf16[3,192,128]{2,1,0:T(8,128)(2,1)}, bf16[3,192,128]{2,1,0:T(8,128)(2,1)}, u32[]{:S(2)}, u32[]{:S(2)}) collective-permute-start(bf16[3,192,128]{2,1,0:T(8,128)(2,1)} %get-tuple-element.100), channel_id=1, source_target_pairs={{0,4},{1,5},{2,6},{3,7},{4,8},{5,9},{6,10},{7,11},{8,12},{9,13},{1... | collective-permute-start | bytes 442376 | tf_op jit(solution)/shard_map/ppermute | solution.py:31
  78.3 2.9 %pack.5 = (bf16[3,192,128]{2,1,0:T(8,128)(2,1)}, bf16[3,192,128]{2,1,0:T(8,128)(2,1)}, bf16[3,192,128]{2,1,0:T(8,128)(2,1)}, bf16[3,192,128]{2,1,0:T(8,128)(2,1)...) custom-call(s32[8]{0:T(128)} %get-tuple-element.189.at_ref, ...), custom_call_target="tpu_custom_call" | custom-call | tf_op jit(solution)/shard_map/pack/pallas_call | solution.py:66
  81.3 2.0 collective-permute-done.16.refs_1_
  89.1 2.9 %collective-permute-start.20 = (bf16[3,192,128]{2,1,0:T(8,128)(2,1)}, bf16[3,192,128]{2,1,0:T(8,128)(2,1)}, u32[]{:S(2)}, u32[]{:S(2)}) collective-permute-start(bf16[3,192,128]{2,1,0:T(8,128)(2,1)} %get-tuple-element.103), channel_id=1, source_target_pairs={{0,10},{1,11},{2,12},{3,13},{4,14},{5,15},{6,0},{7,1},{8,2},{9,3},... | collective-permute-start | bytes 442376 | tf_op jit(solution)/shard_map/ppermute | solution.py:31
  92.9 4.3 %collective-permute-start.22 = (bf16[3,192,128]{2,1,0:T(8,128)(2,1)}, bf16[3,192,128]{2,1,0:T(8,128)(2,1)S(1)}, u32[]{:S(2)}, u32[]{:S(2)}) collective-permute-start(bf16[3,192,128]{2,1,0:T(8,128)(2,1)} %get-tuple-element.105), channel_id=1, source_target_pairs={{0,14},{1,15},{2,0},{3,1},{4,2},{5,3},{6,4},{7,5},{8,6},{9,7},{10,... | collective-permute-start | bytes 442376 | tf_op jit(solution)/shard_map/ppermute | solution.py:31
  97.2 22.3 %attend.3.refs_0_ = f32[8,192,128]{2,1,0:T(8,128)} custom-call(s32[16]{0:T(128)} %select_n.109.t_ref, f32[16,2,1,128]{3,2,1,0:T(1,128)} %slice.39.sc_ref, f32[2,128,128]{2,1,0:T(8,128)} %pad_slice_fusion.1.w_ref, bf16[3,192,256]{2,1,0:T(8,128)(2,1)} %get-tuple-element.82.refs_0_, bf16[3,192,256]{2,1,0:T(8,128)(2,1)} %copy-done.14, ...), custom_call_target="tpu_custom_call" | custom-call | flops 4831838208 | bytes 3145728 | tf_op jit(solution)/shard_map/attend/pallas_call | solution.py:256
  120.4 8.4 %collective-permute-done.31.refs_3_ = bf16[3,192,128]{2,1,0:T(8,128)(2,1)S(1)} collective-permute-done((bf16[3,192,128]{2,1,0:T(8,128)(2,1)}, bf16[3,192,128]{2,1,0:T(8,128)(2,1)S(1)}, u32[]{:S(2)}, u32[]{:S(2)}) %collective-permute-start.31) | collective-permute-done | bytes 147488 | tf_op jit(solution)/shard_map/ppermute | solution.py:31
  133.7 2.9 %collective-permute-start.35 = (bf16[3,192,128]{2,1,0:T(8,128)(2,1)}, bf16[3,192,128]{2,1,0:T(8,128)(2,1)S(1)}, u32[]{:S(2)}, u32[]{:S(2)}) collective-permute-start(bf16[3,192,128]{2,1,0:T(8,128)(2,1)} %get-tuple-element.128), channel_id=1, source_target_pairs={{0,10},{1,11},{2,12},{3,13},{4,14},{5,15},{6,0},{7,1},{8,2},{9,3},... | collective-permute-start | bytes 442376 | tf_op jit(solution)/shard_map/ppermute | solution.py:31
  137.6 4.3 %collective-permute-start.37 = (bf16[3,192,128]{2,1,0:T(8,128)(2,1)S(1)}, bf16[3,192,128]{2,1,0:T(8,128)(2,1)S(1)}, u32[]{:S(2)}, u32[]{:S(2)}) collective-permute-start(bf16[3,192,128]{2,1,0:T(8,128)(2,1)S(1)} %copy-done.22), channel_id=1, source_target_pairs={{0,14},{1,15},{2,0},{3,1},{4,2},{5,3},{6,4},{7,5},{8,6},{9,7},{10,... | collective-permute-start | bytes 442376 | tf_op jit(solution)/shard_map/ppermute | solution.py:31
  141.9 12.8 %attend.4.refs_1_ = f32[8,192,128]{2,1,0:T(8,128)} custom-call(s32[16]{0:T(128)} %select_n.109.t_ref, f32[16,1,1,128]{3,2,1,0:T(1,128)} %get-tuple-element.184.sc_ref, f32[1,128,128]{2,1,0:T(8,128)} %get-tuple-element.182.w_ref, bf16[3,192,128]{2,1,0:T(8,128)(2,1)} %get-tuple-element.107.refs_0_, bf16[3,192,128]{2,1,0:T(8,128)(2,1)} %collective-permute-done.16.refs_1_, ...), custom_call_target="tpu_custom_call" | custom-call | flops 2415919104 | bytes 1572864 | tf_op jit(solution)/shard_map/attend/pallas_call | solution.py:256
  160.0 13.9 %attend.5 = (bf16[224,128]{1,0:T(8,128)(2,1)}, bf16[224,128]{1,0:T(8,128)(2,1)}, bf16[224,128]{1,0:T(8,128)(2,1)}, bf16[224,128]{1,0:T(8,128)(2,1)}, bf16[224,12...) custom-call(s32[16]{0:T(128)} %select_n.109.t_ref, ...), custom_call_target="tpu_custom_call" | custom-call | flops 2415919104 | bytes 1572864 | tf_op jit(solution)/shard_map/attend/pallas_call | solution.py:256
  173.9 3.2 %collective-permute-start.46 = (bf16[224,128]{1,0:T(8,128)(2,1)}, bf16[224,128]{1,0:T(8,128)(2,1)S(1)}, u32[]{:S(2)}, u32[]{:S(2)}) collective-permute-start(bf16[224,128]{1,0:T(8,128)(2,1)} %get-tuple-element.141), channel_id=1, source_target_pairs={{0,8},{1,9},{2,10},{3,11},{4,12},{5,13},{6,14},{7,15},{8,0},{9,1},... | collective-permute-start | bytes 172040 | tf_op jit(solution)/shard_map/ppermute | solution.py:31
  177.1 1.7 fusion.16
  178.9 3.1 %collective-permute-start.48 = (bf16[224,128]{1,0:T(8,128)(2,1)}, bf16[224,128]{1,0:T(8,128)(2,1)}, u32[]{:S(2)}, u32[]{:S(2)}) collective-permute-start(bf16[224,128]{1,0:T(8,128)(2,1)} %get-tuple-element.143), channel_id=1, source_target_pairs={{0,6},{1,7},{2,8},{3,9},{4,10},{5,11},{6,12},{7,13},{8,14},{9,15},... | collective-permute-start | bytes 172040 | tf_op jit(solution)/shard_map/ppermute | solution.py:31
  182.0 2.9 %collective-permute-start.49 = (bf16[224,128]{1,0:T(8,128)(2,1)}, bf16[224,128]{1,0:T(8,128)(2,1)}, u32[]{:S(2)}, u32[]{:S(2)}) collective-permute-start(bf16[224,128]{1,0:T(8,128)(2,1)} %get-tuple-element.144), channel_id=1, source_target_pairs={{0,12},{1,13},{2,14},{3,15},{4,0},{5,1},{6,2},{7,3},{8,4},{9,5},{1... | collective-permute-start | bytes 172040 | tf_op jit(solution)/shard_map/ppermute | solution.py:31
  184.9 5.9 %collective-permute-start.51 = (bf16[224,128]{1,0:T(8,128)(2,1)}, bf16[224,128]{1,0:T(8,128)(2,1)}, u32[]{:S(2)}, u32[]{:S(2)}) collective-permute-start(bf16[224,128]{1,0:T(8,128)(2,1)} %get-tuple-element.146), channel_id=1, source_target_pairs={{0,14},{1,15},{2,0},{3,1},{4,2},{5,3},{6,4},{7,5},{8,6},{9,7},{10,... | collective-permute-start | bytes 172040 | tf_op jit(solution)/shard_map/ppermute | solution.py:31
  193.0 5.1 %collective-permute-done.52.refs_7_ = bf16[224,128]{1,0:T(8,128)(2,1)} collective-permute-done((bf16[224,128]{1,0:T(8,128)(2,1)}, bf16[224,128]{1,0:T(8,128)(2,1)}, u32[]{:S(2)}, u32[]{:S(2)}) %collective-permute-start.52) | collective-permute-done | bytes 57376 | tf_op jit(solution)/shard_map/ppermute | solution.py:31
  198.1 4.2 %latent.1 = (f32[192,64]{1,0:T(8,128)}, bf16[192,256]{1,0:T(8,128)(2,1)}, bf16[192,256]{1,0:T(8,128)(2,1)}, bf16[192,256]{1,0:T(8,128)(2,1)}) custom-call(s32[2]{0:T(128)} %pad_add_fusion.1.flag_ref, f32[4]{0:T(128)} %get-tuple-element.174.dt_ref, bf16[224,128]{1,0:T(8,128)(2,1)} %get-tuple-element.140.refs_0_, bf16[224,128]{1,0:T(8,128)(2,1)} %copy-done.7, ...), custom_call_target="tpu_custom_call" | custom-call | tf_op jit(solution)/shard_map/latent/pallas_call | solution.py:383
  206.2 17.1 %decode.1 = (bf16[768,384]{1,0:T(8,128)(2,1)}, f32[16,2,768]{2,1,0:T(2,128)}) custom-call(s32[1]{0:T(128)} %bitcast.12.lead_ref, bf16[192,256]{1,0:T(8,128)(2,1)} %get-tuple-element.150.far_ref, bf16[192,256]{1,0:T(8,128)(2,1)} %copy-done.4, bf16[192,256]{1,0:T(8,128)(2,1)} %get-tuple-element.152.own_ref, bf16[768,1536]{1,0:T(8,128)(2,1)} %pad_maximum_fusion.w1_ref, ...), custom_call_target="tpu_custom_call" | custom-call | tf_op jit(solution)/shard_map/decode/pallas_call | solution.py:586
  223.3 3.5 %all-to-all-start.1 = ((f32[16,2,768]{2,1,0:T(2,128)}), f32[16,2,768]{2,1,0:T(2,128)S(1)}, u32[]{:S(2)}, u32[]{:S(2)}) async-start(f32[16,2,768]{2,1,0:T(2,128)} %get-tuple-element.155), calls=%async_computation.1 | async-start | bytes 196608 | tf_op jit(solution)/shard_map/all_to_all | solution.py:789
  228.2 6.0 %all-to-all-done.1.got_ref = f32[16,2,768]{2,1,0:T(2,128)S(1)} async-done(((f32[16,2,768]{2,1,0:T(2,128)}), f32[16,2,768]{2,1,0:T(2,128)S(1)}, u32[]{:S(2)}, u32[]{:S(2)}) %all-to-all-start.1) | async-done | bytes 98336 | tf_op jit(solution)/shard_map/all_to_all | solution.py:789
  234.8 1.8 rate.1
  (222 shorter events, 38.2 us)
Async XLA Ops:
  6.4 79.3 %all-to-all-start = ((f32[16,1,768]{2,1,0:T(1,128)}), f32[16,1,768]{2,1,0:T(1,128)S(1)}, u32[]{:S(2)}, u32[]{:S(2)}) async-start(f32[16,1,768]{2,1,0:T(1,128)} %broadcast_in_dim.28), calls=%async_computation | async-start | bytes 98304 | tf_op jit(solution)/shard_map/all_to_all | solution.py:731
  13.8 17.3 %collective-permute-start = (f32[64,192]{1,0:T(8,128)}, f32[64,192]{1,0:T(8,128)S(1)}, u32[]{:S(2)}, u32[]{:S(2)}) collective-permute-start(f32[64,192]{1,0:T(8,128)} %bitcast.40), channel_id=1, source_target_pairs={{0,2},{1,3},{2,4},{3,5},{4,6},{5,7},{6,8},{7,9},{8,10},{9,11},{10,... | collective-permute-start | bytes 147464 | tf_op jit(solution)/shard_map/ppermute | solution.py:31
  19.7 12.9 %collective-permute-start.1 = (bf16[3,192,256]{2,1,0:T(8,128)(2,1)}, bf16[3,192,256]{2,1,0:T(8,128)(2,1)S(1)}, u32[]{:S(2)}, u32[]{:S(2)}) collective-permute-start(bf16[3,192,256]{2,1,0:T(8,128)(2,1)} %get-tuple-element.83), channel_id=1, source_target_pairs={{0,2},{1,3},{2,4},{3,5},{4,6},{5,7},{6,8},{7,9},{8,10},{9,11},{10,... | collective-permute-start | bytes 884744 | tf_op jit(solution)/shard_map/ppermute | solution.py:31
  21.2 13.9 %collective-permute-start.2 = (bf16[3,192,256]{2,1,0:T(8,128)(2,1)}, bf16[3,192,256]{2,1,0:T(8,128)(2,1)S(1)}, u32[]{:S(2)}, u32[]{:S(2)}) collective-permute-start(bf16[3,192,256]{2,1,0:T(8,128)(2,1)} %get-tuple-element.84), channel_id=1, source_target_pairs={{0,4},{1,5},{2,6},{3,7},{4,8},{5,9},{6,10},{7,11},{8,12},{9,13},{1... | collective-permute-start | bytes 884744 | tf_op jit(solution)/shard_map/ppermute | solution.py:31
  22.6 34.3 %collective-permute-start.3 = (bf16[3,192,256]{2,1,0:T(8,128)(2,1)}, bf16[3,192,256]{2,1,0:T(8,128)(2,1)}, u32[]{:S(2)}, u32[]{:S(2)}) collective-permute-start(bf16[3,192,256]{2,1,0:T(8,128)(2,1)} %get-tuple-element.85), channel_id=1, source_target_pairs={{0,6},{1,7},{2,8},{3,9},{4,10},{5,11},{6,12},{7,13},{8,14},{9,15},... | collective-permute-start | bytes 884744 | tf_op jit(solution)/shard_map/ppermute | solution.py:31
  25.0 32.2 %collective-permute-start.4 = (bf16[3,192,256]{2,1,0:T(8,128)(2,1)}, bf16[3,192,256]{2,1,0:T(8,128)(2,1)}, u32[]{:S(2)}, u32[]{:S(2)}) collective-permute-start(bf16[3,192,256]{2,1,0:T(8,128)(2,1)} %get-tuple-element.86), channel_id=1, source_target_pairs={{0,8},{1,9},{2,10},{3,11},{4,12},{5,13},{6,14},{7,15},{8,0},{9,1},... | collective-permute-start | bytes 884744 | tf_op jit(solution)/shard_map/ppermute | solution.py:31
  31.1 26.3 %collective-permute-start.5 = (bf16[3,192,256]{2,1,0:T(8,128)(2,1)}, bf16[3,192,256]{2,1,0:T(8,128)(2,1)S(1)}, u32[]{:S(2)}, u32[]{:S(2)}) collective-permute-start(bf16[3,192,256]{2,1,0:T(8,128)(2,1)} %get-tuple-element.87), channel_id=1, source_target_pairs={{0,10},{1,11},{2,12},{3,13},{4,14},{5,15},{6,0},{7,1},{8,2},{9,3},... | collective-permute-start | bytes 884744 | tf_op jit(solution)/shard_map/ppermute | solution.py:31
  32.6 25.2 %collective-permute-start.6 = (bf16[3,192,256]{2,1,0:T(8,128)(2,1)}, bf16[3,192,256]{2,1,0:T(8,128)(2,1)S(1)}, u32[]{:S(2)}, u32[]{:S(2)}) collective-permute-start(bf16[3,192,256]{2,1,0:T(8,128)(2,1)} %get-tuple-element.88), channel_id=1, source_target_pairs={{0,12},{1,13},{2,14},{3,15},{4,0},{5,1},{6,2},{7,3},{8,4},{9,5},{1... | collective-permute-start | bytes 884744 | tf_op jit(solution)/shard_map/ppermute | solution.py:31
  35.1 29.8 %collective-permute-start.7 = (bf16[3,192,256]{2,1,0:T(8,128)(2,1)}, bf16[3,192,256]{2,1,0:T(8,128)(2,1)S(1)}, u32[]{:S(2)}, u32[]{:S(2)}) collective-permute-start(bf16[3,192,256]{2,1,0:T(8,128)(2,1)} %get-tuple-element.89), channel_id=1, source_target_pairs={{0,14},{1,15},{2,0},{3,1},{4,2},{5,3},{6,4},{7,5},{8,6},{9,7},{10,... | collective-permute-start | bytes 884744 | tf_op jit(solution)/shard_map/ppermute | solution.py:31
  56.9 24.3 %collective-permute-start.8 = (bf16[3,192,256]{2,1,0:T(8,128)(2,1)S(1)}, bf16[3,192,256]{2,1,0:T(8,128)(2,1)}, u32[]{:S(2)}, u32[]{:S(2)}) collective-permute-start(bf16[3,192,256]{2,1,0:T(8,128)(2,1)S(1)} %copy-done.13), channel_id=1, source_target_pairs={{0,1},{1,0},{2,3},{3,2},{4,5},{5,4},{6,7},{7,6},{8,9},{9,8},{10,11... | collective-permute-start | bytes 884744 | tf_op jit(solution)/shard_map/ppermute | solution.py:36
  57.2 26.7 %collective-permute-start.9 = (bf16[3,192,256]{2,1,0:T(8,128)(2,1)S(1)}, bf16[3,192,256]{2,1,0:T(8,128)(2,1)}, u32[]{:S(2)}, u32[]{:S(2)}) collective-permute-start(bf16[3,192,256]{2,1,0:T(8,128)(2,1)S(1)} %collective-permute-done.1.refs_1_), channel_id=1, source_target_pairs={{0,1},{1,0},{2,3},{3,2},{4,5},{5,4},{6,7},{7,6},{8,9},{9,8},{10,11... | collective-permute-start | bytes 884744 | tf_op jit(solution)/shard_map/ppermute | solution.py:36
  57.4 26.6 %collective-permute-start.10 = (bf16[3,192,256]{2,1,0:T(8,128)(2,1)S(1)}, bf16[3,192,256]{2,1,0:T(8,128)(2,1)}, u32[]{:S(2)}, u32[]{:S(2)}) collective-permute-start(bf16[3,192,256]{2,1,0:T(8,128)(2,1)S(1)} %collective-permute-done.2.refs_2_), channel_id=1, source_target_pairs={{0,1},{1,0},{2,3},{3,2},{4,5},{5,4},{6,7},{7,6},{8,9},{9,8},{10,11... | collective-permute-start | bytes 884744 | tf_op jit(solution)/shard_map/ppermute | solution.py:36
  57.8 25.6 %collective-permute-start.16 = (bf16[3,192,128]{2,1,0:T(8,128)(2,1)}, bf16[3,192,128]{2,1,0:T(8,128)(2,1)}, u32[]{:S(2)}, u32[]{:S(2)}) collective-permute-start(bf16[3,192,128]{2,1,0:T(8,128)(2,1)} %get-tuple-element.99), channel_id=1, source_target_pairs={{0,2},{1,3},{2,4},{3,5},{4,6},{5,7},{6,8},{7,9},{8,10},{9,11},{10,... | collective-permute-start | bytes 442376 | tf_op jit(solution)/shard_map/ppermute | solution.py:31
  65.0 18.5 %collective-permute-start.17 = (bf16[3,192,128]{2,1,0:T(8,128)(2,1)}, bf16[3,192,128]{2,1,0:T(8,128)(2,1)}, u32[]{:S(2)}, u32[]{:S(2)}) collective-permute-start(bf16[3,192,128]{2,1,0:T(8,128)(2,1)} %get-tuple-element.100), channel_id=1, source_target_pairs={{0,4},{1,5},{2,6},{3,7},{4,8},{5,9},{6,10},{7,11},{8,12},{9,13},{1... | collective-permute-start | bytes 442376 | tf_op jit(solution)/shard_map/ppermute | solution.py:31
  86.4 33.2 %collective-permute-start.18 = (bf16[3,192,128]{2,1,0:T(8,128)(2,1)}, bf16[3,192,128]{2,1,0:T(8,128)(2,1)}, u32[]{:S(2)}, u32[]{:S(2)}) collective-permute-start(bf16[3,192,128]{2,1,0:T(8,128)(2,1)} %get-tuple-element.101), channel_id=1, source_target_pairs={{0,6},{1,7},{2,8},{3,9},{4,10},{5,11},{6,12},{7,13},{8,14},{9,15},... | collective-permute-start | bytes 442376 | tf_op jit(solution)/shard_map/ppermute | solution.py:31
  88.0 31.6 %collective-permute-start.19 = (bf16[3,192,128]{2,1,0:T(8,128)(2,1)}, bf16[3,192,128]{2,1,0:T(8,128)(2,1)}, u32[]{:S(2)}, u32[]{:S(2)}) collective-permute-start(bf16[3,192,128]{2,1,0:T(8,128)(2,1)} %get-tuple-element.102), channel_id=1, source_target_pairs={{0,8},{1,9},{2,10},{3,11},{4,12},{5,13},{6,14},{7,15},{8,0},{9,1},... | collective-permute-start | bytes 442376 | tf_op jit(solution)/shard_map/ppermute | solution.py:31
  89.1 30.6 %collective-permute-start.20 = (bf16[3,192,128]{2,1,0:T(8,128)(2,1)}, bf16[3,192,128]{2,1,0:T(8,128)(2,1)}, u32[]{:S(2)}, u32[]{:S(2)}) collective-permute-start(bf16[3,192,128]{2,1,0:T(8,128)(2,1)} %get-tuple-element.103), channel_id=1, source_target_pairs={{0,10},{1,11},{2,12},{3,13},{4,14},{5,15},{6,0},{7,1},{8,2},{9,3},... | collective-permute-start | bytes 442376 | tf_op jit(solution)/shard_map/ppermute | solution.py:31
  92.0 27.7 %collective-permute-start.21 = (bf16[3,192,128]{2,1,0:T(8,128)(2,1)}, bf16[3,192,128]{2,1,0:T(8,128)(2,1)S(1)}, u32[]{:S(2)}, u32[]{:S(2)}) collective-permute-start(bf16[3,192,128]{2,1,0:T(8,128)(2,1)} %get-tuple-element.104), channel_id=1, source_target_pairs={{0,12},{1,13},{2,14},{3,15},{4,0},{5,1},{6,2},{7,3},{8,4},{9,5},{1... | collective-permute-start | bytes 442376 | tf_op jit(solution)/shard_map/ppermute | solution.py:31
  92.9 26.8 %collective-permute-start.22 = (bf16[3,192,128]{2,1,0:T(8,128)(2,1)}, bf16[3,192,128]{2,1,0:T(8,128)(2,1)S(1)}, u32[]{:S(2)}, u32[]{:S(2)}) collective-permute-start(bf16[3,192,128]{2,1,0:T(8,128)(2,1)} %get-tuple-element.105), channel_id=1, source_target_pairs={{0,14},{1,15},{2,0},{3,1},{4,2},{5,3},{6,4},{7,5},{8,6},{9,7},{10,... | collective-permute-start | bytes 442376 | tf_op jit(solution)/shard_map/ppermute | solution.py:31
  119.7 9.6 %collective-permute-start.23 = (bf16[3,192,128]{2,1,0:T(8,128)(2,1)S(1)}, bf16[3,192,128]{2,1,0:T(8,128)(2,1)S(1)}, u32[]{:S(2)}, u32[]{:S(2)}) collective-permute-start(bf16[3,192,128]{2,1,0:T(8,128)(2,1)S(1)} %copy-done.21), channel_id=1, source_target_pairs={{0,1},{1,0},{2,3},{3,2},{4,5},{5,4},{6,7},{7,6},{8,9},{9,8},{10,11... | collective-permute-start | bytes 442376 | tf_op jit(solution)/shard_map/ppermute | solution.py:36
  119.8 9.6 %collective-permute-start.24 = (bf16[3,192,128]{2,1,0:T(8,128)(2,1)}, bf16[3,192,128]{2,1,0:T(8,128)(2,1)S(1)}, u32[]{:S(2)}, u32[]{:S(2)}) collective-permute-start(bf16[3,192,128]{2,1,0:T(8,128)(2,1)} %collective-permute-done.16.refs_1_), channel_id=1, source_target_pairs={{0,1},{1,0},{2,3},{3,2},{4,5},{5,4},{6,7},{7,6},{8,9},{9,8},{10,11... | collective-permute-start | bytes 442376 | tf_op jit(solution)/shard_map/ppermute | solution.py:36
  120.3 9.6 %collective-permute-start.25 = (bf16[3,192,128]{2,1,0:T(8,128)(2,1)}, bf16[3,192,128]{2,1,0:T(8,128)(2,1)S(1)}, u32[]{:S(2)}, u32[]{:S(2)}) collective-permute-start(bf16[3,192,128]{2,1,0:T(8,128)(2,1)} %collective-permute-done.17.refs_2_), channel_id=1, source_target_pairs={{0,1},{1,0},{2,3},{3,2},{4,5},{5,4},{6,7},{7,6},{8,9},{9,8},{10,11... | collective-permute-start | bytes 442376 | tf_op jit(solution)/shard_map/ppermute | solution.py:36
  132.1 22.6 %collective-permute-start.33 = (bf16[3,192,128]{2,1,0:T(8,128)(2,1)}, bf16[3,192,128]{2,1,0:T(8,128)(2,1)S(1)}, u32[]{:S(2)}, u32[]{:S(2)}) collective-permute-start(bf16[3,192,128]{2,1,0:T(8,128)(2,1)} %get-tuple-element.126), channel_id=1, source_target_pairs={{0,6},{1,7},{2,8},{3,9},{4,10},{5,11},{6,12},{7,13},{8,14},{9,15},... | collective-permute-start | bytes 442376 | tf_op jit(solution)/shard_map/ppermute | solution.py:31
  132.1 22.6 %collective-permute-start.34 = (bf16[3,192,128]{2,1,0:T(8,128)(2,1)}, bf16[3,192,128]{2,1,0:T(8,128)(2,1)S(1)}, u32[]{:S(2)}, u32[]{:S(2)}) collective-permute-start(bf16[3,192,128]{2,1,0:T(8,128)(2,1)} %get-tuple-element.127), channel_id=1, source_target_pairs={{0,8},{1,9},{2,10},{3,11},{4,12},{5,13},{6,14},{7,15},{8,0},{9,1},... | collective-permute-start | bytes 442376 | tf_op jit(solution)/shard_map/ppermute | solution.py:31
  133.7 21.0 %collective-permute-start.35 = (bf16[3,192,128]{2,1,0:T(8,128)(2,1)}, bf16[3,192,128]{2,1,0:T(8,128)(2,1)S(1)}, u32[]{:S(2)}, u32[]{:S(2)}) collective-permute-start(bf16[3,192,128]{2,1,0:T(8,128)(2,1)} %get-tuple-element.128), channel_id=1, source_target_pairs={{0,10},{1,11},{2,12},{3,13},{4,14},{5,15},{6,0},{7,1},{8,2},{9,3},... | collective-permute-start | bytes 442376 | tf_op jit(solution)/shard_map/ppermute | solution.py:31
  136.6 18.2 %collective-permute-start.36 = (bf16[3,192,128]{2,1,0:T(8,128)(2,1)}, bf16[3,192,128]{2,1,0:T(8,128)(2,1)S(1)}, u32[]{:S(2)}, u32[]{:S(2)}) collective-permute-start(bf16[3,192,128]{2,1,0:T(8,128)(2,1)} %get-tuple-element.129), channel_id=1, source_target_pairs={{0,12},{1,13},{2,14},{3,15},{4,0},{5,1},{6,2},{7,3},{8,4},{9,5},{1... | collective-permute-start | bytes 442376 | tf_op jit(solution)/shard_map/ppermute | solution.py:31
  137.6 17.2 %collective-permute-start.37 = (bf16[3,192,128]{2,1,0:T(8,128)(2,1)S(1)}, bf16[3,192,128]{2,1,0:T(8,128)(2,1)S(1)}, u32[]{:S(2)}, u32[]{:S(2)}) collective-permute-start(bf16[3,192,128]{2,1,0:T(8,128)(2,1)S(1)} %copy-done.22), channel_id=1, source_target_pairs={{0,14},{1,15},{2,0},{3,1},{4,2},{5,3},{6,4},{7,5},{8,6},{9,7},{10,... | collective-permute-start | bytes 442376 | tf_op jit(solution)/shard_map/ppermute | solution.py:31
  173.9 11.0 %collective-permute-start.46 = (bf16[224,128]{1,0:T(8,128)(2,1)}, bf16[224,128]{1,0:T(8,128)(2,1)S(1)}, u32[]{:S(2)}, u32[]{:S(2)}) collective-permute-start(bf16[224,128]{1,0:T(8,128)(2,1)} %get-tuple-element.141), channel_id=1, source_target_pairs={{0,8},{1,9},{2,10},{3,11},{4,12},{5,13},{6,14},{7,15},{8,0},{9,1},... | collective-permute-start | bytes 172040 | tf_op jit(solution)/shard_map/ppermute | solution.py:31
  177.1 13.8 %collective-permute-start.47 = (bf16[224,128]{1,0:T(8,128)(2,1)}, bf16[224,128]{1,0:T(8,128)(2,1)S(1)}, u32[]{:S(2)}, u32[]{:S(2)}) collective-permute-start(bf16[224,128]{1,0:T(8,128)(2,1)} %get-tuple-element.142), channel_id=1, source_target_pairs={{0,10},{1,11},{2,12},{3,13},{4,14},{5,15},{6,0},{7,1},{8,2},{9,3},... | collective-permute-start | bytes 172040 | tf_op jit(solution)/shard_map/ppermute | solution.py:31
  178.9 12.6 %collective-permute-start.48 = (bf16[224,128]{1,0:T(8,128)(2,1)}, bf16[224,128]{1,0:T(8,128)(2,1)}, u32[]{:S(2)}, u32[]{:S(2)}) collective-permute-start(bf16[224,128]{1,0:T(8,128)(2,1)} %get-tuple-element.143), channel_id=1, source_target_pairs={{0,6},{1,7},{2,8},{3,9},{4,10},{5,11},{6,12},{7,13},{8,14},{9,15},... | collective-permute-start | bytes 172040 | tf_op jit(solution)/shard_map/ppermute | solution.py:31
  182.0 9.4 %collective-permute-start.49 = (bf16[224,128]{1,0:T(8,128)(2,1)}, bf16[224,128]{1,0:T(8,128)(2,1)}, u32[]{:S(2)}, u32[]{:S(2)}) collective-permute-start(bf16[224,128]{1,0:T(8,128)(2,1)} %get-tuple-element.144), channel_id=1, source_target_pairs={{0,12},{1,13},{2,14},{3,15},{4,0},{5,1},{6,2},{7,3},{8,4},{9,5},{1... | collective-permute-start | bytes 172040 | tf_op jit(solution)/shard_map/ppermute | solution.py:31
  223.3 10.9 %all-to-all-start.1 = ((f32[16,2,768]{2,1,0:T(2,128)}), f32[16,2,768]{2,1,0:T(2,128)S(1)}, u32[]{:S(2)}, u32[]{:S(2)}) async-start(f32[16,2,768]{2,1,0:T(2,128)} %get-tuple-element.155), calls=%async_computation.1 | async-start | bytes 196608 | tf_op jit(solution)/shard_map/all_to_all | solution.py:789
  (70 other events, 1009.1 us)

commit v3 on v2

--- a/solution.py
+++ b/solution.py
@@ -17,7 +17,7 @@
 CH = 384
 TEXT_W = 768
 KEY_CHUNK = 512
-GATES = (2, 4)
+GATES = (2,)
 
 
 highest = lax.Precision.HIGHEST
@@ -677,8 +677,8 @@
     me = lax.axis_index("seq")
     chip, core = me // 2, me % 2
 
-    tail = max(1, heads // 4)
-    phases = tuple(n for n in (heads - 2 * tail, tail, tail) if n > 0) if heads > tail else (tail,)
+    tail = max(1, heads // 2)
+    phases = (heads - tail, tail) if heads > tail else (tail,)
     firsts = [sum(phases[:n]) for n in range(len(phases))]
 
     order = sorted(range(1, chips), key=lambda t: abs(2 * t - chips))

time: 238 us -> 234 us (0.983)
  starting transfers between devices: 87.9 us -> 93.7 us
  Pallas kernels: 85.7 us -> 80.3 us
    ppermute x29 -> x22, starting transfers between devices: 71.6 us -> 79.5 us  [rotate(): lax.ppermute(value, axis, [(i, (i + 2 * steps) % count) for i in range(co...]
    pallas_call x3 -> x2, Pallas kernels: 49 us -> 45.9 us  [attend(): pl.pallas_call(functools.partial(attend_kernel, blocks, heads, frames, le...]
    ppermute x29 -> x22, waiting for transfers between devices: 35.2 us -> 32.7 us  [rotate(): lax.ppermute(value, axis, [(i, (i + 2 * steps) % count) for i in range(co...]
    pallas_call x3 -> x2, Pallas kernels: 9.3 us -> 7.04 us  [pack(): pl.pallas_call(functools.partial(pack_kernel, blocks), out_shape=[jax.Sha...]
    ppermute x25 -> x17, starting transfers between devices: 5.35 us -> 3.26 us  [swap_core(): return lax.ppermute(value, axis, [(i, i ^ 1) for i in range(count)])]
  transfers between devices with their start and end apart: 56 -> 41, of which waited for: 9 -> 11; matrix products, arithmetic and copies ran while one was open for 7% -> 6% of each run, Pallas kernels for 19% -> 13%
where the time goes in v3:
time: 234 us; the launch traced here: 233 us
  starting transfers between devices  93.7 us (40%)
  Pallas kernels  80.3 us (34%)
  waiting for transfers between devices  38.9 us (17%)
  local copies, waits for them, and re-layouts  13.5 us (6%)
  other arithmetic  4.19 us (2%)
    ppermute x22, starting transfers between devices, rotate(): lax.ppermute(value, axis, [(i, (i + 2 * steps) % count) for i in range(co...  79.5 us
    pallas_call x2, Pallas kernels, attend(): pl.pallas_call(functools.partial(attend_kernel, blocks, heads, frames, le...  45.9 us
    ppermute x22, waiting for transfers between devices, rotate(): lax.ppermute(value, axis, [(i, (i + 2 * steps) % count) for i in range(co...  32.7 us
    pallas_call x1, Pallas kernels, decode(): pl.pallas_call(functools.partial(decode_kernel, frames), out_shape=[jax.S...  17.1 us
    all_to_all x1, starting transfers between devices, local(): lax.all_to_all(words, 'seq', split_axis=0, concat_axis=0, tiled=True)  7.41 us
    pallas_call x2, Pallas kernels, pack(): pl.pallas_call(functools.partial(pack_kernel, blocks), out_shape=[jax.Sha...  7.04 us
    all_to_all x1, waiting for transfers between devices, local(): lax.all_to_all(sent, 'seq', split_axis=0, concat_axis=0, tiled=True)  6.06 us
  transfers between devices with their start and end apart: 41, of which 11 were waited for; matrix products, arithmetic and copies ran while one was open for 6% of the time, Pallas kernels for 13%

profile of v3, /device:TPU:0, one launch (start us, length us, event | category | flops | bytes accessed | tf_op | source)
XLA Modules:
  0.0 233.4 jit_solution(14394486701767490389)
XLA Ops:
  0.7 4.3 %text.1 = f32[1,768]{1,0:T(1,128)} custom-call(s32[1]{0:T(128)} %bitcast.6.at_ref, s32[77]{0:T(128)} %id_ref.1, bf16[48,24704]{1,0:T(8,128)(2,1)} %bitcast.31), custom_call_target="tpu_custom_call" | custom-call | tf_op jit(solution)/shard_map/text/pallas_call | solution.py:427
  6.4 7.4 %all-to-all-start = ((f32[16,1,768]{2,1,0:T(1,128)}), f32[16,1,768]{2,1,0:T(1,128)S(1)}, u32[]{:S(2)}, u32[]{:S(2)}) async-start(f32[16,1,768]{2,1,0:T(1,128)} %broadcast_in_dim.28), calls=%async_computation | async-start | bytes 98304 | tf_op jit(solution)/shard_map/all_to_all | solution.py:731
  13.8 1.9 collective-permute-start
  16.2 3.4 %pack.2 = (bf16[3,192,256]{2,1,0:T(8,128)(2,1)}, bf16[3,192,256]{2,1,0:T(8,128)(2,1)}, bf16[3,192,256]{2,1,0:T(8,128)(2,1)}, bf16[3,192,256]{2,1,0:T(8,128)(2,1)...) custom-call(s32[8]{0:T(128)} %get-tuple-element.138.at_ref, ...), custom_call_target="tpu_custom_call" | custom-call | tf_op jit(solution)/shard_map/pack/pallas_call | solution.py:66
  19.7 1.5 collective-permute-start.1
  22.7 2.4 %collective-permute-start.3 = (bf16[3,192,256]{2,1,0:T(8,128)(2,1)}, bf16[3,192,256]{2,1,0:T(8,128)(2,1)S(1)}, u32[]{:S(2)}, u32[]{:S(2)}) collective-permute-start(bf16[3,192,256]{2,1,0:T(8,128)(2,1)} %get-tuple-element.60), channel_id=1, source_target_pairs={{0,6},{1,7},{2,8},{3,9},{4,10},{5,11},{6,12},{7,13},{8,14},{9,15},... | collective-permute-start | bytes 884744 | tf_op jit(solution)/shard_map/ppermute | solution.py:31
  28.8 3.9 %collective-permute-done.1.refs_1_ = bf16[3,192,256]{2,1,0:T(8,128)(2,1)S(1)} collective-permute-done((bf16[3,192,256]{2,1,0:T(8,128)(2,1)}, bf16[3,192,256]{2,1,0:T(8,128)(2,1)S(1)}, u32[]{:S(2)}, u32[]{:S(2)}) %collective-permute-start.1) | collective-permute-done | bytes 294944 | tf_op jit(solution)/shard_map/ppermute | solution.py:31
  34.0 5.6 %collective-permute-start.7 = (bf16[3,192,256]{2,1,0:T(8,128)(2,1)}, bf16[3,192,256]{2,1,0:T(8,128)(2,1)S(1)}, u32[]{:S(2)}, u32[]{:S(2)}) collective-permute-start(bf16[3,192,256]{2,1,0:T(8,128)(2,1)} %get-tuple-element.64), channel_id=1, source_target_pairs={{0,14},{1,15},{2,0},{3,1},{4,2},{5,3},{6,4},{7,5},{8,6},{9,7},{10,... | collective-permute-start | bytes 884744 | tf_op jit(solution)/shard_map/ppermute | solution.py:31
  39.6 17.2 %collective-permute-done.3.refs_3_ = bf16[3,192,256]{2,1,0:T(8,128)(2,1)S(1)} collective-permute-done((bf16[3,192,256]{2,1,0:T(8,128)(2,1)}, bf16[3,192,256]{2,1,0:T(8,128)(2,1)S(1)}, u32[]{:S(2)}, u32[]{:S(2)}) %collective-permute-start.3) | collective-permute-done | bytes 294944 | tf_op jit(solution)/shard_map/ppermute | solution.py:31
  57.8 2.8 %collective-permute-done.7.refs_7_ = bf16[3,192,256]{2,1,0:T(8,128)(2,1)S(1)} collective-permute-done((bf16[3,192,256]{2,1,0:T(8,128)(2,1)}, bf16[3,192,256]{2,1,0:T(8,128)(2,1)S(1)}, u32[]{:S(2)}, u32[]{:S(2)}) %collective-permute-start.7) | collective-permute-done | bytes 294944 | tf_op jit(solution)/shard_map/ppermute | solution.py:31
  62.3 3.6 %pack.3 = (bf16[3,192,256]{2,1,0:T(8,128)(2,1)}, bf16[3,192,256]{2,1,0:T(8,128)(2,1)}, bf16[3,192,256]{2,1,0:T(8,128)(2,1)}, bf16[3,192,256]{2,1,0:T(8,128)(2,1)...) custom-call(s32[8]{0:T(128)} %get-tuple-element.139.at_ref, ...), custom_call_target="tpu_custom_call" | custom-call | tf_op jit(solution)/shard_map/pack/pallas_call | solution.py:66
  66.0 4.8 %collective-permute-start.16 = (bf16[3,192,256]{2,1,0:T(8,128)(2,1)}, bf16[3,192,256]{2,1,0:T(8,128)(2,1)}, u32[]{:S(2)}, u32[]{:S(2)}) collective-permute-start(bf16[3,192,256]{2,1,0:T(8,128)(2,1)} %get-tuple-element.74), channel_id=1, source_target_pairs={{0,2},{1,3},{2,4},{3,5},{4,6},{5,7},{6,8},{7,9},{8,10},{9,11},{10,... | collective-permute-start | bytes 884744 | tf_op jit(solution)/shard_map/ppermute | solution.py:31
  70.8 12.6 %collective-permute-start.17 = (bf16[3,192,256]{2,1,0:T(8,128)(2,1)}, bf16[3,192,256]{2,1,0:T(8,128)(2,1)}, u32[]{:S(2)}, u32[]{:S(2)}) collective-permute-start(bf16[3,192,256]{2,1,0:T(8,128)(2,1)} %get-tuple-element.75), channel_id=1, source_target_pairs={{0,4},{1,5},{2,6},{3,7},{4,8},{5,9},{6,10},{7,11},{8,12},{9,13},{1... | collective-permute-start | bytes 884744 | tf_op jit(solution)/shard_map/ppermute | solution.py:31
  86.0 2.5 %collective-permute-start.19 = (bf16[3,192,256]{2,1,0:T(8,128)(2,1)}, bf16[3,192,256]{2,1,0:T(8,128)(2,1)S(1)}, u32[]{:S(2)}, u32[]{:S(2)}) collective-permute-start(bf16[3,192,256]{2,1,0:T(8,128)(2,1)} %get-tuple-element.77), channel_id=1, source_target_pairs={{0,8},{1,9},{2,10},{3,11},{4,12},{5,13},{6,14},{7,15},{8,0},{9,1},... | collective-permute-start | bytes 884744 | tf_op jit(solution)/shard_map/ppermute | solution.py:31
  88.5 3.3 %collective-permute-start.20 = (bf16[3,192,256]{2,1,0:T(8,128)(2,1)}, bf16[3,192,256]{2,1,0:T(8,128)(2,1)}, u32[]{:S(2)}, u32[]{:S(2)}) collective-permute-start(bf16[3,192,256]{2,1,0:T(8,128)(2,1)} %get-tuple-element.78), channel_id=1, source_target_pairs={{0,10},{1,11},{2,12},{3,13},{4,14},{5,15},{6,0},{7,1},{8,2},{9,3},... | collective-permute-start | bytes 884744 | tf_op jit(solution)/shard_map/ppermute | solution.py:31
  93.1 5.3 %collective-permute-start.22 = (bf16[3,192,256]{2,1,0:T(8,128)(2,1)}, bf16[3,192,256]{2,1,0:T(8,128)(2,1)}, u32[]{:S(2)}, u32[]{:S(2)}) collective-permute-start(bf16[3,192,256]{2,1,0:T(8,128)(2,1)} %get-tuple-element.80), channel_id=1, source_target_pairs={{0,14},{1,15},{2,0},{3,1},{4,2},{5,3},{6,4},{7,5},{8,6},{9,7},{10,... | collective-permute-start | bytes 884744 | tf_op jit(solution)/shard_map/ppermute | solution.py:31
  98.4 22.4 %attend.2.refs_0_ = f32[8,192,128]{2,1,0:T(8,128)} custom-call(s32[16]{0:T(128)} %select_n.107.t_ref, f32[16,2,1,128]{3,2,1,0:T(1,128)} %get-tuple-element.134.sc_ref, f32[2,128,128]{2,1,0:T(8,128)} %get-tuple-element.132.w_ref, bf16[3,192,256]{2,1,0:T(8,128)(2,1)} %get-tuple-element.57.refs_0_, bf16[3,192,256]{2,1,0:T(8,128)(2,1)} %copy-done.13, ...), custom_call_target="tpu_custom_call" | custom-call | flops 4831838208 | bytes 3145728 | tf_op jit(solution)/shard_map/attend/pallas_call | solution.py:256
  125.6 1.6 fusion.refs_10_
  127.9 23.5 %attend.3 = (bf16[224,128]{1,0:T(8,128)(2,1)}, bf16[224,128]{1,0:T(8,128)(2,1)}, bf16[224,128]{1,0:T(8,128)(2,1)}, bf16[224,128]{1,0:T(8,128)(2,1)}, bf16[224,12...) custom-call(s32[16]{0:T(128)} %select_n.107.t_ref, ...), custom_call_target="tpu_custom_call" | custom-call | flops 4831838208 | bytes 3145728 | tf_op jit(solution)/shard_map/attend/pallas_call | solution.py:256
  151.4 24.6 %collective-permute-start.31 = (bf16[224,128]{1,0:T(8,128)(2,1)}, bf16[224,128]{1,0:T(8,128)(2,1)S(1)}, u32[]{:S(2)}, u32[]{:S(2)}) collective-permute-start(bf16[224,128]{1,0:T(8,128)(2,1)} %get-tuple-element.91), channel_id=1, source_target_pairs={{0,8},{1,9},{2,10},{3,11},{4,12},{5,13},{6,14},{7,15},{8,0},{9,1},... | collective-permute-start | bytes 172040 | tf_op jit(solution)/shard_map/ppermute | solution.py:31
  176.6 1.7 fusion.16
  178.4 2.3 collective-permute-start.33
  180.7 3.9 %collective-permute-start.34 = (bf16[224,128]{1,0:T(8,128)(2,1)}, bf16[224,128]{1,0:T(8,128)(2,1)}, u32[]{:S(2)}, u32[]{:S(2)}) collective-permute-start(bf16[224,128]{1,0:T(8,128)(2,1)} %get-tuple-element.94), channel_id=1, source_target_pairs={{0,12},{1,13},{2,14},{3,15},{4,0},{5,1},{6,2},{7,3},{8,4},{9,5},{1... | collective-permute-start | bytes 172040 | tf_op jit(solution)/shard_map/ppermute | solution.py:31
  184.7 2.9 %collective-permute-start.36 = (bf16[224,128]{1,0:T(8,128)(2,1)}, bf16[224,128]{1,0:T(8,128)(2,1)}, u32[]{:S(2)}, u32[]{:S(2)}) collective-permute-start(bf16[224,128]{1,0:T(8,128)(2,1)} %get-tuple-element.96), channel_id=1, source_target_pairs={{0,14},{1,15},{2,0},{3,1},{4,2},{5,3},{6,4},{7,5},{8,6},{9,7},{10,... | collective-permute-start | bytes 172040 | tf_op jit(solution)/shard_map/ppermute | solution.py:31
  188.1 2.8 %collective-permute-done.35.refs_5_ = bf16[224,128]{1,0:T(8,128)(2,1)} collective-permute-done((bf16[224,128]{1,0:T(8,128)(2,1)}, bf16[224,128]{1,0:T(8,128)(2,1)}, u32[]{:S(2)}, u32[]{:S(2)}) %collective-permute-start.35) | collective-permute-done | bytes 57376 | tf_op jit(solution)/shard_map/ppermute | solution.py:31
  190.9 3.8 %collective-permute-done.37.refs_7_ = bf16[224,128]{1,0:T(8,128)(2,1)} collective-permute-done((bf16[224,128]{1,0:T(8,128)(2,1)}, bf16[224,128]{1,0:T(8,128)(2,1)}, u32[]{:S(2)}, u32[]{:S(2)}) %collective-permute-start.37) | collective-permute-done | bytes 57376 | tf_op jit(solution)/shard_map/ppermute | solution.py:31
  194.7 4.2 %latent.1 = (f32[192,64]{1,0:T(8,128)}, bf16[192,256]{1,0:T(8,128)(2,1)}, bf16[192,256]{1,0:T(8,128)(2,1)}, bf16[192,256]{1,0:T(8,128)(2,1)}) custom-call(s32[2]{0:T(128)} %pad_add_fusion.1.flag_ref, f32[4]{0:T(128)} %get-tuple-element.124.dt_ref, bf16[224,128]{1,0:T(8,128)(2,1)} %get-tuple-element.90.refs_0_, bf16[224,128]{1,0:T(8,128)(2,1)} %copy-done.7, ...), custom_call_target="tpu_custom_call" | custom-call | tf_op jit(solution)/shard_map/latent/pallas_call | solution.py:383
  198.9 1.6 pad_maximum_fusion.w1_ref
  202.8 17.1 %decode.1 = (bf16[768,384]{1,0:T(8,128)(2,1)}, f32[16,2,768]{2,1,0:T(2,128)}) custom-call(s32[1]{0:T(128)} %bitcast.12.lead_ref, bf16[192,256]{1,0:T(8,128)(2,1)} %get-tuple-element.100.far_ref, bf16[192,256]{1,0:T(8,128)(2,1)} %copy-done.4, bf16[192,256]{1,0:T(8,128)(2,1)} %get-tuple-element.102.own_ref, bf16[768,1536]{1,0:T(8,128)(2,1)} %pad_maximum_fusion.w1_ref, ...), custom_call_target="tpu_custom_call" | custom-call | tf_op jit(solution)/shard_map/decode/pallas_call | solution.py:586
  219.9 3.5 %all-to-all-start.1 = ((f32[16,2,768]{2,1,0:T(2,128)}), f32[16,2,768]{2,1,0:T(2,128)S(1)}, u32[]{:S(2)}, u32[]{:S(2)}) async-start(f32[16,2,768]{2,1,0:T(2,128)} %get-tuple-element.105), calls=%async_computation.1 | async-start | bytes 196608 | tf_op jit(solution)/shard_map/all_to_all | solution.py:789
  224.7 6.1 %all-to-all-done.1.got_ref = f32[16,2,768]{2,1,0:T(2,128)S(1)} async-done(((f32[16,2,768]{2,1,0:T(2,128)}), f32[16,2,768]{2,1,0:T(2,128)S(1)}, u32[]{:S(2)}, u32[]{:S(2)}) %all-to-all-start.1) | async-done | bytes 98336 | tf_op jit(solution)/shard_map/all_to_all | solution.py:789
  231.4 1.8 rate.1
  (153 shorter events, 26.0 us)
Async XLA Ops:
  6.4 79.0 %all-to-all-start = ((f32[16,1,768]{2,1,0:T(1,128)}), f32[16,1,768]{2,1,0:T(1,128)S(1)}, u32[]{:S(2)}, u32[]{:S(2)}) async-start(f32[16,1,768]{2,1,0:T(1,128)} %broadcast_in_dim.28), calls=%async_computation | async-start | bytes 98304 | tf_op jit(solution)/shard_map/all_to_all | solution.py:731
  13.8 13.9 %collective-permute-start = (f32[64,192]{1,0:T(8,128)}, f32[64,192]{1,0:T(8,128)S(1)}, u32[]{:S(2)}, u32[]{:S(2)}) collective-permute-start(f32[64,192]{1,0:T(8,128)} %bitcast.39), channel_id=1, source_target_pairs={{0,2},{1,3},{2,4},{3,5},{4,6},{5,7},{6,8},{7,9},{8,10},{9,11},{10,... | collective-permute-start | bytes 147464 | tf_op jit(solution)/shard_map/ppermute | solution.py:31
  19.7 13.0 %collective-permute-start.1 = (bf16[3,192,256]{2,1,0:T(8,128)(2,1)}, bf16[3,192,256]{2,1,0:T(8,128)(2,1)S(1)}, u32[]{:S(2)}, u32[]{:S(2)}) collective-permute-start(bf16[3,192,256]{2,1,0:T(8,128)(2,1)} %get-tuple-element.58), channel_id=1, source_target_pairs={{0,2},{1,3},{2,4},{3,5},{4,6},{5,7},{6,8},{7,9},{8,10},{9,11},{10,... | collective-permute-start | bytes 884744 | tf_op jit(solution)/shard_map/ppermute | solution.py:31
  21.2 12.8 %collective-permute-start.2 = (bf16[3,192,256]{2,1,0:T(8,128)(2,1)}, bf16[3,192,256]{2,1,0:T(8,128)(2,1)S(1)}, u32[]{:S(2)}, u32[]{:S(2)}) collective-permute-start(bf16[3,192,256]{2,1,0:T(8,128)(2,1)} %get-tuple-element.59), channel_id=1, source_target_pairs={{0,4},{1,5},{2,6},{3,7},{4,8},{5,9},{6,10},{7,11},{8,12},{9,13},{1... | collective-permute-start | bytes 884744 | tf_op jit(solution)/shard_map/ppermute | solution.py:31
  22.7 34.1 %collective-permute-start.3 = (bf16[3,192,256]{2,1,0:T(8,128)(2,1)}, bf16[3,192,256]{2,1,0:T(8,128)(2,1)S(1)}, u32[]{:S(2)}, u32[]{:S(2)}) collective-permute-start(bf16[3,192,256]{2,1,0:T(8,128)(2,1)} %get-tuple-element.60), channel_id=1, source_target_pairs={{0,6},{1,7},{2,8},{3,9},{4,10},{5,11},{6,12},{7,13},{8,14},{9,15},... | collective-permute-start | bytes 884744 | tf_op jit(solution)/shard_map/ppermute | solution.py:31
  25.0 32.1 %collective-permute-start.4 = (bf16[3,192,256]{2,1,0:T(8,128)(2,1)}, bf16[3,192,256]{2,1,0:T(8,128)(2,1)S(1)}, u32[]{:S(2)}, u32[]{:S(2)}) collective-permute-start(bf16[3,192,256]{2,1,0:T(8,128)(2,1)} %get-tuple-element.61), channel_id=1, source_target_pairs={{0,8},{1,9},{2,10},{3,11},{4,12},{5,13},{6,14},{7,15},{8,0},{9,1},... | collective-permute-start | bytes 884744 | tf_op jit(solution)/shard_map/ppermute | solution.py:31
  27.7 29.6 %collective-permute-start.5 = (bf16[3,192,256]{2,1,0:T(8,128)(2,1)}, bf16[3,192,256]{2,1,0:T(8,128)(2,1)S(1)}, u32[]{:S(2)}, u32[]{:S(2)}) collective-permute-start(bf16[3,192,256]{2,1,0:T(8,128)(2,1)} %get-tuple-element.62), channel_id=1, source_target_pairs={{0,10},{1,11},{2,12},{3,13},{4,14},{5,15},{6,0},{7,1},{8,2},{9,3},... | collective-permute-start | bytes 884744 | tf_op jit(solution)/shard_map/ppermute | solution.py:31
  32.7 24.9 %collective-permute-start.6 = (bf16[3,192,256]{2,1,0:T(8,128)(2,1)}, bf16[3,192,256]{2,1,0:T(8,128)(2,1)S(1)}, u32[]{:S(2)}, u32[]{:S(2)}) collective-permute-start(bf16[3,192,256]{2,1,0:T(8,128)(2,1)} %get-tuple-element.63), channel_id=1, source_target_pairs={{0,12},{1,13},{2,14},{3,15},{4,0},{5,1},{6,2},{7,3},{8,4},{9,5},{1... | collective-permute-start | bytes 884744 | tf_op jit(solution)/shard_map/ppermute | solution.py:31
  34.0 26.6 %collective-permute-start.7 = (bf16[3,192,256]{2,1,0:T(8,128)(2,1)}, bf16[3,192,256]{2,1,0:T(8,128)(2,1)S(1)}, u32[]{:S(2)}, u32[]{:S(2)}) collective-permute-start(bf16[3,192,256]{2,1,0:T(8,128)(2,1)} %get-tuple-element.64), channel_id=1, source_target_pairs={{0,14},{1,15},{2,0},{3,1},{4,2},{5,3},{6,4},{7,5},{8,6},{9,7},{10,... | collective-permute-start | bytes 884744 | tf_op jit(solution)/shard_map/ppermute | solution.py:31
  56.8 9.2 %collective-permute-start.8 = (bf16[3,192,256]{2,1,0:T(8,128)(2,1)}, bf16[3,192,256]{2,1,0:T(8,128)(2,1)}, u32[]{:S(2)}, u32[]{:S(2)}) collective-permute-start(bf16[3,192,256]{2,1,0:T(8,128)(2,1)} %get-tuple-element.57.refs_0_), channel_id=1, source_target_pairs={{0,1},{1,0},{2,3},{3,2},{4,5},{5,4},{6,7},{7,6},{8,9},{9,8},{10,11... | collective-permute-start | bytes 884744 | tf_op jit(solution)/shard_map/ppermute | solution.py:36
  57.1 13.7 %collective-permute-start.9 = (bf16[3,192,256]{2,1,0:T(8,128)(2,1)S(1)}, bf16[3,192,256]{2,1,0:T(8,128)(2,1)}, u32[]{:S(2)}, u32[]{:S(2)}) collective-permute-start(bf16[3,192,256]{2,1,0:T(8,128)(2,1)S(1)} %collective-permute-done.1.refs_1_), channel_id=1, source_target_pairs={{0,1},{1,0},{2,3},{3,2},{4,5},{5,4},{6,7},{7,6},{8,9},{9,8},{10,11... | collective-permute-start | bytes 884744 | tf_op jit(solution)/shard_map/ppermute | solution.py:36
  57.3 26.1 %collective-permute-start.10 = (bf16[3,192,256]{2,1,0:T(8,128)(2,1)S(1)}, bf16[3,192,256]{2,1,0:T(8,128)(2,1)}, u32[]{:S(2)}, u32[]{:S(2)}) collective-permute-start(bf16[3,192,256]{2,1,0:T(8,128)(2,1)S(1)} %collective-permute-done.2.refs_2_), channel_id=1, source_target_pairs={{0,1},{1,0},{2,3},{3,2},{4,5},{5,4},{6,7},{7,6},{8,9},{9,8},{10,11... | collective-permute-start | bytes 884744 | tf_op jit(solution)/shard_map/ppermute | solution.py:36
  57.6 25.8 %collective-permute-start.11 = (bf16[3,192,256]{2,1,0:T(8,128)(2,1)S(1)}, bf16[3,192,256]{2,1,0:T(8,128)(2,1)}, u32[]{:S(2)}, u32[]{:S(2)}) collective-permute-start(bf16[3,192,256]{2,1,0:T(8,128)(2,1)S(1)} %collective-permute-done.3.refs_3_), channel_id=1, source_target_pairs={{0,1},{1,0},{2,3},{3,2},{4,5},{5,4},{6,7},{7,6},{8,9},{9,8},{10,11... | collective-permute-start | bytes 884744 | tf_op jit(solution)/shard_map/ppermute | solution.py:36
  60.6 23.3 %collective-permute-start.12 = (bf16[3,192,256]{2,1,0:T(8,128)(2,1)S(1)}, bf16[3,192,256]{2,1,0:T(8,128)(2,1)}, u32[]{:S(2)}, u32[]{:S(2)}) collective-permute-start(bf16[3,192,256]{2,1,0:T(8,128)(2,1)S(1)} %collective-permute-done.4.refs_4_), channel_id=1, source_target_pairs={{0,1},{1,0},{2,3},{3,2},{4,5},{5,4},{6,7},{7,6},{8,9},{9,8},{10,11... | collective-permute-start | bytes 884744 | tf_op jit(solution)/shard_map/ppermute | solution.py:36
  66.0 26.6 %collective-permute-start.16 = (bf16[3,192,256]{2,1,0:T(8,128)(2,1)}, bf16[3,192,256]{2,1,0:T(8,128)(2,1)}, u32[]{:S(2)}, u32[]{:S(2)}) collective-permute-start(bf16[3,192,256]{2,1,0:T(8,128)(2,1)} %get-tuple-element.74), channel_id=1, source_target_pairs={{0,2},{1,3},{2,4},{3,5},{4,6},{5,7},{6,8},{7,9},{8,10},{9,11},{10,... | collective-permute-start | bytes 884744 | tf_op jit(solution)/shard_map/ppermute | solution.py:31
  70.8 22.2 %collective-permute-start.17 = (bf16[3,192,256]{2,1,0:T(8,128)(2,1)}, bf16[3,192,256]{2,1,0:T(8,128)(2,1)}, u32[]{:S(2)}, u32[]{:S(2)}) collective-permute-start(bf16[3,192,256]{2,1,0:T(8,128)(2,1)} %get-tuple-element.75), channel_id=1, source_target_pairs={{0,4},{1,5},{2,6},{3,7},{4,8},{5,9},{6,10},{7,11},{8,12},{9,13},{1... | collective-permute-start | bytes 884744 | tf_op jit(solution)/shard_map/ppermute | solution.py:31
  83.9 4.5 %collective-permute-start.15 = (bf16[3,192,256]{2,1,0:T(8,128)(2,1)}, bf16[3,192,256]{2,1,0:T(8,128)(2,1)}, u32[]{:S(2)}, u32[]{:S(2)}) collective-permute-start(bf16[3,192,256]{2,1,0:T(8,128)(2,1)} %copy-done.21), channel_id=1, source_target_pairs={{0,1},{1,0},{2,3},{3,2},{4,5},{5,4},{6,7},{7,6},{8,9},{9,8},{10,11... | collective-permute-start | bytes 884744 | tf_op jit(solution)/shard_map/ppermute | solution.py:36
  86.0 34.8 %collective-permute-start.18 = (bf16[3,192,256]{2,1,0:T(8,128)(2,1)}, bf16[3,192,256]{2,1,0:T(8,128)(2,1)S(1)}, u32[]{:S(2)}, u32[]{:S(2)}) collective-permute-start(bf16[3,192,256]{2,1,0:T(8,128)(2,1)} %get-tuple-element.76), channel_id=1, source_target_pairs={{0,6},{1,7},{2,8},{3,9},{4,10},{5,11},{6,12},{7,13},{8,14},{9,15},... | collective-permute-start | bytes 884744 | tf_op jit(solution)/shard_map/ppermute | solution.py:31
  86.0 34.8 %collective-permute-start.19 = (bf16[3,192,256]{2,1,0:T(8,128)(2,1)}, bf16[3,192,256]{2,1,0:T(8,128)(2,1)S(1)}, u32[]{:S(2)}, u32[]{:S(2)}) collective-permute-start(bf16[3,192,256]{2,1,0:T(8,128)(2,1)} %get-tuple-element.77), channel_id=1, source_target_pairs={{0,8},{1,9},{2,10},{3,11},{4,12},{5,13},{6,14},{7,15},{8,0},{9,1},... | collective-permute-start | bytes 884744 | tf_op jit(solution)/shard_map/ppermute | solution.py:31
  88.5 32.4 %collective-permute-start.20 = (bf16[3,192,256]{2,1,0:T(8,128)(2,1)}, bf16[3,192,256]{2,1,0:T(8,128)(2,1)}, u32[]{:S(2)}, u32[]{:S(2)}) collective-permute-start(bf16[3,192,256]{2,1,0:T(8,128)(2,1)} %get-tuple-element.78), channel_id=1, source_target_pairs={{0,10},{1,11},{2,12},{3,13},{4,14},{5,15},{6,0},{7,1},{8,2},{9,3},... | collective-permute-start | bytes 884744 | tf_op jit(solution)/shard_map/ppermute | solution.py:31
  92.5 28.3 %collective-permute-start.21 = (bf16[3,192,256]{2,1,0:T(8,128)(2,1)}, bf16[3,192,256]{2,1,0:T(8,128)(2,1)}, u32[]{:S(2)}, u32[]{:S(2)}) collective-permute-start(bf16[3,192,256]{2,1,0:T(8,128)(2,1)} %get-tuple-element.79), channel_id=1, source_target_pairs={{0,12},{1,13},{2,14},{3,15},{4,0},{5,1},{6,2},{7,3},{8,4},{9,5},{1... | collective-permute-start | bytes 884744 | tf_op jit(solution)/shard_map/ppermute | solution.py:31
  93.1 28.5 %collective-permute-start.22 = (bf16[3,192,256]{2,1,0:T(8,128)(2,1)}, bf16[3,192,256]{2,1,0:T(8,128)(2,1)}, u32[]{:S(2)}, u32[]{:S(2)}) collective-permute-start(bf16[3,192,256]{2,1,0:T(8,128)(2,1)} %get-tuple-element.80), channel_id=1, source_target_pairs={{0,14},{1,15},{2,0},{3,1},{4,2},{5,3},{6,4},{7,5},{8,6},{9,7},{10,... | collective-permute-start | bytes 884744 | tf_op jit(solution)/shard_map/ppermute | solution.py:31
  122.7 4.4 %collective-permute-start.26 = (bf16[3,192,256]{2,1,0:T(8,128)(2,1)S(1)}, bf16[3,192,256]{2,1,0:T(8,128)(2,1)}, u32[]{:S(2)}, u32[]{:S(2)}) collective-permute-start(bf16[3,192,256]{2,1,0:T(8,128)(2,1)S(1)} %collective-permute-done.18.refs_4_), channel_id=1, source_target_pairs={{0,1},{1,0},{2,3},{3,2},{4,5},{5,4},{6,7},{7,6},{8,9},{9,8},{10,11... | collective-permute-start | bytes 884744 | tf_op jit(solution)/shard_map/ppermute | solution.py:36
  123.2 3.9 %collective-permute-start.27 = (bf16[3,192,256]{2,1,0:T(8,128)(2,1)S(1)}, bf16[3,192,256]{2,1,0:T(8,128)(2,1)}, u32[]{:S(2)}, u32[]{:S(2)}) collective-permute-start(bf16[3,192,256]{2,1,0:T(8,128)(2,1)S(1)} %collective-permute-done.19.refs_5_), channel_id=1, source_target_pairs={{0,1},{1,0},{2,3},{3,2},{4,5},{5,4},{6,7},{7,6},{8,9},{9,8},{10,11... | collective-permute-start | bytes 884744 | tf_op jit(solution)/shard_map/ppermute | solution.py:36
  151.4 33.3 %collective-permute-start.31 = (bf16[224,128]{1,0:T(8,128)(2,1)}, bf16[224,128]{1,0:T(8,128)(2,1)S(1)}, u32[]{:S(2)}, u32[]{:S(2)}) collective-permute-start(bf16[224,128]{1,0:T(8,128)(2,1)} %get-tuple-element.91), channel_id=1, source_target_pairs={{0,8},{1,9},{2,10},{3,11},{4,12},{5,13},{6,14},{7,15},{8,0},{9,1},... | collective-permute-start | bytes 172040 | tf_op jit(solution)/shard_map/ppermute | solution.py:31
  175.9 11.6 %collective-permute-start.32 = (bf16[224,128]{1,0:T(8,128)(2,1)}, bf16[224,128]{1,0:T(8,128)(2,1)S(1)}, u32[]{:S(2)}, u32[]{:S(2)}) collective-permute-start(bf16[224,128]{1,0:T(8,128)(2,1)} %get-tuple-element.92), channel_id=1, source_target_pairs={{0,10},{1,11},{2,12},{3,13},{4,14},{5,15},{6,0},{7,1},{8,2},{9,3},... | collective-permute-start | bytes 172040 | tf_op jit(solution)/shard_map/ppermute | solution.py:31
  178.4 9.7 %collective-permute-start.33 = (bf16[224,128]{1,0:T(8,128)(2,1)}, bf16[224,128]{1,0:T(8,128)(2,1)}, u32[]{:S(2)}, u32[]{:S(2)}) collective-permute-start(bf16[224,128]{1,0:T(8,128)(2,1)} %get-tuple-element.93), channel_id=1, source_target_pairs={{0,6},{1,7},{2,8},{3,9},{4,10},{5,11},{6,12},{7,13},{8,14},{9,15},... | collective-permute-start | bytes 172040 | tf_op jit(solution)/shard_map/ppermute | solution.py:31
  180.7 7.4 %collective-permute-start.34 = (bf16[224,128]{1,0:T(8,128)(2,1)}, bf16[224,128]{1,0:T(8,128)(2,1)}, u32[]{:S(2)}, u32[]{:S(2)}) collective-permute-start(bf16[224,128]{1,0:T(8,128)(2,1)} %get-tuple-element.94), channel_id=1, source_target_pairs={{0,12},{1,13},{2,14},{3,15},{4,0},{5,1},{6,2},{7,3},{8,4},{9,5},{1... | collective-permute-start | bytes 172040 | tf_op jit(solution)/shard_map/ppermute | solution.py:31
  184.6 6.3 %collective-permute-start.35 = (bf16[224,128]{1,0:T(8,128)(2,1)}, bf16[224,128]{1,0:T(8,128)(2,1)}, u32[]{:S(2)}, u32[]{:S(2)}) collective-permute-start(bf16[224,128]{1,0:T(8,128)(2,1)} %get-tuple-element.95), channel_id=1, source_target_pairs={{0,4},{1,5},{2,6},{3,7},{4,8},{5,9},{6,10},{7,11},{8,12},{9,13},{1... | collective-permute-start | bytes 172040 | tf_op jit(solution)/shard_map/ppermute | solution.py:31
  184.7 6.3 %collective-permute-start.36 = (bf16[224,128]{1,0:T(8,128)(2,1)}, bf16[224,128]{1,0:T(8,128)(2,1)}, u32[]{:S(2)}, u32[]{:S(2)}) collective-permute-start(bf16[224,128]{1,0:T(8,128)(2,1)} %get-tuple-element.96), channel_id=1, source_target_pairs={{0,14},{1,15},{2,0},{3,1},{4,2},{5,3},{6,4},{7,5},{8,6},{9,7},{10,... | collective-permute-start | bytes 172040 | tf_op jit(solution)/shard_map/ppermute | solution.py:31
  187.5 7.2 %collective-permute-start.37 = (bf16[224,128]{1,0:T(8,128)(2,1)}, bf16[224,128]{1,0:T(8,128)(2,1)}, u32[]{:S(2)}, u32[]{:S(2)}) collective-permute-start(bf16[224,128]{1,0:T(8,128)(2,1)} %get-tuple-element.97), channel_id=1, source_target_pairs={{0,2},{1,3},{2,4},{3,5},{4,6},{5,7},{6,8},{7,9},{8,10},{9,11},{10,... | collective-permute-start | bytes 172040 | tf_op jit(solution)/shard_map/ppermute | solution.py:31
  219.9 10.9 %all-to-all-start.1 = ((f32[16,2,768]{2,1,0:T(2,128)}), f32[16,2,768]{2,1,0:T(2,128)S(1)}, u32[]{:S(2)}, u32[]{:S(2)}) async-start(f32[16,2,768]{2,1,0:T(2,128)} %get-tuple-element.105), calls=%async_computation.1 | async-start | bytes 196608 | tf_op jit(solution)/shard_map/all_to_all | solution.py:789
  (38 other events, 667.5 us)

commit v4 on v3

--- a/solution.py
+++ b/solution.py
@@ -16,8 +16,8 @@
 LAT_C = 16
 CH = 384
 TEXT_W = 768
-KEY_CHUNK = 512
-GATES = (2,)
+KEY_CHUNK = 256
+GATES = (1,)
 
 
 highest = lax.Precision.HIGHEST
@@ -152,16 +152,18 @@
         return part + jnp.where(lane >= LAT, square, 0.0)
 
     def one_unit(h, now, top_ref, next_h, next_b, later, later_top_ref):
-        top = top_ref[:, :1]
+        top = top_ref[...]
         peak, total = None, None
         acc = jnp.zeros((rows, HD), jnp.float32)
         for at in chunks:
             peak = logits(next_h, next_b, at, later, peak)
-            e = jnp.exp2(now[:, at : at + KEY_CHUNK] * scale - top)
-            folded = functools.reduce(jnp.add, [e[:, i : i + 128] for i in range(0, KEY_CHUNK, 128)])
-            total = folded if total is None else total + folded
+            weights = []
+            for i in range(at, at + KEY_CHUNK, 128):
+                e = jnp.exp2(now[:, i : i + 128] * scale - top)
+                total = e if total is None else total + e
+                weights.append(e.astype(jnp.bfloat16))
             acc = acc + jnp.dot(
-                e.astype(jnp.bfloat16),
+                jnp.concatenate(weights, axis=1),
                 v_s[h, at : at + KEY_CHUNK, :],
                 preferred_element_type=jnp.float32,
             )

time: 234 us -> 230 us (0.983)
  Pallas kernels: 80.3 us -> 76.6 us
    pallas_call x2, Pallas kernels: 45.9 us -> 42.2 us  [attend(): pl.pallas_call(functools.partial(attend_kernel, blocks, heads, frames, le...]
  transfers between devices with their start and end apart: 41 -> 41, of which waited for: 11 -> 11; matrix products, arithmetic and copies ran while one was open for 6% -> 7% of each run, Pallas kernels for 13% -> 12%
where the time goes in v4:
time: 230 us
  starting transfers between devices  91.9 us (40%)
  Pallas kernels  76.6 us (33%)
  waiting for transfers between devices  40.7 us (18%)
  local copies, waits for them, and re-layouts  13.5 us (6%)
  other arithmetic  4.19 us (2%)
    ppermute x22, starting transfers between devices, rotate(): lax.ppermute(value, axis, [(i, (i + 2 * steps) % count) for i in range(co...  77.7 us
    pallas_call x2, Pallas kernels, attend(): pl.pallas_call(functools.partial(attend_kernel, blocks, heads, frames, le...  42.2 us
    ppermute x22, waiting for transfers between devices, rotate(): lax.ppermute(value, axis, [(i, (i + 2 * steps) % count) for i in range(co...  34.5 us
    pallas_call x1, Pallas kernels, decode(): pl.pallas_call(functools.partial(decode_kernel, frames), out_shape=[jax.S...  17.1 us
    all_to_all x1, starting transfers between devices, local(): lax.all_to_all(words, 'seq', split_axis=0, concat_axis=0, tiled=True)  7.41 us
    pallas_call x2, Pallas kernels, pack(): pl.pallas_call(functools.partial(pack_kernel, blocks), out_shape=[jax.Sha...  7.04 us
    all_to_all x1, waiting for transfers between devices, local(): lax.all_to_all(sent, 'seq', split_axis=0, concat_axis=0, tiled=True)  6.06 us
  transfers between devices with their start and end apart: 41, of which 11 were waited for; matrix products, arithmetic and copies ran while one was open for 7% of the time, Pallas kernels for 12%

profile of v4, /device:TPU:0, one launch (start us, length us, event | category | flops | bytes accessed | tf_op | source)
XLA Modules:
  0.0 229.7 jit_solution(9107735564528540560)
XLA Ops:
  0.7 4.3 %text.1 = f32[1,768]{1,0:T(1,128)} custom-call(s32[1]{0:T(128)} %bitcast.6.at_ref, s32[77]{0:T(128)} %id_ref.1, bf16[48,24704]{1,0:T(8,128)(2,1)} %bitcast.31), custom_call_target="tpu_custom_call" | custom-call | tf_op jit(solution)/shard_map/text/pallas_call | solution.py:429
  6.4 7.4 %all-to-all-start = ((f32[16,1,768]{2,1,0:T(1,128)}), f32[16,1,768]{2,1,0:T(1,128)S(1)}, u32[]{:S(2)}, u32[]{:S(2)}) async-start(f32[16,1,768]{2,1,0:T(1,128)} %broadcast_in_dim.28), calls=%async_computation | async-start | bytes 98304 | tf_op jit(solution)/shard_map/all_to_all | solution.py:733
  13.8 1.9 collective-permute-start
  16.2 3.4 %pack.2 = (bf16[3,192,256]{2,1,0:T(8,128)(2,1)}, bf16[3,192,256]{2,1,0:T(8,128)(2,1)}, bf16[3,192,256]{2,1,0:T(8,128)(2,1)}, bf16[3,192,256]{2,1,0:T(8,128)(2,1)...) custom-call(s32[8]{0:T(128)} %get-tuple-element.138.at_ref, ...), custom_call_target="tpu_custom_call" | custom-call | tf_op jit(solution)/shard_map/pack/pallas_call | solution.py:66
  22.7 2.4 %collective-permute-start.3 = (bf16[3,192,256]{2,1,0:T(8,128)(2,1)}, bf16[3,192,256]{2,1,0:T(8,128)(2,1)S(1)}, u32[]{:S(2)}, u32[]{:S(2)}) collective-permute-start(bf16[3,192,256]{2,1,0:T(8,128)(2,1)} %get-tuple-element.60), channel_id=1, source_target_pairs={{0,6},{1,7},{2,8},{3,9},{4,10},{5,11},{6,12},{7,13},{8,14},{9,15},... | collective-permute-start | bytes 884744 | tf_op jit(solution)/shard_map/ppermute | solution.py:31
  28.8 3.9 %collective-permute-done.1.refs_1_ = bf16[3,192,256]{2,1,0:T(8,128)(2,1)S(1)} collective-permute-done((bf16[3,192,256]{2,1,0:T(8,128)(2,1)}, bf16[3,192,256]{2,1,0:T(8,128)(2,1)S(1)}, u32[]{:S(2)}, u32[]{:S(2)}) %collective-permute-start.1) | collective-permute-done | bytes 294944 | tf_op jit(solution)/shard_map/ppermute | solution.py:31
  34.0 5.6 %collective-permute-start.7 = (bf16[3,192,256]{2,1,0:T(8,128)(2,1)}, bf16[3,192,256]{2,1,0:T(8,128)(2,1)S(1)}, u32[]{:S(2)}, u32[]{:S(2)}) collective-permute-start(bf16[3,192,256]{2,1,0:T(8,128)(2,1)} %get-tuple-element.64), channel_id=1, source_target_pairs={{0,14},{1,15},{2,0},{3,1},{4,2},{5,3},{6,4},{7,5},{8,6},{9,7},{10,... | collective-permute-start | bytes 884744 | tf_op jit(solution)/shard_map/ppermute | solution.py:31
  39.6 17.2 %collective-permute-done.3.refs_3_ = bf16[3,192,256]{2,1,0:T(8,128)(2,1)S(1)} collective-permute-done((bf16[3,192,256]{2,1,0:T(8,128)(2,1)}, bf16[3,192,256]{2,1,0:T(8,128)(2,1)S(1)}, u32[]{:S(2)}, u32[]{:S(2)}) %collective-permute-start.3) | collective-permute-done | bytes 294944 | tf_op jit(solution)/shard_map/ppermute | solution.py:31
  57.8 2.8 %collective-permute-done.7.refs_7_ = bf16[3,192,256]{2,1,0:T(8,128)(2,1)S(1)} collective-permute-done((bf16[3,192,256]{2,1,0:T(8,128)(2,1)}, bf16[3,192,256]{2,1,0:T(8,128)(2,1)S(1)}, u32[]{:S(2)}, u32[]{:S(2)}) %collective-permute-start.7) | collective-permute-done | bytes 294944 | tf_op jit(solution)/shard_map/ppermute | solution.py:31
  62.3 3.6 %pack.3 = (bf16[3,192,256]{2,1,0:T(8,128)(2,1)}, bf16[3,192,256]{2,1,0:T(8,128)(2,1)}, bf16[3,192,256]{2,1,0:T(8,128)(2,1)}, bf16[3,192,256]{2,1,0:T(8,128)(2,1)...) custom-call(s32[8]{0:T(128)} %get-tuple-element.139.at_ref, ...), custom_call_target="tpu_custom_call" | custom-call | tf_op jit(solution)/shard_map/pack/pallas_call | solution.py:66
  66.0 4.8 %collective-permute-start.16 = (bf16[3,192,256]{2,1,0:T(8,128)(2,1)}, bf16[3,192,256]{2,1,0:T(8,128)(2,1)}, u32[]{:S(2)}, u32[]{:S(2)}) collective-permute-start(bf16[3,192,256]{2,1,0:T(8,128)(2,1)} %get-tuple-element.74), channel_id=1, source_target_pairs={{0,2},{1,3},{2,4},{3,5},{4,6},{5,7},{6,8},{7,9},{8,10},{9,11},{10,... | collective-permute-start | bytes 884744 | tf_op jit(solution)/shard_map/ppermute | solution.py:31
  70.8 12.6 %collective-permute-start.17 = (bf16[3,192,256]{2,1,0:T(8,128)(2,1)}, bf16[3,192,256]{2,1,0:T(8,128)(2,1)}, u32[]{:S(2)}, u32[]{:S(2)}) collective-permute-start(bf16[3,192,256]{2,1,0:T(8,128)(2,1)} %get-tuple-element.75), channel_id=1, source_target_pairs={{0,4},{1,5},{2,6},{3,7},{4,8},{5,9},{6,10},{7,11},{8,12},{9,13},{1... | collective-permute-start | bytes 884744 | tf_op jit(solution)/shard_map/ppermute | solution.py:31
  86.0 2.5 %collective-permute-start.19 = (bf16[3,192,256]{2,1,0:T(8,128)(2,1)}, bf16[3,192,256]{2,1,0:T(8,128)(2,1)S(1)}, u32[]{:S(2)}, u32[]{:S(2)}) collective-permute-start(bf16[3,192,256]{2,1,0:T(8,128)(2,1)} %get-tuple-element.77), channel_id=1, source_target_pairs={{0,8},{1,9},{2,10},{3,11},{4,12},{5,13},{6,14},{7,15},{8,0},{9,1},... | collective-permute-start | bytes 884744 | tf_op jit(solution)/shard_map/ppermute | solution.py:31
  88.5 3.3 %collective-permute-start.20 = (bf16[3,192,256]{2,1,0:T(8,128)(2,1)}, bf16[3,192,256]{2,1,0:T(8,128)(2,1)}, u32[]{:S(2)}, u32[]{:S(2)}) collective-permute-start(bf16[3,192,256]{2,1,0:T(8,128)(2,1)} %get-tuple-element.78), channel_id=1, source_target_pairs={{0,10},{1,11},{2,12},{3,13},{4,14},{5,15},{6,0},{7,1},{8,2},{9,3},... | collective-permute-start | bytes 884744 | tf_op jit(solution)/shard_map/ppermute | solution.py:31
  93.1 5.3 %collective-permute-start.22 = (bf16[3,192,256]{2,1,0:T(8,128)(2,1)}, bf16[3,192,256]{2,1,0:T(8,128)(2,1)}, u32[]{:S(2)}, u32[]{:S(2)}) collective-permute-start(bf16[3,192,256]{2,1,0:T(8,128)(2,1)} %get-tuple-element.80), channel_id=1, source_target_pairs={{0,14},{1,15},{2,0},{3,1},{4,2},{5,3},{6,4},{7,5},{8,6},{9,7},{10,... | collective-permute-start | bytes 884744 | tf_op jit(solution)/shard_map/ppermute | solution.py:31
  98.4 20.6 %attend.2.refs_0_ = f32[8,192,128]{2,1,0:T(8,128)} custom-call(s32[16]{0:T(128)} %select_n.107.t_ref, f32[16,2,1,128]{3,2,1,0:T(1,128)} %get-tuple-element.134.sc_ref, f32[2,128,128]{2,1,0:T(8,128)} %get-tuple-element.132.w_ref, bf16[3,192,256]{2,1,0:T(8,128)(2,1)} %get-tuple-element.57.refs_0_, bf16[3,192,256]{2,1,0:T(8,128)(2,1)} %copy-done.13, ...), custom_call_target="tpu_custom_call" | custom-call | flops 4831838208 | bytes 3145728 | tf_op jit(solution)/shard_map/attend/pallas_call | solution.py:258
  119.0 2.5 %collective-permute-done.22.refs_8_ = bf16[3,192,256]{2,1,0:T(8,128)(2,1)} collective-permute-done((bf16[3,192,256]{2,1,0:T(8,128)(2,1)}, bf16[3,192,256]{2,1,0:T(8,128)(2,1)}, u32[]{:S(2)}, u32[]{:S(2)}) %collective-permute-start.22) | collective-permute-done | bytes 294944 | tf_op jit(solution)/shard_map/ppermute | solution.py:31
  125.6 1.6 fusion.refs_10_
  127.9 21.6 %attend.3 = (bf16[224,128]{1,0:T(8,128)(2,1)}, bf16[224,128]{1,0:T(8,128)(2,1)}, bf16[224,128]{1,0:T(8,128)(2,1)}, bf16[224,128]{1,0:T(8,128)(2,1)}, bf16[224,12...) custom-call(s32[16]{0:T(128)} %select_n.107.t_ref, ...), custom_call_target="tpu_custom_call" | custom-call | flops 4831838208 | bytes 3145728 | tf_op jit(solution)/shard_map/attend/pallas_call | solution.py:258
  149.5 22.8 %collective-permute-start.31 = (bf16[224,128]{1,0:T(8,128)(2,1)}, bf16[224,128]{1,0:T(8,128)(2,1)S(1)}, u32[]{:S(2)}, u32[]{:S(2)}) collective-permute-start(bf16[224,128]{1,0:T(8,128)(2,1)} %get-tuple-element.91), channel_id=1, source_target_pairs={{0,8},{1,9},{2,10},{3,11},{4,12},{5,13},{6,14},{7,15},{8,0},{9,1},... | collective-permute-start | bytes 172040 | tf_op jit(solution)/shard_map/ppermute | solution.py:31
  173.0 1.7 fusion.16
  174.8 2.3 %collective-permute-start.33 = (bf16[224,128]{1,0:T(8,128)(2,1)}, bf16[224,128]{1,0:T(8,128)(2,1)}, u32[]{:S(2)}, u32[]{:S(2)}) collective-permute-start(bf16[224,128]{1,0:T(8,128)(2,1)} %get-tuple-element.93), channel_id=1, source_target_pairs={{0,6},{1,7},{2,8},{3,9},{4,10},{5,11},{6,12},{7,13},{8,14},{9,15},... | collective-permute-start | bytes 172040 | tf_op jit(solution)/shard_map/ppermute | solution.py:31
  177.1 3.9 %collective-permute-start.34 = (bf16[224,128]{1,0:T(8,128)(2,1)}, bf16[224,128]{1,0:T(8,128)(2,1)}, u32[]{:S(2)}, u32[]{:S(2)}) collective-permute-start(bf16[224,128]{1,0:T(8,128)(2,1)} %get-tuple-element.94), channel_id=1, source_target_pairs={{0,12},{1,13},{2,14},{3,15},{4,0},{5,1},{6,2},{7,3},{8,4},{9,5},{1... | collective-permute-start | bytes 172040 | tf_op jit(solution)/shard_map/ppermute | solution.py:31
  181.0 2.9 %collective-permute-start.36 = (bf16[224,128]{1,0:T(8,128)(2,1)}, bf16[224,128]{1,0:T(8,128)(2,1)}, u32[]{:S(2)}, u32[]{:S(2)}) collective-permute-start(bf16[224,128]{1,0:T(8,128)(2,1)} %get-tuple-element.96), channel_id=1, source_target_pairs={{0,14},{1,15},{2,0},{3,1},{4,2},{5,3},{6,4},{7,5},{8,6},{9,7},{10,... | collective-permute-start | bytes 172040 | tf_op jit(solution)/shard_map/ppermute | solution.py:31
  184.5 2.8 %collective-permute-done.35.refs_5_ = bf16[224,128]{1,0:T(8,128)(2,1)} collective-permute-done((bf16[224,128]{1,0:T(8,128)(2,1)}, bf16[224,128]{1,0:T(8,128)(2,1)}, u32[]{:S(2)}, u32[]{:S(2)}) %collective-permute-start.35) | collective-permute-done | bytes 57376 | tf_op jit(solution)/shard_map/ppermute | solution.py:31
  187.3 3.8 %collective-permute-done.37.refs_7_ = bf16[224,128]{1,0:T(8,128)(2,1)} collective-permute-done((bf16[224,128]{1,0:T(8,128)(2,1)}, bf16[224,128]{1,0:T(8,128)(2,1)}, u32[]{:S(2)}, u32[]{:S(2)}) %collective-permute-start.37) | collective-permute-done | bytes 57376 | tf_op jit(solution)/shard_map/ppermute | solution.py:31
  191.1 4.2 %latent.1 = (f32[192,64]{1,0:T(8,128)}, bf16[192,256]{1,0:T(8,128)(2,1)}, bf16[192,256]{1,0:T(8,128)(2,1)}, bf16[192,256]{1,0:T(8,128)(2,1)}) custom-call(s32[2]{0:T(128)} %pad_add_fusion.1.flag_ref, f32[4]{0:T(128)} %get-tuple-element.124.dt_ref, bf16[224,128]{1,0:T(8,128)(2,1)} %get-tuple-element.90.refs_0_, bf16[224,128]{1,0:T(8,128)(2,1)} %copy-done.7, ...), custom_call_target="tpu_custom_call" | custom-call | tf_op jit(solution)/shard_map/latent/pallas_call | solution.py:385
  195.3 1.6 pad_maximum_fusion.w1_ref
  199.2 17.1 %decode.1 = (bf16[768,384]{1,0:T(8,128)(2,1)}, f32[16,2,768]{2,1,0:T(2,128)}) custom-call(s32[1]{0:T(128)} %bitcast.12.lead_ref, bf16[192,256]{1,0:T(8,128)(2,1)} %get-tuple-element.100.far_ref, bf16[192,256]{1,0:T(8,128)(2,1)} %copy-done.4, bf16[192,256]{1,0:T(8,128)(2,1)} %get-tuple-element.102.own_ref, bf16[768,1536]{1,0:T(8,128)(2,1)} %pad_maximum_fusion.w1_ref, ...), custom_call_target="tpu_custom_call" | custom-call | tf_op jit(solution)/shard_map/decode/pallas_call | solution.py:588
  216.3 3.5 %all-to-all-start.1 = ((f32[16,2,768]{2,1,0:T(2,128)}), f32[16,2,768]{2,1,0:T(2,128)S(1)}, u32[]{:S(2)}, u32[]{:S(2)}) async-start(f32[16,2,768]{2,1,0:T(2,128)} %get-tuple-element.105), calls=%async_computation.1 | async-start | bytes 196608 | tf_op jit(solution)/shard_map/all_to_all | solution.py:791
  221.1 6.1 %all-to-all-done.1.got_ref = f32[16,2,768]{2,1,0:T(2,128)S(1)} async-done(((f32[16,2,768]{2,1,0:T(2,128)}), f32[16,2,768]{2,1,0:T(2,128)S(1)}, u32[]{:S(2)}, u32[]{:S(2)}) %all-to-all-start.1) | async-done | bytes 98336 | tf_op jit(solution)/shard_map/all_to_all | solution.py:791
  227.8 1.8 rate.1
  (153 shorter events, 26.9 us)
Async XLA Ops:
  6.4 79.0 %all-to-all-start = ((f32[16,1,768]{2,1,0:T(1,128)}), f32[16,1,768]{2,1,0:T(1,128)S(1)}, u32[]{:S(2)}, u32[]{:S(2)}) async-start(f32[16,1,768]{2,1,0:T(1,128)} %broadcast_in_dim.28), calls=%async_computation | async-start | bytes 98304 | tf_op jit(solution)/shard_map/all_to_all | solution.py:733
  13.8 13.9 %collective-permute-start = (f32[64,192]{1,0:T(8,128)}, f32[64,192]{1,0:T(8,128)S(1)}, u32[]{:S(2)}, u32[]{:S(2)}) collective-permute-start(f32[64,192]{1,0:T(8,128)} %bitcast.39), channel_id=1, source_target_pairs={{0,2},{1,3},{2,4},{3,5},{4,6},{5,7},{6,8},{7,9},{8,10},{9,11},{10,... | collective-permute-start | bytes 147464 | tf_op jit(solution)/shard_map/ppermute | solution.py:31
  19.7 13.0 %collective-permute-start.1 = (bf16[3,192,256]{2,1,0:T(8,128)(2,1)}, bf16[3,192,256]{2,1,0:T(8,128)(2,1)S(1)}, u32[]{:S(2)}, u32[]{:S(2)}) collective-permute-start(bf16[3,192,256]{2,1,0:T(8,128)(2,1)} %get-tuple-element.58), channel_id=1, source_target_pairs={{0,2},{1,3},{2,4},{3,5},{4,6},{5,7},{6,8},{7,9},{8,10},{9,11},{10,... | collective-permute-start | bytes 884744 | tf_op jit(solution)/shard_map/ppermute | solution.py:31
  21.2 12.8 %collective-permute-start.2 = (bf16[3,192,256]{2,1,0:T(8,128)(2,1)}, bf16[3,192,256]{2,1,0:T(8,128)(2,1)S(1)}, u32[]{:S(2)}, u32[]{:S(2)}) collective-permute-start(bf16[3,192,256]{2,1,0:T(8,128)(2,1)} %get-tuple-element.59), channel_id=1, source_target_pairs={{0,4},{1,5},{2,6},{3,7},{4,8},{5,9},{6,10},{7,11},{8,12},{9,13},{1... | collective-permute-start | bytes 884744 | tf_op jit(solution)/shard_map/ppermute | solution.py:31
  22.7 34.1 %collective-permute-start.3 = (bf16[3,192,256]{2,1,0:T(8,128)(2,1)}, bf16[3,192,256]{2,1,0:T(8,128)(2,1)S(1)}, u32[]{:S(2)}, u32[]{:S(2)}) collective-permute-start(bf16[3,192,256]{2,1,0:T(8,128)(2,1)} %get-tuple-element.60), channel_id=1, source_target_pairs={{0,6},{1,7},{2,8},{3,9},{4,10},{5,11},{6,12},{7,13},{8,14},{9,15},... | collective-permute-start | bytes 884744 | tf_op jit(solution)/shard_map/ppermute | solution.py:31
  25.0 32.1 %collective-permute-start.4 = (bf16[3,192,256]{2,1,0:T(8,128)(2,1)}, bf16[3,192,256]{2,1,0:T(8,128)(2,1)S(1)}, u32[]{:S(2)}, u32[]{:S(2)}) collective-permute-start(bf16[3,192,256]{2,1,0:T(8,128)(2,1)} %get-tuple-element.61), channel_id=1, source_target_pairs={{0,8},{1,9},{2,10},{3,11},{4,12},{5,13},{6,14},{7,15},{8,0},{9,1},... | collective-permute-start | bytes 884744 | tf_op jit(solution)/shard_map/ppermute | solution.py:31
  27.7 29.6 %collective-permute-start.5 = (bf16[3,192,256]{2,1,0:T(8,128)(2,1)}, bf16[3,192,256]{2,1,0:T(8,128)(2,1)S(1)}, u32[]{:S(2)}, u32[]{:S(2)}) collective-permute-start(bf16[3,192,256]{2,1,0:T(8,128)(2,1)} %get-tuple-element.62), channel_id=1, source_target_pairs={{0,10},{1,11},{2,12},{3,13},{4,14},{5,15},{6,0},{7,1},{8,2},{9,3},... | collective-permute-start | bytes 884744 | tf_op jit(solution)/shard_map/ppermute | solution.py:31
  32.7 24.9 %collective-permute-start.6 = (bf16[3,192,256]{2,1,0:T(8,128)(2,1)}, bf16[3,192,256]{2,1,0:T(8,128)(2,1)S(1)}, u32[]{:S(2)}, u32[]{:S(2)}) collective-permute-start(bf16[3,192,256]{2,1,0:T(8,128)(2,1)} %get-tuple-element.63), channel_id=1, source_target_pairs={{0,12},{1,13},{2,14},{3,15},{4,0},{5,1},{6,2},{7,3},{8,4},{9,5},{1... | collective-permute-start | bytes 884744 | tf_op jit(solution)/shard_map/ppermute | solution.py:31
  34.0 26.6 %collective-permute-start.7 = (bf16[3,192,256]{2,1,0:T(8,128)(2,1)}, bf16[3,192,256]{2,1,0:T(8,128)(2,1)S(1)}, u32[]{:S(2)}, u32[]{:S(2)}) collective-permute-start(bf16[3,192,256]{2,1,0:T(8,128)(2,1)} %get-tuple-element.64), channel_id=1, source_target_pairs={{0,14},{1,15},{2,0},{3,1},{4,2},{5,3},{6,4},{7,5},{8,6},{9,7},{10,... | collective-permute-start | bytes 884744 | tf_op jit(solution)/shard_map/ppermute | solution.py:31
  56.8 9.2 %collective-permute-start.8 = (bf16[3,192,256]{2,1,0:T(8,128)(2,1)}, bf16[3,192,256]{2,1,0:T(8,128)(2,1)}, u32[]{:S(2)}, u32[]{:S(2)}) collective-permute-start(bf16[3,192,256]{2,1,0:T(8,128)(2,1)} %get-tuple-element.57.refs_0_), channel_id=1, source_target_pairs={{0,1},{1,0},{2,3},{3,2},{4,5},{5,4},{6,7},{7,6},{8,9},{9,8},{10,11... | collective-permute-start | bytes 884744 | tf_op jit(solution)/shard_map/ppermute | solution.py:36
  57.1 13.7 %collective-permute-start.9 = (bf16[3,192,256]{2,1,0:T(8,128)(2,1)S(1)}, bf16[3,192,256]{2,1,0:T(8,128)(2,1)}, u32[]{:S(2)}, u32[]{:S(2)}) collective-permute-start(bf16[3,192,256]{2,1,0:T(8,128)(2,1)S(1)} %collective-permute-done.1.refs_1_), channel_id=1, source_target_pairs={{0,1},{1,0},{2,3},{3,2},{4,5},{5,4},{6,7},{7,6},{8,9},{9,8},{10,11... | collective-permute-start | bytes 884744 | tf_op jit(solution)/shard_map/ppermute | solution.py:36
  57.3 26.1 %collective-permute-start.10 = (bf16[3,192,256]{2,1,0:T(8,128)(2,1)S(1)}, bf16[3,192,256]{2,1,0:T(8,128)(2,1)}, u32[]{:S(2)}, u32[]{:S(2)}) collective-permute-start(bf16[3,192,256]{2,1,0:T(8,128)(2,1)S(1)} %collective-permute-done.2.refs_2_), channel_id=1, source_target_pairs={{0,1},{1,0},{2,3},{3,2},{4,5},{5,4},{6,7},{7,6},{8,9},{9,8},{10,11... | collective-permute-start | bytes 884744 | tf_op jit(solution)/shard_map/ppermute | solution.py:36
  57.6 25.8 %collective-permute-start.11 = (bf16[3,192,256]{2,1,0:T(8,128)(2,1)S(1)}, bf16[3,192,256]{2,1,0:T(8,128)(2,1)}, u32[]{:S(2)}, u32[]{:S(2)}) collective-permute-start(bf16[3,192,256]{2,1,0:T(8,128)(2,1)S(1)} %collective-permute-done.3.refs_3_), channel_id=1, source_target_pairs={{0,1},{1,0},{2,3},{3,2},{4,5},{5,4},{6,7},{7,6},{8,9},{9,8},{10,11... | collective-permute-start | bytes 884744 | tf_op jit(solution)/shard_map/ppermute | solution.py:36
  60.6 23.3 %collective-permute-start.12 = (bf16[3,192,256]{2,1,0:T(8,128)(2,1)S(1)}, bf16[3,192,256]{2,1,0:T(8,128)(2,1)}, u32[]{:S(2)}, u32[]{:S(2)}) collective-permute-start(bf16[3,192,256]{2,1,0:T(8,128)(2,1)S(1)} %collective-permute-done.4.refs_4_), channel_id=1, source_target_pairs={{0,1},{1,0},{2,3},{3,2},{4,5},{5,4},{6,7},{7,6},{8,9},{9,8},{10,11... | collective-permute-start | bytes 884744 | tf_op jit(solution)/shard_map/ppermute | solution.py:36
  66.0 26.6 %collective-permute-start.16 = (bf16[3,192,256]{2,1,0:T(8,128)(2,1)}, bf16[3,192,256]{2,1,0:T(8,128)(2,1)}, u32[]{:S(2)}, u32[]{:S(2)}) collective-permute-start(bf16[3,192,256]{2,1,0:T(8,128)(2,1)} %get-tuple-element.74), channel_id=1, source_target_pairs={{0,2},{1,3},{2,4},{3,5},{4,6},{5,7},{6,8},{7,9},{8,10},{9,11},{10,... | collective-permute-start | bytes 884744 | tf_op jit(solution)/shard_map/ppermute | solution.py:31
  70.8 22.2 %collective-permute-start.17 = (bf16[3,192,256]{2,1,0:T(8,128)(2,1)}, bf16[3,192,256]{2,1,0:T(8,128)(2,1)}, u32[]{:S(2)}, u32[]{:S(2)}) collective-permute-start(bf16[3,192,256]{2,1,0:T(8,128)(2,1)} %get-tuple-element.75), channel_id=1, source_target_pairs={{0,4},{1,5},{2,6},{3,7},{4,8},{5,9},{6,10},{7,11},{8,12},{9,13},{1... | collective-permute-start | bytes 884744 | tf_op jit(solution)/shard_map/ppermute | solution.py:31
  83.9 4.5 %collective-permute-start.15 = (bf16[3,192,256]{2,1,0:T(8,128)(2,1)}, bf16[3,192,256]{2,1,0:T(8,128)(2,1)}, u32[]{:S(2)}, u32[]{:S(2)}) collective-permute-start(bf16[3,192,256]{2,1,0:T(8,128)(2,1)} %copy-done.21), channel_id=1, source_target_pairs={{0,1},{1,0},{2,3},{3,2},{4,5},{5,4},{6,7},{7,6},{8,9},{9,8},{10,11... | collective-permute-start | bytes 884744 | tf_op jit(solution)/shard_map/ppermute | solution.py:36
  86.0 33.0 %collective-permute-start.18 = (bf16[3,192,256]{2,1,0:T(8,128)(2,1)}, bf16[3,192,256]{2,1,0:T(8,128)(2,1)S(1)}, u32[]{:S(2)}, u32[]{:S(2)}) collective-permute-start(bf16[3,192,256]{2,1,0:T(8,128)(2,1)} %get-tuple-element.76), channel_id=1, source_target_pairs={{0,6},{1,7},{2,8},{3,9},{4,10},{5,11},{6,12},{7,13},{8,14},{9,15},... | collective-permute-start | bytes 884744 | tf_op jit(solution)/shard_map/ppermute | solution.py:31
  86.0 33.0 %collective-permute-start.19 = (bf16[3,192,256]{2,1,0:T(8,128)(2,1)}, bf16[3,192,256]{2,1,0:T(8,128)(2,1)S(1)}, u32[]{:S(2)}, u32[]{:S(2)}) collective-permute-start(bf16[3,192,256]{2,1,0:T(8,128)(2,1)} %get-tuple-element.77), channel_id=1, source_target_pairs={{0,8},{1,9},{2,10},{3,11},{4,12},{5,13},{6,14},{7,15},{8,0},{9,1},... | collective-permute-start | bytes 884744 | tf_op jit(solution)/shard_map/ppermute | solution.py:31
  88.5 30.6 %collective-permute-start.20 = (bf16[3,192,256]{2,1,0:T(8,128)(2,1)}, bf16[3,192,256]{2,1,0:T(8,128)(2,1)}, u32[]{:S(2)}, u32[]{:S(2)}) collective-permute-start(bf16[3,192,256]{2,1,0:T(8,128)(2,1)} %get-tuple-element.78), channel_id=1, source_target_pairs={{0,10},{1,11},{2,12},{3,13},{4,14},{5,15},{6,0},{7,1},{8,2},{9,3},... | collective-permute-start | bytes 884744 | tf_op jit(solution)/shard_map/ppermute | solution.py:31
  92.5 26.5 %collective-permute-start.21 = (bf16[3,192,256]{2,1,0:T(8,128)(2,1)}, bf16[3,192,256]{2,1,0:T(8,128)(2,1)}, u32[]{:S(2)}, u32[]{:S(2)}) collective-permute-start(bf16[3,192,256]{2,1,0:T(8,128)(2,1)} %get-tuple-element.79), channel_id=1, source_target_pairs={{0,12},{1,13},{2,14},{3,15},{4,0},{5,1},{6,2},{7,3},{8,4},{9,5},{1... | collective-permute-start | bytes 884744 | tf_op jit(solution)/shard_map/ppermute | solution.py:31
  93.1 28.5 %collective-permute-start.22 = (bf16[3,192,256]{2,1,0:T(8,128)(2,1)}, bf16[3,192,256]{2,1,0:T(8,128)(2,1)}, u32[]{:S(2)}, u32[]{:S(2)}) collective-permute-start(bf16[3,192,256]{2,1,0:T(8,128)(2,1)} %get-tuple-element.80), channel_id=1, source_target_pairs={{0,14},{1,15},{2,0},{3,1},{4,2},{5,3},{6,4},{7,5},{8,6},{9,7},{10,... | collective-permute-start | bytes 884744 | tf_op jit(solution)/shard_map/ppermute | solution.py:31
  122.7 4.4 %collective-permute-start.26 = (bf16[3,192,256]{2,1,0:T(8,128)(2,1)S(1)}, bf16[3,192,256]{2,1,0:T(8,128)(2,1)}, u32[]{:S(2)}, u32[]{:S(2)}) collective-permute-start(bf16[3,192,256]{2,1,0:T(8,128)(2,1)S(1)} %collective-permute-done.18.refs_4_), channel_id=1, source_target_pairs={{0,1},{1,0},{2,3},{3,2},{4,5},{5,4},{6,7},{7,6},{8,9},{9,8},{10,11... | collective-permute-start | bytes 884744 | tf_op jit(solution)/shard_map/ppermute | solution.py:36
  123.2 3.9 %collective-permute-start.27 = (bf16[3,192,256]{2,1,0:T(8,128)(2,1)S(1)}, bf16[3,192,256]{2,1,0:T(8,128)(2,1)}, u32[]{:S(2)}, u32[]{:S(2)}) collective-permute-start(bf16[3,192,256]{2,1,0:T(8,128)(2,1)S(1)} %collective-permute-done.19.refs_5_), channel_id=1, source_target_pairs={{0,1},{1,0},{2,3},{3,2},{4,5},{5,4},{6,7},{7,6},{8,9},{9,8},{10,11... | collective-permute-start | bytes 884744 | tf_op jit(solution)/shard_map/ppermute | solution.py:36
  149.5 31.5 %collective-permute-start.31 = (bf16[224,128]{1,0:T(8,128)(2,1)}, bf16[224,128]{1,0:T(8,128)(2,1)S(1)}, u32[]{:S(2)}, u32[]{:S(2)}) collective-permute-start(bf16[224,128]{1,0:T(8,128)(2,1)} %get-tuple-element.91), channel_id=1, source_target_pairs={{0,8},{1,9},{2,10},{3,11},{4,12},{5,13},{6,14},{7,15},{8,0},{9,1},... | collective-permute-start | bytes 172040 | tf_op jit(solution)/shard_map/ppermute | solution.py:31
  172.3 11.6 %collective-permute-start.32 = (bf16[224,128]{1,0:T(8,128)(2,1)}, bf16[224,128]{1,0:T(8,128)(2,1)S(1)}, u32[]{:S(2)}, u32[]{:S(2)}) collective-permute-start(bf16[224,128]{1,0:T(8,128)(2,1)} %get-tuple-element.92), channel_id=1, source_target_pairs={{0,10},{1,11},{2,12},{3,13},{4,14},{5,15},{6,0},{7,1},{8,2},{9,3},... | collective-permute-start | bytes 172040 | tf_op jit(solution)/shard_map/ppermute | solution.py:31
  174.8 9.7 %collective-permute-start.33 = (bf16[224,128]{1,0:T(8,128)(2,1)}, bf16[224,128]{1,0:T(8,128)(2,1)}, u32[]{:S(2)}, u32[]{:S(2)}) collective-permute-start(bf16[224,128]{1,0:T(8,128)(2,1)} %get-tuple-element.93), channel_id=1, source_target_pairs={{0,6},{1,7},{2,8},{3,9},{4,10},{5,11},{6,12},{7,13},{8,14},{9,15},... | collective-permute-start | bytes 172040 | tf_op jit(solution)/shard_map/ppermute | solution.py:31
  177.1 7.4 %collective-permute-start.34 = (bf16[224,128]{1,0:T(8,128)(2,1)}, bf16[224,128]{1,0:T(8,128)(2,1)}, u32[]{:S(2)}, u32[]{:S(2)}) collective-permute-start(bf16[224,128]{1,0:T(8,128)(2,1)} %get-tuple-element.94), channel_id=1, source_target_pairs={{0,12},{1,13},{2,14},{3,15},{4,0},{5,1},{6,2},{7,3},{8,4},{9,5},{1... | collective-permute-start | bytes 172040 | tf_op jit(solution)/shard_map/ppermute | solution.py:31
  181.0 6.3 %collective-permute-start.35 = (bf16[224,128]{1,0:T(8,128)(2,1)}, bf16[224,128]{1,0:T(8,128)(2,1)}, u32[]{:S(2)}, u32[]{:S(2)}) collective-permute-start(bf16[224,128]{1,0:T(8,128)(2,1)} %get-tuple-element.95), channel_id=1, source_target_pairs={{0,4},{1,5},{2,6},{3,7},{4,8},{5,9},{6,10},{7,11},{8,12},{9,13},{1... | collective-permute-start | bytes 172040 | tf_op jit(solution)/shard_map/ppermute | solution.py:31
  181.0 6.3 %collective-permute-start.36 = (bf16[224,128]{1,0:T(8,128)(2,1)}, bf16[224,128]{1,0:T(8,128)(2,1)}, u32[]{:S(2)}, u32[]{:S(2)}) collective-permute-start(bf16[224,128]{1,0:T(8,128)(2,1)} %get-tuple-element.96), channel_id=1, source_target_pairs={{0,14},{1,15},{2,0},{3,1},{4,2},{5,3},{6,4},{7,5},{8,6},{9,7},{10,... | collective-permute-start | bytes 172040 | tf_op jit(solution)/shard_map/ppermute | solution.py:31
  183.9 7.2 %collective-permute-start.37 = (bf16[224,128]{1,0:T(8,128)(2,1)}, bf16[224,128]{1,0:T(8,128)(2,1)}, u32[]{:S(2)}, u32[]{:S(2)}) collective-permute-start(bf16[224,128]{1,0:T(8,128)(2,1)} %get-tuple-element.97), channel_id=1, source_target_pairs={{0,2},{1,3},{2,4},{3,5},{4,6},{5,7},{6,8},{7,9},{8,10},{9,11},{10,... | collective-permute-start | bytes 172040 | tf_op jit(solution)/shard_map/ppermute | solution.py:31
  216.3 10.9 %all-to-all-start.1 = ((f32[16,2,768]{2,1,0:T(2,128)}), f32[16,2,768]{2,1,0:T(2,128)S(1)}, u32[]{:S(2)}, u32[]{:S(2)}) async-start(f32[16,2,768]{2,1,0:T(2,128)} %get-tuple-element.105), calls=%async_computation.1 | async-start | bytes 196608 | tf_op jit(solution)/shard_map/all_to_all | solution.py:791
  (38 other events, 669.4 us)

commit v5 on v4

--- a/solution.py
+++ b/solution.py
@@ -77,11 +77,11 @@
     )(starts, keys, values, queries)
 
 
-def attend_kernel(blocks, heads, frames, earlier, last, t_ref, sc_ref, w_ref, *refs):
+def attend_kernel(blocks, heads, frames, earlier, last, chip_ref, t_ref, sc_ref, w_ref, *refs):
     prev_refs, refs = refs[:earlier], refs[earlier:]
     near_refs, far_refs, refs = refs[:blocks], refs[blocks : 2 * blocks], refs[2 * blocks :]
     if last:
-        out_refs, refs = refs[:blocks], refs[blocks:]
+        out_ref, refs = refs[0], refs[1:]
     else:
         sum_ref, refs = refs[0], refs[1:]
     q_s, k_s, v_s, s_a, s_b, m_a, m_b, acc_s, tot_s, sem, q_sem = refs[:11]
@@ -219,12 +219,13 @@
             for n in range(earlier):
                 share = share + prev_s[n, b]
             half = PATCH + 8 * frames
-            spots = ((out_refs[b], 0), (out_refs[(b - 1) % blocks], half))
+            owner = lax.rem(chip_ref[0] - b + blocks, blocks)
+            spots = ((owner, 0), (lax.rem(owner + 1, blocks), half))
             beside = jnp.concatenate(
                 [share[f * PATCH : (f + 1) * PATCH, :LAT] for f in range(frames)], axis=1
             ).astype(jnp.bfloat16)
-            for ref, at in spots:
-                ref[at : at + PATCH] = beside
+            for to, at in spots:
+                out_ref[to, at : at + PATCH] = beside
             for f in range(frames):
                 square = lax.dot_general(
                     pick,
@@ -238,28 +239,27 @@
                 )
                 high = square.astype(jnp.bfloat16).astype(jnp.float32)
                 both = jnp.where(row == 0, high, jnp.where(row == 1, square - high, 0.0))
-                for ref, at in spots:
+                for to, at in spots:
                     at = at + PATCH + 8 * f
-                    ref[at : at + 8] = both.astype(jnp.bfloat16)
-
-
-def attend(near, far, steps, scale, weight, earlier, last):
+                    out_ref[to, at : at + 8] = both.astype(jnp.bfloat16)
+
+
+def attend(near, far, chip, steps, scale, weight, earlier, last):
     blocks = len(near)
     _, rows, cols = near[0].shape
     heads, keys = cols // HD, 2 * blocks * rows
     frames = rows // PATCH
     sums = (blocks, rows, 128)
     if last:
-        share = (2 * (PATCH + 8 * frames), frames * LAT)
-        out_shape = [jax.ShapeDtypeStruct(share, jnp.bfloat16)] * blocks
-        out_specs = [VM] * blocks
+        share = (blocks, 2 * (PATCH + 8 * frames), frames * LAT)
+        out_shape = jax.ShapeDtypeStruct(share, jnp.bfloat16)
     else:
-        out_shape, out_specs = jax.ShapeDtypeStruct(sums, jnp.float32), VM
+        out_shape = jax.ShapeDtypeStruct(sums, jnp.float32)
     return pl.pallas_call(
         functools.partial(attend_kernel, blocks, heads, frames, len(earlier), last),
         out_shape=out_shape,
-        in_specs=[SM, VM, VM] + [ANY] * (len(earlier) + 2 * blocks),
-        out_specs=out_specs,
+        in_specs=[SM, SM, VM, VM] + [ANY] * (len(earlier) + 2 * blocks),
+        out_specs=VM,
         scratch_shapes=[
             pltpu.VMEM((blocks, rows, cols), jnp.bfloat16),
             pltpu.VMEM((heads, keys, HD), jnp.bfloat16),
@@ -285,7 +285,7 @@
             transcendentals=blocks * rows * keys * heads,
         ),
         name="attend",
-    )(steps, scale, weight, *earlier, *near, *far)
+    )(chip, steps, scale, weight, *earlier, *near, *far)
 
 
 WINDOW = ((-1, 1), (0, 0), (0, 1), (1, 0))
@@ -333,12 +333,11 @@
     return as_matrix(col == source)
 
 
-def latent_kernel(parts, width, frames, flag_ref, dt_ref, *refs):
-    part_refs, refs = refs[:parts], refs[parts:]
+def latent_kernel(width, frames, flag_ref, dt_ref, part_ref, *refs):
     own_ref, far_ref, base_ref, next_ref, win_ref, before_ref, pass_ref = refs
-    total = part_refs[0][...].astype(jnp.float32)
-    for r in part_refs[1:]:
-        total = total + r[...].astype(jnp.float32)
+    total = part_ref[0].astype(jnp.float32)
+    for n in range(1, part_ref.shape[0]):
+        total = total + part_ref[n].astype(jnp.float32)
     row, _ = grid_iota(8, 128)
     pick = jnp.where(row < 2, 1.0, 0.0)
     cols = 16 * LAT_C
@@ -383,12 +382,12 @@
     rows = own.shape[1]
     window = jax.ShapeDtypeStruct((rows, 16 * LAT_C), jnp.bfloat16)
     return pl.pallas_call(
-        functools.partial(latent_kernel, len(parts), width, rows // PATCH),
+        functools.partial(latent_kernel, width, rows // PATCH),
         out_shape=[jax.ShapeDtypeStruct((rows, LAT), jnp.float32), window, window, window],
-        in_specs=[SM, SM] + [VM] * (len(parts) + 3),
+        in_specs=[SM, SM] + [VM] * 4,
         out_specs=[VM] * 4,
         name="latent",
-    )(flags, step_dt, *parts, own, far, base)
+    )(flags, step_dt, parts, own, far, base)
 
 
 def text_kernel(at_ref, id_ref, table_hbm, out_ref, buf, sem):
@@ -726,6 +725,7 @@
         patch_gain=patch_gain.reshape(1, -1),
         post_gain=post_gain.reshape(1, -1),
         lead=(me == 0).astype(jnp.int32).reshape(1),
+        chip=chip.astype(jnp.int32).reshape(1),
         flags=jnp.stack([chip == 0, core]).astype(jnp.int32),
         later=[packed(f, n) for f, n in zip(firsts[1:], phases[1:])],
     )
@@ -733,7 +733,7 @@
     words = lax.all_to_all(words, "seq", split_axis=0, concat_axis=0, tiled=True)
     words = jnp.sum(words, axis=0)
     far_latent = rotate(latent_in.T, "seq", 1)
-    steps, words, far_latent = lax.optimization_barrier((prepared["steps"], words, far_latent))
+    steps = prepared["steps"]
     phase_blocks = [got]
     for gate, blocks in zip(GATES, prepared["later"]):
         before = phase_blocks[0][order[min(gate, len(order) - 1)]]
@@ -745,12 +745,15 @@
     sums = []
     for n, got in enumerate(phase_blocks):
         if n:
-            sums[-1], *got = lax.optimization_barrier((sums[-1], *got))
+            sums[-1], words, far_latent, *got = lax.optimization_barrier(
+                (sums[-1], words, far_latent, *got)
+            )
         other = [swap_core(block, "seq") for block in got]
         last = n + 1 == len(phase_blocks)
         shares = attend(
             got,
             other,
+            prepared["chip"],
             steps,
             prepared["scales"][n],
             prepared["weights"][n],
@@ -759,7 +762,10 @@
         )
         if not last:
             sums.append(shares)
-    parts = [shares[0]] + [rotate(shares[t], "seq", chips - t) for t in order]
+    same_core = [list(range(k, devices, 2)) for k in (0, 1)]
+    parts = lax.all_to_all(
+        shares, "seq", split_axis=0, concat_axis=0, axis_index_groups=same_core, tiled=True
+    )
 
     latent_next, window, far, passed = step_latent(
         prepared["flags"],

time: 230 us -> 227 us (0.987)
  starting transfers between devices: 91.9 us -> 84.9 us
  waiting for transfers between devices: 40.7 us -> 44.7 us
    ppermute x22 -> x15, starting transfers between devices: 77.7 us -> 45.4 us  [rotate(): lax.ppermute(value, axis, [(i, (i + 2 * steps) % count) for i in range(co...]
    all_to_all x0 -> x1, starting transfers between devices: none -> 25.4 us  [local(): lax.all_to_all(shares, 'seq', split_axis=0, concat_axis=0, axis_index_gro...]
    all_to_all x0 -> x1, waiting for transfers between devices: none -> 7.5 us  [local(): lax.all_to_all(shares, 'seq', split_axis=0, concat_axis=0, axis_index_gro...]
    ppermute x22 -> x15, waiting for transfers between devices: 34.5 us -> 28.3 us  [rotate(): lax.ppermute(value, axis, [(i, (i + 2 * steps) % count) for i in range(co...]
    ppermute x17, waiting for transfers between devices: 0.16 us -> 2.85 us  [swap_core(): return lax.ppermute(value, axis, [(i, i ^ 1) for i in range(count)])]
  transfers between devices with their start and end apart: 41 -> 35, of which waited for: 11 -> 17; matrix products, arithmetic and copies ran while one was open for 7% -> 7% of each run, Pallas kernels for 12% -> 12%
where the time goes in v5:
time: 227 us; the launch traced here: 226 us
  starting transfers between devices  84.9 us (37%)
  Pallas kernels  76.5 us (34%)
  waiting for transfers between devices  44.7 us (20%)
  local copies, waits for them, and re-layouts  13 us (6%)
  other arithmetic  4.2 us (2%)
    ppermute x15, starting transfers between devices, rotate(): lax.ppermute(value, axis, [(i, (i + 2 * steps) % count) for i in range(co...  45.4 us
    pallas_call x2, Pallas kernels, attend(): pl.pallas_call(functools.partial(attend_kernel, blocks, heads, frames, le...  42.3 us
    ppermute x15, waiting for transfers between devices, rotate(): lax.ppermute(value, axis, [(i, (i + 2 * steps) % count) for i in range(co...  28.3 us
    all_to_all x1, starting transfers between devices, local(): lax.all_to_all(shares, 'seq', split_axis=0, concat_axis=0, axis_index_gro...  25.4 us
    pallas_call x1, Pallas kernels, decode(): pl.pallas_call(functools.partial(decode_kernel, frames), out_shape=[jax.S...  17.1 us
    all_to_all x1, waiting for transfers between devices, local(): lax.all_to_all(shares, 'seq', split_axis=0, concat_axis=0, axis_index_gro...  7.5 us
    all_to_all x1, starting transfers between devices, local(): lax.all_to_all(words, 'seq', split_axis=0, concat_axis=0, tiled=True)  7.41 us
    pallas_call x2, Pallas kernels, pack(): pl.pallas_call(functools.partial(pack_kernel, blocks), out_shape=[jax.Sha...  6.84 us
  transfers between devices with their start and end apart: 35, of which 17 were waited for; matrix products, arithmetic and copies ran while one was open for 7% of the time, Pallas kernels for 12%

profile of v5, /device:TPU:0, one launch (start us, length us, event | category | flops | bytes accessed | tf_op | source)
XLA Modules:
  0.0 226.0 jit_solution(14065808431173104597)
XLA Ops:
  0.7 4.3 %text.1 = f32[1,768]{1,0:T(1,128)} custom-call(s32[1]{0:T(128)} %bitcast.9.at_ref, s32[77]{0:T(128)} %id_ref.1, bf16[48,24704]{1,0:T(8,128)(2,1)} %bitcast.32), custom_call_target="tpu_custom_call" | custom-call | tf_op jit(solution)/shard_map/text/pallas_call | solution.py:428
  6.4 7.4 %all-to-all-start = ((f32[16,1,768]{2,1,0:T(1,128)}), f32[16,1,768]{2,1,0:T(1,128)S(1)}, u32[]{:S(2)}, u32[]{:S(2)}) async-start(f32[16,1,768]{2,1,0:T(1,128)} %broadcast_in_dim.28), calls=%async_computation | async-start | bytes 98304 | tf_op jit(solution)/shard_map/all_to_all | solution.py:733
  13.8 1.9 collective-permute-start.15
  16.2 3.4 %pack.2 = (bf16[3,192,256]{2,1,0:T(8,128)(2,1)}, bf16[3,192,256]{2,1,0:T(8,128)(2,1)}, bf16[3,192,256]{2,1,0:T(8,128)(2,1)}, bf16[3,192,256]{2,1,0:T(8,128)(2,1)...) custom-call(s32[8]{0:T(128)} %get-tuple-element.120.at_ref, ...), custom_call_target="tpu_custom_call" | custom-call | tf_op jit(solution)/shard_map/pack/pallas_call | solution.py:66
  19.7 1.5 collective-permute-start
  21.2 1.5 collective-permute-start.1
  22.6 2.4 %collective-permute-start.2 = (bf16[3,192,256]{2,1,0:T(8,128)(2,1)}, bf16[3,192,256]{2,1,0:T(8,128)(2,1)}, u32[]{:S(2)}, u32[]{:S(2)}) collective-permute-start(bf16[3,192,256]{2,1,0:T(8,128)(2,1)} %get-tuple-element.50), channel_id=1, source_target_pairs={{0,6},{1,7},{2,8},{3,9},{4,10},{5,11},{6,12},{7,13},{8,14},{9,15},... | collective-permute-start | bytes 884744 | tf_op jit(solution)/shard_map/ppermute | solution.py:31
  25.0 1.5 collective-permute-start.3
  28.2 4.4 %collective-permute-done.refs_1_ = bf16[3,192,256]{2,1,0:T(8,128)(2,1)S(1)} collective-permute-done((bf16[3,192,256]{2,1,0:T(8,128)(2,1)}, bf16[3,192,256]{2,1,0:T(8,128)(2,1)S(1)}, u32[]{:S(2)}, u32[]{:S(2)}) %collective-permute-start) | collective-permute-done | bytes 294944 | tf_op jit(solution)/shard_map/ppermute | solution.py:31
  32.7 1.3 collective-permute-start.5
  34.0 5.6 %collective-permute-start.6 = (bf16[3,192,256]{2,1,0:T(8,128)(2,1)}, bf16[3,192,256]{2,1,0:T(8,128)(2,1)}, u32[]{:S(2)}, u32[]{:S(2)}) collective-permute-start(bf16[3,192,256]{2,1,0:T(8,128)(2,1)} %get-tuple-element.54), channel_id=1, source_target_pairs={{0,14},{1,15},{2,0},{3,1},{4,2},{5,3},{6,4},{7,5},{8,6},{9,7},{10,... | collective-permute-start | bytes 884744 | tf_op jit(solution)/shard_map/ppermute | solution.py:31
  40.1 16.7 %collective-permute-done.2.refs_3_ = bf16[3,192,256]{2,1,0:T(8,128)(2,1)} collective-permute-done((bf16[3,192,256]{2,1,0:T(8,128)(2,1)}, bf16[3,192,256]{2,1,0:T(8,128)(2,1)}, u32[]{:S(2)}, u32[]{:S(2)}) %collective-permute-start.2) | collective-permute-done | bytes 294944 | tf_op jit(solution)/shard_map/ppermute | solution.py:31
  57.9 2.7 %collective-permute-done.6.refs_7_ = bf16[3,192,256]{2,1,0:T(8,128)(2,1)} collective-permute-done((bf16[3,192,256]{2,1,0:T(8,128)(2,1)}, bf16[3,192,256]{2,1,0:T(8,128)(2,1)}, u32[]{:S(2)}, u32[]{:S(2)}) %collective-permute-start.6) | collective-permute-done | bytes 294944 | tf_op jit(solution)/shard_map/ppermute | solution.py:31
  61.5 3.4 %pack.3 = (bf16[3,192,256]{2,1,0:T(8,128)(2,1)}, bf16[3,192,256]{2,1,0:T(8,128)(2,1)}, bf16[3,192,256]{2,1,0:T(8,128)(2,1)}, bf16[3,192,256]{2,1,0:T(8,128)(2,1)...) custom-call(s32[8]{0:T(128)} %get-tuple-element.121.at_ref, ...), custom_call_target="tpu_custom_call" | custom-call | tf_op jit(solution)/shard_map/pack/pallas_call | solution.py:66
  65.0 4.9 %collective-permute-start.16 = (bf16[3,192,256]{2,1,0:T(8,128)(2,1)}, bf16[3,192,256]{2,1,0:T(8,128)(2,1)S(1)}, u32[]{:S(2)}, u32[]{:S(2)}) collective-permute-start(bf16[3,192,256]{2,1,0:T(8,128)(2,1)} %get-tuple-element.64), channel_id=1, source_target_pairs={{0,2},{1,3},{2,4},{3,5},{4,6},{5,7},{6,8},{7,9},{8,10},{9,11},{10,... | collective-permute-start | bytes 884744 | tf_op jit(solution)/shard_map/ppermute | solution.py:31
  69.9 12.6 %collective-permute-start.17 = (bf16[3,192,256]{2,1,0:T(8,128)(2,1)}, bf16[3,192,256]{2,1,0:T(8,128)(2,1)S(1)}, u32[]{:S(2)}, u32[]{:S(2)}) collective-permute-start(bf16[3,192,256]{2,1,0:T(8,128)(2,1)} %get-tuple-element.65), channel_id=1, source_target_pairs={{0,4},{1,5},{2,6},{3,7},{4,8},{5,9},{6,10},{7,11},{8,12},{9,13},{1... | collective-permute-start | bytes 884744 | tf_op jit(solution)/shard_map/ppermute | solution.py:31
  85.1 2.4 %collective-permute-start.19 = (bf16[3,192,256]{2,1,0:T(8,128)(2,1)}, bf16[3,192,256]{2,1,0:T(8,128)(2,1)}, u32[]{:S(2)}, u32[]{:S(2)}) collective-permute-start(bf16[3,192,256]{2,1,0:T(8,128)(2,1)} %get-tuple-element.67), channel_id=1, source_target_pairs={{0,8},{1,9},{2,10},{3,11},{4,12},{5,13},{6,14},{7,15},{8,0},{9,1},... | collective-permute-start | bytes 884744 | tf_op jit(solution)/shard_map/ppermute | solution.py:31
  87.6 3.3 %collective-permute-start.20 = (bf16[3,192,256]{2,1,0:T(8,128)(2,1)}, bf16[3,192,256]{2,1,0:T(8,128)(2,1)}, u32[]{:S(2)}, u32[]{:S(2)}) collective-permute-start(bf16[3,192,256]{2,1,0:T(8,128)(2,1)} %get-tuple-element.68), channel_id=1, source_target_pairs={{0,10},{1,11},{2,12},{3,13},{4,14},{5,15},{6,0},{7,1},{8,2},{9,3},... | collective-permute-start | bytes 884744 | tf_op jit(solution)/shard_map/ppermute | solution.py:31
  92.0 5.4 %collective-permute-start.22 = (bf16[3,192,256]{2,1,0:T(8,128)(2,1)}, bf16[3,192,256]{2,1,0:T(8,128)(2,1)}, u32[]{:S(2)}, u32[]{:S(2)}) collective-permute-start(bf16[3,192,256]{2,1,0:T(8,128)(2,1)} %get-tuple-element.70), channel_id=1, source_target_pairs={{0,14},{1,15},{2,0},{3,1},{4,2},{5,3},{6,4},{7,5},{8,6},{9,7},{10,... | collective-permute-start | bytes 884744 | tf_op jit(solution)/shard_map/ppermute | solution.py:31
  97.4 20.5 %attend.2.refs_0_ = f32[8,192,128]{2,1,0:T(8,128)} custom-call(s32[1]{0:T(128)} %bitcast.5.chip_ref, s32[16]{0:T(128)} %select_n.107.t_ref, f32[16,2,1,128]{3,2,1,0:T(1,128)} %get-tuple-element.116.sc_ref, f32[2,128,128]{2,1,0:T(8,128)} %get-tuple-element.114.w_ref, bf16[3,192,256]{2,1,0:T(8,128)(2,1)} %get-tuple-element.47.refs_0_, ...), custom_call_target="tpu_custom_call" | custom-call | flops 4831838208 | bytes 3145728 | tf_op jit(solution)/shard_map/attend/pallas_call | solution.py:258
  118.0 3.1 %collective-permute-done.22.refs_8_ = bf16[3,192,256]{2,1,0:T(8,128)(2,1)} collective-permute-done((bf16[3,192,256]{2,1,0:T(8,128)(2,1)}, bf16[3,192,256]{2,1,0:T(8,128)(2,1)}, u32[]{:S(2)}, u32[]{:S(2)}) %collective-permute-start.22) | collective-permute-done | bytes 294944 | tf_op jit(solution)/shard_map/ppermute | solution.py:31
  126.4 21.7 %attend.3 = bf16[8,224,128]{2,1,0:T(8,128)(2,1)} custom-call(s32[1]{0:T(128)} %bitcast.5.chip_ref, s32[16]{0:T(128)} %select_n.107.t_ref, f32[16,2,1,128]{3,2,1,0:T(1,128)} %get-tuple-element.117.sc_ref, f32[2,128,128]{2,1,0:T(8,128)} %get-tuple-element.115.w_ref, f32[8,192,128]{2,1,0:T(8,128)} %attend.2.refs_0_, ...), custom_call_target="tpu_custom_call" | custom-call | flops 4831838208 | bytes 3145728 | tf_op jit(solution)/shard_map/attend/pallas_call | solution.py:258
  148.1 25.4 %all-to-all-start.1 = ((bf16[8,224,128]{2,1,0:T(8,128)(2,1)}), bf16[8,224,128]{2,1,0:T(8,128)(2,1)}, u32[]{:S(2)}, u32[]{:S(2)}) async-start(bf16[8,224,128]{2,1,0:T(8,128)(2,1)} %attend.3), calls=%async_computation.1 | async-start | bytes 917504 | tf_op jit(solution)/shard_map/all_to_all | solution.py:766
  175.6 1.8 fusion.16
  177.9 1.6 fusion.refs_2_
  179.5 7.5 %all-to-all-done.1.part_ref = bf16[8,224,128]{2,1,0:T(8,128)(2,1)} async-done(((bf16[8,224,128]{2,1,0:T(8,128)(2,1)}), bf16[8,224,128]{2,1,0:T(8,128)(2,1)}, u32[]{:S(2)}, u32[]{:S(2)}) %all-to-all-start.1) | async-done | bytes 458784 | tf_op jit(solution)/shard_map/all_to_all | solution.py:766
  187.0 4.1 %latent.1 = (f32[192,64]{1,0:T(8,128)}, bf16[192,256]{1,0:T(8,128)(2,1)}, bf16[192,256]{1,0:T(8,128)(2,1)}, bf16[192,256]{1,0:T(8,128)(2,1)}) custom-call(s32[2]{0:T(128)} %pad_add_fusion.1.flag_ref, f32[4]{0:T(128)} %get-tuple-element.106.dt_ref, bf16[8,224,128]{2,1,0:T(8,128)(2,1)} %all-to-all-done.1.part_ref, f32[64,192]{1,0:T(8,128)} %bitcast.41, ...), custom_call_target="tpu_custom_call" | custom-call | tf_op jit(solution)/shard_map/latent/pallas_call | solution.py:384
  191.1 1.6 pad_maximum_fusion.w1_ref
  195.1 17.1 %decode.1 = (bf16[768,384]{1,0:T(8,128)(2,1)}, f32[16,2,768]{2,1,0:T(2,128)}) custom-call(s32[1]{0:T(128)} %bitcast.13.lead_ref, bf16[192,256]{1,0:T(8,128)(2,1)} %get-tuple-element.82.far_ref, bf16[192,256]{1,0:T(8,128)(2,1)} %copy-done.4, bf16[192,256]{1,0:T(8,128)(2,1)} %get-tuple-element.84.own_ref, bf16[768,1536]{1,0:T(8,128)(2,1)} %pad_maximum_fusion.w1_ref, ...), custom_call_target="tpu_custom_call" | custom-call | tf_op jit(solution)/shard_map/decode/pallas_call | solution.py:587
  212.2 3.9 %all-to-all-start.2 = ((f32[16,2,768]{2,1,0:T(2,128)}), f32[16,2,768]{2,1,0:T(2,128)S(1)}, u32[]{:S(2)}, u32[]{:S(2)}) async-start(f32[16,2,768]{2,1,0:T(2,128)} %get-tuple-element.87), calls=%async_computation.2 | async-start | bytes 196608 | tf_op jit(solution)/shard_map/all_to_all | solution.py:797
  217.4 6.0 %all-to-all-done.2.got_ref = f32[16,2,768]{2,1,0:T(2,128)S(1)} async-done(((f32[16,2,768]{2,1,0:T(2,128)}), f32[16,2,768]{2,1,0:T(2,128)S(1)}, u32[]{:S(2)}, u32[]{:S(2)}) %all-to-all-start.2) | async-done | bytes 98336 | tf_op jit(solution)/shard_map/all_to_all | solution.py:797
  224.1 1.8 rate.1
  (131 shorter events, 22.1 us)
Async XLA Ops:
  6.4 78.1 %all-to-all-start = ((f32[16,1,768]{2,1,0:T(1,128)}), f32[16,1,768]{2,1,0:T(1,128)S(1)}, u32[]{:S(2)}, u32[]{:S(2)}) async-start(f32[16,1,768]{2,1,0:T(1,128)} %broadcast_in_dim.28), calls=%async_computation | async-start | bytes 98304 | tf_op jit(solution)/shard_map/all_to_all | solution.py:733
  13.8 13.3 %collective-permute-start.15 = (f32[64,192]{1,0:T(8,128)}, f32[64,192]{1,0:T(8,128)S(1)}, u32[]{:S(2)}, u32[]{:S(2)}) collective-permute-start(f32[64,192]{1,0:T(8,128)} %bitcast.40), channel_id=1, source_target_pairs={{0,2},{1,3},{2,4},{3,5},{4,6},{5,7},{6,8},{7,9},{8,10},{9,11},{10,... | collective-permute-start | bytes 147464 | tf_op jit(solution)/shard_map/ppermute | solution.py:31
  19.7 13.0 %collective-permute-start = (bf16[3,192,256]{2,1,0:T(8,128)(2,1)}, bf16[3,192,256]{2,1,0:T(8,128)(2,1)S(1)}, u32[]{:S(2)}, u32[]{:S(2)}) collective-permute-start(bf16[3,192,256]{2,1,0:T(8,128)(2,1)} %get-tuple-element.48), channel_id=1, source_target_pairs={{0,2},{1,3},{2,4},{3,5},{4,6},{5,7},{6,8},{7,9},{8,10},{9,11},{10,... | collective-permute-start | bytes 884744 | tf_op jit(solution)/shard_map/ppermute | solution.py:31
  21.2 12.8 %collective-permute-start.1 = (bf16[3,192,256]{2,1,0:T(8,128)(2,1)}, bf16[3,192,256]{2,1,0:T(8,128)(2,1)S(1)}, u32[]{:S(2)}, u32[]{:S(2)}) collective-permute-start(bf16[3,192,256]{2,1,0:T(8,128)(2,1)} %get-tuple-element.49), channel_id=1, source_target_pairs={{0,4},{1,5},{2,6},{3,7},{4,8},{5,9},{6,10},{7,11},{8,12},{9,13},{1... | collective-permute-start | bytes 884744 | tf_op jit(solution)/shard_map/ppermute | solution.py:31
  22.6 34.3 %collective-permute-start.2 = (bf16[3,192,256]{2,1,0:T(8,128)(2,1)}, bf16[3,192,256]{2,1,0:T(8,128)(2,1)}, u32[]{:S(2)}, u32[]{:S(2)}) collective-permute-start(bf16[3,192,256]{2,1,0:T(8,128)(2,1)} %get-tuple-element.50), channel_id=1, source_target_pairs={{0,6},{1,7},{2,8},{3,9},{4,10},{5,11},{6,12},{7,13},{8,14},{9,15},... | collective-permute-start | bytes 884744 | tf_op jit(solution)/shard_map/ppermute | solution.py:31
  25.0 32.2 %collective-permute-start.3 = (bf16[3,192,256]{2,1,0:T(8,128)(2,1)}, bf16[3,192,256]{2,1,0:T(8,128)(2,1)}, u32[]{:S(2)}, u32[]{:S(2)}) collective-permute-start(bf16[3,192,256]{2,1,0:T(8,128)(2,1)} %get-tuple-element.51), channel_id=1, source_target_pairs={{0,8},{1,9},{2,10},{3,11},{4,12},{5,13},{6,14},{7,15},{8,0},{9,1},... | collective-permute-start | bytes 884744 | tf_op jit(solution)/shard_map/ppermute | solution.py:31
  27.1 30.3 %collective-permute-start.4 = (bf16[3,192,256]{2,1,0:T(8,128)(2,1)}, bf16[3,192,256]{2,1,0:T(8,128)(2,1)S(1)}, u32[]{:S(2)}, u32[]{:S(2)}) collective-permute-start(bf16[3,192,256]{2,1,0:T(8,128)(2,1)} %get-tuple-element.52), channel_id=1, source_target_pairs={{0,10},{1,11},{2,12},{3,13},{4,14},{5,15},{6,0},{7,1},{8,2},{9,3},... | collective-permute-start | bytes 884744 | tf_op jit(solution)/shard_map/ppermute | solution.py:31
  32.7 25.0 %collective-permute-start.5 = (bf16[3,192,256]{2,1,0:T(8,128)(2,1)}, bf16[3,192,256]{2,1,0:T(8,128)(2,1)S(1)}, u32[]{:S(2)}, u32[]{:S(2)}) collective-permute-start(bf16[3,192,256]{2,1,0:T(8,128)(2,1)} %get-tuple-element.53), channel_id=1, source_target_pairs={{0,12},{1,13},{2,14},{3,15},{4,0},{5,1},{6,2},{7,3},{8,4},{9,5},{1... | collective-permute-start | bytes 884744 | tf_op jit(solution)/shard_map/ppermute | solution.py:31
  34.0 26.6 %collective-permute-start.6 = (bf16[3,192,256]{2,1,0:T(8,128)(2,1)}, bf16[3,192,256]{2,1,0:T(8,128)(2,1)}, u32[]{:S(2)}, u32[]{:S(2)}) collective-permute-start(bf16[3,192,256]{2,1,0:T(8,128)(2,1)} %get-tuple-element.54), channel_id=1, source_target_pairs={{0,14},{1,15},{2,0},{3,1},{4,2},{5,3},{6,4},{7,5},{8,6},{9,7},{10,... | collective-permute-start | bytes 884744 | tf_op jit(solution)/shard_map/ppermute | solution.py:31
  56.9 8.1 %collective-permute-start.7 = (bf16[3,192,256]{2,1,0:T(8,128)(2,1)}, bf16[3,192,256]{2,1,0:T(8,128)(2,1)}, u32[]{:S(2)}, u32[]{:S(2)}) collective-permute-start(bf16[3,192,256]{2,1,0:T(8,128)(2,1)} %get-tuple-element.47.refs_0_), channel_id=1, source_target_pairs={{0,1},{1,0},{2,3},{3,2},{4,5},{5,4},{6,7},{7,6},{8,9},{9,8},{10,11... | collective-permute-start | bytes 884744 | tf_op jit(solution)/shard_map/ppermute | solution.py:36
  57.2 12.7 %collective-permute-start.8 = (bf16[3,192,256]{2,1,0:T(8,128)(2,1)S(1)}, bf16[3,192,256]{2,1,0:T(8,128)(2,1)}, u32[]{:S(2)}, u32[]{:S(2)}) collective-permute-start(bf16[3,192,256]{2,1,0:T(8,128)(2,1)S(1)} %collective-permute-done.refs_1_), channel_id=1, source_target_pairs={{0,1},{1,0},{2,3},{3,2},{4,5},{5,4},{6,7},{7,6},{8,9},{9,8},{10,11... | collective-permute-start | bytes 884744 | tf_op jit(solution)/shard_map/ppermute | solution.py:36
  57.4 25.1 %collective-permute-start.9 = (bf16[3,192,256]{2,1,0:T(8,128)(2,1)S(1)}, bf16[3,192,256]{2,1,0:T(8,128)(2,1)}, u32[]{:S(2)}, u32[]{:S(2)}) collective-permute-start(bf16[3,192,256]{2,1,0:T(8,128)(2,1)S(1)} %collective-permute-done.1.refs_2_), channel_id=1, source_target_pairs={{0,1},{1,0},{2,3},{3,2},{4,5},{5,4},{6,7},{7,6},{8,9},{9,8},{10,11... | collective-permute-start | bytes 884744 | tf_op jit(solution)/shard_map/ppermute | solution.py:36
  57.7 24.8 %collective-permute-start.10 = (bf16[3,192,256]{2,1,0:T(8,128)(2,1)}, bf16[3,192,256]{2,1,0:T(8,128)(2,1)}, u32[]{:S(2)}, u32[]{:S(2)}) collective-permute-start(bf16[3,192,256]{2,1,0:T(8,128)(2,1)} %collective-permute-done.2.refs_3_), channel_id=1, source_target_pairs={{0,1},{1,0},{2,3},{3,2},{4,5},{5,4},{6,7},{7,6},{8,9},{9,8},{10,11... | collective-permute-start | bytes 884744 | tf_op jit(solution)/shard_map/ppermute | solution.py:36
  60.6 22.4 %collective-permute-start.11 = (bf16[3,192,256]{2,1,0:T(8,128)(2,1)}, bf16[3,192,256]{2,1,0:T(8,128)(2,1)}, u32[]{:S(2)}, u32[]{:S(2)}) collective-permute-start(bf16[3,192,256]{2,1,0:T(8,128)(2,1)} %collective-permute-done.3.refs_4_), channel_id=1, source_target_pairs={{0,1},{1,0},{2,3},{3,2},{4,5},{5,4},{6,7},{7,6},{8,9},{9,8},{10,11... | collective-permute-start | bytes 884744 | tf_op jit(solution)/shard_map/ppermute | solution.py:36
  65.0 26.5 %collective-permute-start.16 = (bf16[3,192,256]{2,1,0:T(8,128)(2,1)}, bf16[3,192,256]{2,1,0:T(8,128)(2,1)S(1)}, u32[]{:S(2)}, u32[]{:S(2)}) collective-permute-start(bf16[3,192,256]{2,1,0:T(8,128)(2,1)} %get-tuple-element.64), channel_id=1, source_target_pairs={{0,2},{1,3},{2,4},{3,5},{4,6},{5,7},{6,8},{7,9},{8,10},{9,11},{10,... | collective-permute-start | bytes 884744 | tf_op jit(solution)/shard_map/ppermute | solution.py:31
  69.9 22.1 %collective-permute-start.17 = (bf16[3,192,256]{2,1,0:T(8,128)(2,1)}, bf16[3,192,256]{2,1,0:T(8,128)(2,1)S(1)}, u32[]{:S(2)}, u32[]{:S(2)}) collective-permute-start(bf16[3,192,256]{2,1,0:T(8,128)(2,1)} %get-tuple-element.65), channel_id=1, source_target_pairs={{0,4},{1,5},{2,6},{3,7},{4,8},{5,9},{6,10},{7,11},{8,12},{9,13},{1... | collective-permute-start | bytes 884744 | tf_op jit(solution)/shard_map/ppermute | solution.py:31
  82.5 2.6 %collective-permute-start.12 = (bf16[3,192,256]{2,1,0:T(8,128)(2,1)}, bf16[3,192,256]{2,1,0:T(8,128)(2,1)}, u32[]{:S(2)}, u32[]{:S(2)}) collective-permute-start(bf16[3,192,256]{2,1,0:T(8,128)(2,1)} %copy-done.16), channel_id=1, source_target_pairs={{0,1},{1,0},{2,3},{3,2},{4,5},{5,4},{6,7},{7,6},{8,9},{9,8},{10,11... | collective-permute-start | bytes 884744 | tf_op jit(solution)/shard_map/ppermute | solution.py:36
  82.5 2.6 %collective-permute-start.13 = (bf16[3,192,256]{2,1,0:T(8,128)(2,1)}, bf16[3,192,256]{2,1,0:T(8,128)(2,1)}, u32[]{:S(2)}, u32[]{:S(2)}) collective-permute-start(bf16[3,192,256]{2,1,0:T(8,128)(2,1)} %copy-done.17), channel_id=1, source_target_pairs={{0,1},{1,0},{2,3},{3,2},{4,5},{5,4},{6,7},{7,6},{8,9},{9,8},{10,11... | collective-permute-start | bytes 884744 | tf_op jit(solution)/shard_map/ppermute | solution.py:36
  83.0 4.5 %collective-permute-start.14 = (bf16[3,192,256]{2,1,0:T(8,128)(2,1)}, bf16[3,192,256]{2,1,0:T(8,128)(2,1)}, u32[]{:S(2)}, u32[]{:S(2)}) collective-permute-start(bf16[3,192,256]{2,1,0:T(8,128)(2,1)} %collective-permute-done.6.refs_7_), channel_id=1, source_target_pairs={{0,1},{1,0},{2,3},{3,2},{4,5},{5,4},{6,7},{7,6},{8,9},{9,8},{10,11... | collective-permute-start | bytes 884744 | tf_op jit(solution)/shard_map/ppermute | solution.py:36
  85.1 32.9 %collective-permute-start.18 = (bf16[3,192,256]{2,1,0:T(8,128)(2,1)}, bf16[3,192,256]{2,1,0:T(8,128)(2,1)}, u32[]{:S(2)}, u32[]{:S(2)}) collective-permute-start(bf16[3,192,256]{2,1,0:T(8,128)(2,1)} %get-tuple-element.66), channel_id=1, source_target_pairs={{0,6},{1,7},{2,8},{3,9},{4,10},{5,11},{6,12},{7,13},{8,14},{9,15},... | collective-permute-start | bytes 884744 | tf_op jit(solution)/shard_map/ppermute | solution.py:31
  85.1 32.9 %collective-permute-start.19 = (bf16[3,192,256]{2,1,0:T(8,128)(2,1)}, bf16[3,192,256]{2,1,0:T(8,128)(2,1)}, u32[]{:S(2)}, u32[]{:S(2)}) collective-permute-start(bf16[3,192,256]{2,1,0:T(8,128)(2,1)} %get-tuple-element.67), channel_id=1, source_target_pairs={{0,8},{1,9},{2,10},{3,11},{4,12},{5,13},{6,14},{7,15},{8,0},{9,1},... | collective-permute-start | bytes 884744 | tf_op jit(solution)/shard_map/ppermute | solution.py:31
  87.6 30.4 %collective-permute-start.20 = (bf16[3,192,256]{2,1,0:T(8,128)(2,1)}, bf16[3,192,256]{2,1,0:T(8,128)(2,1)}, u32[]{:S(2)}, u32[]{:S(2)}) collective-permute-start(bf16[3,192,256]{2,1,0:T(8,128)(2,1)} %get-tuple-element.68), channel_id=1, source_target_pairs={{0,10},{1,11},{2,12},{3,13},{4,14},{5,15},{6,0},{7,1},{8,2},{9,3},... | collective-permute-start | bytes 884744 | tf_op jit(solution)/shard_map/ppermute | solution.py:31
  91.5 26.5 %collective-permute-start.21 = (bf16[3,192,256]{2,1,0:T(8,128)(2,1)}, bf16[3,192,256]{2,1,0:T(8,128)(2,1)}, u32[]{:S(2)}, u32[]{:S(2)}) collective-permute-start(bf16[3,192,256]{2,1,0:T(8,128)(2,1)} %get-tuple-element.69), channel_id=1, source_target_pairs={{0,12},{1,13},{2,14},{3,15},{4,0},{5,1},{6,2},{7,3},{8,4},{9,5},{1... | collective-permute-start | bytes 884744 | tf_op jit(solution)/shard_map/ppermute | solution.py:31
  92.0 29.1 %collective-permute-start.22 = (bf16[3,192,256]{2,1,0:T(8,128)(2,1)}, bf16[3,192,256]{2,1,0:T(8,128)(2,1)}, u32[]{:S(2)}, u32[]{:S(2)}) collective-permute-start(bf16[3,192,256]{2,1,0:T(8,128)(2,1)} %get-tuple-element.70), channel_id=1, source_target_pairs={{0,14},{1,15},{2,0},{3,1},{4,2},{5,3},{6,4},{7,5},{8,6},{9,7},{10,... | collective-permute-start | bytes 884744 | tf_op jit(solution)/shard_map/ppermute | solution.py:31
  121.6 2.0 collective-permute-start.25
  121.8 2.3 %collective-permute-start.26 = (bf16[3,192,256]{2,1,0:T(8,128)(2,1)}, bf16[3,192,256]{2,1,0:T(8,128)(2,1)}, u32[]{:S(2)}, u32[]{:S(2)}) collective-permute-start(bf16[3,192,256]{2,1,0:T(8,128)(2,1)} %collective-permute-done.18.refs_4_), channel_id=1, source_target_pairs={{0,1},{1,0},{2,3},{3,2},{4,5},{5,4},{6,7},{7,6},{8,9},{9,8},{10,11... | collective-permute-start | bytes 884744 | tf_op jit(solution)/shard_map/ppermute | solution.py:36
  122.2 2.3 %collective-permute-start.27 = (bf16[3,192,256]{2,1,0:T(8,128)(2,1)}, bf16[3,192,256]{2,1,0:T(8,128)(2,1)}, u32[]{:S(2)}, u32[]{:S(2)}) collective-permute-start(bf16[3,192,256]{2,1,0:T(8,128)(2,1)} %collective-permute-done.19.refs_5_), channel_id=1, source_target_pairs={{0,1},{1,0},{2,3},{3,2},{4,5},{5,4},{6,7},{7,6},{8,9},{9,8},{10,11... | collective-permute-start | bytes 884744 | tf_op jit(solution)/shard_map/ppermute | solution.py:36
  122.7 2.1 collective-permute-start.28
  123.1 2.1 collective-permute-start.29
  148.1 38.9 %all-to-all-start.1 = ((bf16[8,224,128]{2,1,0:T(8,128)(2,1)}), bf16[8,224,128]{2,1,0:T(8,128)(2,1)}, u32[]{:S(2)}, u32[]{:S(2)}) async-start(bf16[8,224,128]{2,1,0:T(8,128)(2,1)} %attend.3), calls=%async_computation.1 | async-start | bytes 917504 | tf_op jit(solution)/shard_map/all_to_all | solution.py:766
  191.1 3.3 %collective-permute-start.31 = (bf16[192,256]{1,0:T(8,128)(2,1)}, bf16[192,256]{1,0:T(8,128)(2,1)S(1)}, u32[]{:S(2)}, u32[]{:S(2)}) collective-permute-start(bf16[192,256]{1,0:T(8,128)(2,1)} %get-tuple-element.83), channel_id=1, source_target_pairs={{0,1},{1,0},{2,3},{3,2},{4,5},{5,4},{6,7},{7,6},{8,9},{9,8},{10,11... | collective-permute-start | bytes 294920 | tf_op jit(solution)/shard_map/ppermute | solution.py:36
  212.2 11.2 %all-to-all-start.2 = ((f32[16,2,768]{2,1,0:T(2,128)}), f32[16,2,768]{2,1,0:T(2,128)S(1)}, u32[]{:S(2)}, u32[]{:S(2)}) async-start(f32[16,2,768]{2,1,0:T(2,128)} %get-tuple-element.87), calls=%async_computation.2 | async-start | bytes 196608 | tf_op jit(solution)/shard_map/all_to_all | solution.py:797
  (27 other events, 572.4 us)

commit v6 on v5

--- a/solution.py
+++ b/solution.py
@@ -284,6 +284,7 @@
             bytes_accessed=4 * keys * cols,
             transcendentals=blocks * rows * keys * heads,
         ),
+        compiler_params=pltpu.CompilerParams(vmem_limit_bytes=40 << 20),
         name="attend",
     )(chip, steps, scale, weight, *earlier, *near, *far)
 
@@ -386,6 +387,7 @@
         out_shape=[jax.ShapeDtypeStruct((rows, LAT), jnp.float32), window, window, window],
         in_specs=[SM, SM] + [VM] * 4,
         out_specs=[VM] * 4,
+        compiler_params=pltpu.CompilerParams(vmem_limit_bytes=16 << 20),
         name="latent",
     )(flags, step_dt, parts, own, far, base)
 
@@ -600,6 +602,7 @@
             pltpu.VMEM((wide * 4 * PATCH, 9 * CH), jnp.bfloat16),
             pltpu.SemaphoreType.DMA((3,)),
         ],
+        compiler_params=pltpu.CompilerParams(vmem_limit_bytes=48 << 20),
         name="decode",
     )(
         lead,
@@ -684,11 +687,14 @@
 
     order = sorted(range(1, chips), key=lambda t: abs(2 * t - chips))
 
-    def packed(first, count):
-        at = ((chip + jnp.arange(chips)) % chips) * cols + first * HD
-        return pack(keys, values, queries, at.astype(jnp.int32), count * HD)
-
-    blocks = packed(firsts[0], phases[0])
+    def packed(first, count, turns):
+        at = ((chip + jnp.asarray(turns, jnp.int32)) % chips) * cols + first * HD
+        blocks = pack(keys, values, queries, at.astype(jnp.int32), count * HD)
+        return dict(zip(turns, blocks))
+
+    early = order[:2]
+    blocks = packed(firsts[0], phases[0], early)
+    blocks |= packed(firsts[0], phases[0], [t for t in range(chips) if t not in early])
     got = [blocks[0]] * chips
     for turn in order:
         got[turn] = rotate(blocks[turn], "seq", turn)
@@ -727,7 +733,7 @@
         lead=(me == 0).astype(jnp.int32).reshape(1),
         chip=chip.astype(jnp.int32).reshape(1),
         flags=jnp.stack([chip == 0, core]).astype(jnp.int32),
-        later=[packed(f, n) for f, n in zip(firsts[1:], phases[1:])],
+        later=[packed(f, n, list(range(chips))) for f, n in zip(firsts[1:], phases[1:])],
     )
     words = jnp.broadcast_to(prepared["text"][None], (devices, 1, TEXT_W))
     words = lax.all_to_all(words, "seq", split_axis=0, concat_axis=0, tiled=True)

time: 227 us -> 226 us (level)
  starting transfers between devices: 84.9 us -> 63 us
  local copies, waits for them, and re-layouts: 13 us -> 26.8 us
  waiting for transfers between devices: 44.7 us -> 53.5 us
    ppermute x15, starting transfers between devices: 45.4 us -> 29.5 us  [rotate(): lax.ppermute(value, axis, [(i, (i + 2 * steps) % count) for i in range(co...]
    unnamed x50 -> x66, local copies, waits for them, and re-layouts: 2.93 us -> 15.8 us
    ppermute x15, waiting for transfers between devices: 28.3 us -> 38.6 us  [rotate(): lax.ppermute(value, axis, [(i, (i + 2 * steps) % count) for i in range(co...]
    all_to_all x1, starting transfers between devices: 25.4 us -> 19.4 us  [local(): lax.all_to_all(shares, 'seq', split_axis=0, concat_axis=0, axis_index_gro...]
    pallas_call x2, Pallas kernels: 42.3 us -> 39.5 us  [attend(): pl.pallas_call(functools.partial(attend_kernel, blocks, heads, frames, le...]
    pallas_call x2 -> x3, Pallas kernels: 6.84 us -> 9.17 us  [pack(): pl.pallas_call(functools.partial(pack_kernel, blocks), out_shape=[jax.Sha...]
  transfers between devices with their start and end apart: 35 -> 35, of which waited for: 17 -> 17; matrix products, arithmetic and copies ran while one was open for 7% -> 8% of each run, Pallas kernels for 12% -> 12%
where the time goes in v6:
time: 226 us; the launch traced here: 225 us
  Pallas kernels  74.5 us (33%)
  starting transfers between devices  63 us (28%)
  waiting for transfers between devices  53.5 us (24%)
  local copies, waits for them, and re-layouts  26.8 us (12%)
  other arithmetic  5.01 us (2%)
    pallas_call x2, Pallas kernels, attend(): pl.pallas_call(functools.partial(attend_kernel, blocks, heads, frames, le...  39.5 us
    ppermute x15, waiting for transfers between devices, rotate(): lax.ppermute(value, axis, [(i, (i + 2 * steps) % count) for i in range(co...  38.6 us
    ppermute x15, starting transfers between devices, rotate(): lax.ppermute(value, axis, [(i, (i + 2 * steps) % count) for i in range(co...  29.5 us
    all_to_all x1, starting transfers between devices, local(): lax.all_to_all(shares, 'seq', split_axis=0, concat_axis=0, axis_index_gro...  19.4 us
    pallas_call x1, Pallas kernels, decode(): pl.pallas_call(functools.partial(decode_kernel, frames), out_shape=[jax.S...  16.1 us
    unnamed x66, local copies, waits for them, and re-layouts  15.8 us
    pallas_call x3, Pallas kernels, pack(): pl.pallas_call(functools.partial(pack_kernel, blocks), out_shape=[jax.Sha...  9.17 us
    all_to_all x1, starting transfers between devices, local(): lax.all_to_all(words, 'seq', split_axis=0, concat_axis=0, tiled=True)  7.41 us
  transfers between devices with their start and end apart: 35, of which 17 were waited for; matrix products, arithmetic and copies ran while one was open for 8% of the time, Pallas kernels for 12%

profile of v6, /device:TPU:0, one launch (start us, length us, event | category | flops | bytes accessed | tf_op | source)
XLA Modules:
  0.0 225.0 jit_solution(1498380961643009685)
XLA Ops:
  0.7 4.3 %text.1 = f32[1,768]{1,0:T(1,128)} custom-call(s32[1]{0:T(128)} %bitcast.9.at_ref, s32[77]{0:T(128)} %id_ref.1, bf16[48,24704]{1,0:T(8,128)(2,1)} %bitcast.36), custom_call_target="tpu_custom_call" | custom-call | tf_op jit(solution)/shard_map/text/pallas_call | solution.py:430
  6.4 7.4 %all-to-all-start = ((f32[16,1,768]{2,1,0:T(1,128)}), f32[16,1,768]{2,1,0:T(1,128)S(1)}, u32[]{:S(2)}, u32[]{:S(2)}) async-start(f32[16,1,768]{2,1,0:T(1,128)} %broadcast_in_dim.28), calls=%async_computation | async-start | bytes 98304 | tf_op jit(solution)/shard_map/all_to_all | solution.py:739
  13.8 1.9 collective-permute-start.15
  16.9 2.6 %pack.4 = (bf16[3,192,256]{2,1,0:T(8,128)(2,1)}, bf16[3,192,256]{2,1,0:T(8,128)(2,1)}) custom-call(s32[2]{0:T(128)} %fusion.7.at_ref, bf16[192,4096]{1,0:T(8,128)(2,1)} %k_hbm.5, bf16[192,4096]{1,0:T(8,128)(2,1)} %v_hbm.5, bf16[192,4096]{1,0:T(8,128)(2,1)} %q_hbm.5), custom_call_target="tpu_custom_call" | custom-call | tf_op jit(solution)/shard_map/pack/pallas_call | solution.py:66
  19.5 2.4 %collective-permute-start.2 = (bf16[3,192,256]{2,1,0:T(8,128)(2,1)}, bf16[3,192,256]{2,1,0:T(8,128)(2,1)S(1)}, u32[]{:S(2)}, u32[]{:S(2)}) collective-permute-start(bf16[3,192,256]{2,1,0:T(8,128)(2,1)} %get-tuple-element.50), channel_id=1, source_target_pairs={{0,6},{1,7},{2,8},{3,9},{4,10},{5,11},{6,12},{7,13},{8,14},{9,15},... | collective-permute-start | bytes 884744 | tf_op jit(solution)/shard_map/ppermute | solution.py:31
  23.5 3.1 %pack.3 = (bf16[3,192,256]{2,1,0:T(8,128)(2,1)}, bf16[3,192,256]{2,1,0:T(8,128)(2,1)}, bf16[3,192,256]{2,1,0:T(8,128)(2,1)}, bf16[3,192,256]{2,1,0:T(8,128)(2,1)...) custom-call(s32[6]{0:T(128)} %fusion.5.at_ref, bf16[192,4096]{1,0:T(8,128)(2,1)} %k_hbm.5, ...), custom_call_target="tpu_custom_call" | custom-call | tf_op jit(solution)/shard_map/pack/pallas_call | solution.py:66
  27.7 1.5 collective-permute-start.1
  29.1 1.4 fusion.20
  31.2 2.9 %collective-permute-start.4 = (bf16[3,192,256]{2,1,0:T(8,128)(2,1)}, bf16[3,192,256]{2,1,0:T(8,128)(2,1)S(1)}, u32[]{:S(2)}, u32[]{:S(2)}) collective-permute-start(bf16[3,192,256]{2,1,0:T(8,128)(2,1)} %get-tuple-element.52), channel_id=1, source_target_pairs={{0,10},{1,11},{2,12},{3,13},{4,14},{5,15},{6,0},{7,1},{8,2},{9,3},... | collective-permute-start | bytes 884744 | tf_op jit(solution)/shard_map/ppermute | solution.py:31
  34.1 22.6 %collective-permute-done.2.refs_3_ = bf16[3,192,256]{2,1,0:T(8,128)(2,1)S(1)} collective-permute-done((bf16[3,192,256]{2,1,0:T(8,128)(2,1)}, bf16[3,192,256]{2,1,0:T(8,128)(2,1)S(1)}, u32[]{:S(2)}, u32[]{:S(2)}) %collective-permute-start.2) | collective-permute-done | bytes 294944 | tf_op jit(solution)/shard_map/ppermute | solution.py:31
  58.5 8.0 %collective-permute-done.4.refs_5_ = bf16[3,192,256]{2,1,0:T(8,128)(2,1)S(1)} collective-permute-done((bf16[3,192,256]{2,1,0:T(8,128)(2,1)}, bf16[3,192,256]{2,1,0:T(8,128)(2,1)S(1)}, u32[]{:S(2)}, u32[]{:S(2)}) %collective-permute-start.4) | collective-permute-done | bytes 294944 | tf_op jit(solution)/shard_map/ppermute | solution.py:31
  66.6 2.8 %collective-permute-done.5.refs_6_ = bf16[3,192,256]{2,1,0:T(8,128)(2,1)} collective-permute-done((bf16[3,192,256]{2,1,0:T(8,128)(2,1)}, bf16[3,192,256]{2,1,0:T(8,128)(2,1)}, u32[]{:S(2)}, u32[]{:S(2)}) %collective-permute-start.5) | collective-permute-done | bytes 294944 | tf_op jit(solution)/shard_map/ppermute | solution.py:31
  69.3 1.6 collective-permute-done.6.refs_7_
  72.4 3.4 %pack.5 = (bf16[3,192,256]{2,1,0:T(8,128)(2,1)}, bf16[3,192,256]{2,1,0:T(8,128)(2,1)}, bf16[3,192,256]{2,1,0:T(8,128)(2,1)}, bf16[3,192,256]{2,1,0:T(8,128)(2,1)...) custom-call(s32[8]{0:T(128)} %fusion.13.at_ref, ...), custom_call_target="tpu_custom_call" | custom-call | tf_op jit(solution)/shard_map/pack/pallas_call | solution.py:66
  77.3 6.0 %collective-permute-start.16 = (bf16[3,192,256]{2,1,0:T(8,128)(2,1)}, bf16[3,192,256]{2,1,0:T(8,128)(2,1)S(1)}, u32[]{:S(2)}, u32[]{:S(2)}) collective-permute-start(bf16[3,192,256]{2,1,0:T(8,128)(2,1)} %get-tuple-element.64), channel_id=1, source_target_pairs={{0,2},{1,3},{2,4},{3,5},{4,6},{5,7},{6,8},{7,9},{8,10},{9,11},{10,... | collective-permute-start | bytes 884744 | tf_op jit(solution)/shard_map/ppermute | solution.py:31
  87.2 2.4 %collective-permute-start.19 = (bf16[3,192,256]{2,1,0:T(8,128)(2,1)}, bf16[3,192,256]{2,1,0:T(8,128)(2,1)}, u32[]{:S(2)}, u32[]{:S(2)}) collective-permute-start(bf16[3,192,256]{2,1,0:T(8,128)(2,1)} %get-tuple-element.67), channel_id=1, source_target_pairs={{0,8},{1,9},{2,10},{3,11},{4,12},{5,13},{6,14},{7,15},{8,0},{9,1},... | collective-permute-start | bytes 884744 | tf_op jit(solution)/shard_map/ppermute | solution.py:31
  89.6 2.4 %collective-permute-start.20 = (bf16[3,192,256]{2,1,0:T(8,128)(2,1)}, bf16[3,192,256]{2,1,0:T(8,128)(2,1)S(1)}, u32[]{:S(2)}, u32[]{:S(2)}) collective-permute-start(bf16[3,192,256]{2,1,0:T(8,128)(2,1)} %get-tuple-element.68), channel_id=1, source_target_pairs={{0,10},{1,11},{2,12},{3,13},{4,14},{5,15},{6,0},{7,1},{8,2},{9,3},... | collective-permute-start | bytes 884744 | tf_op jit(solution)/shard_map/ppermute | solution.py:31
  94.0 1.5 collective-permute-done.17.refs_3_
  95.5 4.2 %collective-permute-start.22 = (bf16[3,192,256]{2,1,0:T(8,128)(2,1)}, bf16[3,192,256]{2,1,0:T(8,128)(2,1)S(1)}, u32[]{:S(2)}, u32[]{:S(2)}) collective-permute-start(bf16[3,192,256]{2,1,0:T(8,128)(2,1)} %get-tuple-element.70), channel_id=1, source_target_pairs={{0,14},{1,15},{2,0},{3,1},{4,2},{5,3},{6,4},{7,5},{8,6},{9,7},{10,... | collective-permute-start | bytes 884744 | tf_op jit(solution)/shard_map/ppermute | solution.py:31
  101.7 18.9 %attend.2.refs_0_ = f32[8,192,128]{2,1,0:T(8,128)S(1)} custom-call(s32[1]{0:T(128)} %bitcast.5.chip_ref, s32[16]{0:T(128)S(1)} %select_n.117.t_ref, f32[16,2,1,128]{3,2,1,0:T(1,128)S(1)} %get-tuple-element.116.sc_ref, f32[2,128,128]{2,1,0:T(8,128)S(1)} %get-tuple-element.114.w_ref, bf16[3,192,256]{2,1,0:T(8,128)(2,1)S(1)} %copy-done.10, ...), custom_call_target="tpu_custom_call" | custom-call | flops 4831838208 | bytes 3145728 | tf_op jit(solution)/shard_map/attend/pallas_call | solution.py:258
  131.4 20.6 %attend.3 = bf16[8,224,128]{2,1,0:T(8,128)(2,1)} custom-call(s32[1]{0:T(128)} %bitcast.5.chip_ref, s32[16]{0:T(128)S(1)} %select_n.117.t_ref, f32[16,2,1,128]{3,2,1,0:T(1,128)S(1)} %get-tuple-element.117.sc_ref, f32[2,128,128]{2,1,0:T(8,128)S(1)} %get-tuple-element.115.w_ref, f32[8,192,128]{2,1,0:T(8,128)S(1)} %copy-done.22, ...), custom_call_target="tpu_custom_call" | custom-call | flops 4831838208 | bytes 3145728 | tf_op jit(solution)/shard_map/attend/pallas_call | solution.py:258
  152.0 19.4 %all-to-all-start.1 = ((bf16[8,224,128]{2,1,0:T(8,128)(2,1)}), bf16[8,224,128]{2,1,0:T(8,128)(2,1)S(1)}, u32[]{:S(2)}, u32[]{:S(2)}) async-start(bf16[8,224,128]{2,1,0:T(8,128)(2,1)} %attend.3), calls=%async_computation.1 | async-start | bytes 917504 | tf_op jit(solution)/shard_map/all_to_all | solution.py:772
  173.9 3.0 %fusion.21 = (bf16[3,4,4,16,384]{4,3,2,1,0:T(8,128)(2,1)}, bf16[3,4,4,16,384]{4,3,2,1,0:T(8,128)(2,1)}, bf16[3,4,4,16,384]{4,3,2,1,0:T(8,128)(2,1)}, bf16[3,4,4,16,384]{4,3,2,1,0:T(8,128)(2,1)}) fusion(bf16[3,3,3,16,384]{4,3,2,1,0:T(8,128)(2,1)} %bitcast.43), kind=kLoop, calls=%fused_computation.59 | loop fusion | bytes 2691072 | tf_op jit(solution)/shard_map/jit(_pad)/pad | solution.py:576
  177.9 6.9 %all-to-all-done.1.part_ref = bf16[8,224,128]{2,1,0:T(8,128)(2,1)S(1)} async-done(((bf16[8,224,128]{2,1,0:T(8,128)(2,1)}), bf16[8,224,128]{2,1,0:T(8,128)(2,1)S(1)}, u32[]{:S(2)}, u32[]{:S(2)}) %all-to-all-start.1) | async-done | bytes 458784 | tf_op jit(solution)/shard_map/all_to_all | solution.py:772
  184.8 3.6 %latent.1 = (f32[192,64]{1,0:T(8,128)S(1)}, bf16[192,256]{1,0:T(8,128)(2,1)S(1)}, bf16[192,256]{1,0:T(8,128)(2,1)S(1)}, bf16[192,256]{1,0:T(8,128)(2,1)}) custom-call(s32[2]{0:T(128)S(1)} %pad_add_fusion.1.flag_ref, f32[4]{0:T(128)S(1)} %get-tuple-element.106.dt_ref, bf16[8,224,128]{2,1,0:T(8,128)(2,1)S(1)} %all-to-all-done.1.part_ref, ...), custom_call_target="tpu_custom_call" | custom-call | tf_op jit(solution)/shard_map/latent/pallas_call | solution.py:385
  189.7 1.8 pad_maximum_fusion.w1_ref
  191.6 1.9 copy-done.1
  194.4 16.1 %decode.1 = (bf16[768,384]{1,0:T(8,128)(2,1)}, f32[16,2,768]{2,1,0:T(2,128)S(1)}) custom-call(s32[1]{0:T(128)} %bitcast.13.lead_ref, bf16[192,256]{1,0:T(8,128)(2,1)S(1)} %copy-done.3, bf16[192,256]{1,0:T(8,128)(2,1)} %collective-permute-done.31.near_ref, bf16[192,256]{1,0:T(8,128)(2,1)S(1)} %get-tuple-element.84.own_ref, ...), custom_call_target="tpu_custom_call" | custom-call | tf_op jit(solution)/shard_map/decode/pallas_call | solution.py:589
  211.2 3.9 %all-to-all-start.2 = ((f32[16,2,768]{2,1,0:T(2,128)}), f32[16,2,768]{2,1,0:T(2,128)S(1)}, u32[]{:S(2)}, u32[]{:S(2)}) async-start(f32[16,2,768]{2,1,0:T(2,128)} %copy-done.5), calls=%async_computation.2 | async-start | bytes 196608 | tf_op jit(solution)/shard_map/all_to_all | solution.py:803
  215.6 1.6 copy.39
  217.2 5.2 %all-to-all-done.2.got_ref = f32[16,2,768]{2,1,0:T(2,128)S(1)} async-done(((f32[16,2,768]{2,1,0:T(2,128)}), f32[16,2,768]{2,1,0:T(2,128)S(1)}, u32[]{:S(2)}, u32[]{:S(2)}) %all-to-all-start.2) | async-done | bytes 98336 | tf_op jit(solution)/shard_map/all_to_all | solution.py:803
  223.0 1.8 rate.1
  (150 shorter events, 36.5 us)
Async XLA Ops:
  6.4 79.2 %all-to-all-start = ((f32[16,1,768]{2,1,0:T(1,128)}), f32[16,1,768]{2,1,0:T(1,128)S(1)}, u32[]{:S(2)}, u32[]{:S(2)}) async-start(f32[16,1,768]{2,1,0:T(1,128)} %broadcast_in_dim.28), calls=%async_computation | async-start | bytes 98304 | tf_op jit(solution)/shard_map/all_to_all | solution.py:739
  13.8 17.4 %collective-permute-start.15 = (f32[64,192]{1,0:T(8,128)}, f32[64,192]{1,0:T(8,128)S(1)}, u32[]{:S(2)}, u32[]{:S(2)}) collective-permute-start(f32[64,192]{1,0:T(8,128)} %bitcast.31), channel_id=1, source_target_pairs={{0,2},{1,3},{2,4},{3,5},{4,6},{5,7},{6,8},{7,9},{8,10},{9,11},{10,... | collective-permute-start | bytes 147464 | tf_op jit(solution)/shard_map/ppermute | solution.py:31
  19.5 37.2 %collective-permute-start.2 = (bf16[3,192,256]{2,1,0:T(8,128)(2,1)}, bf16[3,192,256]{2,1,0:T(8,128)(2,1)S(1)}, u32[]{:S(2)}, u32[]{:S(2)}) collective-permute-start(bf16[3,192,256]{2,1,0:T(8,128)(2,1)} %get-tuple-element.50), channel_id=1, source_target_pairs={{0,6},{1,7},{2,8},{3,9},{4,10},{5,11},{6,12},{7,13},{8,14},{9,15},... | collective-permute-start | bytes 884744 | tf_op jit(solution)/shard_map/ppermute | solution.py:31
  21.9 34.8 %collective-permute-start.3 = (bf16[3,192,256]{2,1,0:T(8,128)(2,1)}, bf16[3,192,256]{2,1,0:T(8,128)(2,1)S(1)}, u32[]{:S(2)}, u32[]{:S(2)}) collective-permute-start(bf16[3,192,256]{2,1,0:T(8,128)(2,1)} %get-tuple-element.51), channel_id=1, source_target_pairs={{0,8},{1,9},{2,10},{3,11},{4,12},{5,13},{6,14},{7,15},{8,0},{9,1},... | collective-permute-start | bytes 884744 | tf_op jit(solution)/shard_map/ppermute | solution.py:31
  26.7 31.3 %collective-permute-start = (bf16[3,192,256]{2,1,0:T(8,128)(2,1)}, bf16[3,192,256]{2,1,0:T(8,128)(2,1)S(1)}, u32[]{:S(2)}, u32[]{:S(2)}) collective-permute-start(bf16[3,192,256]{2,1,0:T(8,128)(2,1)} %get-tuple-element.48), channel_id=1, source_target_pairs={{0,2},{1,3},{2,4},{3,5},{4,6},{5,7},{6,8},{7,9},{8,10},{9,11},{10,... | collective-permute-start | bytes 884744 | tf_op jit(solution)/shard_map/ppermute | solution.py:31
  27.7 30.3 %collective-permute-start.1 = (bf16[3,192,256]{2,1,0:T(8,128)(2,1)}, bf16[3,192,256]{2,1,0:T(8,128)(2,1)S(1)}, u32[]{:S(2)}, u32[]{:S(2)}) collective-permute-start(bf16[3,192,256]{2,1,0:T(8,128)(2,1)} %get-tuple-element.49), channel_id=1, source_target_pairs={{0,4},{1,5},{2,6},{3,7},{4,8},{5,9},{6,10},{7,11},{8,12},{9,13},{1... | collective-permute-start | bytes 884744 | tf_op jit(solution)/shard_map/ppermute | solution.py:31
  31.2 35.3 %collective-permute-start.4 = (bf16[3,192,256]{2,1,0:T(8,128)(2,1)}, bf16[3,192,256]{2,1,0:T(8,128)(2,1)S(1)}, u32[]{:S(2)}, u32[]{:S(2)}) collective-permute-start(bf16[3,192,256]{2,1,0:T(8,128)(2,1)} %get-tuple-element.52), channel_id=1, source_target_pairs={{0,10},{1,11},{2,12},{3,13},{4,14},{5,15},{6,0},{7,1},{8,2},{9,3},... | collective-permute-start | bytes 884744 | tf_op jit(solution)/shard_map/ppermute | solution.py:31
  56.7 12.6 %collective-permute-start.5 = (bf16[3,192,256]{2,1,0:T(8,128)(2,1)}, bf16[3,192,256]{2,1,0:T(8,128)(2,1)}, u32[]{:S(2)}, u32[]{:S(2)}) collective-permute-start(bf16[3,192,256]{2,1,0:T(8,128)(2,1)} %get-tuple-element.53), channel_id=1, source_target_pairs={{0,12},{1,13},{2,14},{3,15},{4,0},{5,1},{6,2},{7,3},{8,4},{9,5},{1... | collective-permute-start | bytes 884744 | tf_op jit(solution)/shard_map/ppermute | solution.py:31
  56.7 14.3 %collective-permute-start.6 = (bf16[3,192,256]{2,1,0:T(8,128)(2,1)}, bf16[3,192,256]{2,1,0:T(8,128)(2,1)}, u32[]{:S(2)}, u32[]{:S(2)}) collective-permute-start(bf16[3,192,256]{2,1,0:T(8,128)(2,1)} %get-tuple-element.54), channel_id=1, source_target_pairs={{0,14},{1,15},{2,0},{3,1},{4,2},{5,3},{6,4},{7,5},{8,6},{9,7},{10,... | collective-permute-start | bytes 884744 | tf_op jit(solution)/shard_map/ppermute | solution.py:31
  57.9 18.7 %collective-permute-start.7 = (bf16[3,192,256]{2,1,0:T(8,128)(2,1)}, bf16[3,192,256]{2,1,0:T(8,128)(2,1)S(1)}, u32[]{:S(2)}, u32[]{:S(2)}) collective-permute-start(bf16[3,192,256]{2,1,0:T(8,128)(2,1)} %get-tuple-element.47.refs_0_), channel_id=1, source_target_pairs={{0,1},{1,0},{2,3},{3,2},{4,5},{5,4},{6,7},{7,6},{8,9},{9,8},{10,11... | collective-permute-start | bytes 884744 | tf_op jit(solution)/shard_map/ppermute | solution.py:36
  58.0 25.4 %collective-permute-start.10 = (bf16[3,192,256]{2,1,0:T(8,128)(2,1)S(1)}, bf16[3,192,256]{2,1,0:T(8,128)(2,1)}, u32[]{:S(2)}, u32[]{:S(2)}) collective-permute-start(bf16[3,192,256]{2,1,0:T(8,128)(2,1)S(1)} %collective-permute-done.2.refs_3_), channel_id=1, source_target_pairs={{0,1},{1,0},{2,3},{3,2},{4,5},{5,4},{6,7},{7,6},{8,9},{9,8},{10,11... | collective-permute-start | bytes 884744 | tf_op jit(solution)/shard_map/ppermute | solution.py:36
  66.6 17.4 %collective-permute-start.11 = (bf16[3,192,256]{2,1,0:T(8,128)(2,1)S(1)}, bf16[3,192,256]{2,1,0:T(8,128)(2,1)}, u32[]{:S(2)}, u32[]{:S(2)}) collective-permute-start(bf16[3,192,256]{2,1,0:T(8,128)(2,1)S(1)} %collective-permute-done.3.refs_4_), channel_id=1, source_target_pairs={{0,1},{1,0},{2,3},{3,2},{4,5},{5,4},{6,7},{7,6},{8,9},{9,8},{10,11... | collective-permute-start | bytes 884744 | tf_op jit(solution)/shard_map/ppermute | solution.py:36
  69.3 14.7 %collective-permute-start.8 = (bf16[3,192,256]{2,1,0:T(8,128)(2,1)S(1)}, bf16[3,192,256]{2,1,0:T(8,128)(2,1)}, u32[]{:S(2)}, u32[]{:S(2)}) collective-permute-start(bf16[3,192,256]{2,1,0:T(8,128)(2,1)S(1)} %collective-permute-done.refs_1_), channel_id=1, source_target_pairs={{0,1},{1,0},{2,3},{3,2},{4,5},{5,4},{6,7},{7,6},{8,9},{9,8},{10,11... | collective-permute-start | bytes 884744 | tf_op jit(solution)/shard_map/ppermute | solution.py:36
  71.0 13.5 %collective-permute-start.9 = (bf16[3,192,256]{2,1,0:T(8,128)(2,1)S(1)}, bf16[3,192,256]{2,1,0:T(8,128)(2,1)}, u32[]{:S(2)}, u32[]{:S(2)}) collective-permute-start(bf16[3,192,256]{2,1,0:T(8,128)(2,1)S(1)} %collective-permute-done.1.refs_2_), channel_id=1, source_target_pairs={{0,1},{1,0},{2,3},{3,2},{4,5},{5,4},{6,7},{7,6},{8,9},{9,8},{10,11... | collective-permute-start | bytes 884744 | tf_op jit(solution)/shard_map/ppermute | solution.py:36
  77.3 15.6 %collective-permute-start.16 = (bf16[3,192,256]{2,1,0:T(8,128)(2,1)}, bf16[3,192,256]{2,1,0:T(8,128)(2,1)S(1)}, u32[]{:S(2)}, u32[]{:S(2)}) collective-permute-start(bf16[3,192,256]{2,1,0:T(8,128)(2,1)} %get-tuple-element.64), channel_id=1, source_target_pairs={{0,2},{1,3},{2,4},{3,5},{4,6},{5,7},{6,8},{7,9},{8,10},{9,11},{10,... | collective-permute-start | bytes 884744 | tf_op jit(solution)/shard_map/ppermute | solution.py:31
  83.4 12.1 %collective-permute-start.17 = (bf16[3,192,256]{2,1,0:T(8,128)(2,1)}, bf16[3,192,256]{2,1,0:T(8,128)(2,1)}, u32[]{:S(2)}, u32[]{:S(2)}) collective-permute-start(bf16[3,192,256]{2,1,0:T(8,128)(2,1)} %get-tuple-element.65), channel_id=1, source_target_pairs={{0,4},{1,5},{2,6},{3,7},{4,8},{5,9},{6,10},{7,11},{8,12},{9,13},{1... | collective-permute-start | bytes 884744 | tf_op jit(solution)/shard_map/ppermute | solution.py:31
  84.0 2.2 collective-permute-start.12
  84.0 3.2 %collective-permute-start.13 = (bf16[3,192,256]{2,1,0:T(8,128)(2,1)}, bf16[3,192,256]{2,1,0:T(8,128)(2,1)}, u32[]{:S(2)}, u32[]{:S(2)}) collective-permute-start(bf16[3,192,256]{2,1,0:T(8,128)(2,1)} %collective-permute-done.5.refs_6_), channel_id=1, source_target_pairs={{0,1},{1,0},{2,3},{3,2},{4,5},{5,4},{6,7},{7,6},{8,9},{9,8},{10,11... | collective-permute-start | bytes 884744 | tf_op jit(solution)/shard_map/ppermute | solution.py:36
  84.5 5.1 %collective-permute-start.14 = (bf16[3,192,256]{2,1,0:T(8,128)(2,1)}, bf16[3,192,256]{2,1,0:T(8,128)(2,1)}, u32[]{:S(2)}, u32[]{:S(2)}) collective-permute-start(bf16[3,192,256]{2,1,0:T(8,128)(2,1)} %collective-permute-done.6.refs_7_), channel_id=1, source_target_pairs={{0,1},{1,0},{2,3},{3,2},{4,5},{5,4},{6,7},{7,6},{8,9},{9,8},{10,11... | collective-permute-start | bytes 884744 | tf_op jit(solution)/shard_map/ppermute | solution.py:36
  86.2 35.2 %collective-permute-start.18 = (bf16[3,192,256]{2,1,0:T(8,128)(2,1)}, bf16[3,192,256]{2,1,0:T(8,128)(2,1)}, u32[]{:S(2)}, u32[]{:S(2)}) collective-permute-start(bf16[3,192,256]{2,1,0:T(8,128)(2,1)} %get-tuple-element.66), channel_id=1, source_target_pairs={{0,6},{1,7},{2,8},{3,9},{4,10},{5,11},{6,12},{7,13},{8,14},{9,15},... | collective-permute-start | bytes 884744 | tf_op jit(solution)/shard_map/ppermute | solution.py:31
  87.2 34.2 %collective-permute-start.19 = (bf16[3,192,256]{2,1,0:T(8,128)(2,1)}, bf16[3,192,256]{2,1,0:T(8,128)(2,1)}, u32[]{:S(2)}, u32[]{:S(2)}) collective-permute-start(bf16[3,192,256]{2,1,0:T(8,128)(2,1)} %get-tuple-element.67), channel_id=1, source_target_pairs={{0,8},{1,9},{2,10},{3,11},{4,12},{5,13},{6,14},{7,15},{8,0},{9,1},... | collective-permute-start | bytes 884744 | tf_op jit(solution)/shard_map/ppermute | solution.py:31
  89.6 31.9 %collective-permute-start.20 = (bf16[3,192,256]{2,1,0:T(8,128)(2,1)}, bf16[3,192,256]{2,1,0:T(8,128)(2,1)S(1)}, u32[]{:S(2)}, u32[]{:S(2)}) collective-permute-start(bf16[3,192,256]{2,1,0:T(8,128)(2,1)} %get-tuple-element.68), channel_id=1, source_target_pairs={{0,10},{1,11},{2,12},{3,13},{4,14},{5,15},{6,0},{7,1},{8,2},{9,3},... | collective-permute-start | bytes 884744 | tf_op jit(solution)/shard_map/ppermute | solution.py:31
  92.9 28.6 %collective-permute-start.21 = (bf16[3,192,256]{2,1,0:T(8,128)(2,1)}, bf16[3,192,256]{2,1,0:T(8,128)(2,1)S(1)}, u32[]{:S(2)}, u32[]{:S(2)}) collective-permute-start(bf16[3,192,256]{2,1,0:T(8,128)(2,1)} %get-tuple-element.69), channel_id=1, source_target_pairs={{0,12},{1,13},{2,14},{3,15},{4,0},{5,1},{6,2},{7,3},{8,4},{9,5},{1... | collective-permute-start | bytes 884744 | tf_op jit(solution)/shard_map/ppermute | solution.py:31
  95.5 27.1 %collective-permute-start.22 = (bf16[3,192,256]{2,1,0:T(8,128)(2,1)}, bf16[3,192,256]{2,1,0:T(8,128)(2,1)S(1)}, u32[]{:S(2)}, u32[]{:S(2)}) collective-permute-start(bf16[3,192,256]{2,1,0:T(8,128)(2,1)} %get-tuple-element.70), channel_id=1, source_target_pairs={{0,14},{1,15},{2,0},{3,1},{4,2},{5,3},{6,4},{7,5},{8,6},{9,7},{10,... | collective-permute-start | bytes 884744 | tf_op jit(solution)/shard_map/ppermute | solution.py:31
  122.6 2.0 collective-permute-start.24
  123.4 2.1 collective-permute-start.26
  123.9 2.0 collective-permute-start.27
  124.2 2.3 %collective-permute-start.28 = (bf16[3,192,256]{2,1,0:T(8,128)(2,1)}, bf16[3,192,256]{2,1,0:T(8,128)(2,1)}, u32[]{:S(2)}, u32[]{:S(2)}) collective-permute-start(bf16[3,192,256]{2,1,0:T(8,128)(2,1)} %copy-done.13), channel_id=1, source_target_pairs={{0,1},{1,0},{2,3},{3,2},{4,5},{5,4},{6,7},{7,6},{8,9},{9,8},{10,11... | collective-permute-start | bytes 884744 | tf_op jit(solution)/shard_map/ppermute | solution.py:36
  124.6 2.3 %collective-permute-start.29 = (bf16[3,192,256]{2,1,0:T(8,128)(2,1)}, bf16[3,192,256]{2,1,0:T(8,128)(2,1)}, u32[]{:S(2)}, u32[]{:S(2)}) collective-permute-start(bf16[3,192,256]{2,1,0:T(8,128)(2,1)} %copy-done.17), channel_id=1, source_target_pairs={{0,1},{1,0},{2,3},{3,2},{4,5},{5,4},{6,7},{7,6},{8,9},{9,8},{10,11... | collective-permute-start | bytes 884744 | tf_op jit(solution)/shard_map/ppermute | solution.py:36
  125.1 2.2 collective-permute-start.30
  152.0 32.9 %all-to-all-start.1 = ((bf16[8,224,128]{2,1,0:T(8,128)(2,1)}), bf16[8,224,128]{2,1,0:T(8,128)(2,1)S(1)}, u32[]{:S(2)}, u32[]{:S(2)}) async-start(bf16[8,224,128]{2,1,0:T(8,128)(2,1)} %attend.3), calls=%async_computation.1 | async-start | bytes 917504 | tf_op jit(solution)/shard_map/all_to_all | solution.py:772
  211.2 11.2 %all-to-all-start.2 = ((f32[16,2,768]{2,1,0:T(2,128)}), f32[16,2,768]{2,1,0:T(2,128)S(1)}, u32[]{:S(2)}, u32[]{:S(2)}) async-start(f32[16,2,768]{2,1,0:T(2,128)} %copy-done.5), calls=%async_computation.2 | async-start | bytes 196608 | tf_op jit(solution)/shard_map/all_to_all | solution.py:803
  (35 other events, 425.7 us)

commit v7 on v6

--- a/solution.py
+++ b/solution.py
@@ -36,12 +36,14 @@
     return lax.ppermute(value, axis, [(i, i ^ 1) for i in range(count)])
 
 
-def pack_kernel(blocks, at_ref, k_hbm, v_hbm, q_hbm, *refs):
+def pack_kernel(turns, chips, cols, first, chip_ref, k_hbm, v_hbm, q_hbm, *refs):
+    blocks = len(turns)
     out_refs, (buf, in_sem, out_sem) = refs[:blocks], refs[blocks:]
     width = buf.shape[3]
     gets = []
     for n in range(blocks):
-        at = pl.multiple_of(at_ref[n], HD)
+        owner = lax.rem(chip_ref[0] + turns[n], chips)
+        at = pl.multiple_of(owner * cols + first, HD)
         gets.append(
             [
                 pltpu.make_async_copy(src.at[:, pl.ds(at, width)], buf.at[n, i], in_sem.at[n, i])
@@ -61,10 +63,11 @@
         put.wait()
 
 
-def pack(keys, values, queries, starts, width):
-    rows, blocks = keys.shape[0], starts.shape[0]
+def pack(keys, values, queries, chip, turns, chips, first, width):
+    rows, blocks = keys.shape[0], len(turns)
+    cols = keys.shape[1] // chips
     return pl.pallas_call(
-        functools.partial(pack_kernel, blocks),
+        functools.partial(pack_kernel, tuple(turns), chips, cols, first),
         out_shape=[jax.ShapeDtypeStruct((3, rows, width), jnp.bfloat16)] * blocks,
         in_specs=[SM, ANY, ANY, ANY],
         out_specs=[ANY] * blocks,
@@ -74,7 +77,7 @@
             pltpu.SemaphoreType.DMA((blocks,)),
         ],
         name="pack",
-    )(starts, keys, values, queries)
+    )(chip, keys, values, queries)
 
 
 def attend_kernel(blocks, heads, frames, earlier, last, chip_ref, t_ref, sc_ref, w_ref, *refs):
@@ -622,7 +625,9 @@
 
 
 def rate_kernel(frames, slot_ref, text_ref, got_ref, vec_ref, score_ref):
-    text = text_ref[...]
+    text = text_ref[0]
+    for n in range(1, text_ref.shape[0]):
+        text = text + text_ref[n]
     text_rms = jnp.sqrt(jnp.mean(text * text) + 1e-06)
     for f in range(frames):
         slot = slot_ref[f]
@@ -688,10 +693,12 @@
     order = sorted(range(1, chips), key=lambda t: abs(2 * t - chips))
 
     def packed(first, count, turns):
-        at = ((chip + jnp.asarray(turns, jnp.int32)) % chips) * cols + first * HD
-        blocks = pack(keys, values, queries, at.astype(jnp.int32), count * HD)
+        blocks = pack(
+            keys, values, queries, chip_at, turns, chips, first * HD, count * HD
+        )
         return dict(zip(turns, blocks))
 
+    chip_at = chip.astype(jnp.int32).reshape(1)
     early = order[:2]
     blocks = packed(firsts[0], phases[0], early)
     blocks |= packed(firsts[0], phases[0], [t for t in range(chips) if t not in early])
@@ -737,7 +744,6 @@
     )
     words = jnp.broadcast_to(prepared["text"][None], (devices, 1, TEXT_W))
     words = lax.all_to_all(words, "seq", split_axis=0, concat_axis=0, tiled=True)
-    words = jnp.sum(words, axis=0)
     far_latent = rotate(latent_in.T, "seq", 1)
     steps = prepared["steps"]
     phase_blocks = [got]

time: 226 us -> 220 us (0.973)
  local copies, waits for them, and re-layouts: 26.8 us -> 23.5 us
  other arithmetic: 5.01 us -> 2.71 us
    unnamed x66 -> x58, local copies, waits for them, and re-layouts: 15.8 us -> 13 us
  transfers between devices with their start and end apart: 35 -> 35, of which waited for: 17 -> 17; matrix products, arithmetic and copies ran while one was open for 8% -> 7% of each run, Pallas kernels for 12% -> 12%
where the time goes in v7:
time: 220 us; the launch traced here: 219 us
  Pallas kernels  72.7 us (33%)
  starting transfers between devices  64.3 us (29%)
  waiting for transfers between devices  53.2 us (24%)
  local copies, waits for them, and re-layouts  23.5 us (11%)
  other arithmetic  2.71 us (1%)
    pallas_call x2, Pallas kernels, attend(): pl.pallas_call(functools.partial(attend_kernel, blocks, heads, frames, le...  39.6 us
    ppermute x15, waiting for transfers between devices, rotate(): lax.ppermute(value, axis, [(i, (i + 2 * steps) % count) for i in range(co...  37.8 us
    ppermute x15, starting transfers between devices, rotate(): lax.ppermute(value, axis, [(i, (i + 2 * steps) % count) for i in range(co...  30.7 us
    all_to_all x1, starting transfers between devices, local(): lax.all_to_all(shares, 'seq', split_axis=0, concat_axis=0, axis_index_gro...  19.2 us
    pallas_call x1, Pallas kernels, decode(): pl.pallas_call(functools.partial(decode_kernel, frames), out_shape=[jax.S...  16.1 us
    unnamed x58, local copies, waits for them, and re-layouts  13 us
    all_to_all x1, starting transfers between devices, local(): lax.all_to_all(words, 'seq', split_axis=0, concat_axis=0, tiled=True)  7.41 us
    pallas_call x3, Pallas kernels, pack(): pl.pallas_call(functools.partial(pack_kernel, tuple(turns), chips, cols,...  7.18 us
  transfers between devices with their start and end apart: 35, of which 17 were waited for; matrix products, arithmetic and copies ran while one was open for 7% of the time, Pallas kernels for 12%

profile of v7, /device:TPU:0, one launch (start us, length us, event | category | flops | bytes accessed | tf_op | source)
XLA Modules:
  0.0 218.6 jit_solution(13542195607486411520)
XLA Ops:
  0.7 4.3 %text.1 = f32[1,768]{1,0:T(1,128)} custom-call(s32[1]{0:T(128)} %bitcast.9.at_ref, s32[77]{0:T(128)} %id_ref.1, bf16[48,24704]{1,0:T(8,128)(2,1)} %bitcast.36), custom_call_target="tpu_custom_call" | custom-call | tf_op jit(solution)/shard_map/text/pallas_call | solution.py:433
  6.4 7.4 %all-to-all-start = ((f32[16,1,768]{2,1,0:T(1,128)}), f32[16,1,768]{2,1,0:T(1,128)S(1)}, u32[]{:S(2)}, u32[]{:S(2)}) async-start(f32[16,1,768]{2,1,0:T(1,128)} %broadcast_in_dim.28), calls=%async_computation | async-start | bytes 98304 | tf_op jit(solution)/shard_map/all_to_all | solution.py:746
  13.8 1.9 collective-permute-start.15
  15.7 1.9 pack.4
  17.6 2.4 %collective-permute-start.2 = (bf16[3,192,256]{2,1,0:T(8,128)(2,1)}, bf16[3,192,256]{2,1,0:T(8,128)(2,1)S(1)}, u32[]{:S(2)}, u32[]{:S(2)}) collective-permute-start(bf16[3,192,256]{2,1,0:T(8,128)(2,1)} %get-tuple-element.50), channel_id=1, source_target_pairs={{0,6},{1,7},{2,8},{3,9},{4,10},{5,11},{6,12},{7,13},{8,14},{9,15},... | collective-permute-start | bytes 884744 | tf_op jit(solution)/shard_map/ppermute | solution.py:31
  21.1 2.5 %pack.3 = (bf16[3,192,256]{2,1,0:T(8,128)(2,1)}, bf16[3,192,256]{2,1,0:T(8,128)(2,1)}, bf16[3,192,256]{2,1,0:T(8,128)(2,1)}, bf16[3,192,256]{2,1,0:T(8,128)(2,1)...) custom-call(s32[1]{0:T(128)} %bitcast.5.chip_ref, bf16[192,4096]{1,0:T(8,128)(2,1)} %k_hbm.5, ...), custom_call_target="tpu_custom_call" | custom-call | tf_op jit(solution)/shard_map/pack/pallas_call | solution.py:69
  24.6 1.5 collective-permute-start.1
  26.1 1.4 fusion.13
  27.5 2.9 %collective-permute-start.4 = (bf16[3,192,256]{2,1,0:T(8,128)(2,1)}, bf16[3,192,256]{2,1,0:T(8,128)(2,1)S(1)}, u32[]{:S(2)}, u32[]{:S(2)}) collective-permute-start(bf16[3,192,256]{2,1,0:T(8,128)(2,1)} %get-tuple-element.52), channel_id=1, source_target_pairs={{0,10},{1,11},{2,12},{3,13},{4,14},{5,15},{6,0},{7,1},{8,2},{9,3},... | collective-permute-start | bytes 884744 | tf_op jit(solution)/shard_map/ppermute | solution.py:31
  30.4 24.4 %collective-permute-done.2.refs_3_ = bf16[3,192,256]{2,1,0:T(8,128)(2,1)S(1)} collective-permute-done((bf16[3,192,256]{2,1,0:T(8,128)(2,1)}, bf16[3,192,256]{2,1,0:T(8,128)(2,1)S(1)}, u32[]{:S(2)}, u32[]{:S(2)}) %collective-permute-start.2) | collective-permute-done | bytes 294944 | tf_op jit(solution)/shard_map/ppermute | solution.py:31
  57.1 4.0 %collective-permute-done.4.refs_5_ = bf16[3,192,256]{2,1,0:T(8,128)(2,1)S(1)} collective-permute-done((bf16[3,192,256]{2,1,0:T(8,128)(2,1)}, bf16[3,192,256]{2,1,0:T(8,128)(2,1)S(1)}, u32[]{:S(2)}, u32[]{:S(2)}) %collective-permute-start.4) | collective-permute-done | bytes 294944 | tf_op jit(solution)/shard_map/ppermute | solution.py:31
  61.1 6.3 %collective-permute-done.5.refs_6_ = bf16[3,192,256]{2,1,0:T(8,128)(2,1)S(1)} collective-permute-done((bf16[3,192,256]{2,1,0:T(8,128)(2,1)}, bf16[3,192,256]{2,1,0:T(8,128)(2,1)S(1)}, u32[]{:S(2)}, u32[]{:S(2)}) %collective-permute-start.5) | collective-permute-done | bytes 294944 | tf_op jit(solution)/shard_map/ppermute | solution.py:31
  68.0 2.8 %pack.5 = (bf16[3,192,256]{2,1,0:T(8,128)(2,1)}, bf16[3,192,256]{2,1,0:T(8,128)(2,1)}, bf16[3,192,256]{2,1,0:T(8,128)(2,1)}, bf16[3,192,256]{2,1,0:T(8,128)(2,1)...) custom-call(s32[1]{0:T(128)} %bitcast.5.chip_ref, ...), custom_call_target="tpu_custom_call" | custom-call | tf_op jit(solution)/shard_map/pack/pallas_call | solution.py:69
  72.7 7.3 %collective-permute-start.16 = (bf16[3,192,256]{2,1,0:T(8,128)(2,1)}, bf16[3,192,256]{2,1,0:T(8,128)(2,1)S(1)}, u32[]{:S(2)}, u32[]{:S(2)}) collective-permute-start(bf16[3,192,256]{2,1,0:T(8,128)(2,1)} %get-tuple-element.64), channel_id=1, source_target_pairs={{0,2},{1,3},{2,4},{3,5},{4,6},{5,7},{6,8},{7,9},{8,10},{9,11},{10,... | collective-permute-start | bytes 884744 | tf_op jit(solution)/shard_map/ppermute | solution.py:31
  83.5 2.2 %collective-permute-start.19 = (bf16[3,192,256]{2,1,0:T(8,128)(2,1)}, bf16[3,192,256]{2,1,0:T(8,128)(2,1)}, u32[]{:S(2)}, u32[]{:S(2)}) collective-permute-start(bf16[3,192,256]{2,1,0:T(8,128)(2,1)} %get-tuple-element.67), channel_id=1, source_target_pairs={{0,8},{1,9},{2,10},{3,11},{4,12},{5,13},{6,14},{7,15},{8,0},{9,1},... | collective-permute-start | bytes 884744 | tf_op jit(solution)/shard_map/ppermute | solution.py:31
  85.8 2.4 %collective-permute-start.20 = (bf16[3,192,256]{2,1,0:T(8,128)(2,1)}, bf16[3,192,256]{2,1,0:T(8,128)(2,1)}, u32[]{:S(2)}, u32[]{:S(2)}) collective-permute-start(bf16[3,192,256]{2,1,0:T(8,128)(2,1)} %get-tuple-element.68), channel_id=1, source_target_pairs={{0,10},{1,11},{2,12},{3,13},{4,14},{5,15},{6,0},{7,1},{8,2},{9,3},... | collective-permute-start | bytes 884744 | tf_op jit(solution)/shard_map/ppermute | solution.py:31
  88.2 1.5 collective-permute-done.16.refs_2_
  90.6 1.5 collective-permute-done.17.refs_3_
  92.1 4.3 %collective-permute-start.22 = (bf16[3,192,256]{2,1,0:T(8,128)(2,1)}, bf16[3,192,256]{2,1,0:T(8,128)(2,1)}, u32[]{:S(2)}, u32[]{:S(2)}) collective-permute-start(bf16[3,192,256]{2,1,0:T(8,128)(2,1)} %get-tuple-element.70), channel_id=1, source_target_pairs={{0,14},{1,15},{2,0},{3,1},{4,2},{5,3},{6,4},{7,5},{8,6},{9,7},{10,... | collective-permute-start | bytes 884744 | tf_op jit(solution)/shard_map/ppermute | solution.py:31
  99.2 18.9 %attend.2.refs_0_ = f32[8,192,128]{2,1,0:T(8,128)S(1)} custom-call(s32[1]{0:T(128)} %bitcast.5.chip_ref, s32[16]{0:T(128)S(1)} %select_n.101.t_ref, f32[16,2,1,128]{3,2,1,0:T(1,128)S(1)} %get-tuple-element.108.sc_ref, f32[2,128,128]{2,1,0:T(8,128)S(1)} %get-tuple-element.106.w_ref, bf16[3,192,256]{2,1,0:T(8,128)(2,1)S(1)} %copy-done.10, ...), custom_call_target="tpu_custom_call" | custom-call | flops 4831838208 | bytes 3145728 | tf_op jit(solution)/shard_map/attend/pallas_call | solution.py:261
  125.1 20.7 %attend.3 = bf16[8,224,128]{2,1,0:T(8,128)(2,1)} custom-call(s32[1]{0:T(128)} %bitcast.5.chip_ref, s32[16]{0:T(128)S(1)} %select_n.101.t_ref, f32[16,2,1,128]{3,2,1,0:T(1,128)S(1)} %get-tuple-element.109.sc_ref, f32[2,128,128]{2,1,0:T(8,128)S(1)} %get-tuple-element.107.w_ref, f32[8,192,128]{2,1,0:T(8,128)S(1)} %copy-done.18, ...), custom_call_target="tpu_custom_call" | custom-call | flops 4831838208 | bytes 3145728 | tf_op jit(solution)/shard_map/attend/pallas_call | solution.py:261
  145.8 19.2 %all-to-all-start.1 = ((bf16[8,224,128]{2,1,0:T(8,128)(2,1)}), bf16[8,224,128]{2,1,0:T(8,128)(2,1)S(1)}, u32[]{:S(2)}, u32[]{:S(2)}) async-start(bf16[8,224,128]{2,1,0:T(8,128)(2,1)} %attend.3), calls=%async_computation.1 | async-start | bytes 917504 | tf_op jit(solution)/shard_map/all_to_all | solution.py:778
  167.6 3.0 %fusion.14 = (bf16[3,4,4,16,384]{4,3,2,1,0:T(8,128)(2,1)}, bf16[3,4,4,16,384]{4,3,2,1,0:T(8,128)(2,1)}, bf16[3,4,4,16,384]{4,3,2,1,0:T(8,128)(2,1)}, bf16[3,4,4,16,384]{4,3,2,1,0:T(8,128)(2,1)}) fusion(bf16[3,3,3,16,384]{4,3,2,1,0:T(8,128)(2,1)} %bitcast.43), kind=kLoop, calls=%fused_computation.43 | loop fusion | bytes 2691072 | tf_op jit(solution)/shard_map/jit(_pad)/pad | solution.py:579
  171.6 6.9 %all-to-all-done.1.part_ref = bf16[8,224,128]{2,1,0:T(8,128)(2,1)S(1)} async-done(((bf16[8,224,128]{2,1,0:T(8,128)(2,1)}), bf16[8,224,128]{2,1,0:T(8,128)(2,1)S(1)}, u32[]{:S(2)}, u32[]{:S(2)}) %all-to-all-start.1) | async-done | bytes 458784 | tf_op jit(solution)/shard_map/all_to_all | solution.py:778
  178.4 3.6 %latent.1 = (f32[192,64]{1,0:T(8,128)S(1)}, bf16[192,256]{1,0:T(8,128)(2,1)S(1)}, bf16[192,256]{1,0:T(8,128)(2,1)S(1)}, bf16[192,256]{1,0:T(8,128)(2,1)}) custom-call(s32[2]{0:T(128)S(1)} %pad_add_fusion.1.flag_ref, f32[4]{0:T(128)S(1)} %get-tuple-element.98.dt_ref, bf16[8,224,128]{2,1,0:T(8,128)(2,1)S(1)} %all-to-all-done.1.part_ref, ...), custom_call_target="tpu_custom_call" | custom-call | tf_op jit(solution)/shard_map/latent/pallas_call | solution.py:388
  183.3 1.8 pad_maximum_fusion.w1_ref
  185.2 1.9 copy-done.1
  187.9 16.1 %decode.1 = (bf16[768,384]{1,0:T(8,128)(2,1)}, f32[16,2,768]{2,1,0:T(2,128)S(1)}) custom-call(s32[1]{0:T(128)} %bitcast.13.lead_ref, bf16[192,256]{1,0:T(8,128)(2,1)S(1)} %copy-done.3, bf16[192,256]{1,0:T(8,128)(2,1)} %collective-permute-done.31.near_ref, bf16[192,256]{1,0:T(8,128)(2,1)S(1)} %get-tuple-element.84.own_ref, ...), custom_call_target="tpu_custom_call" | custom-call | tf_op jit(solution)/shard_map/decode/pallas_call | solution.py:592
  204.8 3.9 %all-to-all-start.2 = ((f32[16,2,768]{2,1,0:T(2,128)}), f32[16,2,768]{2,1,0:T(2,128)S(1)}, u32[]{:S(2)}, u32[]{:S(2)}) async-start(f32[16,2,768]{2,1,0:T(2,128)} %copy-done.5), calls=%async_computation.2 | async-start | bytes 196608 | tf_op jit(solution)/shard_map/all_to_all | solution.py:809
  209.3 1.6 copy.29
  210.9 5.1 %all-to-all-done.2.got_ref = f32[16,2,768]{2,1,0:T(2,128)S(1)} async-done(((f32[16,2,768]{2,1,0:T(2,128)}), f32[16,2,768]{2,1,0:T(2,128)S(1)}, u32[]{:S(2)}, u32[]{:S(2)}) %all-to-all-start.2) | async-done | bytes 98336 | tf_op jit(solution)/shard_map/all_to_all | solution.py:809
  216.6 1.8 rate.1
  (137 shorter events, 30.1 us)
Async XLA Ops:
  6.4 112.7 %all-to-all-start = ((f32[16,1,768]{2,1,0:T(1,128)}), f32[16,1,768]{2,1,0:T(1,128)S(1)}, u32[]{:S(2)}, u32[]{:S(2)}) async-start(f32[16,1,768]{2,1,0:T(1,128)} %broadcast_in_dim.28), calls=%async_computation | async-start | bytes 98304 | tf_op jit(solution)/shard_map/all_to_all | solution.py:746
  13.8 13.8 %collective-permute-start.15 = (f32[64,192]{1,0:T(8,128)}, f32[64,192]{1,0:T(8,128)S(1)}, u32[]{:S(2)}, u32[]{:S(2)}) collective-permute-start(f32[64,192]{1,0:T(8,128)} %bitcast.31), channel_id=1, source_target_pairs={{0,2},{1,3},{2,4},{3,5},{4,6},{5,7},{6,8},{7,9},{8,10},{9,11},{10,... | collective-permute-start | bytes 147464 | tf_op jit(solution)/shard_map/ppermute | solution.py:31
  17.6 37.2 %collective-permute-start.2 = (bf16[3,192,256]{2,1,0:T(8,128)(2,1)}, bf16[3,192,256]{2,1,0:T(8,128)(2,1)S(1)}, u32[]{:S(2)}, u32[]{:S(2)}) collective-permute-start(bf16[3,192,256]{2,1,0:T(8,128)(2,1)} %get-tuple-element.50), channel_id=1, source_target_pairs={{0,6},{1,7},{2,8},{3,9},{4,10},{5,11},{6,12},{7,13},{8,14},{9,15},... | collective-permute-start | bytes 884744 | tf_op jit(solution)/shard_map/ppermute | solution.py:31
  20.1 34.8 %collective-permute-start.3 = (bf16[3,192,256]{2,1,0:T(8,128)(2,1)}, bf16[3,192,256]{2,1,0:T(8,128)(2,1)S(1)}, u32[]{:S(2)}, u32[]{:S(2)}) collective-permute-start(bf16[3,192,256]{2,1,0:T(8,128)(2,1)} %get-tuple-element.51), channel_id=1, source_target_pairs={{0,8},{1,9},{2,10},{3,11},{4,12},{5,13},{6,14},{7,15},{8,0},{9,1},... | collective-permute-start | bytes 884744 | tf_op jit(solution)/shard_map/ppermute | solution.py:31
  23.6 32.9 %collective-permute-start = (bf16[3,192,256]{2,1,0:T(8,128)(2,1)}, bf16[3,192,256]{2,1,0:T(8,128)(2,1)S(1)}, u32[]{:S(2)}, u32[]{:S(2)}) collective-permute-start(bf16[3,192,256]{2,1,0:T(8,128)(2,1)} %get-tuple-element.48), channel_id=1, source_target_pairs={{0,2},{1,3},{2,4},{3,5},{4,6},{5,7},{6,8},{7,9},{8,10},{9,11},{10,... | collective-permute-start | bytes 884744 | tf_op jit(solution)/shard_map/ppermute | solution.py:31
  24.6 32.0 %collective-permute-start.1 = (bf16[3,192,256]{2,1,0:T(8,128)(2,1)}, bf16[3,192,256]{2,1,0:T(8,128)(2,1)S(1)}, u32[]{:S(2)}, u32[]{:S(2)}) collective-permute-start(bf16[3,192,256]{2,1,0:T(8,128)(2,1)} %get-tuple-element.49), channel_id=1, source_target_pairs={{0,4},{1,5},{2,6},{3,7},{4,8},{5,9},{6,10},{7,11},{8,12},{9,13},{1... | collective-permute-start | bytes 884744 | tf_op jit(solution)/shard_map/ppermute | solution.py:31
  27.5 33.5 %collective-permute-start.4 = (bf16[3,192,256]{2,1,0:T(8,128)(2,1)}, bf16[3,192,256]{2,1,0:T(8,128)(2,1)S(1)}, u32[]{:S(2)}, u32[]{:S(2)}) collective-permute-start(bf16[3,192,256]{2,1,0:T(8,128)(2,1)} %get-tuple-element.52), channel_id=1, source_target_pairs={{0,10},{1,11},{2,12},{3,13},{4,14},{5,15},{6,0},{7,1},{8,2},{9,3},... | collective-permute-start | bytes 884744 | tf_op jit(solution)/shard_map/ppermute | solution.py:31
  54.8 12.5 %collective-permute-start.5 = (bf16[3,192,256]{2,1,0:T(8,128)(2,1)}, bf16[3,192,256]{2,1,0:T(8,128)(2,1)S(1)}, u32[]{:S(2)}, u32[]{:S(2)}) collective-permute-start(bf16[3,192,256]{2,1,0:T(8,128)(2,1)} %get-tuple-element.53), channel_id=1, source_target_pairs={{0,12},{1,13},{2,14},{3,15},{4,0},{5,1},{6,2},{7,3},{8,4},{9,5},{1... | collective-permute-start | bytes 884744 | tf_op jit(solution)/shard_map/ppermute | solution.py:31
  54.8 12.6 %collective-permute-start.6 = (bf16[3,192,256]{2,1,0:T(8,128)(2,1)}, bf16[3,192,256]{2,1,0:T(8,128)(2,1)}, u32[]{:S(2)}, u32[]{:S(2)}) collective-permute-start(bf16[3,192,256]{2,1,0:T(8,128)(2,1)} %get-tuple-element.54), channel_id=1, source_target_pairs={{0,14},{1,15},{2,0},{3,1},{4,2},{5,3},{6,4},{7,5},{8,6},{9,7},{10,... | collective-permute-start | bytes 884744 | tf_op jit(solution)/shard_map/ppermute | solution.py:31
  56.5 16.2 %collective-permute-start.7 = (bf16[3,192,256]{2,1,0:T(8,128)(2,1)}, bf16[3,192,256]{2,1,0:T(8,128)(2,1)}, u32[]{:S(2)}, u32[]{:S(2)}) collective-permute-start(bf16[3,192,256]{2,1,0:T(8,128)(2,1)} %get-tuple-element.47.refs_0_), channel_id=1, source_target_pairs={{0,1},{1,0},{2,3},{3,2},{4,5},{5,4},{6,7},{7,6},{8,9},{9,8},{10,11... | collective-permute-start | bytes 884744 | tf_op jit(solution)/shard_map/ppermute | solution.py:36
  56.6 23.5 %collective-permute-start.10 = (bf16[3,192,256]{2,1,0:T(8,128)(2,1)S(1)}, bf16[3,192,256]{2,1,0:T(8,128)(2,1)}, u32[]{:S(2)}, u32[]{:S(2)}) collective-permute-start(bf16[3,192,256]{2,1,0:T(8,128)(2,1)S(1)} %collective-permute-done.2.refs_3_), channel_id=1, source_target_pairs={{0,1},{1,0},{2,3},{3,2},{4,5},{5,4},{6,7},{7,6},{8,9},{9,8},{10,11... | collective-permute-start | bytes 884744 | tf_op jit(solution)/shard_map/ppermute | solution.py:36
  61.1 19.7 %collective-permute-start.11 = (bf16[3,192,256]{2,1,0:T(8,128)(2,1)S(1)}, bf16[3,192,256]{2,1,0:T(8,128)(2,1)}, u32[]{:S(2)}, u32[]{:S(2)}) collective-permute-start(bf16[3,192,256]{2,1,0:T(8,128)(2,1)S(1)} %collective-permute-done.3.refs_4_), channel_id=1, source_target_pairs={{0,1},{1,0},{2,3},{3,2},{4,5},{5,4},{6,7},{7,6},{8,9},{9,8},{10,11... | collective-permute-start | bytes 884744 | tf_op jit(solution)/shard_map/ppermute | solution.py:36
  67.4 13.3 %collective-permute-start.8 = (bf16[3,192,256]{2,1,0:T(8,128)(2,1)S(1)}, bf16[3,192,256]{2,1,0:T(8,128)(2,1)}, u32[]{:S(2)}, u32[]{:S(2)}) collective-permute-start(bf16[3,192,256]{2,1,0:T(8,128)(2,1)S(1)} %collective-permute-done.refs_1_), channel_id=1, source_target_pairs={{0,1},{1,0},{2,3},{3,2},{4,5},{5,4},{6,7},{7,6},{8,9},{9,8},{10,11... | collective-permute-start | bytes 884744 | tf_op jit(solution)/shard_map/ppermute | solution.py:36
  67.4 13.8 %collective-permute-start.9 = (bf16[3,192,256]{2,1,0:T(8,128)(2,1)S(1)}, bf16[3,192,256]{2,1,0:T(8,128)(2,1)}, u32[]{:S(2)}, u32[]{:S(2)}) collective-permute-start(bf16[3,192,256]{2,1,0:T(8,128)(2,1)S(1)} %collective-permute-done.1.refs_2_), channel_id=1, source_target_pairs={{0,1},{1,0},{2,3},{3,2},{4,5},{5,4},{6,7},{7,6},{8,9},{9,8},{10,11... | collective-permute-start | bytes 884744 | tf_op jit(solution)/shard_map/ppermute | solution.py:36
  72.7 17.0 %collective-permute-start.16 = (bf16[3,192,256]{2,1,0:T(8,128)(2,1)}, bf16[3,192,256]{2,1,0:T(8,128)(2,1)S(1)}, u32[]{:S(2)}, u32[]{:S(2)}) collective-permute-start(bf16[3,192,256]{2,1,0:T(8,128)(2,1)} %get-tuple-element.64), channel_id=1, source_target_pairs={{0,2},{1,3},{2,4},{3,5},{4,6},{5,7},{6,8},{7,9},{8,10},{9,11},{10,... | collective-permute-start | bytes 884744 | tf_op jit(solution)/shard_map/ppermute | solution.py:31
  80.1 12.0 %collective-permute-start.17 = (bf16[3,192,256]{2,1,0:T(8,128)(2,1)}, bf16[3,192,256]{2,1,0:T(8,128)(2,1)S(1)}, u32[]{:S(2)}, u32[]{:S(2)}) collective-permute-start(bf16[3,192,256]{2,1,0:T(8,128)(2,1)} %get-tuple-element.65), channel_id=1, source_target_pairs={{0,4},{1,5},{2,6},{3,7},{4,8},{5,9},{6,10},{7,11},{8,12},{9,13},{1... | collective-permute-start | bytes 884744 | tf_op jit(solution)/shard_map/ppermute | solution.py:31
  80.7 2.8 %collective-permute-start.13 = (bf16[3,192,256]{2,1,0:T(8,128)(2,1)}, bf16[3,192,256]{2,1,0:T(8,128)(2,1)S(1)}, u32[]{:S(2)}, u32[]{:S(2)}) collective-permute-start(bf16[3,192,256]{2,1,0:T(8,128)(2,1)} %copy-done.15), channel_id=1, source_target_pairs={{0,1},{1,0},{2,3},{3,2},{4,5},{5,4},{6,7},{7,6},{8,9},{9,8},{10,11... | collective-permute-start | bytes 884744 | tf_op jit(solution)/shard_map/ppermute | solution.py:36
  81.2 4.6 %collective-permute-start.14 = (bf16[3,192,256]{2,1,0:T(8,128)(2,1)}, bf16[3,192,256]{2,1,0:T(8,128)(2,1)S(1)}, u32[]{:S(2)}, u32[]{:S(2)}) collective-permute-start(bf16[3,192,256]{2,1,0:T(8,128)(2,1)} %collective-permute-done.6.refs_7_), channel_id=1, source_target_pairs={{0,1},{1,0},{2,3},{3,2},{4,5},{5,4},{6,7},{7,6},{8,9},{9,8},{10,11... | collective-permute-start | bytes 884744 | tf_op jit(solution)/shard_map/ppermute | solution.py:36
  82.5 36.6 %collective-permute-start.18 = (bf16[3,192,256]{2,1,0:T(8,128)(2,1)}, bf16[3,192,256]{2,1,0:T(8,128)(2,1)}, u32[]{:S(2)}, u32[]{:S(2)}) collective-permute-start(bf16[3,192,256]{2,1,0:T(8,128)(2,1)} %get-tuple-element.66), channel_id=1, source_target_pairs={{0,6},{1,7},{2,8},{3,9},{4,10},{5,11},{6,12},{7,13},{8,14},{9,15},... | collective-permute-start | bytes 884744 | tf_op jit(solution)/shard_map/ppermute | solution.py:31
  83.5 35.5 %collective-permute-start.19 = (bf16[3,192,256]{2,1,0:T(8,128)(2,1)}, bf16[3,192,256]{2,1,0:T(8,128)(2,1)}, u32[]{:S(2)}, u32[]{:S(2)}) collective-permute-start(bf16[3,192,256]{2,1,0:T(8,128)(2,1)} %get-tuple-element.67), channel_id=1, source_target_pairs={{0,8},{1,9},{2,10},{3,11},{4,12},{5,13},{6,14},{7,15},{8,0},{9,1},... | collective-permute-start | bytes 884744 | tf_op jit(solution)/shard_map/ppermute | solution.py:31
  85.8 33.3 %collective-permute-start.20 = (bf16[3,192,256]{2,1,0:T(8,128)(2,1)}, bf16[3,192,256]{2,1,0:T(8,128)(2,1)}, u32[]{:S(2)}, u32[]{:S(2)}) collective-permute-start(bf16[3,192,256]{2,1,0:T(8,128)(2,1)} %get-tuple-element.68), channel_id=1, source_target_pairs={{0,10},{1,11},{2,12},{3,13},{4,14},{5,15},{6,0},{7,1},{8,2},{9,3},... | collective-permute-start | bytes 884744 | tf_op jit(solution)/shard_map/ppermute | solution.py:31
  89.7 29.4 %collective-permute-start.21 = (bf16[3,192,256]{2,1,0:T(8,128)(2,1)}, bf16[3,192,256]{2,1,0:T(8,128)(2,1)}, u32[]{:S(2)}, u32[]{:S(2)}) collective-permute-start(bf16[3,192,256]{2,1,0:T(8,128)(2,1)} %get-tuple-element.69), channel_id=1, source_target_pairs={{0,12},{1,13},{2,14},{3,15},{4,0},{5,1},{6,2},{7,3},{8,4},{9,5},{1... | collective-permute-start | bytes 884744 | tf_op jit(solution)/shard_map/ppermute | solution.py:31
  92.1 27.2 %collective-permute-start.22 = (bf16[3,192,256]{2,1,0:T(8,128)(2,1)}, bf16[3,192,256]{2,1,0:T(8,128)(2,1)}, u32[]{:S(2)}, u32[]{:S(2)}) collective-permute-start(bf16[3,192,256]{2,1,0:T(8,128)(2,1)} %get-tuple-element.70), channel_id=1, source_target_pairs={{0,14},{1,15},{2,0},{3,1},{4,2},{5,3},{6,4},{7,5},{8,6},{9,7},{10,... | collective-permute-start | bytes 884744 | tf_op jit(solution)/shard_map/ppermute | solution.py:31
  119.3 2.0 collective-permute-start.24
  119.8 1.9 collective-permute-start.25
  119.9 2.3 %collective-permute-start.26 = (bf16[3,192,256]{2,1,0:T(8,128)(2,1)}, bf16[3,192,256]{2,1,0:T(8,128)(2,1)S(1)}, u32[]{:S(2)}, u32[]{:S(2)}) collective-permute-start(bf16[3,192,256]{2,1,0:T(8,128)(2,1)} %collective-permute-done.18.refs_4_), channel_id=1, source_target_pairs={{0,1},{1,0},{2,3},{3,2},{4,5},{5,4},{6,7},{7,6},{8,9},{9,8},{10,11... | collective-permute-start | bytes 884744 | tf_op jit(solution)/shard_map/ppermute | solution.py:36
  120.4 2.3 %collective-permute-start.27 = (bf16[3,192,256]{2,1,0:T(8,128)(2,1)}, bf16[3,192,256]{2,1,0:T(8,128)(2,1)}, u32[]{:S(2)}, u32[]{:S(2)}) collective-permute-start(bf16[3,192,256]{2,1,0:T(8,128)(2,1)} %collective-permute-done.19.refs_5_), channel_id=1, source_target_pairs={{0,1},{1,0},{2,3},{3,2},{4,5},{5,4},{6,7},{7,6},{8,9},{9,8},{10,11... | collective-permute-start | bytes 884744 | tf_op jit(solution)/shard_map/ppermute | solution.py:36
  120.9 2.2 %collective-permute-start.28 = (bf16[3,192,256]{2,1,0:T(8,128)(2,1)}, bf16[3,192,256]{2,1,0:T(8,128)(2,1)}, u32[]{:S(2)}, u32[]{:S(2)}) collective-permute-start(bf16[3,192,256]{2,1,0:T(8,128)(2,1)} %collective-permute-done.20.refs_6_), channel_id=1, source_target_pairs={{0,1},{1,0},{2,3},{3,2},{4,5},{5,4},{6,7},{7,6},{8,9},{9,8},{10,11... | collective-permute-start | bytes 884744 | tf_op jit(solution)/shard_map/ppermute | solution.py:36
  121.3 2.2 %collective-permute-start.29 = (bf16[3,192,256]{2,1,0:T(8,128)(2,1)}, bf16[3,192,256]{2,1,0:T(8,128)(2,1)}, u32[]{:S(2)}, u32[]{:S(2)}) collective-permute-start(bf16[3,192,256]{2,1,0:T(8,128)(2,1)} %collective-permute-done.21.refs_7_), channel_id=1, source_target_pairs={{0,1},{1,0},{2,3},{3,2},{4,5},{5,4},{6,7},{7,6},{8,9},{9,8},{10,11... | collective-permute-start | bytes 884744 | tf_op jit(solution)/shard_map/ppermute | solution.py:36
  121.7 2.2 %collective-permute-start.30 = (bf16[3,192,256]{2,1,0:T(8,128)(2,1)}, bf16[3,192,256]{2,1,0:T(8,128)(2,1)}, u32[]{:S(2)}, u32[]{:S(2)}) collective-permute-start(bf16[3,192,256]{2,1,0:T(8,128)(2,1)} %collective-permute-done.22.refs_8_), channel_id=1, source_target_pairs={{0,1},{1,0},{2,3},{3,2},{4,5},{5,4},{6,7},{7,6},{8,9},{9,8},{10,11... | collective-permute-start | bytes 884744 | tf_op jit(solution)/shard_map/ppermute | solution.py:36
  145.8 32.6 %all-to-all-start.1 = ((bf16[8,224,128]{2,1,0:T(8,128)(2,1)}), bf16[8,224,128]{2,1,0:T(8,128)(2,1)S(1)}, u32[]{:S(2)}, u32[]{:S(2)}) async-start(bf16[8,224,128]{2,1,0:T(8,128)(2,1)} %attend.3), calls=%async_computation.1 | async-start | bytes 917504 | tf_op jit(solution)/shard_map/all_to_all | solution.py:778
  204.8 11.2 %all-to-all-start.2 = ((f32[16,2,768]{2,1,0:T(2,128)}), f32[16,2,768]{2,1,0:T(2,128)S(1)}, u32[]{:S(2)}, u32[]{:S(2)}) async-start(f32[16,2,768]{2,1,0:T(2,128)} %copy-done.5), calls=%async_computation.2 | async-start | bytes 196608 | tf_op jit(solution)/shard_map/all_to_all | solution.py:809
  (31 other events, 451.0 us)

commit v8 on v7

--- a/solution.py
+++ b/solution.py
@@ -757,9 +757,8 @@
     sums = []
     for n, got in enumerate(phase_blocks):
         if n:
-            sums[-1], words, far_latent, *got = lax.optimization_barrier(
-                (sums[-1], words, far_latent, *got)
-            )
+            words, far_latent, _ = lax.optimization_barrier((words, far_latent, sums[-1]))
+            got = [lax.optimization_barrier((block, sums[-1]))[0] for block in got]
         other = [swap_core(block, "seq") for block in got]
         last = n + 1 == len(phase_blocks)
         shares = attend(

time: 220 us -> 224 us (1.018)
  waiting for transfers between devices: 53.2 us -> 41.9 us
  local copies, waits for them, and re-layouts: 23.5 us -> 31.3 us
  starting transfers between devices: 64.3 us -> 71.2 us
    all_to_all x1, starting transfers between devices: 7.41 us -> 22.3 us  [local(): lax.all_to_all(words, 'seq', split_axis=0, concat_axis=0, tiled=True)]
    all_to_all x1, starting transfers between devices: 19.2 us -> 5.77 us  [local(): lax.all_to_all(shares, 'seq', split_axis=0, concat_axis=0, axis_index_gro...]
    ppermute x15, waiting for transfers between devices: 37.8 us -> 30 us  [rotate(): lax.ppermute(value, axis, [(i, (i + 2 * steps) % count) for i in range(co...]
    unnamed x58 -> x72, local copies, waits for them, and re-layouts: 13 us -> 19.4 us
    ppermute x15, starting transfers between devices: 30.7 us -> 35.6 us  [rotate(): lax.ppermute(value, axis, [(i, (i + 2 * steps) % count) for i in range(co...]
    ppermute x17, waiting for transfers between devices: 3.42 us -> 0.04 us  [swap_core(): return lax.ppermute(value, axis, [(i, i ^ 1) for i in range(count)])]
  transfers between devices with their start and end apart: 35 -> 35, of which waited for: 17 -> 7; matrix products, arithmetic and copies ran while one was open for 7% -> 8% of each run, Pallas kernels for 12% -> 22%
where the time goes in v8:
time: 224 us; the launch traced here: 222 us
  Pallas kernels  73 us (33%)
  starting transfers between devices  71.2 us (32%)
  waiting for transfers between devices  41.9 us (19%)
  local copies, waits for them, and re-layouts  31.3 us (14%)
  other arithmetic  2.72 us (1%)
    pallas_call x2, Pallas kernels, attend(): pl.pallas_call(functools.partial(attend_kernel, blocks, heads, frames, le...  39.8 us
    ppermute x15, starting transfers between devices, rotate(): lax.ppermute(value, axis, [(i, (i + 2 * steps) % count) for i in range(co...  35.6 us
    ppermute x15, waiting for transfers between devices, rotate(): lax.ppermute(value, axis, [(i, (i + 2 * steps) % count) for i in range(co...  30 us
    all_to_all x1, starting transfers between devices, local(): lax.all_to_all(words, 'seq', split_axis=0, concat_axis=0, tiled=True)  22.3 us
    unnamed x72, local copies, waits for them, and re-layouts  19.4 us
    pallas_call x1, Pallas kernels, decode(): pl.pallas_call(functools.partial(decode_kernel, frames), out_shape=[jax.S...  16.4 us
    pallas_call x3, Pallas kernels, pack(): pl.pallas_call(functools.partial(pack_kernel, tuple(turns), chips, cols,...  7.27 us
    all_to_all x1, waiting for transfers between devices, local(): lax.all_to_all(shares, 'seq', split_axis=0, concat_axis=0, axis_index_gro...  6.84 us
  transfers between devices with their start and end apart: 35, of which 7 were waited for; matrix products, arithmetic and copies ran while one was open for 8% of the time, Pallas kernels for 22%

profile of v8, /device:TPU:0, one launch (start us, length us, event | category | flops | bytes accessed | tf_op | source)
XLA Modules:
  0.0 222.3 jit_solution(3753867241597631520)
XLA Ops:
  0.7 2.0 pack.4
  2.7 4.1 %collective-permute-start.2 = (bf16[3,192,256]{2,1,0:T(8,128)(2,1)}, bf16[3,192,256]{2,1,0:T(8,128)(2,1)S(1)}, u32[]{:S(2)}, u32[]{:S(2)}) collective-permute-start(bf16[3,192,256]{2,1,0:T(8,128)(2,1)} %get-tuple-element.49), channel_id=1, source_target_pairs={{0,6},{1,7},{2,8},{3,9},{4,10},{5,11},{6,12},{7,13},{8,14},{9,15},... | collective-permute-start | bytes 884744 | tf_op jit(solution)/shard_map/ppermute | solution.py:31
  6.7 2.6 %collective-permute-start.3 = (bf16[3,192,256]{2,1,0:T(8,128)(2,1)}, bf16[3,192,256]{2,1,0:T(8,128)(2,1)S(1)}, u32[]{:S(2)}, u32[]{:S(2)}) collective-permute-start(bf16[3,192,256]{2,1,0:T(8,128)(2,1)} %get-tuple-element.50), channel_id=1, source_target_pairs={{0,8},{1,9},{2,10},{3,11},{4,12},{5,13},{6,14},{7,15},{8,0},{9,1},... | collective-permute-start | bytes 884744 | tf_op jit(solution)/shard_map/ppermute | solution.py:31
  9.3 2.5 %pack.3 = (bf16[3,192,256]{2,1,0:T(8,128)(2,1)}, bf16[3,192,256]{2,1,0:T(8,128)(2,1)}, bf16[3,192,256]{2,1,0:T(8,128)(2,1)}, bf16[3,192,256]{2,1,0:T(8,128)(2,1)...) custom-call(s32[1]{0:T(128)} %bitcast.5.chip_ref, bf16[192,4096]{1,0:T(8,128)(2,1)} %k_hbm.5, ...), custom_call_target="tpu_custom_call" | custom-call | tf_op jit(solution)/shard_map/pack/pallas_call | solution.py:69
  12.7 4.4 %collective-permute-start.4 = (bf16[3,192,256]{2,1,0:T(8,128)(2,1)}, bf16[3,192,256]{2,1,0:T(8,128)(2,1)S(1)}, u32[]{:S(2)}, u32[]{:S(2)}) collective-permute-start(bf16[3,192,256]{2,1,0:T(8,128)(2,1)} %get-tuple-element.51), channel_id=1, source_target_pairs={{0,10},{1,11},{2,12},{3,13},{4,14},{5,15},{6,0},{7,1},{8,2},{9,3},... | collective-permute-start | bytes 884744 | tf_op jit(solution)/shard_map/ppermute | solution.py:31
  17.2 2.7 %fusion.13 = (f32[16,1,4096]{2,1,0:T(1,128)}, f32[16,1,4096]{2,1,0:T(1,128)}) fusion(f32[16,2,4096]{2,1,0:T(2,128)} %param.24), kind=kLoop, calls=%fused_computation.42 | loop fusion | bytes 1048576 | tf_op jit(solution)/shard_map/slice | solution.py:720
  20.6 20.6 %collective-permute-done.2.refs_3_ = bf16[3,192,256]{2,1,0:T(8,128)(2,1)S(1)} collective-permute-done((bf16[3,192,256]{2,1,0:T(8,128)(2,1)}, bf16[3,192,256]{2,1,0:T(8,128)(2,1)S(1)}, u32[]{:S(2)}, u32[]{:S(2)}) %collective-permute-start.2) | collective-permute-done | bytes 294944 | tf_op jit(solution)/shard_map/ppermute | solution.py:31
  42.9 2.8 %pack.5 = (bf16[3,192,256]{2,1,0:T(8,128)(2,1)}, bf16[3,192,256]{2,1,0:T(8,128)(2,1)}, bf16[3,192,256]{2,1,0:T(8,128)(2,1)}, bf16[3,192,256]{2,1,0:T(8,128)(2,1)...) custom-call(s32[1]{0:T(128)} %bitcast.5.chip_ref, ...), custom_call_target="tpu_custom_call" | custom-call | tf_op jit(solution)/shard_map/pack/pallas_call | solution.py:69
  47.7 6.2 %collective-permute-done.5.refs_6_ = bf16[3,192,256]{2,1,0:T(8,128)(2,1)S(1)} collective-permute-done((bf16[3,192,256]{2,1,0:T(8,128)(2,1)}, bf16[3,192,256]{2,1,0:T(8,128)(2,1)S(1)}, u32[]{:S(2)}, u32[]{:S(2)}) %collective-permute-start.5) | collective-permute-done | bytes 294944 | tf_op jit(solution)/shard_map/ppermute | solution.py:31
  56.5 7.8 %collective-permute-start.15 = (bf16[3,192,256]{2,1,0:T(8,128)(2,1)}, bf16[3,192,256]{2,1,0:T(8,128)(2,1)S(1)}, u32[]{:S(2)}, u32[]{:S(2)}) collective-permute-start(bf16[3,192,256]{2,1,0:T(8,128)(2,1)} %get-tuple-element.64), channel_id=1, source_target_pairs={{0,2},{1,3},{2,4},{3,5},{4,6},{5,7},{6,8},{7,9},{8,10},{9,11},{10,... | collective-permute-start | bytes 884744 | tf_op jit(solution)/shard_map/ppermute | solution.py:31
  64.3 4.4 %collective-permute-start.16 = (bf16[3,192,256]{2,1,0:T(8,128)(2,1)}, bf16[3,192,256]{2,1,0:T(8,128)(2,1)S(1)}, u32[]{:S(2)}, u32[]{:S(2)}) collective-permute-start(bf16[3,192,256]{2,1,0:T(8,128)(2,1)} %get-tuple-element.66), channel_id=1, source_target_pairs={{0,4},{1,5},{2,6},{3,7},{4,8},{5,9},{6,10},{7,11},{8,12},{9,13},{1... | collective-permute-start | bytes 884744 | tf_op jit(solution)/shard_map/ppermute | solution.py:31
  68.7 1.9 collective-permute-start.17
  70.6 1.9 collective-permute-start.18
  72.5 3.3 %collective-permute-start.19 = (bf16[3,192,256]{2,1,0:T(8,128)(2,1)}, bf16[3,192,256]{2,1,0:T(8,128)(2,1)S(1)}, u32[]{:S(2)}, u32[]{:S(2)}) collective-permute-start(bf16[3,192,256]{2,1,0:T(8,128)(2,1)} %get-tuple-element.72), channel_id=1, source_target_pairs={{0,10},{1,11},{2,12},{3,13},{4,14},{5,15},{6,0},{7,1},{8,2},{9,3},... | collective-permute-start | bytes 884744 | tf_op jit(solution)/shard_map/ppermute | solution.py:31
  79.6 19.0 %attend.2.refs_0_ = f32[8,192,128]{2,1,0:T(8,128)S(1)} custom-call(s32[1]{0:T(128)} %bitcast.5.chip_ref, s32[16]{0:T(128)S(1)} %select_n.101.t_ref, f32[16,2,1,128]{3,2,1,0:T(1,128)S(1)} %get-tuple-element.106.sc_ref, f32[2,128,128]{2,1,0:T(8,128)S(1)} %get-tuple-element.104.w_ref, bf16[3,192,256]{2,1,0:T(8,128)(2,1)S(1)} %copy-done.10, ...), custom_call_target="tpu_custom_call" | custom-call | flops 4831838208 | bytes 3145728 | tf_op jit(solution)/shard_map/attend/pallas_call | solution.py:261
  99.5 1.5 collective-permute-start.20
  101.0 2.8 %collective-permute-done.17.refs_4_ = bf16[3,192,256]{2,1,0:T(8,128)(2,1)S(1)} collective-permute-done((bf16[3,192,256]{2,1,0:T(8,128)(2,1)}, bf16[3,192,256]{2,1,0:T(8,128)(2,1)S(1)}, u32[]{:S(2)}, u32[]{:S(2)}) %collective-permute-start.17) | collective-permute-done | bytes 294944 | tf_op jit(solution)/shard_map/ppermute | solution.py:31
  105.7 4.2 %text.1 = f32[1,768]{1,0:T(1,128)} custom-call(s32[1]{0:T(128)} %bitcast.10.at_ref, s32[77]{0:T(128)} %id_ref.1, bf16[48,24704]{1,0:T(8,128)(2,1)} %bitcast.36), custom_call_target="tpu_custom_call" | custom-call | tf_op jit(solution)/shard_map/text/pallas_call | solution.py:433
  111.3 22.3 %all-to-all-start.1 = ((f32[16,1,768]{2,1,0:T(1,128)}), f32[16,1,768]{2,1,0:T(1,128)S(1)}, u32[]{:S(2)}, u32[]{:S(2)}) async-start(f32[16,1,768]{2,1,0:T(1,128)} %broadcast_in_dim.28), calls=%async_computation.1 | async-start | bytes 98304 | tf_op jit(solution)/shard_map/all_to_all | solution.py:746
  136.0 1.9 collective-permute-start.30
  141.9 20.8 %attend.3 = bf16[8,224,128]{2,1,0:T(8,128)(2,1)} custom-call(s32[1]{0:T(128)} %bitcast.5.chip_ref, s32[16]{0:T(128)S(1)} %select_n.101.t_ref, f32[16,2,1,128]{3,2,1,0:T(1,128)S(1)} %get-tuple-element.107.sc_ref, f32[2,128,128]{2,1,0:T(8,128)S(1)} %get-tuple-element.105.w_ref, f32[8,192,128]{2,1,0:T(8,128)S(1)} %copy-done.26, ...), custom_call_target="tpu_custom_call" | custom-call | flops 4831838208 | bytes 3145728 | tf_op jit(solution)/shard_map/attend/pallas_call | solution.py:261
  162.7 5.8 %all-to-all-start = ((bf16[8,224,128]{2,1,0:T(8,128)(2,1)}), bf16[8,224,128]{2,1,0:T(8,128)(2,1)S(1)}, u32[]{:S(2)}, u32[]{:S(2)}) async-start(bf16[8,224,128]{2,1,0:T(8,128)(2,1)} %attend.3), calls=%async_computation | async-start | bytes 917504 | tf_op jit(solution)/shard_map/all_to_all | solution.py:777
  170.9 3.0 %fusion.14 = (bf16[3,4,4,16,384]{4,3,2,1,0:T(8,128)(2,1)}, bf16[3,4,4,16,384]{4,3,2,1,0:T(8,128)(2,1)}, bf16[3,4,4,16,384]{4,3,2,1,0:T(8,128)(2,1)}, bf16[3,4,4,16,384]{4,3,2,1,0:T(8,128)(2,1)}) fusion(bf16[3,3,3,16,384]{4,3,2,1,0:T(8,128)(2,1)} %bitcast.43), kind=kLoop, calls=%fused_computation.43 | loop fusion | bytes 2691072 | tf_op jit(solution)/shard_map/jit(_pad)/pad | solution.py:579
  175.0 6.8 %all-to-all-done.part_ref = bf16[8,224,128]{2,1,0:T(8,128)(2,1)S(1)} async-done(((bf16[8,224,128]{2,1,0:T(8,128)(2,1)}), bf16[8,224,128]{2,1,0:T(8,128)(2,1)S(1)}, u32[]{:S(2)}, u32[]{:S(2)}) %all-to-all-start) | async-done | bytes 458784 | tf_op jit(solution)/shard_map/all_to_all | solution.py:777
  181.9 3.6 %latent.1 = (f32[192,64]{1,0:T(8,128)S(1)}, bf16[192,256]{1,0:T(8,128)(2,1)S(1)}, bf16[192,256]{1,0:T(8,128)(2,1)S(1)}, bf16[192,256]{1,0:T(8,128)(2,1)}) custom-call(s32[2]{0:T(128)S(1)} %pad_add_fusion.1.flag_ref, f32[4]{0:T(128)S(1)} %get-tuple-element.96.dt_ref, bf16[8,224,128]{2,1,0:T(8,128)(2,1)S(1)} %all-to-all-done.part_ref, f32[64,192]{1,0:T(8,128)S(1)} %bitcast.32, ...), custom_call_target="tpu_custom_call" | custom-call | tf_op jit(solution)/shard_map/latent/pallas_call | solution.py:388
  186.8 1.8 pad_maximum_fusion.w1_ref
  188.7 1.9 copy-done.1
  191.4 16.4 %decode.1 = (bf16[768,384]{1,0:T(8,128)(2,1)}, f32[16,2,768]{2,1,0:T(2,128)S(1)}) custom-call(s32[1]{0:T(128)} %bitcast.13.lead_ref, bf16[192,256]{1,0:T(8,128)(2,1)S(1)} %copy-done.3, bf16[192,256]{1,0:T(8,128)(2,1)} %collective-permute-done.31.near_ref, bf16[192,256]{1,0:T(8,128)(2,1)S(1)} %get-tuple-element.82.own_ref, ...), custom_call_target="tpu_custom_call" | custom-call | tf_op jit(solution)/shard_map/decode/pallas_call | solution.py:592
  208.4 3.9 %all-to-all-start.2 = ((f32[16,2,768]{2,1,0:T(2,128)}), f32[16,2,768]{2,1,0:T(2,128)S(1)}, u32[]{:S(2)}, u32[]{:S(2)}) async-start(f32[16,2,768]{2,1,0:T(2,128)} %copy-done.5), calls=%async_computation.2 | async-start | bytes 196608 | tf_op jit(solution)/shard_map/all_to_all | solution.py:808
  213.0 1.6 copy.29
  214.6 5.1 %all-to-all-done.2.got_ref = f32[16,2,768]{2,1,0:T(2,128)S(1)} async-done(((f32[16,2,768]{2,1,0:T(2,128)}), f32[16,2,768]{2,1,0:T(2,128)S(1)}, u32[]{:S(2)}, u32[]{:S(2)}) %all-to-all-start.2) | async-done | bytes 98336 | tf_op jit(solution)/shard_map/all_to_all | solution.py:808
  220.3 1.8 rate.1
  (151 shorter events, 29.9 us)
Async XLA Ops:
  2.7 38.5 %collective-permute-start.2 = (bf16[3,192,256]{2,1,0:T(8,128)(2,1)}, bf16[3,192,256]{2,1,0:T(8,128)(2,1)S(1)}, u32[]{:S(2)}, u32[]{:S(2)}) collective-permute-start(bf16[3,192,256]{2,1,0:T(8,128)(2,1)} %get-tuple-element.49), channel_id=1, source_target_pairs={{0,6},{1,7},{2,8},{3,9},{4,10},{5,11},{6,12},{7,13},{8,14},{9,15},... | collective-permute-start | bytes 884744 | tf_op jit(solution)/shard_map/ppermute | solution.py:31
  6.7 34.6 %collective-permute-start.3 = (bf16[3,192,256]{2,1,0:T(8,128)(2,1)}, bf16[3,192,256]{2,1,0:T(8,128)(2,1)S(1)}, u32[]{:S(2)}, u32[]{:S(2)}) collective-permute-start(bf16[3,192,256]{2,1,0:T(8,128)(2,1)} %get-tuple-element.50), channel_id=1, source_target_pairs={{0,8},{1,9},{2,10},{3,11},{4,12},{5,13},{6,14},{7,15},{8,0},{9,1},... | collective-permute-start | bytes 884744 | tf_op jit(solution)/shard_map/ppermute | solution.py:31
  11.8 30.5 %collective-permute-start = (bf16[3,192,256]{2,1,0:T(8,128)(2,1)}, bf16[3,192,256]{2,1,0:T(8,128)(2,1)S(1)}, u32[]{:S(2)}, u32[]{:S(2)}) collective-permute-start(bf16[3,192,256]{2,1,0:T(8,128)(2,1)} %get-tuple-element.47), channel_id=1, source_target_pairs={{0,2},{1,3},{2,4},{3,5},{4,6},{5,7},{6,8},{7,9},{8,10},{9,11},{10,... | collective-permute-start | bytes 884744 | tf_op jit(solution)/shard_map/ppermute | solution.py:31
  11.9 30.4 %collective-permute-start.1 = (bf16[3,192,256]{2,1,0:T(8,128)(2,1)}, bf16[3,192,256]{2,1,0:T(8,128)(2,1)S(1)}, u32[]{:S(2)}, u32[]{:S(2)}) collective-permute-start(bf16[3,192,256]{2,1,0:T(8,128)(2,1)} %get-tuple-element.48), channel_id=1, source_target_pairs={{0,4},{1,5},{2,6},{3,7},{4,8},{5,9},{6,10},{7,11},{8,12},{9,13},{1... | collective-permute-start | bytes 884744 | tf_op jit(solution)/shard_map/ppermute | solution.py:31
  12.7 30.1 %collective-permute-start.4 = (bf16[3,192,256]{2,1,0:T(8,128)(2,1)}, bf16[3,192,256]{2,1,0:T(8,128)(2,1)S(1)}, u32[]{:S(2)}, u32[]{:S(2)}) collective-permute-start(bf16[3,192,256]{2,1,0:T(8,128)(2,1)} %get-tuple-element.51), channel_id=1, source_target_pairs={{0,10},{1,11},{2,12},{3,13},{4,14},{5,15},{6,0},{7,1},{8,2},{9,3},... | collective-permute-start | bytes 884744 | tf_op jit(solution)/shard_map/ppermute | solution.py:31
  41.2 12.7 %collective-permute-start.5 = (bf16[3,192,256]{2,1,0:T(8,128)(2,1)}, bf16[3,192,256]{2,1,0:T(8,128)(2,1)S(1)}, u32[]{:S(2)}, u32[]{:S(2)}) collective-permute-start(bf16[3,192,256]{2,1,0:T(8,128)(2,1)} %get-tuple-element.52), channel_id=1, source_target_pairs={{0,12},{1,13},{2,14},{3,15},{4,0},{5,1},{6,2},{7,3},{8,4},{9,5},{1... | collective-permute-start | bytes 884744 | tf_op jit(solution)/shard_map/ppermute | solution.py:31
  41.3 12.7 %collective-permute-start.6 = (bf16[3,192,256]{2,1,0:T(8,128)(2,1)}, bf16[3,192,256]{2,1,0:T(8,128)(2,1)}, u32[]{:S(2)}, u32[]{:S(2)}) collective-permute-start(bf16[3,192,256]{2,1,0:T(8,128)(2,1)} %get-tuple-element.53), channel_id=1, source_target_pairs={{0,14},{1,15},{2,0},{3,1},{4,2},{5,3},{6,4},{7,5},{8,6},{9,7},{10,... | collective-permute-start | bytes 884744 | tf_op jit(solution)/shard_map/ppermute | solution.py:31
  42.3 12.2 %collective-permute-start.7 = (bf16[3,192,256]{2,1,0:T(8,128)(2,1)}, bf16[3,192,256]{2,1,0:T(8,128)(2,1)}, u32[]{:S(2)}, u32[]{:S(2)}) collective-permute-start(bf16[3,192,256]{2,1,0:T(8,128)(2,1)} %get-tuple-element.46.refs_0_), channel_id=1, source_target_pairs={{0,1},{1,0},{2,3},{3,2},{4,5},{5,4},{6,7},{7,6},{8,9},{9,8},{10,11... | collective-permute-start | bytes 884744 | tf_op jit(solution)/shard_map/ppermute | solution.py:36
  42.3 12.2 %collective-permute-start.10 = (bf16[3,192,256]{2,1,0:T(8,128)(2,1)S(1)}, bf16[3,192,256]{2,1,0:T(8,128)(2,1)}, u32[]{:S(2)}, u32[]{:S(2)}) collective-permute-start(bf16[3,192,256]{2,1,0:T(8,128)(2,1)S(1)} %collective-permute-done.2.refs_3_), channel_id=1, source_target_pairs={{0,1},{1,0},{2,3},{3,2},{4,5},{5,4},{6,7},{7,6},{8,9},{9,8},{10,11... | collective-permute-start | bytes 884744 | tf_op jit(solution)/shard_map/ppermute | solution.py:36
  42.8 12.9 %collective-permute-start.11 = (bf16[3,192,256]{2,1,0:T(8,128)(2,1)S(1)}, bf16[3,192,256]{2,1,0:T(8,128)(2,1)}, u32[]{:S(2)}, u32[]{:S(2)}) collective-permute-start(bf16[3,192,256]{2,1,0:T(8,128)(2,1)S(1)} %collective-permute-done.3.refs_4_), channel_id=1, source_target_pairs={{0,1},{1,0},{2,3},{3,2},{4,5},{5,4},{6,7},{7,6},{8,9},{9,8},{10,11... | collective-permute-start | bytes 884744 | tf_op jit(solution)/shard_map/ppermute | solution.py:36
  53.9 2.6 %collective-permute-start.8 = (bf16[3,192,256]{2,1,0:T(8,128)(2,1)S(1)}, bf16[3,192,256]{2,1,0:T(8,128)(2,1)S(1)}, u32[]{:S(2)}, u32[]{:S(2)}) collective-permute-start(bf16[3,192,256]{2,1,0:T(8,128)(2,1)S(1)} %collective-permute-done.refs_1_), channel_id=1, source_target_pairs={{0,1},{1,0},{2,3},{3,2},{4,5},{5,4},{6,7},{7,6},{8,9},{9,8},{10,11... | collective-permute-start | bytes 884744 | tf_op jit(solution)/shard_map/ppermute | solution.py:36
  54.0 10.4 %collective-permute-start.9 = (bf16[3,192,256]{2,1,0:T(8,128)(2,1)S(1)}, bf16[3,192,256]{2,1,0:T(8,128)(2,1)S(1)}, u32[]{:S(2)}, u32[]{:S(2)}) collective-permute-start(bf16[3,192,256]{2,1,0:T(8,128)(2,1)S(1)} %collective-permute-done.1.refs_2_), channel_id=1, source_target_pairs={{0,1},{1,0},{2,3},{3,2},{4,5},{5,4},{6,7},{7,6},{8,9},{9,8},{10,11... | collective-permute-start | bytes 884744 | tf_op jit(solution)/shard_map/ppermute | solution.py:36
  54.4 14.3 %collective-permute-start.12 = (bf16[3,192,256]{2,1,0:T(8,128)(2,1)S(1)}, bf16[3,192,256]{2,1,0:T(8,128)(2,1)S(1)}, u32[]{:S(2)}, u32[]{:S(2)}) collective-permute-start(bf16[3,192,256]{2,1,0:T(8,128)(2,1)S(1)} %collective-permute-done.4.refs_5_), channel_id=1, source_target_pairs={{0,1},{1,0},{2,3},{3,2},{4,5},{5,4},{6,7},{7,6},{8,9},{9,8},{10,11... | collective-permute-start | bytes 884744 | tf_op jit(solution)/shard_map/ppermute | solution.py:36
  54.5 16.1 %collective-permute-start.13 = (bf16[3,192,256]{2,1,0:T(8,128)(2,1)S(1)}, bf16[3,192,256]{2,1,0:T(8,128)(2,1)S(1)}, u32[]{:S(2)}, u32[]{:S(2)}) collective-permute-start(bf16[3,192,256]{2,1,0:T(8,128)(2,1)S(1)} %collective-permute-done.5.refs_6_), channel_id=1, source_target_pairs={{0,1},{1,0},{2,3},{3,2},{4,5},{5,4},{6,7},{7,6},{8,9},{9,8},{10,11... | collective-permute-start | bytes 884744 | tf_op jit(solution)/shard_map/ppermute | solution.py:36
  55.7 16.8 %collective-permute-start.14 = (bf16[3,192,256]{2,1,0:T(8,128)(2,1)}, bf16[3,192,256]{2,1,0:T(8,128)(2,1)S(1)}, u32[]{:S(2)}, u32[]{:S(2)}) collective-permute-start(bf16[3,192,256]{2,1,0:T(8,128)(2,1)} %collective-permute-done.6.refs_7_), channel_id=1, source_target_pairs={{0,1},{1,0},{2,3},{3,2},{4,5},{5,4},{6,7},{7,6},{8,9},{9,8},{10,11... | collective-permute-start | bytes 884744 | tf_op jit(solution)/shard_map/ppermute | solution.py:36
  56.5 42.9 %collective-permute-start.15 = (bf16[3,192,256]{2,1,0:T(8,128)(2,1)}, bf16[3,192,256]{2,1,0:T(8,128)(2,1)S(1)}, u32[]{:S(2)}, u32[]{:S(2)}) collective-permute-start(bf16[3,192,256]{2,1,0:T(8,128)(2,1)} %get-tuple-element.64), channel_id=1, source_target_pairs={{0,2},{1,3},{2,4},{3,5},{4,6},{5,7},{6,8},{7,9},{8,10},{9,11},{10,... | collective-permute-start | bytes 884744 | tf_op jit(solution)/shard_map/ppermute | solution.py:31
  64.3 36.7 %collective-permute-start.16 = (bf16[3,192,256]{2,1,0:T(8,128)(2,1)}, bf16[3,192,256]{2,1,0:T(8,128)(2,1)S(1)}, u32[]{:S(2)}, u32[]{:S(2)}) collective-permute-start(bf16[3,192,256]{2,1,0:T(8,128)(2,1)} %get-tuple-element.66), channel_id=1, source_target_pairs={{0,4},{1,5},{2,6},{3,7},{4,8},{5,9},{6,10},{7,11},{8,12},{9,13},{1... | collective-permute-start | bytes 884744 | tf_op jit(solution)/shard_map/ppermute | solution.py:31
  68.7 35.0 %collective-permute-start.17 = (bf16[3,192,256]{2,1,0:T(8,128)(2,1)}, bf16[3,192,256]{2,1,0:T(8,128)(2,1)S(1)}, u32[]{:S(2)}, u32[]{:S(2)}) collective-permute-start(bf16[3,192,256]{2,1,0:T(8,128)(2,1)} %get-tuple-element.68), channel_id=1, source_target_pairs={{0,6},{1,7},{2,8},{3,9},{4,10},{5,11},{6,12},{7,13},{8,14},{9,15},... | collective-permute-start | bytes 884744 | tf_op jit(solution)/shard_map/ppermute | solution.py:31
  70.6 33.4 %collective-permute-start.18 = (bf16[3,192,256]{2,1,0:T(8,128)(2,1)}, bf16[3,192,256]{2,1,0:T(8,128)(2,1)S(1)}, u32[]{:S(2)}, u32[]{:S(2)}) collective-permute-start(bf16[3,192,256]{2,1,0:T(8,128)(2,1)} %get-tuple-element.70), channel_id=1, source_target_pairs={{0,8},{1,9},{2,10},{3,11},{4,12},{5,13},{6,14},{7,15},{8,0},{9,1},... | collective-permute-start | bytes 884744 | tf_op jit(solution)/shard_map/ppermute | solution.py:31
  72.5 32.2 %collective-permute-start.19 = (bf16[3,192,256]{2,1,0:T(8,128)(2,1)}, bf16[3,192,256]{2,1,0:T(8,128)(2,1)S(1)}, u32[]{:S(2)}, u32[]{:S(2)}) collective-permute-start(bf16[3,192,256]{2,1,0:T(8,128)(2,1)} %get-tuple-element.72), channel_id=1, source_target_pairs={{0,10},{1,11},{2,12},{3,13},{4,14},{5,15},{6,0},{7,1},{8,2},{9,3},... | collective-permute-start | bytes 884744 | tf_op jit(solution)/shard_map/ppermute | solution.py:31
  99.5 34.3 %collective-permute-start.20 = (bf16[3,192,256]{2,1,0:T(8,128)(2,1)}, bf16[3,192,256]{2,1,0:T(8,128)(2,1)S(1)}, u32[]{:S(2)}, u32[]{:S(2)}) collective-permute-start(bf16[3,192,256]{2,1,0:T(8,128)(2,1)} %get-tuple-element.74), channel_id=1, source_target_pairs={{0,12},{1,13},{2,14},{3,15},{4,0},{5,1},{6,2},{7,3},{8,4},{9,5},{1... | collective-permute-start | bytes 884744 | tf_op jit(solution)/shard_map/ppermute | solution.py:31
  101.0 33.1 %collective-permute-start.21 = (bf16[3,192,256]{2,1,0:T(8,128)(2,1)}, bf16[3,192,256]{2,1,0:T(8,128)(2,1)S(1)}, u32[]{:S(2)}, u32[]{:S(2)}) collective-permute-start(bf16[3,192,256]{2,1,0:T(8,128)(2,1)} %get-tuple-element.76), channel_id=1, source_target_pairs={{0,14},{1,15},{2,0},{3,1},{4,2},{5,3},{6,4},{7,5},{8,6},{9,7},{10,... | collective-permute-start | bytes 884744 | tf_op jit(solution)/shard_map/ppermute | solution.py:31
  103.8 30.5 %collective-permute-start.22 = (bf16[3,192,256]{2,1,0:T(8,128)(2,1)S(1)}, bf16[3,192,256]{2,1,0:T(8,128)(2,1)S(1)}, u32[]{:S(2)}, u32[]{:S(2)}) collective-permute-start(bf16[3,192,256]{2,1,0:T(8,128)(2,1)S(1)} %copy-done.9), channel_id=1, source_target_pairs={{0,1},{1,0},{2,3},{3,2},{4,5},{5,4},{6,7},{7,6},{8,9},{9,8},{10,11... | collective-permute-start | bytes 884744 | tf_op jit(solution)/shard_map/ppermute | solution.py:36
  104.0 31.4 %collective-permute-start.23 = (bf16[3,192,256]{2,1,0:T(8,128)(2,1)S(1)}, bf16[3,192,256]{2,1,0:T(8,128)(2,1)}, u32[]{:S(2)}, u32[]{:S(2)}) collective-permute-start(bf16[3,192,256]{2,1,0:T(8,128)(2,1)S(1)} %collective-permute-done.15.refs_2_), channel_id=1, source_target_pairs={{0,1},{1,0},{2,3},{3,2},{4,5},{5,4},{6,7},{7,6},{8,9},{9,8},{10,11... | collective-permute-start | bytes 884744 | tf_op jit(solution)/shard_map/ppermute | solution.py:36
  105.5 30.0 %collective-permute-start.24 = (bf16[3,192,256]{2,1,0:T(8,128)(2,1)S(1)}, bf16[3,192,256]{2,1,0:T(8,128)(2,1)}, u32[]{:S(2)}, u32[]{:S(2)}) collective-permute-start(bf16[3,192,256]{2,1,0:T(8,128)(2,1)S(1)} %collective-permute-done.16.refs_3_), channel_id=1, source_target_pairs={{0,1},{1,0},{2,3},{3,2},{4,5},{5,4},{6,7},{7,6},{8,9},{9,8},{10,11... | collective-permute-start | bytes 884744 | tf_op jit(solution)/shard_map/ppermute | solution.py:36
  111.3 51.4 %all-to-all-start.1 = ((f32[16,1,768]{2,1,0:T(1,128)}), f32[16,1,768]{2,1,0:T(1,128)S(1)}, u32[]{:S(2)}, u32[]{:S(2)}) async-start(f32[16,1,768]{2,1,0:T(1,128)} %broadcast_in_dim.28), calls=%async_computation.1 | async-start | bytes 98304 | tf_op jit(solution)/shard_map/all_to_all | solution.py:746
  134.2 3.7 %collective-permute-start.26 = (bf16[3,192,256]{2,1,0:T(8,128)(2,1)}, bf16[3,192,256]{2,1,0:T(8,128)(2,1)}, u32[]{:S(2)}, u32[]{:S(2)}) collective-permute-start(bf16[3,192,256]{2,1,0:T(8,128)(2,1)} %copy-done.15), channel_id=1, source_target_pairs={{0,1},{1,0},{2,3},{3,2},{4,5},{5,4},{6,7},{7,6},{8,9},{9,8},{10,11... | collective-permute-start | bytes 884744 | tf_op jit(solution)/shard_map/ppermute | solution.py:36
  135.0 2.9 %collective-permute-start.27 = (bf16[3,192,256]{2,1,0:T(8,128)(2,1)}, bf16[3,192,256]{2,1,0:T(8,128)(2,1)}, u32[]{:S(2)}, u32[]{:S(2)}) collective-permute-start(bf16[3,192,256]{2,1,0:T(8,128)(2,1)} %copy-done.19), channel_id=1, source_target_pairs={{0,1},{1,0},{2,3},{3,2},{4,5},{5,4},{6,7},{7,6},{8,9},{9,8},{10,11... | collective-permute-start | bytes 884744 | tf_op jit(solution)/shard_map/ppermute | solution.py:36
  135.4 2.5 %collective-permute-start.28 = (bf16[3,192,256]{2,1,0:T(8,128)(2,1)S(1)}, bf16[3,192,256]{2,1,0:T(8,128)(2,1)}, u32[]{:S(2)}, u32[]{:S(2)}) collective-permute-start(bf16[3,192,256]{2,1,0:T(8,128)(2,1)S(1)} %collective-permute-done.20.refs_7_), channel_id=1, source_target_pairs={{0,1},{1,0},{2,3},{3,2},{4,5},{5,4},{6,7},{7,6},{8,9},{9,8},{10,11... | collective-permute-start | bytes 884744 | tf_op jit(solution)/shard_map/ppermute | solution.py:36
  136.0 39.0 %collective-permute-start.30 = (f32[64,192]{1,0:T(8,128)S(1)}, f32[64,192]{1,0:T(8,128)S(1)}, u32[]{:S(2)}, u32[]{:S(2)}) collective-permute-start(f32[64,192]{1,0:T(8,128)S(1)} %bitcast.31), channel_id=1, source_target_pairs={{0,2},{1,3},{2,4},{3,5},{4,6},{5,7},{6,8},{7,9},{8,10},{9,11},{10,... | collective-permute-start | bytes 147464 | tf_op jit(solution)/shard_map/ppermute | solution.py:31
  162.7 19.2 %all-to-all-start = ((bf16[8,224,128]{2,1,0:T(8,128)(2,1)}), bf16[8,224,128]{2,1,0:T(8,128)(2,1)S(1)}, u32[]{:S(2)}, u32[]{:S(2)}) async-start(bf16[8,224,128]{2,1,0:T(8,128)(2,1)} %attend.3), calls=%async_computation | async-start | bytes 917504 | tf_op jit(solution)/shard_map/all_to_all | solution.py:777
  208.4 11.2 %all-to-all-start.2 = ((f32[16,2,768]{2,1,0:T(2,128)}), f32[16,2,768]{2,1,0:T(2,128)S(1)}, u32[]{:S(2)}, u32[]{:S(2)}) async-start(f32[16,2,768]{2,1,0:T(2,128)} %copy-done.5), calls=%async_computation.2 | async-start | bytes 196608 | tf_op jit(solution)/shard_map/all_to_all | solution.py:808
  (38 other events, 416.0 us)
